TPU v7x, 128 devices: a whole 4x4x4 slice. The times are simulated.
128 devices in a mesh: dp: 4 (over x_lo, core), expert: 32 (over y, z, x_hi).
Axes of the slice: x: 4 (x_hi: 2, x_lo: 2; x = x_hi * 2 + x_lo), y: 4, z: 4, core: 2. Of those that a mesh axis runs over, the one named last changes fastest.
Arguments:
- tokens: bfloat16 [16384, 3584], P(('dp', 'expert')), may hold values from -6 to 6
- cotangent: bfloat16 [16384, 3584], P(('dp', 'expert')), may hold values from -6 to 6
- expert_ids: int32 [16384, 2], P(('dp', 'expert')), may hold values from 0 to 31, all different within a row; in each aligned block of 128 rows (0 to 127, 128 to 255, ...) at most 12 rows name the same one
- combine: float32 [16384, 2], P(('dp', 'expert')), may hold values from 0.2 to 1
- slot_expert: int32 [32], replicated, may hold values from 0 to 31, each once
- swap_flag: int32 [32], replicated, may hold values from 0 to 1, as said below
- w_gate_up: bfloat16 [32, 2, 3584, 1024], P('expert', None, None, 'dp'), may hold values from -0.09375 to 0.09375
- w_down: bfloat16 [32, 1024, 3584], P('expert', 'dp'), may hold values from -0.1875 to 0.1875
- first_gate_up: bfloat16 [32, 2, 3584, 1024], P('expert', None, None, 'dp'), may hold values from -9 to 9
- first_down: bfloat16 [32, 1024, 3584], P('expert', 'dp'), may hold values from -9 to 9
- second_gate_up: bfloat16 [32, 2, 3584, 1024], P('expert', None, None, 'dp'), may hold values from 1 to 100
- second_down: bfloat16 [32, 1024, 3584], P('expert', 'dp'), may hold values from 1 to 100
Outputs:
- step_gate_up: bfloat16 [32, 2, 3584, 1024], P('expert', None, None, 'dp')
- step_down: bfloat16 [32, 1024, 3584], P('expert', 'dp')
Inputs may be any that keep to these rules, and one draw needn't show every extreme that they name: `expert_ids`: among the routes of the rows of one device, no expert is named more than 12 times, and in every draw some device names some expert exactly 12 times. `slot_expert`: each expert once. `swap_flag`: entry k equals entry (k + 16) mod 32; entry 31 is always 1.
All inputs are finite; a program needn't handle non-finite values.
Results may differ from a plain program's by a relative error of at most 0.0087.
Values may be sent and summed in bfloat16 or wider, within the bound.
No kernel may reach another device: no remote copies, remote signals or barrier semaphores. Data moves between devices by JAX's collectives and lax.ppermute only.
A program may use at most 192 MiB of HBM per device.

v0:
```python
import jax
import jax.numpy as jnp
from jax import lax
from jax.sharding import PartitionSpec as P


def partner(value, axis, apart):
    mask = 2**apart
    pairs = [(source, source ^ mask) for source in range(lax.axis_size(axis))]
    return lax.ppermute(value, axis, pairs)


def side_by_side(arrays, axis, split_dim, concat_dim, along):
    both = jnp.concatenate(arrays, axis=along)
    result, at, finished = (
        lax.all_to_all(both, axis, split_axis=split_dim, concat_axis=concat_dim, tiled=True),
        0,
        [],
    )
    for a in arrays:
        finished.append(lax.slice_in_dim(result, at, at + a.shape[along], axis=along))
        at += a.shape[along]
    return tuple(finished)


def side_by_side_2(arrays, axis, dim, along):
    widths = [a.shape[along] for a in arrays]
    both = jnp.concatenate(arrays, axis=along)
    result = lax.all_gather(both, axis, axis=dim, tiled=True)
    return tuple(jnp.split(result, [sum(widths[:k]) for k in range(1, len(widths))], axis=along))


def slot_owner(slot_expert, swap_flag):
    experts = slot_expert.shape[0]
    slot_ids = jnp.arange(experts, dtype=jnp.int32)
    moved_expert = jnp.where(swap_flag == 1, jnp.roll(slot_expert, -(experts // 2)), slot_expert)
    owner_slot = jnp.sum(
        jnp.where(moved_expert[:, None] == slot_ids[None, :], slot_ids[:, None], 0), axis=0
    )
    return owner_slot


def adam_step(gradient, first_moment, second_moment):
    first_new = 0.9 * first_moment.astype(jnp.float32) + 0.1 * gradient
    second_new = 0.95 * second_moment.astype(jnp.float32) + 0.05 * gradient * gradient
    return (first_new / (jnp.sqrt(second_new) + 1e-08)).astype(jnp.bfloat16)


def contract_rows(left, right):
    return lax.dot_general(
        left, right, (((0,), (0,)), ((), ())), preferred_element_type=jnp.float32
    )


def expert_step(
    rows, grads_in, gate_up, down, gate_up_first, down_first, gate_up_second, down_second
):
    gate_pre = jnp.dot(rows, gate_up[0], preferred_element_type=jnp.float32)
    up_pre = jnp.dot(rows, gate_up[1], preferred_element_type=jnp.float32)
    sigmoid_gate = jax.nn.sigmoid(gate_pre)
    silu_gate = gate_pre * sigmoid_gate
    hidden = (silu_gate * up_pre).astype(jnp.bfloat16)
    down_grad = contract_rows(hidden, grads_in)
    hidden_grad = lax.dot_general(
        grads_in, down, (((1,), (1,)), ((), ())), preferred_element_type=jnp.float32
    )
    gate_back = (
        hidden_grad * up_pre * sigmoid_gate * (1.0 + gate_pre * (1.0 - sigmoid_gate))
    ).astype(jnp.bfloat16)
    up_back = (hidden_grad * silu_gate).astype(jnp.bfloat16)
    gate_up_grad = jnp.stack([contract_rows(rows, gate_back), contract_rows(rows, up_back)])
    return (
        adam_step(gate_up_grad, gate_up_first, gate_up_second),
        adam_step(down_grad, down_first, down_second),
    )


def local(
    tokens,
    cotangent,
    expert_ids,
    combine,
    slot_expert,
    swap_flag,
    w_gate_up,
    w_down,
    first_gate_up,
    first_down,
    second_gate_up,
    second_down,
):
    experts = lax.axis_size("expert")
    partner_bit = experts.bit_length() - 2
    my_slot = lax.axis_index("expert")
    swapping = swap_flag[my_slot] == 1

    def relocate(resident):
        partner_copy = partner(resident, "expert", partner_bit)
        return jnp.where(swapping, partner_copy, resident)

    gate_up = relocate(w_gate_up)
    down = relocate(w_down)
    gate_up_first = relocate(first_gate_up)
    down_first = relocate(first_down)
    gate_up_second = relocate(second_gate_up)
    down_second = relocate(second_down)
    owner_slot = slot_owner(slot_expert, swap_flag)
    tok_count = tokens.shape[0]
    top_count = expert_ids.shape[1]
    model_width = tokens.shape[1]
    capacity = 3 * tok_count * top_count // (2 * experts)
    slot_ids = jnp.arange(experts, dtype=jnp.int32)
    expert_hits = expert_ids[:, :, None] == slot_ids[None, None, :]
    route_slot = jnp.sum(jnp.where(expert_hits, owner_slot[None, None, :], 0), axis=2).reshape(-1)
    slot_hits = (route_slot[:, None] == slot_ids[None, :]).astype(jnp.int32)
    position = jnp.sum(jnp.cumsum(slot_hits, axis=0) * slot_hits, axis=1) - 1
    route_count = route_slot.shape[0]
    slot_table = (
        jnp.full((experts * capacity,), -1, jnp.int32)
        .at[route_slot * capacity + position]
        .set(jnp.arange(route_count, dtype=jnp.int32))
    )
    filled = (slot_table >= 0)[:, None]
    clipped = jnp.maximum(slot_table, 0)
    token_row = clipped // top_count
    sent_rows = jnp.where(filled, tokens[token_row], jnp.zeros((), tokens.dtype)).reshape(
        experts, capacity, model_width
    )
    scaled = cotangent[token_row].astype(jnp.float32) * combine.reshape(-1)[clipped][:, None]
    sent_grads = (
        jnp.where(filled, scaled, 0.0).astype(jnp.bfloat16).reshape(experts, capacity, model_width)
    )
    owner_rows, owner_grads = side_by_side((sent_rows, sent_grads), "expert", 0, 0, 1)
    rows_in, grads_in = side_by_side_2((owner_rows, owner_grads), "dp", 0, 1)
    rows_in = rows_in.reshape(-1, model_width)
    grads_in = grads_in.reshape(-1, model_width)
    step_gate_up, step_down = expert_step(
        rows_in,
        grads_in,
        gate_up[0],
        down[0],
        gate_up_first[0],
        down_first[0],
        gate_up_second[0],
        down_second[0],
    )
    step_gate_up = step_gate_up[None]
    step_down = step_down[None]
    return (step_gate_up, step_down)


def solution(mesh):
    return jax.shard_map(
        local,
        mesh=mesh,
        in_specs=(
            P(("dp", "expert"), None),
            P(("dp", "expert"), None),
            P(("dp", "expert"), None),
            P(("dp", "expert"), None),
            P(),
            P(),
            P("expert", None, None, "dp"),
            P("expert", "dp", None),
            P("expert", None, None, "dp"),
            P("expert", "dp", None),
            P("expert", None, None, "dp"),
            P("expert", "dp", None),
        ),
        out_specs=(P("expert", None, None, "dp"), P("expert", "dp", None)),
        check_vma=False,
    )
```

profile of v0, /device:TPU:64, one launch (start us, length us, event | category | flops | bytes accessed | tf_op | source)
XLA Modules:
  0.0 494.4 jit_solution(18193114692149629419)
XLA Ops:
  7.2 0.0 copy-start
  7.2 0.0 all-gather.2.cloned.1.call-start
  7.2 0.8 fusion.32
  8.0 0.7 compare_select_fusion.2
  8.8 0.1 select_reduce_fusion.1
  8.9 0.8 select_reduce_fusion
  9.6 0.1 copy.22
  9.8 0.1 eq.77
  9.9 0.1 eq.73
  10.1 0.6 reduce-window.6
  10.7 0.2 slice_reduce_fusion
  10.9 0.1 fusion.23
  11.0 0.1 copy.21
  11.1 0.1 mul.138
  11.3 1.4 scatter_custom_fusion
  12.7 0.0 copy-done
  12.7 3.9 gather_fusion.1
  16.6 5.8 %reshape.190 = f32[32,12,3584]{2,1,0:T(8,128)} reshape(bf16[384,3584]{1,0:T(8,128)(2,1)} %gather_fusion.1) | data formatting | bytes 8257536 | tf_op jit(solution)/shard_map/convert_element_type | solution.py:129
  22.4 0.0 copy-done.9
  22.4 0.1 copy.25
  22.5 0.1 reshape.187
  22.6 2.8 gather_fusion.2
  25.5 0.1 mul.140
  25.6 0.1 broadcast_in_dim.77
  25.7 3.9 gather_fusion
  29.5 5.3 %gather.12 = bf16[32,12,3584]{2,1,0:T(8,128)(2,1)} reshape(bf16[384,3584]{1,0:T(8,128)(2,1)} %gather_fusion) | data formatting | bytes 5505024 | tf_op jit(solution)/shard_map/gather | solution.py:126
  34.8 2.5 broadcast_select_fusion
  37.3 1.7 copy-done.3
  39.0 3.3 select_convert_fusion
  42.3 3.6 pad_maximum_fusion.1
  45.9 75.2 %all_to_all.5 = bf16[32,24,3584]{2,1,0:T(8,128)(2,1)} all-to-all(bf16[32,24,3584]{2,1,0:T(8,128)(2,1)S(1)} %pad_maximum_fusion.1), channel_id=1, replica_groups=mesh['dp'=4,'expert'=32] {'expert'}, dimensions={0} | all-to-all | bytes 11010048 | tf_op jit(solution)/shard_map/all_to_all | solution.py:16
  121.1 0.0 all-gather.2.cloned.1.call-update
  121.1 1.4 collective-permute-start.2
  122.5 2.2 collective-permute-start.4
  124.7 1.3 collective-permute-start.5
  126.0 2.2 collective-permute-start.1
  128.3 1.3 collective-permute-start
  129.6 0.6 dynamic_slice.3
  130.8 74.4 %collective-permute-done.2 = bf16[1,2,3584,256]{3,2,1,0:T(8,128)(2,1)} collective-permute-done((bf16[1,2,3584,256]{3,2,1,0:T(8,128)(2,1)}, bf16[1,2,3584,256]{3,2,1,0:T(8,128)(2,1)}, u32[]{:S(2)}, u32[]{:S(2)}) %collective-permute-start.2) | collective-permute-done | bytes 3670048 | tf_op jit(solution)/shard_map/ppermute | solution.py:10
  205.2 1.3 collective-permute-start.3
  206.5 4.3 broadcast_select_fusion.1
  210.8 104.1 %all-gather.2.cloned.1.call-done = bf16[128,24,3584]{2,1,0:T(8,128)(2,1)} async-done(((bf16[32,24,3584]{2,1,0:T(8,128)(2,1)}), bf16[128,24,3584]{2,1,0:T(8,128)(2,1)}) %all-gather.2.cloned.1.call-update) | async-done | bytes 22020112 | tf_op jit(solution)/shard_map/all_gather | solution.py:29
  314.9 24.3 %fusion.31 = (bf16[128,12,3584]{2,1,0:T(8,128)(2,1)}, bf16[128,12,3584]{2,1,0:T(8,128)(2,1)}) fusion(bf16[128,24,3584]{2,1,0:T(8,128)(2,1)} %all-gather.2.cloned.1.call-done), kind=kLoop, calls=%fused_computation.70 | loop fusion | bytes 44040192 | tf_op jit(solution)/shard_map/split | solution.py:30
  339.1 17.2 %reshape.188 = bf16[1536,3584]{1,0:T(8,128)(2,1)} reshape(bf16[128,12,3584]{2,1,0:T(8,128)(2,1)} %get-tuple-element.3) | data formatting | bytes 22020096 | tf_op jit(solution)/shard_map/reshape | solution.py:135
  356.3 17.1 %reshape.189 = bf16[1536,3584]{1,0:T(8,128)(2,1)} reshape(bf16[128,12,3584]{2,1,0:T(8,128)(2,1)} %get-tuple-element.2) | data formatting | bytes 22020096 | tf_op jit(solution)/shard_map/reshape | solution.py:136
  373.4 6.5 %fusion.10 = f32[1536,256]{1,0:T(8,128)S(1)} fusion(bf16[1536,3584]{1,0:T(8,128)(2,1)} %reshape.188, bf16[1,2,3584,256]{3,2,1,0:T(8,128)(2,1)} %broadcast_select_fusion.1), kind=kOutput, calls=%fused_computation.25 | convolution fusion | flops 2818572288 | bytes 14417920 | tf_op jit(solution)/shard_map/dot_general | solution.py:58
  379.9 0.0 copy-start.13
  379.9 0.0 slice-start.2
  379.9 0.0 collective-permute-done.1
  380.0 1.9 copy-done.4
  381.8 5.6 %fusion.12 = f32[1536,256]{1,0:T(8,128)S(1)} fusion(bf16[1536,3584]{1,0:T(8,128)(2,1)S(1)} %copy-done.4, bf16[1,256,3584]{2,1,0:T(8,128)(2,1)} %collective-permute-done.1, bf16[1,256,3584]{2,1,0:T(8,128)(2,1)S(1)} %copy-done.11, pred[]{:T(512)} %bitcast), kind=kOutput, calls=%fused_computation.28 | convolution fusion | flops 2819489792 | bytes 16252929 | tf_op jit(solution)/shard_map/dot_general | solution.py:64
  387.5 0.0 copy-start.5
  387.5 5.1 %convolution_bitcast_fusion = f32[1,1,3584,256]{3,2,1,0:T(8,128)} fusion(bf16[1536,3584]{1,0:T(8,128)(2,1)S(1)} %bitcast.54, f32[1536,256]{1,0:T(8,128)S(1)} %fusion.12, f32[1536,256]{1,0:T(8,128)S(1)} %fusion.10), kind=kOutput, calls=%fused_computation.14 | convolution fusion | flops 2820931584 | bytes 17825792 | tf_op jit(solution)/shard_map/dot_general | solution.py:50
  392.6 3.2 fusion.11
  395.8 0.0 copy-start.14
  395.8 0.0 copy-start.12
  395.8 5.1 %convolution_bitcast_fusion.1 = f32[1,1,3584,256]{3,2,1,0:T(8,128)} fusion(bf16[1536,3584]{1,0:T(8,128)(2,1)S(1)} %bitcast.54, f32[1536,256]{1,0:T(8,128)S(1)} %fusion.10, f32[1536,256]{1,0:T(8,128)S(1)} %fusion.12, f32[1536,256]{1,0:T(8,128)S(1)} %fusion.11), kind=kOutput, calls=%fused_computation.15 | convolution fusion | flops 2822504448 | bytes 19398656 | tf_op jit(solution)/shard_map/dot_general | solution.py:50
  401.0 0.0 collective-permute-done.4
  401.0 0.0 collective-permute-done.5
  401.0 9.5 %fusion.16 = bf16[1,256,3584]{2,1,0:T(8,128)(2,1)} fusion(bf16[1,256,3584]{2,1,0:T(8,128)(2,1)} %collective-permute-done.5, bf16[1,256,3584]{2,1,0:T(8,128)(2,1)S(1)} %copy-done.12, bf16[1,256,3584]{2,1,0:T(8,128)(2,1)} %collective-permute-done.4, bf16[1,256,3584]{2,1,0:T(8,128)(2,1)} %param.21, pred[]{:T(512)} %bitcast, ...), kind=kOutput, calls=%fused_computation.32 | convolution fusion | flops 2833776640 | bytes 23330816 | tf_op jit(solution)/shard_map/dot_general | solution.py:50
  410.5 0.0 collective-permute-done
  410.5 67.5 %collective-permute-done.3 = bf16[1,2,3584,256]{3,2,1,0:T(8,128)(2,1)} collective-permute-done((bf16[1,2,3584,256]{3,2,1,0:T(8,128)(2,1)}, bf16[1,2,3584,256]{3,2,1,0:T(8,128)(2,1)}, u32[]{:S(2)}, u32[]{:S(2)}) %collective-permute-start.3) | collective-permute-done | bytes 3670048 | tf_op jit(solution)/shard_map/ppermute | solution.py:10
  478.0 0.0 copy-start.1
  478.0 9.5 %fusion.4 = bf16[1,2,3584,256]{3,2,1,0:T(8,128)(2,1)} fusion(f32[1,1,3584,256]{3,2,1,0:T(8,128)S(1)} %copy-done.8, f32[1,1,3584,256]{3,2,1,0:T(8,128)} %convolution_bitcast_fusion.1, bf16[1,2,3584,256]{3,2,1,0:T(8,128)(2,1)} %collective-permute-done.3, bf16[1,2,3584,256]{3,2,1,0:T(8,128)(2,1)S(1)} %copy-done.6, ...), kind=kLoop, calls=%fused_computation.11 | loop fusion | flops 27525120 | bytes 25690112 | tf_op jit(solution)/shard_map/convert_element_type | solution.py:46
  (36 shorter events, 0.1 us)
Async XLA Ops:
  7.2 5.6 %copy-start = (bf16[128,3584]{1,0:T(8,128)(2,1)S(1)}, bf16[128,3584]{1,0:T(8,128)(2,1)}, u32[]{:S(2)}) copy-start(bf16[128,3584]{1,0:T(8,128)(2,1)} %param.13) | copy-start | bytes 2752516
  7.2 307.7 %all-gather.2.cloned.1.call-start = ((), (), s32[]{:S(2)}) async-start(), calls=%async_computation.1 | async-start | bytes 27525120 | tf_op jit(solution)/shard_map/all_gather | solution.py:29
  16.6 5.8 %copy-start.9 = (f32[128,2]{0,1:T(2,128)S(1)}, f32[128,2]{0,1:T(2,128)}, u32[]{:S(2)}) copy-start(f32[128,2]{0,1:T(2,128)} %param.15) | copy-start | bytes 3076
  16.6 9.1 %copy-start.2 = (bf16[128,3584]{1,0:T(8,128)(2,1)S(1)}, bf16[128,3584]{1,0:T(8,128)(2,1)}, u32[]{:S(2)}) copy-start(bf16[128,3584]{1,0:T(8,128)(2,1)} %param.12) | copy-start | bytes 2752516
  34.8 4.2 copy-start.3
  121.1 4.9 copy-start.11
  121.1 8.5 %copy-start.10 = (s32[32]{0:T(128)S(1)}, s32[32]{0:T(128)}, u32[]{:S(2)}) copy-start(s32[32]{0:T(128)} %param.17) | copy-start | bytes 388
  121.1 84.1 %collective-permute-start.2 = (bf16[1,2,3584,256]{3,2,1,0:T(8,128)(2,1)}, bf16[1,2,3584,256]{3,2,1,0:T(8,128)(2,1)}, u32[]{:S(2)}, u32[]{:S(2)}) collective-permute-start(bf16[1,2,3584,256]{3,2,1,0:T(8,128)(2,1)} %param.18), channel_id=1, source_target_pairs={{0,16},{1,17},{2,18},{3,19},{4,20},{5,21},{6,22},{7,23},{8,24},{9,... | collective-permute-start | bytes 11010056 | tf_op jit(solution)/shard_map/ppermute | solution.py:10
  122.5 278.5 %collective-permute-start.4 = (bf16[1,256,3584]{2,1,0:T(8,128)(2,1)}, bf16[1,256,3584]{2,1,0:T(8,128)(2,1)}, u32[]{:S(2)}, u32[]{:S(2)}) collective-permute-start(bf16[1,256,3584]{2,1,0:T(8,128)(2,1)} %param.21), channel_id=1, source_target_pairs={{0,16},{1,17},{2,18},{3,19},{4,20},{5,21},{6,22},{7,23},{8,24},{9,... | collective-permute-start | bytes 5505032 | tf_op jit(solution)/shard_map/ppermute | solution.py:10
  124.7 276.2 %collective-permute-start.5 = (bf16[1,256,3584]{2,1,0:T(8,128)(2,1)}, bf16[1,256,3584]{2,1,0:T(8,128)(2,1)}, u32[]{:S(2)}, u32[]{:S(2)}) collective-permute-start(bf16[1,256,3584]{2,1,0:T(8,128)(2,1)} %param.23), channel_id=1, source_target_pairs={{0,16},{1,17},{2,18},{3,19},{4,20},{5,21},{6,22},{7,23},{8,24},{9,... | collective-permute-start | bytes 5505032 | tf_op jit(solution)/shard_map/ppermute | solution.py:10
  126.0 253.9 %collective-permute-start.1 = (bf16[1,256,3584]{2,1,0:T(8,128)(2,1)S(1)}, bf16[1,256,3584]{2,1,0:T(8,128)(2,1)}, u32[]{:S(2)}, u32[]{:S(2)}) collective-permute-start(bf16[1,256,3584]{2,1,0:T(8,128)(2,1)S(1)} %copy-done.11), channel_id=1, source_target_pairs={{0,16},{1,17},{2,18},{3,19},{4,20},{5,21},{6,22},{7,23},{8,24},{9,... | collective-permute-start | bytes 5505032 | tf_op jit(solution)/shard_map/ppermute | solution.py:10
  128.3 282.2 %collective-permute-start = (bf16[1,2,3584,256]{3,2,1,0:T(8,128)(2,1)}, bf16[1,2,3584,256]{3,2,1,0:T(8,128)(2,1)}, u32[]{:S(2)}, u32[]{:S(2)}) collective-permute-start(bf16[1,2,3584,256]{3,2,1,0:T(8,128)(2,1)} %param.20), channel_id=1, source_target_pairs={{0,16},{1,17},{2,18},{3,19},{4,20},{5,21},{6,22},{7,23},{8,24},{9,... | collective-permute-start | bytes 11010056 | tf_op jit(solution)/shard_map/ppermute | solution.py:10
  205.2 272.8 %collective-permute-start.3 = (bf16[1,2,3584,256]{3,2,1,0:T(8,128)(2,1)}, bf16[1,2,3584,256]{3,2,1,0:T(8,128)(2,1)}, u32[]{:S(2)}, u32[]{:S(2)}) collective-permute-start(bf16[1,2,3584,256]{3,2,1,0:T(8,128)(2,1)} %param.22), channel_id=1, source_target_pairs={{0,16},{1,17},{2,18},{3,19},{4,20},{5,21},{6,22},{7,23},{8,24},{9,... | collective-permute-start | bytes 11010056 | tf_op jit(solution)/shard_map/ppermute | solution.py:10
  373.4 8.4 %copy-start.4 = (bf16[1536,3584]{1,0:T(8,128)(2,1)S(1)}, bf16[1536,3584]{1,0:T(8,128)(2,1)}, u32[]{:S(2)}) copy-start(bf16[1536,3584]{1,0:T(8,128)(2,1)} %reshape.189) | copy-start | bytes 33030148
  373.4 14.0 %slice-start = ((s8[11010048]{0:T(1024)(128)(4,1)}), s8[4194304]{0:T(1024)(128)(4,1)S(1)}, s32[]{:S(2)}) async-start(s8[11010048]{0:T(1024)(128)(4,1)} %bitcast.53), calls=%async_computation.2 | async-start | bytes 8388608
  373.4 14.0 %slice-start.1 = ((s8[11010048]{0:T(1024)(128)(4,1)}), s8[4194304]{0:T(1024)(128)(4,1)S(1)}, s32[]{:S(2)}) async-start(s8[11010048]{0:T(1024)(128)(4,1)} %bitcast.53), calls=%async_computation.3 | async-start | bytes 8388608
  379.9 15.9 %copy-start.13 = (f32[1536,256]{1,0:T(8,128)}, f32[1536,256]{1,0:T(8,128)S(1)}, u32[]{:S(2)}) copy-start(f32[1536,256]{1,0:T(8,128)S(1)} %fusion.10) | copy-start | bytes 4718596
  379.9 7.5 %slice-start.2 = ((s8[11010048]{0:T(1024)(128)(4,1)}), s8[2621440]{0:T(1024)(128)(4,1)S(1)}, s32[]{:S(2)}) async-start(s8[11010048]{0:T(1024)(128)(4,1)} %bitcast.53), calls=%async_computation.4 | async-start | bytes 5242880
  387.5 5.1 %copy-start.5 = (bf16[1,2,3584,256]{3,2,1,0:T(8,128)(2,1)S(1)}, bf16[1,2,3584,256]{3,2,1,0:T(8,128)(2,1)}, u32[]{:S(2)}) copy-start(bf16[1,2,3584,256]{3,2,1,0:T(8,128)(2,1)} %broadcast_select_fusion.1) | copy-start | bytes 11010052
  395.8 5.2 %copy-start.14 = (f32[1536,256]{1,0:T(8,128)}, f32[1536,256]{1,0:T(8,128)S(1)}, u32[]{:S(2)}) copy-start(f32[1536,256]{1,0:T(8,128)S(1)} %fusion.11) | copy-start | bytes 4718596
  395.8 5.2 %copy-start.12 = (bf16[1,256,3584]{2,1,0:T(8,128)(2,1)S(1)}, bf16[1,256,3584]{2,1,0:T(8,128)(2,1)}, u32[]{:S(2)}) copy-start(bf16[1,256,3584]{2,1,0:T(8,128)(2,1)} %param.23) | copy-start | bytes 5505028
  400.9 77.1 %copy-start.6 = (bf16[1,2,3584,256]{3,2,1,0:T(8,128)(2,1)S(1)}, bf16[1,2,3584,256]{3,2,1,0:T(8,128)(2,1)}, u32[]{:S(2)}) copy-start(bf16[1,2,3584,256]{3,2,1,0:T(8,128)(2,1)} %param.22) | copy-start | bytes 11010052
  400.9 77.1 %copy-start.7 = (bf16[1,2,3584,256]{3,2,1,0:T(8,128)(2,1)S(1)}, bf16[1,2,3584,256]{3,2,1,0:T(8,128)(2,1)}, u32[]{:S(2)}) copy-start(bf16[1,2,3584,256]{3,2,1,0:T(8,128)(2,1)} %param.20) | copy-start | bytes 11010052
  400.9 77.1 %copy-start.8 = (f32[1,1,3584,256]{3,2,1,0:T(8,128)S(1)}, f32[1,1,3584,256]{3,2,1,0:T(8,128)}, u32[]{:S(2)}) copy-start(f32[1,1,3584,256]{3,2,1,0:T(8,128)} %convolution_bitcast_fusion) | copy-start | bytes 11010052
  478.0 9.5 %copy-start.1 = (bf16[128,3584]{1,0:T(8,128)(2,1)S(1)}, bf16[128,3584]{1,0:T(8,128)(2,1)}, u32[]{:S(2)}) copy-start(bf16[128,3584]{1,0:T(8,128)(2,1)} %param.13) | copy-start | bytes 2752516
Sparse Core Ops, SparseCore 0:
  121.2 193.5 all-gather.1
where the time goes:
time: 498 us; the launch traced here: 494 us
  waiting for transfers between devices  246 us (49%)
  local copies, waits for them, and re-layouts  87.9 us (18%)
  blocking collectives  75.2 us (15%)
  matrix products  35 us (7%)
  other arithmetic  25.5 us (5%)
  between operations  15 us (3%)
  starting transfers between devices  9.75 us (2%)
    ppermute x6, waiting for transfers between devices, partner(): return lax.ppermute(value, axis, pairs)  142 us
    all_gather x1, waiting for transfers between devices, side_by_side_2(): result = lax.all_gather(both, axis, axis=dim, tiled=True)  104 us
    all_to_all x1, blocking collectives, side_by_side(): lax.all_to_all(both, axis, split_axis=split_dim, concat_axis=concat_dim,...  75.2 us
    split x1, local copies, waits for them, and re-layouts, side_by_side_2(): jnp.split(result, [sum(widths[:k]) for k in range(1, len(widths))], axis=...  24.3 us
    dot_general x3, matrix products, contract_rows(): lax.dot_general(left, right, (((0,), (0,)), ((), ())), preferred_element_...  19.7 us
    reshape x1, local copies, waits for them, and re-layouts, local(): rows_in = rows_in.reshape(-1, model_width)  17.2 us
    reshape x1, local copies, waits for them, and re-layouts, local(): grads_in = grads_in.reshape(-1, model_width)  17.1 us
  transfers between devices with their start and end apart: 7, of which 3 were waited for; matrix products, arithmetic and copies ran while one was open for 20% of the time, Pallas kernels for 0%

commit v1 on v0

v1 whole, which is shorter than its diff:
```python
import functools

import jax
import jax.numpy as jnp
from jax import lax
from jax.experimental import pallas as pl
from jax.experimental.pallas import tpu as pltpu
from jax.sharding import PartitionSpec as P

INTERPRET = False
AXES = ("dp", "expert")
YZ = 16
CAP = 12
PAIR = 2 * CAP
F32 = jnp.float32
BF16 = jnp.bfloat16
VMEM_LIMIT = 48 * 1024 * 1024


def device_id(xl, c, yz, xh):
    return ((xl * 2 + c) * YZ + yz) * 2 + xh


def send(value, target):
    pairs = []
    for xl in range(2):
        for c in range(2):
            for yz in range(YZ):
                for xh in range(2):
                    goal = target(xl, c, yz, xh)
                    if goal is not None:
                        pairs.append((device_id(xl, c, yz, xh), device_id(*goal)))
    return lax.ppermute(value, AXES, pairs)


def to_core(xl, c, yz, xh):
    return (xl, 1 - c, yz, xh)


def to_swap(xl, c, yz, xh):
    return (xl, c, yz ^ (YZ // 2), xh)


def token_1(xl, c, yz, xh):
    return None if c == xh else (1 - xl, 1 - c, yz, 1 - xh)


def token_2(xl, c, yz, xh):
    return (1 - xl, c, yz, 1 - xh) if c == xh else (xl, 1 - c, yz, xh)


def token_3(xl, c, yz, xh):
    return (1 - xl, c, yz, xh) if c == xh else (xl, 1 - c, yz, 1 - xh)


def token_4(xl, c, yz, xh):
    return (xl, c, yz, 1 - xh) if c == xh else (1 - xl, 1 - c, yz, xh)


def grad_12(xl, c, yz, xh):
    return (1 - xl, c, yz, xh) if c == xh else (1 - xl, 1 - c, yz, 1 - xh)


def grad_3(xl, c, yz, xh):
    return None if c == xh else (xl, 1 - c, yz, 1 - xh)


def over_yz(value):
    groups = [[yz * 2 + xh for yz in range(YZ)] for xh in range(2)]
    return lax.all_to_all(value, "expert", 0, 0, axis_index_groups=groups, tiled=True)


def params(count=1):
    return pltpu.CompilerParams(
        dimension_semantics=("arbitrary",) * count, vmem_limit_bytes=VMEM_LIMIT
    )


def cost(flops, size):
    return pl.CostEstimate(flops=int(flops), bytes_accessed=int(size), transcendentals=0)


def row_select(side, slots_ref, small_refs):
    rows = YZ * PAIR
    tokens = small_refs[0].shape[1]
    row = lax.broadcasted_iota(jnp.int32, (rows, 1), 0).astype(F32)
    twelve = jnp.floor((row + 0.5) * (1.0 / CAP))
    place = row - twelve * CAP
    dest = jnp.floor((twelve + 0.5) * 0.5)
    block = twelve - dest * 2
    slots = slots_ref[...].astype(F32)
    lane = lax.broadcasted_iota(jnp.int32, (rows, slots.shape[1]), 1).astype(F32)
    named = jnp.sum(
        jnp.where(lane == dest * 2 + side.astype(F32), slots, 0.0), axis=1, keepdims=True
    )
    before = lax.broadcasted_iota(jnp.int32, (tokens, tokens), 0)
    after = lax.broadcasted_iota(jnp.int32, (tokens, tokens), 1)
    earlier = jnp.where(before < after, 1.0, 0.0).astype(BF16)
    picks, weight = [], jnp.zeros((rows, 1), F32)
    for b, small in enumerate(small_refs):
        first = small[0:1, :] == named
        second = small[1:2, :] == named
        hit = jnp.where(first, 1.0, jnp.where(second, 1.0, 0.0))
        position = jnp.dot(hit.astype(BF16), earlier, preferred_element_type=F32)
        wanted = jnp.where(block == float(b), place, -1.0)
        pick = jnp.where(position == wanted, hit, 0.0)
        share = jnp.where(first, small[2:3, :], small[3:4, :])
        weight = weight + jnp.sum(pick * share, axis=1, keepdims=True)
        picks.append(pick.astype(BF16))
    return picks, weight


def grads_kernel(side, slots, small_a, small_b, data_a, data_b, out, picks, weights):
    @pl.when(pl.program_id(0) == 0)
    def _():
        found, weight = row_select(side[0], slots, (small_a, small_b))
        picks[0] = found[0]
        picks[1] = found[1]
        weights[...] = weight

    rows = jnp.dot(picks[0], data_a[...], preferred_element_type=F32)
    rows = rows + jnp.dot(picks[1], data_b[...], preferred_element_type=F32)
    rows = (rows * weights[...]).astype(BF16)
    for yz in range(YZ):
        out[yz] = rows[yz * PAIR : (yz + 1) * PAIR]


def tokens_kernel(
    side, slots, sa, sb, sc, sd, own, data_a, data_b, data_c, data_d, out, picks
):
    @pl.when(pl.program_id(0) == 0)
    def _():
        for group, smalls in enumerate(((sa, sb), (sc, sd))):
            found, _ = row_select(side[0], slots, smalls)
            picks[2 * group] = found[0]
            picks[2 * group + 1] = found[1]

    first = jnp.where(side[1] == 1, own[...], data_a[...])
    for group, (left, right) in enumerate(
        ((first, data_b[...]), (data_c[...], data_d[...]))
    ):
        rows = jnp.dot(picks[2 * group], left, preferred_element_type=F32)
        rows = rows + jnp.dot(picks[2 * group + 1], right, preferred_element_type=F32)
        rows = rows.astype(BF16)
        for yz in range(YZ):
            out[yz, group * PAIR : (group + 1) * PAIR] = rows[yz * PAIR : (yz + 1) * PAIR]


def gather_call(kernel, side, slots, smalls, data, groups, extra):
    count, width = data[0].shape
    step = width // 4
    whole = lambda shape: pl.BlockSpec(shape, lambda j: (0,) * len(shape))
    rows = YZ * PAIR
    return pl.pallas_call(
        kernel,
        grid=(width // step,),
        in_specs=[pl.BlockSpec(memory_space=pltpu.SMEM), whole(slots.shape)]
        + [whole(s.shape) for s in smalls]
        + [pl.BlockSpec((count, step), lambda j: (0, j)) for _ in data],
        out_specs=pl.BlockSpec((YZ, groups * PAIR, step), lambda j: (0, 0, j)),
        out_shape=jax.ShapeDtypeStruct((YZ, groups * PAIR, width), BF16),
        scratch_shapes=[pltpu.VMEM((2 * groups, rows, count), BF16)] + extra,
        compiler_params=params(),
        cost_estimate=cost(
            4 * groups * rows * count * width, 2 * width * (len(data) * count + groups * rows)
        ),
        interpret=INTERPRET,
    )(side, slots, *smalls, *data)


def forward_kernel(rows, grads, gate_up, down, hidden_t, gate_back, up_back, total):
    k = pl.program_id(0)

    @pl.when(k == 0)
    def _():
        total[...] = jnp.zeros_like(total)

    total[0] += jnp.dot(rows[...], gate_up[0, 0], preferred_element_type=F32)
    total[1] += jnp.dot(rows[...], gate_up[0, 1], preferred_element_type=F32)
    total[2] += lax.dot_general(
        grads[...], down[0], (((1,), (1,)), ((), ())), preferred_element_type=F32
    )

    @pl.when(k == pl.num_programs(0) - 1)
    def _():
        gate, up, hidden_grad = total[0], total[1], total[2]
        sigmoid = jax.nn.sigmoid(gate)
        silu = gate * sigmoid
        hidden_t[...] = jnp.transpose(silu * up).astype(BF16)
        gate_back[...] = (
            hidden_grad * up * sigmoid * (1.0 + gate * (1.0 - sigmoid))
        ).astype(BF16)
        up_back[...] = (hidden_grad * silu).astype(BF16)


def forward_call(rows, grads, gate_up, down):
    count, width = rows.shape
    units = down.shape[1]
    step = width // 7
    return pl.pallas_call(
        forward_kernel,
        grid=(width // step,),
        in_specs=[
            pl.BlockSpec((count, step), lambda k: (0, k)),
            pl.BlockSpec((count, step), lambda k: (0, k)),
            pl.BlockSpec((1, 2, step, units), lambda k: (0, 0, k, 0)),
            pl.BlockSpec((1, units, step), lambda k: (0, 0, k)),
        ],
        out_specs=[
            pl.BlockSpec((units, count), lambda k: (0, 0)),
            pl.BlockSpec((count, units), lambda k: (0, 0)),
            pl.BlockSpec((count, units), lambda k: (0, 0)),
        ],
        out_shape=[
            jax.ShapeDtypeStruct((units, count), BF16),
            jax.ShapeDtypeStruct((count, units), BF16),
            jax.ShapeDtypeStruct((count, units), BF16),
        ],
        scratch_shapes=[pltpu.VMEM((3, count, units), F32)],
        compiler_params=params(),
        cost_estimate=cost(
            6 * count * width * units, 2 * width * (2 * count + 3 * units)
        ),
        interpret=INTERPRET,
    )(rows, grads, gate_up, down)


def adam(gradient, first, second):
    first_new = 0.9 * first.astype(F32) + 0.1 * gradient
    second_new = 0.95 * second.astype(F32) + 0.05 * gradient * gradient
    return (first_new / (jnp.sqrt(second_new) + 1e-08)).astype(BF16)


def down_kernel(hidden_a, hidden_b, grads_a, grads_b, first, second, out):
    gradient = jnp.dot(hidden_a[...], grads_a[...], preferred_element_type=F32)
    gradient = gradient + jnp.dot(hidden_b[...], grads_b[...], preferred_element_type=F32)
    out[0] = adam(gradient, first[0], second[0])


def down_call(hiddens, grads, first, second, start, units, step):
    count, width = grads[0].shape
    inner = first.shape[1]
    part = pl.BlockSpec((count, step), lambda j: (0, start + j))
    moment = pl.BlockSpec((1, inner, step), lambda j: (0, 0, start + j))
    whole = pl.BlockSpec((inner, count), lambda j: (0, 0))
    return pl.pallas_call(
        down_kernel,
        grid=(units,),
        in_specs=[whole, whole, part, part, moment, moment],
        out_specs=pl.BlockSpec((1, inner, step), lambda j: (0, 0, j)),
        out_shape=jax.ShapeDtypeStruct((1, inner, units * step), BF16),
        compiler_params=params(),
        cost_estimate=cost(
            4 * count * inner * units * step, 2 * units * step * (2 * count + 3 * inner)
        ),
        interpret=INTERPRET,
    )(*hiddens, *grads, first, second)


def contract_rows(left, right):
    return lax.dot_general(left, right, (((0,), (0,)), ((), ())), preferred_element_type=F32)


def gate_up_kernel(
    rows_a, rows_b, gate_a, up_a, gate_b, up_b, first, second, out
):
    for half, (back_a, back_b) in enumerate(((gate_a, gate_b), (up_a, up_b))):
        gradient = contract_rows(rows_a[...], back_a[...])
        gradient = gradient + contract_rows(rows_b[...], back_b[...])
        out[0, half] = adam(gradient, first[0, half], second[0, half])


def gate_up_call(rows, backs, first, second, start, units, step):
    count, width = rows[0].shape
    inner = first.shape[3]
    part = pl.BlockSpec((count, step), lambda j: (0, start + j))
    moment = pl.BlockSpec((1, 2, step, inner), lambda j: (0, 0, start + j, 0))
    whole = pl.BlockSpec((count, inner), lambda j: (0, 0))
    return pl.pallas_call(
        gate_up_kernel,
        grid=(units,),
        in_specs=[part, part, whole, whole, whole, whole, moment, moment],
        out_specs=pl.BlockSpec((1, 2, step, inner), lambda j: (0, 0, j, 0)),
        out_shape=jax.ShapeDtypeStruct((1, 2, units * step, inner), BF16),
        compiler_params=params(),
        cost_estimate=cost(
            8 * count * inner * units * step, 2 * units * step * (2 * count + 6 * inner)
        ),
        interpret=INTERPRET,
    )(*rows, *backs, first, second)


def place_kernel(swapping, mine, theirs, *rest):
    out = rest[-1]

    @pl.when(swapping[0] == 1)
    def _():
        out[...] = theirs[...]

    @pl.when(swapping[0] != 1)
    def _():
        out[...] = mine[...]


def place(swapping, mine, theirs, whole, shape, start, units, axis):
    block = tuple(
        mine.shape[axis] // units if k == axis else n for k, n in enumerate(mine.shape)
    )
    at = lambda base: lambda j: tuple(base + j if k == axis else 0 for k in range(len(block)))
    old = [] if whole is None else [whole]
    return pl.pallas_call(
        place_kernel,
        grid=(units,),
        in_specs=[
            pl.BlockSpec(memory_space=pltpu.SMEM),
            pl.BlockSpec(block, at(0)),
            pl.BlockSpec(block, at(0)),
        ]
        + [pl.BlockSpec(memory_space=pl.ANY) for _ in old],
        out_specs=pl.BlockSpec(block, at(start)),
        out_shape=jax.ShapeDtypeStruct(shape, BF16),
        input_output_aliases={3: 0} if old else {},
        compiler_params=params(),
        cost_estimate=cost(0, 6 * mine.size),
        interpret=INTERPRET,
    )(swapping, mine, theirs, *old)


def local(
    tokens,
    cotangent,
    expert_ids,
    combine,
    slot_expert,
    swap_flag,
    w_gate_up,
    w_down,
    first_gate_up,
    first_down,
    second_gate_up,
    second_down,
):
    width = tokens.shape[1]
    core = lax.axis_index("dp") % 2
    my_slot = lax.axis_index("expert")
    side = my_slot % 2
    near = (core == side).astype(jnp.int32)
    slots = slot_expert[None, :]
    small = jnp.concatenate([expert_ids.T.astype(F32), combine.T], axis=0)

    small_core = send(small, to_core)
    cotangent_core = send(cotangent, to_core)
    tokens_in = [send(tokens, t) for t in (token_1, token_2, token_3, token_4)]
    scaled = gather_call(
        grads_kernel,
        jnp.stack([core, near]).astype(jnp.int32),
        slots,
        [small, small_core],
        [cotangent, cotangent_core],
        1,
        [pltpu.VMEM((YZ * PAIR, 1), F32)],
    )
    small_in = [send(small, t) for t in (token_1, token_2, token_3, token_4)]
    small_in[0] = jnp.where(near == 1, small, small_in[0])
    grads_0 = over_yz(scaled)

    sent_rows = gather_call(
        tokens_kernel,
        jnp.stack([side, near]).astype(jnp.int32),
        slots,
        small_in,
        [tokens] + tokens_in,
        2,
        [],
    )
    grads_12 = send(grads_0, grad_12)
    grads_3 = send(grads_0, grad_3)
    rows_a = over_yz(sent_rows).reshape(-1, width)
    grads_a = jnp.concatenate(
        [
            jnp.where(near == 1, grads_0, grads_12),
            jnp.where(near == 1, grads_12, grads_3),
        ],
        axis=1,
    ).reshape(-1, width)
    grads_b = send(grads_a, to_core)
    rows_b = send(rows_a, to_core)

    hidden_a, gate_a, up_a = forward_call(rows_a, grads_a, w_gate_up, w_down)
    hidden_b, gate_b, up_b = forward_call(rows_b, grads_b, w_gate_up, w_down)

    swapping = swap_flag[my_slot].reshape(1)
    step = width // 7
    step_down = step_gate_up = None
    pending, start = [], 0
    for units in (1, 3, 3):
        mine = down_call(
            (hidden_a, hidden_b), (grads_a, grads_b), first_down, second_down, start, units, step
        )
        pending.append((0, mine, send(mine, to_swap), start, units))
        start += units
    start = 0
    for units in (2, 2, 2, 1):
        mine = gate_up_call(
            (rows_a, rows_b),
            (gate_a, up_a, gate_b, up_b),
            first_gate_up,
            second_gate_up,
            start,
            units,
            step,
        )
        pending.append((1, mine, send(mine, to_swap), start, units))
        start += units
    for kind, mine, theirs, start, units in pending:
        if kind == 0:
            step_down = place(
                swapping, mine, theirs, step_down, w_down.shape, start, units, 2
            )
        else:
            step_gate_up = place(
                swapping, mine, theirs, step_gate_up, w_gate_up.shape, start, units, 2
            )
    return (step_gate_up, step_down)


def solution(mesh):
    return jax.shard_map(
        local,
        mesh=mesh,
        in_specs=(
            P(("dp", "expert"), None),
            P(("dp", "expert"), None),
            P(("dp", "expert"), None),
            P(("dp", "expert"), None),
            P(),
            P(),
            P("expert", None, None, "dp"),
            P("expert", "dp", None),
            P("expert", None, None, "dp"),
            P("expert", "dp", None),
            P("expert", None, None, "dp"),
            P("expert", "dp", None),
        ),
        out_specs=(P("expert", None, None, "dp"), P("expert", "dp", None)),
        check_vma=False,
    )
```

time: 498 us -> 338 us (0.68)
  local copies, waits for them, and re-layouts: 87.9 us -> 4.33 us
  Pallas kernels: 0 us -> 80.3 us
  blocking collectives: 75.2 us -> 0 us
  waiting for transfers between devices: 246 us -> 185 us
  starting transfers between devices: 9.75 us -> 59.2 us
  matrix products: 35 us -> 0 us
  other arithmetic: 25.5 us -> 7.47 us
  between operations: 15 us -> 0.86 us
    all_gather x1 -> x0, waiting for transfers between devices: 104 us -> none  [side_by_side_2(): result = lax.all_gather(both, axis, axis=dim, tiled=True)]
    pallas_call x0 -> x18, Pallas kernels: none -> 80.3 us  [the longest x2 20 us: forward_call(): pl.pallas_call(forward_kernel, grid=(width // step,), in_specs=[pl.BlockS...]
    all_to_all x0 -> x2, waiting for transfers between devices: none -> 80.1 us  [over_yz(): lax.all_to_all(value, 'expert', 0, 0, axis_index_groups=groups, tiled=True)]
    all_to_all x1 -> x0, blocking collectives: 75.2 us -> none  [side_by_side(): lax.all_to_all(both, axis, split_axis=split_dim, concat_axis=concat_dim,...]
    ppermute x6 -> x21, waiting for transfers between devices: 142 us -> 105 us  [send(): return lax.ppermute(value, AXES, pairs)]
    dot_general x6 -> x0, matrix products: 35 us -> none  [the longest x3 19.7 us: contract_rows(): lax.dot_general(left, right, (((0,), (0,)), ((), ())), preferred_element_...]
    ppermute x6 -> x21, starting transfers between devices: 9.71 us -> 44.2 us  [send(): return lax.ppermute(value, AXES, pairs)]
    reshape x3 -> x0, local copies, waits for them, and re-layouts: 34.4 us -> none  [the longest x1 17.2 us: local(): rows_in = rows_in.reshape(-1, model_width)]
  transfers between devices with their start and end apart: 7 -> 23, of which waited for: 3 -> 7; matrix products, arithmetic and copies ran while one was open for 20% -> 2% of each run, Pallas kernels for 0% -> 18%
where the time goes in v1:
time: 338 us; the launch traced here: 337 us
  waiting for transfers between devices  185 us (55%)
  Pallas kernels  80.3 us (24%)
  starting transfers between devices  59.2 us (18%)
  other arithmetic  7.47 us (2%)
  local copies, waits for them, and re-layouts  4.33 us (1%)
    ppermute x21, waiting for transfers between devices, send(): return lax.ppermute(value, AXES, pairs)  105 us
    all_to_all x2, waiting for transfers between devices, over_yz(): lax.all_to_all(value, 'expert', 0, 0, axis_index_groups=groups, tiled=True)  80.1 us
    ppermute x21, starting transfers between devices, send(): return lax.ppermute(value, AXES, pairs)  44.2 us
    pallas_call x2, Pallas kernels, forward_call(): pl.pallas_call(forward_kernel, grid=(width // step,), in_specs=[pl.BlockS...  20 us
    pallas_call x4, Pallas kernels, gate_up_call(): pl.pallas_call(gate_up_kernel, grid=(units,), in_specs=[part, part, whole...  19.3 us
    pallas_call x7, Pallas kernels, place(): pl.pallas_call(place_kernel, grid=(units,), in_specs=[pl.BlockSpec(memory...  18 us
    all_to_all x2, starting transfers between devices, over_yz(): lax.all_to_all(value, 'expert', 0, 0, axis_index_groups=groups, tiled=True)  15 us
    pallas_call x3, Pallas kernels, down_call(): pl.pallas_call(down_kernel, grid=(units,), in_specs=[whole, whole, part,...  11.9 us
  transfers between devices with their start and end apart: 23, of which 7 were waited for; matrix products, arithmetic and copies ran while one was open for 2% of the time, Pallas kernels for 18%

profile of v1, /device:TPU:64, one launch (start us, length us, event | category | flops | bytes accessed | tf_op | source)
XLA Modules:
  0.0 336.9 jit_solution(7989128759984231158)
XLA Ops:
  0.6 0.1 collective-permute-start.10
  0.7 0.7 convert_bitcast_fusion
  1.4 0.7 pad_maximum_fusion.1.small_a
  2.1 0.5 collective-permute-start.9
  2.6 0.1 pad_add_fusion.1.side
  2.7 0.7 collective-permute-done.9.small_b
  3.4 1.2 copy-done.7
  4.6 0.7 copy-done.12
  5.2 4.3 %shard_map.132 = bf16[16,24,3584]{2,1,0:T(8,128)(2,1)} custom-call(s32[2]{0:T(128)S(1)} %pad_add_fusion.1.side, s32[1,32]{1,0:T(1,128)S(1)} %bitcast.9, f32[4,128]{1,0:T(4,128)S(1)} %pad_maximum_fusion.1.small_a, f32[4,128]{1,0:T(4,128)S(1)} %collective-permute-done.9.small_b, bf16[128,3584]{1,0:T(8,128)(2,1)S(1)} %copy-done.7, ...), custom_call_target="tpu_custom_call" | custom-call | flops 704643072 | bytes 4587520 | tf_op jit(solution)/shard_map/pallas_call | solution.py:154
  9.5 7.8 %all-to-all-start.1 = ((bf16[16,24,3584]{2,1,0:T(8,128)(2,1)}), bf16[16,24,3584]{2,1,0:T(8,128)(2,1)}, u32[]{:S(2)}, u32[]{:S(2)}) async-start(bf16[16,24,3584]{2,1,0:T(8,128)(2,1)} %shard_map.132), calls=%async_computation.1 | async-start | bytes 5505024 | tf_op jit(solution)/shard_map/all_to_all | solution.py:70
  17.3 1.6 collective-permute-start.6
  18.9 2.1 collective-permute-start.5
  20.9 1.6 collective-permute-start.4
  22.5 2.3 collective-permute-start.7
  24.8 1.4 collective-permute-start.3
  26.1 34.3 %collective-permute-done.3.sd = f32[4,128]{1,0:T(4,128)S(1)} collective-permute-done((f32[4,128]{1,0:T(4,128)S(1)}, f32[4,128]{1,0:T(4,128)S(1)}, u32[]{:S(2)}, u32[]{:S(2)}) %collective-permute-start.3) | collective-permute-done | bytes 2080 | tf_op jit(solution)/shard_map/ppermute | solution.py:33
  60.4 1.5 collective-permute-start.2
  61.9 2.1 collective-permute-done.2.sc
  64.0 0.7 collective-permute-start
  64.7 0.1 pad_add_fusion.side
  64.8 0.0 collective-permute-done
  64.8 7.9 %collective-permute-start.1 = (f32[4,128]{1,0:T(4,128)S(1)}, f32[4,128]{1,0:T(4,128)S(1)}, u32[]{:S(2)}, u32[]{:S(2)}) collective-permute-start(f32[4,128]{1,0:T(4,128)S(1)} %pad_maximum_fusion.1.small_a), channel_id=1, source_target_pairs={{0,65},{1,33},{2,67},{3,35},{4,69},{5,37},{6,71},{7,39},{8,73},{9,... | collective-permute-start | bytes 6152 | tf_op jit(solution)/shard_map/ppermute | solution.py:33
  72.7 1.3 collective-permute-done.1.sb
  74.0 0.0 collective-permute-done.6.data_c
  74.0 6.9 %shard_map.131 = bf16[16,48,3584]{2,1,0:T(8,128)(2,1)} custom-call(s32[2]{0:T(128)S(1)} %pad_add_fusion.side, s32[1,32]{1,0:T(1,128)S(1)} %bitcast.10, f32[4,128]{1,0:T(4,128)S(1)} %broadcast_select_fusion.2.sa, f32[4,128]{1,0:T(4,128)S(1)} %collective-permute-done.1.sb, f32[4,128]{1,0:T(4,128)S(1)} %collective-permute-done.2.sc, ...), custom_call_target="tpu_custom_call" | custom-call | flops 1409286144 | bytes 10092544 | tf_op jit(solution)/shard_map/pallas_call | solution.py:154
  81.0 7.2 %all-to-all-start = ((bf16[16,48,3584]{2,1,0:T(8,128)(2,1)}), bf16[16,48,3584]{2,1,0:T(8,128)(2,1)}, u32[]{:S(2)}, u32[]{:S(2)}) async-start(bf16[16,48,3584]{2,1,0:T(8,128)(2,1)} %shard_map.131), calls=%async_computation | async-start | bytes 11010048 | tf_op jit(solution)/shard_map/all_to_all | solution.py:70
  88.2 0.8 collective-permute-start.12
  89.0 0.1 collective-permute-start.11
  89.1 80.1 %all-to-all-done = bf16[16,48,3584]{2,1,0:T(8,128)(2,1)} async-done(((bf16[16,48,3584]{2,1,0:T(8,128)(2,1)}), bf16[16,48,3584]{2,1,0:T(8,128)(2,1)}, u32[]{:S(2)}, u32[]{:S(2)}) %all-to-all-start) | async-done | bytes 5505056 | tf_op jit(solution)/shard_map/all_to_all | solution.py:70
  169.2 0.1 collective-permute-start.8
  169.3 3.1 broadcast_select_fusion.1
  172.4 0.0 copy-start.3
  172.4 2.9 pad_maximum_fusion
  175.3 10.0 %shard_map.133 = (bf16[256,768]{1,0:T(8,128)(2,1)S(1)}, bf16[768,256]{1,0:T(8,128)(2,1)S(1)}, bf16[768,256]{1,0:T(8,128)(2,1)S(1)}) custom-call(bf16[768,3584]{1,0:T(8,128)(2,1)} %bitcast.5.rows.rows_a, bf16[768,3584]{1,0:T(8,128)(2,1)} %bitcast.7.grads.grads_a, bf16[1,2,3584,256]{3,2,1,0:T(8,128)(2,1)} %gate_up.3, bf16[1,256,3584]{2,1,0:T(8,128)(2,1)S(1)} %copy-done.3), custom_call_target="tpu_custom_call" | custom-call | flops 4227858432 | bytes 16515072 | tf_op jit(solution)/shard_map/pallas_call | solution.py:200
  185.3 0.0 copy-start.1
  185.3 0.0 copy-start.2
  185.3 1.1 collective-permute-done.13.grads.grads_b
  186.5 10.0 %shard_map.134 = (bf16[256,768]{1,0:T(8,128)(2,1)S(1)}, bf16[768,256]{1,0:T(8,128)(2,1)S(1)}, bf16[768,256]{1,0:T(8,128)(2,1)S(1)}) custom-call(bf16[768,3584]{1,0:T(8,128)(2,1)} %collective-permute-done.8.rows.rows_b, bf16[768,3584]{1,0:T(8,128)(2,1)} %collective-permute-done.13.grads.grads_b, bf16[1,2,3584,256]{3,2,1,0:T(8,128)(2,1)} %gate_up.3, ...), custom_call_target="tpu_custom_call" | custom-call | flops 4227858432 | bytes 16515072 | tf_op jit(solution)/shard_map/pallas_call | solution.py:200
  196.5 2.2 shard_map.145.mine
  198.7 12.7 %collective-permute-start.20 = (bf16[1,256,512]{2,1,0:T(8,128)(2,1)S(1)}, bf16[1,256,512]{2,1,0:T(8,128)(2,1)S(1)}, u32[]{:S(2)}, u32[]{:S(2)}) collective-permute-start(bf16[1,256,512]{2,1,0:T(8,128)(2,1)S(1)} %shard_map.145.mine), channel_id=1, source_target_pairs={{0,16},{1,17},{2,18},{3,19},{4,20},{5,21},{6,22},{7,23},{8,24},{9,... | collective-permute-start | bytes 786440 | tf_op jit(solution)/shard_map/ppermute | solution.py:33
  211.3 4.5 %shard_map.144.mine = bf16[1,256,1536]{2,1,0:T(8,128)(2,1)S(1)} custom-call(bf16[256,768]{1,0:T(8,128)(2,1)S(1)} %get-tuple-element.12.hidden_a, bf16[256,768]{1,0:T(8,128)(2,1)S(1)} %get-tuple-element.13.hidden_b, bf16[768,3584]{1,0:T(8,128)(2,1)} %bitcast.7.grads.grads_a, bf16[768,3584]{1,0:T(8,128)(2,1)} %collective-permute-done.13.grads.grads_b, ...), custom_call_target="tpu_custom_call" | custom-call | flops 1207959552 | bytes 7077888 | tf_op jit(solution)/shard_map/pallas_call | solution.py:246
  215.8 0.3 collective-permute-start.19
  216.1 4.9 %shard_map.137.mine = bf16[1,2,1024,256]{3,2,1,0:T(8,128)(2,1)S(1)} custom-call(bf16[768,3584]{1,0:T(8,128)(2,1)} %bitcast.5.rows.rows_a, bf16[768,3584]{1,0:T(8,128)(2,1)} %collective-permute-done.8.rows.rows_b, bf16[768,256]{1,0:T(8,128)(2,1)S(1)} %get-tuple-element.8.gate_a, bf16[768,256]{1,0:T(8,128)(2,1)S(1)} %get-tuple-element.9.up_a, ...), custom_call_target="tpu_custom_call" | custom-call | flops 1610612736 | bytes 6291456 | tf_op jit(solution)/shard_map/pallas_call | solution.py:279
  221.0 3.6 %collective-permute-start.16 = (bf16[1,2,1024,256]{3,2,1,0:T(8,128)(2,1)S(1)}, bf16[1,2,1024,256]{3,2,1,0:T(8,128)(2,1)}, u32[]{:S(2)}, u32[]{:S(2)}) collective-permute-start(bf16[1,2,1024,256]{3,2,1,0:T(8,128)(2,1)S(1)} %shard_map.137.mine), channel_id=1, source_target_pairs={{0,16},{1,17},{2,18},{3,19},{4,20},{5,21},{6,22},{7,23},{8,24},{9,... | collective-permute-start | bytes 3145736 | tf_op jit(solution)/shard_map/ppermute | solution.py:33
  224.6 5.7 %shard_map.138.mine = bf16[1,2,1024,256]{3,2,1,0:T(8,128)(2,1)} custom-call(bf16[768,3584]{1,0:T(8,128)(2,1)} %bitcast.5.rows.rows_a, bf16[768,3584]{1,0:T(8,128)(2,1)} %collective-permute-done.8.rows.rows_b, bf16[768,256]{1,0:T(8,128)(2,1)S(1)} %get-tuple-element.8.gate_a, bf16[768,256]{1,0:T(8,128)(2,1)S(1)} %get-tuple-element.9.up_a, ...), custom_call_target="tpu_custom_call" | custom-call | flops 1610612736 | bytes 6291456 | tf_op jit(solution)/shard_map/pallas_call | solution.py:279
  230.2 0.0 collective-permute-start.17
  230.3 4.9 %shard_map.136.mine = bf16[1,2,1024,256]{3,2,1,0:T(8,128)(2,1)S(1)} custom-call(bf16[768,3584]{1,0:T(8,128)(2,1)} %bitcast.5.rows.rows_a, bf16[768,3584]{1,0:T(8,128)(2,1)} %collective-permute-done.8.rows.rows_b, bf16[768,256]{1,0:T(8,128)(2,1)S(1)} %get-tuple-element.8.gate_a, bf16[768,256]{1,0:T(8,128)(2,1)S(1)} %get-tuple-element.9.up_a, ...), custom_call_target="tpu_custom_call" | custom-call | flops 1610612736 | bytes 6291456 | tf_op jit(solution)/shard_map/pallas_call | solution.py:279
  235.1 0.0 copy-start
  235.1 3.6 %collective-permute-start.15 = (bf16[1,2,1024,256]{3,2,1,0:T(8,128)(2,1)S(1)}, bf16[1,2,1024,256]{3,2,1,0:T(8,128)(2,1)}, u32[]{:S(2)}, u32[]{:S(2)}) collective-permute-start(bf16[1,2,1024,256]{3,2,1,0:T(8,128)(2,1)S(1)} %shard_map.136.mine), channel_id=1, source_target_pairs={{0,16},{1,17},{2,18},{3,19},{4,20},{5,21},{6,22},{7,23},{8,24},{9,... | collective-permute-start | bytes 3145736 | tf_op jit(solution)/shard_map/ppermute | solution.py:33
  238.7 5.2 %shard_map.143.mine = bf16[1,256,1536]{2,1,0:T(8,128)(2,1)} custom-call(bf16[256,768]{1,0:T(8,128)(2,1)S(1)} %get-tuple-element.12.hidden_a, bf16[256,768]{1,0:T(8,128)(2,1)S(1)} %get-tuple-element.13.hidden_b, bf16[768,3584]{1,0:T(8,128)(2,1)} %bitcast.7.grads.grads_a, bf16[768,3584]{1,0:T(8,128)(2,1)} %collective-permute-done.13.grads.grads_b, ...), custom_call_target="tpu_custom_call" | custom-call | flops 1207959552 | bytes 7077888 | tf_op jit(solution)/shard_map/pallas_call | solution.py:246
  244.0 0.3 collective-permute-start.18
  244.2 3.9 %shard_map.135.mine = bf16[1,2,512,256]{3,2,1,0:T(8,128)(2,1)} custom-call(bf16[768,3584]{1,0:T(8,128)(2,1)} %bitcast.5.rows.rows_a, bf16[768,3584]{1,0:T(8,128)(2,1)} %collective-permute-done.8.rows.rows_b, bf16[768,256]{1,0:T(8,128)(2,1)S(1)} %get-tuple-element.8.gate_a, bf16[768,256]{1,0:T(8,128)(2,1)S(1)} %get-tuple-element.9.up_a, ...), custom_call_target="tpu_custom_call" | custom-call | flops 805306368 | bytes 3145728 | tf_op jit(solution)/shard_map/pallas_call | solution.py:279
  248.1 0.9 copy-done.8
  249.0 3.3 collective-permute-start.14
  252.4 0.6 dynamic_slice.3.swapping
  253.0 0.9 copy-done.11
  253.9 1.3 shard_map.146.rest_0_
  255.2 2.1 shard_map.147.rest_0_
  257.4 65.0 %collective-permute-done.18.theirs = bf16[1,256,1536]{2,1,0:T(8,128)(2,1)} collective-permute-done((bf16[1,256,1536]{2,1,0:T(8,128)(2,1)}, bf16[1,256,1536]{2,1,0:T(8,128)(2,1)}, u32[]{:S(2)}, u32[]{:S(2)}) %collective-permute-start.18) | collective-permute-done | bytes 786464 | tf_op jit(solution)/shard_map/ppermute | solution.py:33
  322.3 3.6 %shard_map.148 = bf16[1,256,3584]{2,1,0:T(8,128)(2,1)} custom-call(s32[1]{0:T(128)} %dynamic_slice.3.swapping, bf16[1,256,1536]{2,1,0:T(8,128)(2,1)} %shard_map.143.mine, bf16[1,256,1536]{2,1,0:T(8,128)(2,1)} %collective-permute-done.18.theirs, bf16[1,256,3584]{2,1,0:T(8,128)(2,1)} %shard_map.147.rest_0_), custom_call_target="tpu_custom_call", output_to_operand_aliasing={{}: (3, {})} | custom-call | bytes 2359296 | tf_op jit(solution)/shard_map/pallas_call | solution.py:311
  326.0 2.9 shard_map.139.rest_0_
  328.9 2.7 shard_map.140.rest_0_
  331.6 2.7 shard_map.141.rest_0_
  334.3 2.6 shard_map.142
  (40 shorter events, 0.1 us)
Async XLA Ops:
  0.6 2.8 collective-permute-start.10
  2.1 1.3 collective-permute-start.9
  3.4 1.2 copy-start.7
  4.6 0.7 copy-start.12
  9.5 7.8 %copy-start.6 = (bf16[128,3584]{1,0:T(8,128)(2,1)S(1)}, bf16[128,3584]{1,0:T(8,128)(2,1)}, u32[]{:S(2)}) copy-start(bf16[128,3584]{1,0:T(8,128)(2,1)} %own.1) | copy-start | bytes 2752516
  9.5 63.2 %copy-start.14 = (f32[128,2]{0,1:T(2,128)S(1)}, f32[128,2]{0,1:T(2,128)}, u32[]{:S(2)}) copy-start(f32[128,2]{0,1:T(2,128)} %param.15) | copy-start | bytes 3076
  9.5 64.5 %copy-start.13 = (s32[32]{0:T(128)S(1)}, s32[32]{0:T(128)}, u32[]{:S(2)}) copy-start(s32[32]{0:T(128)} %param.16) | copy-start | bytes 388
  9.5 71.4 %all-to-all-start.1 = ((bf16[16,24,3584]{2,1,0:T(8,128)(2,1)}), bf16[16,24,3584]{2,1,0:T(8,128)(2,1)}, u32[]{:S(2)}, u32[]{:S(2)}) async-start(bf16[16,24,3584]{2,1,0:T(8,128)(2,1)} %shard_map.132), calls=%async_computation.1 | async-start | bytes 5505024 | tf_op jit(solution)/shard_map/all_to_all | solution.py:70
  17.3 56.7 %collective-permute-start.6 = (bf16[128,3584]{1,0:T(8,128)(2,1)S(1)}, bf16[128,3584]{1,0:T(8,128)(2,1)S(1)}, u32[]{:S(2)}, u32[]{:S(2)}) collective-permute-start(bf16[128,3584]{1,0:T(8,128)(2,1)S(1)} %copy-done.6), channel_id=1, source_target_pairs={{0,64},{1,32},{2,66},{3,34},{4,68},{5,36},{6,70},{7,38},{8,72},{9,... | collective-permute-start | bytes 2752520 | tf_op jit(solution)/shard_map/ppermute | solution.py:33
  18.9 55.2 %collective-permute-start.5 = (bf16[128,3584]{1,0:T(8,128)(2,1)S(1)}, bf16[128,3584]{1,0:T(8,128)(2,1)S(1)}, u32[]{:S(2)}, u32[]{:S(2)}) collective-permute-start(bf16[128,3584]{1,0:T(8,128)(2,1)S(1)} %copy-done.6), channel_id=1, source_target_pairs={{0,65},{1,33},{2,67},{3,35},{4,69},{5,37},{6,71},{7,39},{8,73},{9,... | collective-permute-start | bytes 2752520 | tf_op jit(solution)/shard_map/ppermute | solution.py:33
  20.9 53.1 %collective-permute-start.4 = (bf16[128,3584]{1,0:T(8,128)(2,1)S(1)}, bf16[128,3584]{1,0:T(8,128)(2,1)}, u32[]{:S(2)}, u32[]{:S(2)}) collective-permute-start(bf16[128,3584]{1,0:T(8,128)(2,1)S(1)} %copy-done.6), channel_id=1, source_target_pairs={{1,96},{3,98},{5,100},{7,102},{9,104},{11,106},{13,108},{15,110},{... | collective-permute-start | bytes 2752520 | tf_op jit(solution)/shard_map/ppermute | solution.py:33
  22.5 51.5 %collective-permute-start.7 = (bf16[128,3584]{1,0:T(8,128)(2,1)S(1)}, bf16[128,3584]{1,0:T(8,128)(2,1)}, u32[]{:S(2)}, u32[]{:S(2)}) collective-permute-start(bf16[128,3584]{1,0:T(8,128)(2,1)S(1)} %copy-done.6), channel_id=1, source_target_pairs={{0,1},{1,97},{2,3},{3,99},{4,5},{5,101},{6,7},{7,103},{8,9},{9,105... | collective-permute-start | bytes 2752520 | tf_op jit(solution)/shard_map/ppermute | solution.py:33
  24.8 35.7 %collective-permute-start.3 = (f32[4,128]{1,0:T(4,128)S(1)}, f32[4,128]{1,0:T(4,128)S(1)}, u32[]{:S(2)}, u32[]{:S(2)}) collective-permute-start(f32[4,128]{1,0:T(4,128)S(1)} %pad_maximum_fusion.1.small_a), channel_id=1, source_target_pairs={{0,1},{1,97},{2,3},{3,99},{4,5},{5,101},{6,7},{7,103},{8,9},{9,105... | collective-permute-start | bytes 6152 | tf_op jit(solution)/shard_map/ppermute | solution.py:33
  60.4 3.6 %collective-permute-start.2 = (f32[4,128]{1,0:T(4,128)S(1)}, f32[4,128]{1,0:T(4,128)S(1)}, u32[]{:S(2)}, u32[]{:S(2)}) collective-permute-start(f32[4,128]{1,0:T(4,128)S(1)} %pad_maximum_fusion.1.small_a), channel_id=1, source_target_pairs={{0,64},{1,32},{2,66},{3,34},{4,68},{5,36},{6,70},{7,38},{8,72},{9,... | collective-permute-start | bytes 6152 | tf_op jit(solution)/shard_map/ppermute | solution.py:33
  64.0 0.7 collective-permute-start
  64.8 9.2 %collective-permute-start.1 = (f32[4,128]{1,0:T(4,128)S(1)}, f32[4,128]{1,0:T(4,128)S(1)}, u32[]{:S(2)}, u32[]{:S(2)}) collective-permute-start(f32[4,128]{1,0:T(4,128)S(1)} %pad_maximum_fusion.1.small_a), channel_id=1, source_target_pairs={{0,65},{1,33},{2,67},{3,35},{4,69},{5,37},{6,71},{7,39},{8,73},{9,... | collective-permute-start | bytes 6152 | tf_op jit(solution)/shard_map/ppermute | solution.py:33
  81.0 88.2 %all-to-all-start = ((bf16[16,48,3584]{2,1,0:T(8,128)(2,1)}), bf16[16,48,3584]{2,1,0:T(8,128)(2,1)}, u32[]{:S(2)}, u32[]{:S(2)}) async-start(bf16[16,48,3584]{2,1,0:T(8,128)(2,1)} %shard_map.131), calls=%async_computation | async-start | bytes 11010048 | tf_op jit(solution)/shard_map/all_to_all | solution.py:70
  88.2 81.1 %collective-permute-start.12 = (bf16[16,24,3584]{2,1,0:T(8,128)(2,1)}, bf16[16,24,3584]{2,1,0:T(8,128)(2,1)S(1)}, u32[]{:S(2)}, u32[]{:S(2)}) collective-permute-start(bf16[16,24,3584]{2,1,0:T(8,128)(2,1)} %all-to-all-done.1), channel_id=1, source_target_pairs={{1,32},{3,34},{5,36},{7,38},{9,40},{11,42},{13,44},{15,46},{17,48}... | collective-permute-start | bytes 8257544 | tf_op jit(solution)/shard_map/ppermute | solution.py:33
  89.0 80.3 %collective-permute-start.11 = (bf16[16,24,3584]{2,1,0:T(8,128)(2,1)}, bf16[16,24,3584]{2,1,0:T(8,128)(2,1)}, u32[]{:S(2)}, u32[]{:S(2)}) collective-permute-start(bf16[16,24,3584]{2,1,0:T(8,128)(2,1)} %all-to-all-done.1), channel_id=1, source_target_pairs={{0,64},{1,96},{2,66},{3,98},{4,68},{5,100},{6,70},{7,102},{8,72},{... | collective-permute-start | bytes 8257544 | tf_op jit(solution)/shard_map/ppermute | solution.py:33
  169.2 16.1 %collective-permute-start.8 = (bf16[768,3584]{1,0:T(8,128)(2,1)}, bf16[768,3584]{1,0:T(8,128)(2,1)}, u32[]{:S(2)}, u32[]{:S(2)}) collective-permute-start(bf16[768,3584]{1,0:T(8,128)(2,1)} %bitcast.5.rows.rows_a), channel_id=1, source_target_pairs={{0,32},{1,33},{2,34},{3,35},{4,36},{5,37},{6,38},{7,39},{8,40},{9,... | collective-permute-start | bytes 16515080 | tf_op jit(solution)/shard_map/ppermute | solution.py:33
  172.4 2.9 copy-start.3
  175.3 11.2 %collective-permute-start.13 = (bf16[768,3584]{1,0:T(8,128)(2,1)}, bf16[768,3584]{1,0:T(8,128)(2,1)}, u32[]{:S(2)}, u32[]{:S(2)}) collective-permute-start(bf16[768,3584]{1,0:T(8,128)(2,1)} %bitcast.7.grads.grads_a), channel_id=1, source_target_pairs={{0,32},{1,33},{2,34},{3,35},{4,36},{5,37},{6,38},{7,39},{8,40},{9,... | collective-permute-start | bytes 16515080 | tf_op jit(solution)/shard_map/ppermute | solution.py:33
  185.3 11.2 %copy-start.1 = (bf16[1,256,3584]{2,1,0:T(8,128)(2,1)S(1)}, bf16[1,256,3584]{2,1,0:T(8,128)(2,1)}, u32[]{:S(2)}) copy-start(bf16[1,256,3584]{2,1,0:T(8,128)(2,1)} %first.13) | copy-start | bytes 5505028
  185.3 11.2 %copy-start.2 = (bf16[1,256,3584]{2,1,0:T(8,128)(2,1)S(1)}, bf16[1,256,3584]{2,1,0:T(8,128)(2,1)}, u32[]{:S(2)}) copy-start(bf16[1,256,3584]{2,1,0:T(8,128)(2,1)} %second.13) | copy-start | bytes 5505028
  198.7 45.3 %collective-permute-start.20 = (bf16[1,256,512]{2,1,0:T(8,128)(2,1)S(1)}, bf16[1,256,512]{2,1,0:T(8,128)(2,1)S(1)}, u32[]{:S(2)}, u32[]{:S(2)}) collective-permute-start(bf16[1,256,512]{2,1,0:T(8,128)(2,1)S(1)} %shard_map.145.mine), channel_id=1, source_target_pairs={{0,16},{1,17},{2,18},{3,19},{4,20},{5,21},{6,22},{7,23},{8,24},{9,... | collective-permute-start | bytes 786440 | tf_op jit(solution)/shard_map/ppermute | solution.py:33
  215.8 5.2 %copy-start.4 = (bf16[1,256,1536]{2,1,0:T(8,128)(2,1)}, bf16[1,256,1536]{2,1,0:T(8,128)(2,1)S(1)}, u32[]{:S(2)}) copy-start(bf16[1,256,1536]{2,1,0:T(8,128)(2,1)S(1)} %shard_map.144.mine) | copy-start | bytes 2359300
  215.8 32.3 %collective-permute-start.19 = (bf16[1,256,1536]{2,1,0:T(8,128)(2,1)S(1)}, bf16[1,256,1536]{2,1,0:T(8,128)(2,1)S(1)}, u32[]{:S(2)}, u32[]{:S(2)}) collective-permute-start(bf16[1,256,1536]{2,1,0:T(8,128)(2,1)S(1)} %shard_map.144.mine), channel_id=1, source_target_pairs={{0,16},{1,17},{2,18},{3,19},{4,20},{5,21},{6,22},{7,23},{8,24},{9,... | collective-permute-start | bytes 2359304 | tf_op jit(solution)/shard_map/ppermute | solution.py:33
  221.0 108.0 %collective-permute-start.16 = (bf16[1,2,1024,256]{3,2,1,0:T(8,128)(2,1)S(1)}, bf16[1,2,1024,256]{3,2,1,0:T(8,128)(2,1)}, u32[]{:S(2)}, u32[]{:S(2)}) collective-permute-start(bf16[1,2,1024,256]{3,2,1,0:T(8,128)(2,1)S(1)} %shard_map.137.mine), channel_id=1, source_target_pairs={{0,16},{1,17},{2,18},{3,19},{4,20},{5,21},{6,22},{7,23},{8,24},{9,... | collective-permute-start | bytes 3145736 | tf_op jit(solution)/shard_map/ppermute | solution.py:33
  230.2 95.8 %collective-permute-start.17 = (bf16[1,2,1024,256]{3,2,1,0:T(8,128)(2,1)}, bf16[1,2,1024,256]{3,2,1,0:T(8,128)(2,1)}, u32[]{:S(2)}, u32[]{:S(2)}) collective-permute-start(bf16[1,2,1024,256]{3,2,1,0:T(8,128)(2,1)} %shard_map.138.mine), channel_id=1, source_target_pairs={{0,16},{1,17},{2,18},{3,19},{4,20},{5,21},{6,22},{7,23},{8,24},{9,... | collective-permute-start | bytes 3145736 | tf_op jit(solution)/shard_map/ppermute | solution.py:33
  235.1 9.1 %copy-start = (bf16[1,2,3584,256]{3,2,1,0:T(8,128)(2,1)S(1)}, bf16[1,2,3584,256]{3,2,1,0:T(8,128)(2,1)}, u32[]{:S(2)}) copy-start(bf16[1,2,3584,256]{3,2,1,0:T(8,128)(2,1)} %first.10) | copy-start | bytes 11010052
  235.1 96.5 %collective-permute-start.15 = (bf16[1,2,1024,256]{3,2,1,0:T(8,128)(2,1)S(1)}, bf16[1,2,1024,256]{3,2,1,0:T(8,128)(2,1)}, u32[]{:S(2)}, u32[]{:S(2)}) collective-permute-start(bf16[1,2,1024,256]{3,2,1,0:T(8,128)(2,1)S(1)} %shard_map.136.mine), channel_id=1, source_target_pairs={{0,16},{1,17},{2,18},{3,19},{4,20},{5,21},{6,22},{7,23},{8,24},{9,... | collective-permute-start | bytes 3145736 | tf_op jit(solution)/shard_map/ppermute | solution.py:33
  243.9 8.4 %copy-start.15 = (s32[32]{0:T(128)S(1)}, s32[32]{0:T(128)}, u32[]{:S(2)}) copy-start(s32[32]{0:T(128)} %param.17) | copy-start | bytes 388
  243.9 4.2 %copy-start.10 = (bf16[1,256,512]{2,1,0:T(8,128)(2,1)}, bf16[1,256,512]{2,1,0:T(8,128)(2,1)S(1)}, u32[]{:S(2)}) copy-start(bf16[1,256,512]{2,1,0:T(8,128)(2,1)S(1)} %collective-permute-done.20.theirs) | copy-start | bytes 786436
  244.0 78.4 %collective-permute-start.18 = (bf16[1,256,1536]{2,1,0:T(8,128)(2,1)}, bf16[1,256,1536]{2,1,0:T(8,128)(2,1)}, u32[]{:S(2)}, u32[]{:S(2)}) collective-permute-start(bf16[1,256,1536]{2,1,0:T(8,128)(2,1)} %shard_map.143.mine), channel_id=1, source_target_pairs={{0,16},{1,17},{2,18},{3,19},{4,20},{5,21},{6,22},{7,23},{8,24},{9,... | collective-permute-start | bytes 2359304 | tf_op jit(solution)/shard_map/ppermute | solution.py:33
  248.1 7.1 %copy-start.5 = (bf16[1,256,1536]{2,1,0:T(8,128)(2,1)S(1)}, bf16[1,256,1536]{2,1,0:T(8,128)(2,1)}, u32[]{:S(2)}) copy-start(bf16[1,256,1536]{2,1,0:T(8,128)(2,1)} %copy-done.4) | copy-start | bytes 2359300
  248.1 0.9 copy-start.8
  249.0 85.3 %collective-permute-start.14 = (bf16[1,2,512,256]{3,2,1,0:T(8,128)(2,1)}, bf16[1,2,512,256]{3,2,1,0:T(8,128)(2,1)}, u32[]{:S(2)}, u32[]{:S(2)}) collective-permute-start(bf16[1,2,512,256]{3,2,1,0:T(8,128)(2,1)} %shard_map.135.mine), channel_id=1, source_target_pairs={{0,16},{1,17},{2,18},{3,19},{4,20},{5,21},{6,22},{7,23},{8,24},{9,... | collective-permute-start | bytes 1572872 | tf_op jit(solution)/shard_map/ppermute | solution.py:33
  252.4 2.8 copy-start.9
  253.0 0.9 copy-start.11

commit v2 on v1

--- a/solution.py
+++ b/solution.py
@@ -1,11 +1,10 @@
-import functools
-
 import jax
 import jax.numpy as jnp
 from jax import lax
 from jax.experimental import pallas as pl
 from jax.experimental.pallas import tpu as pltpu
 from jax.sharding import PartitionSpec as P
+
 
 INTERPRET = False
 AXES = ("dp", "expert")
@@ -14,7 +13,6 @@
 PAIR = 2 * CAP
 F32 = jnp.float32
 BF16 = jnp.bfloat16
-VMEM_LIMIT = 48 * 1024 * 1024
 
 
 def device_id(xl, c, yz, xh):
@@ -72,7 +70,7 @@
 
 def params(count=1):
     return pltpu.CompilerParams(
-        dimension_semantics=("arbitrary",) * count, vmem_limit_bytes=VMEM_LIMIT
+        dimension_semantics=("arbitrary",) * count
     )
 
 
@@ -168,61 +166,88 @@
     )(side, slots, *smalls, *data)
 
 
-def forward_kernel(rows, grads, gate_up, down, hidden_t, gate_back, up_back, total):
+def hidden_grad_kernel(grads, down_a, down_b, out):
+    @pl.when(pl.program_id(0) == 0)
+    def _():
+        out[...] = jnp.zeros_like(out)
+
+    for k, down in enumerate((down_a, down_b)):
+        out[k] += lax.dot_general(
+            grads[...], down[0], (((1,), (1,)), ((), ())), preferred_element_type=F32
+        )
+
+
+def hidden_grad_call(grads, down_a, down_b):
+    count, width = grads.shape
+    units = down_a.shape[1]
+    step = width // 7
+    weight = pl.BlockSpec((1, units, step), lambda k: (0, 0, k))
+    return pl.pallas_call(
+        hidden_grad_kernel,
+        grid=(width // step,),
+        in_specs=[pl.BlockSpec((count, step), lambda k: (0, k)), weight, weight],
+        out_specs=pl.BlockSpec((2, count, units), lambda k: (0, 0, 0)),
+        out_shape=jax.ShapeDtypeStruct((2, count, units), F32),
+        compiler_params=params(),
+        cost_estimate=cost(
+            4 * count * width * units, 2 * width * (count + 2 * units) + 8 * count * units
+        ),
+        interpret=INTERPRET,
+    )(grads, down_a, down_b)
+
+
+def forward_kernel(
+    rows, gate_up_a, gate_up_b, hidden_grads, hidden_a, hidden_b, back_a, back_b, total
+):
     k = pl.program_id(0)
 
     @pl.when(k == 0)
     def _():
         total[...] = jnp.zeros_like(total)
 
-    total[0] += jnp.dot(rows[...], gate_up[0, 0], preferred_element_type=F32)
-    total[1] += jnp.dot(rows[...], gate_up[0, 1], preferred_element_type=F32)
-    total[2] += lax.dot_general(
-        grads[...], down[0], (((1,), (1,)), ((), ())), preferred_element_type=F32
-    )
+    for owner, gate_up in enumerate((gate_up_a, gate_up_b)):
+        for half in range(2):
+            total[2 * owner + half] += jnp.dot(
+                rows[...], gate_up[0, half], preferred_element_type=F32
+            )
 
     @pl.when(k == pl.num_programs(0) - 1)
     def _():
-        gate, up, hidden_grad = total[0], total[1], total[2]
-        sigmoid = jax.nn.sigmoid(gate)
-        silu = gate * sigmoid
-        hidden_t[...] = jnp.transpose(silu * up).astype(BF16)
-        gate_back[...] = (
-            hidden_grad * up * sigmoid * (1.0 + gate * (1.0 - sigmoid))
-        ).astype(BF16)
-        up_back[...] = (hidden_grad * silu).astype(BF16)
-
-
-def forward_call(rows, grads, gate_up, down):
+        units = hidden_a.shape[0]
+        for owner, (hidden_t, back) in enumerate(((hidden_a, back_a), (hidden_b, back_b))):
+            gate, up, hidden_grad = total[2 * owner], total[2 * owner + 1], hidden_grads[owner]
+            sigmoid = jax.nn.sigmoid(gate)
+            silu = gate * sigmoid
+            hidden_t[...] = jnp.transpose(silu * up).astype(BF16)
+            back[:, :units] = (
+                hidden_grad * up * sigmoid * (1.0 + gate * (1.0 - sigmoid))
+            ).astype(BF16)
+            back[:, units:] = (hidden_grad * silu).astype(BF16)
+
+
+def forward_call(rows, gate_up_a, gate_up_b, hidden_grads):
     count, width = rows.shape
-    units = down.shape[1]
+    units = gate_up_a.shape[3]
     step = width // 7
+    weight = pl.BlockSpec((1, 2, step, units), lambda k: (0, 0, k, 0))
+    whole = lambda shape: pl.BlockSpec(shape, lambda k: (0,) * len(shape))
+    shapes = [(units, count), (units, count), (count, 2 * units), (count, 2 * units)]
     return pl.pallas_call(
         forward_kernel,
         grid=(width // step,),
         in_specs=[
             pl.BlockSpec((count, step), lambda k: (0, k)),
-            pl.BlockSpec((count, step), lambda k: (0, k)),
-            pl.BlockSpec((1, 2, step, units), lambda k: (0, 0, k, 0)),
-            pl.BlockSpec((1, units, step), lambda k: (0, 0, k)),
+            weight,
+            weight,
+            whole(hidden_grads.shape),
         ],
-        out_specs=[
-            pl.BlockSpec((units, count), lambda k: (0, 0)),
-            pl.BlockSpec((count, units), lambda k: (0, 0)),
-            pl.BlockSpec((count, units), lambda k: (0, 0)),
-        ],
-        out_shape=[
-            jax.ShapeDtypeStruct((units, count), BF16),
-            jax.ShapeDtypeStruct((count, units), BF16),
-            jax.ShapeDtypeStruct((count, units), BF16),
-        ],
-        scratch_shapes=[pltpu.VMEM((3, count, units), F32)],
-        compiler_params=params(),
-        cost_estimate=cost(
-            6 * count * width * units, 2 * width * (2 * count + 3 * units)
-        ),
-        interpret=INTERPRET,
-    )(rows, grads, gate_up, down)
+        out_specs=[whole(s) for s in shapes],
+        out_shape=[jax.ShapeDtypeStruct(s, BF16) for s in shapes],
+        scratch_shapes=[pltpu.VMEM((4, count, units), F32)],
+        compiler_params=params(),
+        cost_estimate=cost(8 * count * width * units, 2 * width * (count + 4 * units)),
+        interpret=INTERPRET,
+    )(rows, gate_up_a, gate_up_b, hidden_grads)
 
 
 def adam(gradient, first, second):
@@ -231,22 +256,27 @@
     return (first_new / (jnp.sqrt(second_new) + 1e-08)).astype(BF16)
 
 
+def after(kernel, count):
+    return lambda *refs: kernel(*refs[count:])
+
+
 def down_kernel(hidden_a, hidden_b, grads_a, grads_b, first, second, out):
     gradient = jnp.dot(hidden_a[...], grads_a[...], preferred_element_type=F32)
     gradient = gradient + jnp.dot(hidden_b[...], grads_b[...], preferred_element_type=F32)
     out[0] = adam(gradient, first[0], second[0])
 
 
-def down_call(hiddens, grads, first, second, start, units, step):
-    count, width = grads[0].shape
+def down_call(behind, hiddens, grads, first, second, start, units, step):
+    count, _ = grads[0].shape
     inner = first.shape[1]
     part = pl.BlockSpec((count, step), lambda j: (0, start + j))
     moment = pl.BlockSpec((1, inner, step), lambda j: (0, 0, start + j))
     whole = pl.BlockSpec((inner, count), lambda j: (0, 0))
     return pl.pallas_call(
-        down_kernel,
+        after(down_kernel, len(behind)),
         grid=(units,),
-        in_specs=[whole, whole, part, part, moment, moment],
+        in_specs=[pl.BlockSpec(memory_space=pl.ANY) for _ in behind]
+        + [whole, whole, part, part, moment, moment],
         out_specs=pl.BlockSpec((1, inner, step), lambda j: (0, 0, j)),
         out_shape=jax.ShapeDtypeStruct((1, inner, units * step), BF16),
         compiler_params=params(),
@@ -254,32 +284,34 @@
             4 * count * inner * units * step, 2 * units * step * (2 * count + 3 * inner)
         ),
         interpret=INTERPRET,
-    )(*hiddens, *grads, first, second)
+    )(*behind, *hiddens, *grads, first, second)
 
 
 def contract_rows(left, right):
     return lax.dot_general(left, right, (((0,), (0,)), ((), ())), preferred_element_type=F32)
 
 
-def gate_up_kernel(
-    rows_a, rows_b, gate_a, up_a, gate_b, up_b, first, second, out
-):
-    for half, (back_a, back_b) in enumerate(((gate_a, gate_b), (up_a, up_b))):
-        gradient = contract_rows(rows_a[...], back_a[...])
-        gradient = gradient + contract_rows(rows_b[...], back_b[...])
-        out[0, half] = adam(gradient, first[0, half], second[0, half])
-
-
-def gate_up_call(rows, backs, first, second, start, units, step):
-    count, width = rows[0].shape
+def gate_up_kernel(rows_a, rows_b, back_a, back_b, first, second, out):
+    inner = first.shape[3]
+    gradient = contract_rows(rows_a[...], back_a[...])
+    gradient = gradient + contract_rows(rows_b[...], back_b[...])
+    for half in range(2):
+        out[0, half] = adam(
+            gradient[:, half * inner : (half + 1) * inner], first[0, half], second[0, half]
+        )
+
+
+def gate_up_call(behind, rows, backs, first, second, start, units, step):
+    count, _ = rows[0].shape
     inner = first.shape[3]
     part = pl.BlockSpec((count, step), lambda j: (0, start + j))
     moment = pl.BlockSpec((1, 2, step, inner), lambda j: (0, 0, start + j, 0))
-    whole = pl.BlockSpec((count, inner), lambda j: (0, 0))
-    return pl.pallas_call(
-        gate_up_kernel,
+    whole = pl.BlockSpec((count, 2 * inner), lambda j: (0, 0))
+    return pl.pallas_call(
+        after(gate_up_kernel, len(behind)),
         grid=(units,),
-        in_specs=[part, part, whole, whole, whole, whole, moment, moment],
+        in_specs=[pl.BlockSpec(memory_space=pl.ANY) for _ in behind]
+        + [part, part, whole, whole, moment, moment],
         out_specs=pl.BlockSpec((1, 2, step, inner), lambda j: (0, 0, j, 0)),
         out_shape=jax.ShapeDtypeStruct((1, 2, units * step, inner), BF16),
         compiler_params=params(),
@@ -287,7 +319,7 @@
             8 * count * inner * units * step, 2 * units * step * (2 * count + 6 * inner)
         ),
         interpret=INTERPRET,
-    )(*rows, *backs, first, second)
+    )(*behind, *rows, *backs, first, second)
 
 
 def place_kernel(swapping, mine, theirs, *rest):
@@ -302,12 +334,10 @@
         out[...] = mine[...]
 
 
-def place(swapping, mine, theirs, whole, shape, start, units, axis):
-    block = tuple(
-        mine.shape[axis] // units if k == axis else n for k, n in enumerate(mine.shape)
-    )
-    at = lambda base: lambda j: tuple(base + j if k == axis else 0 for k in range(len(block)))
-    old = [] if whole is None else [whole]
+def place(behind, swapping, mine, theirs, whole, shape, start, units):
+    block = tuple(n // units if k == 2 else n for k, n in enumerate(mine.shape))
+    at = lambda base: lambda j: tuple(base + j if k == 2 else 0 for k in range(len(block)))
+    old = behind + ([] if whole is None else [whole])
     return pl.pallas_call(
         place_kernel,
         grid=(units,),
@@ -319,7 +349,7 @@
         + [pl.BlockSpec(memory_space=pl.ANY) for _ in old],
         out_specs=pl.BlockSpec(block, at(start)),
         out_shape=jax.ShapeDtypeStruct(shape, BF16),
-        input_output_aliases={3: 0} if old else {},
+        input_output_aliases={} if whole is None else {2 + len(old): 0},
         compiler_params=params(),
         cost_estimate=cost(0, 6 * mine.size),
         interpret=INTERPRET,
@@ -347,10 +377,12 @@
     near = (core == side).astype(jnp.int32)
     slots = slot_expert[None, :]
     small = jnp.concatenate([expert_ids.T.astype(F32), combine.T], axis=0)
+    token_goals = (token_1, token_2, token_3, token_4)
 
     small_core = send(small, to_core)
     cotangent_core = send(cotangent, to_core)
-    tokens_in = [send(tokens, t) for t in (token_1, token_2, token_3, token_4)]
+    small_in = [send(small, t) for t in token_goals]
+    tokens_in = [send(tokens, t) for t in token_goals]
     scaled = gather_call(
         grads_kernel,
         jnp.stack([core, near]).astype(jnp.int32),
@@ -360,9 +392,10 @@
         1,
         [pltpu.VMEM((YZ * PAIR, 1), F32)],
     )
-    small_in = [send(small, t) for t in (token_1, token_2, token_3, token_4)]
     small_in[0] = jnp.where(near == 1, small, small_in[0])
     grads_0 = over_yz(scaled)
+    down_core = send(w_down, to_core)
+    gate_up_core = send(w_gate_up, to_core)
 
     sent_rows = gather_call(
         tokens_kernel,
@@ -384,44 +417,55 @@
         axis=1,
     ).reshape(-1, width)
     grads_b = send(grads_a, to_core)
+    hidden_grads = hidden_grad_call(grads_a, w_down, down_core)
+
+    hidden_a, hidden_other, back_a, back_other = forward_call(
+        rows_a, w_gate_up, gate_up_core, hidden_grads
+    )
+    hidden_b = send(hidden_other, to_core)
+    back_b = send(back_other, to_core)
     rows_b = send(rows_a, to_core)
 
-    hidden_a, gate_a, up_a = forward_call(rows_a, grads_a, w_gate_up, w_down)
-    hidden_b, gate_b, up_b = forward_call(rows_b, grads_b, w_gate_up, w_down)
-
     swapping = swap_flag[my_slot].reshape(1)
-    step = width // 7
-    step_down = step_gate_up = None
-    pending, start = [], 0
+    pending, behind, start, step = [], [], 0, width // 7
     for units in (1, 3, 3):
         mine = down_call(
-            (hidden_a, hidden_b), (grads_a, grads_b), first_down, second_down, start, units, step
+            behind,
+            (hidden_a, hidden_b),
+            (grads_a, grads_b),
+            first_down,
+            second_down,
+            start,
+            units,
+            step,
         )
-        pending.append((0, mine, send(mine, to_swap), start, units))
-        start += units
-    start = 0
-    for units in (2, 2, 2, 1):
+        theirs = send(mine, to_swap)
+        pending.append((mine, theirs, start, units))
+        behind, start = [mine], start + units
+    downs = len(pending)
+    start, step = 0, width // 14
+    for units in (4, 4, 4, 1, 1):
         mine = gate_up_call(
+            behind,
             (rows_a, rows_b),
-            (gate_a, up_a, gate_b, up_b),
+            (back_a, back_b),
             first_gate_up,
             second_gate_up,
             start,
             units,
             step,
         )
-        pending.append((1, mine, send(mine, to_swap), start, units))
-        start += units
-    for kind, mine, theirs, start, units in pending:
-        if kind == 0:
-            step_down = place(
-                swapping, mine, theirs, step_down, w_down.shape, start, units, 2
-            )
-        else:
-            step_gate_up = place(
-                swapping, mine, theirs, step_gate_up, w_gate_up.shape, start, units, 2
-            )
-    return (step_gate_up, step_down)
+        theirs = send(mine, to_swap)
+        pending.append((mine, theirs, start, units))
+        behind, start = [mine], start + units
+    whole = None
+    for mine, theirs, start, units in pending[:downs]:
+        whole = place([], swapping, mine, theirs, whole, w_down.shape, start, units)
+    step_down, whole, behind = whole, None, [whole]
+    for mine, theirs, start, units in pending[downs:]:
+        whole = place(behind, swapping, mine, theirs, whole, w_gate_up.shape, start, units)
+        behind = []
+    return (whole, step_down)
 
 
 def solution(mesh):

time: 338 us -> 387 us (1.14)
  Pallas kernels: 80.3 us -> 103 us
  waiting for transfers between devices: 185 us -> 206 us
    ppermute x21 -> x26, waiting for transfers between devices: 105 us -> 196 us  [send(): return lax.ppermute(value, AXES, pairs)]
    all_to_all x2, waiting for transfers between devices: 80.1 us -> 10.7 us  [over_yz(): lax.all_to_all(value, 'expert', 0, 0, axis_index_groups=groups, tiled=True)]
    pallas_call x7 -> x9, Pallas kernels: 31.2 us -> 50.7 us  [the longest x5 26.6 us: gate_up_call(): pl.pallas_call(after(gate_up_kernel, len(behind)), grid=(units,), in_spec...]
    pallas_call x7 -> x8, Pallas kernels: 18 us -> 26.6 us  [place(): pl.pallas_call(place_kernel, grid=(units,), in_specs=[pl.BlockSpec(memory...]
    pallas_call x2 -> x1, Pallas kernels: 20 us -> 12.8 us  [forward_call(): pl.pallas_call(forward_kernel, grid=(width // step,), in_specs=[pl.BlockS...]
    ppermute x21 -> x26, starting transfers between devices: 44.2 us -> 47 us  [send(): return lax.ppermute(value, AXES, pairs)]
  transfers between devices with their start and end apart: 23 -> 28, of which waited for: 7 -> 10; matrix products, arithmetic and copies ran while one was open for 2% -> 2% of each run, Pallas kernels for 18% -> 25%
where the time goes in v2:
time: 387 us; the launch traced here: 385 us
  waiting for transfers between devices  206 us (53%)
  Pallas kernels  103 us (27%)
  starting transfers between devices  62 us (16%)
  other arithmetic  6.57 us (2%)
  local copies, waits for them, and re-layouts  6.07 us (2%)
    ppermute x26, waiting for transfers between devices, send(): return lax.ppermute(value, AXES, pairs)  196 us
    ppermute x26, starting transfers between devices, send(): return lax.ppermute(value, AXES, pairs)  47 us
    pallas_call x8, Pallas kernels, place(): pl.pallas_call(place_kernel, grid=(units,), in_specs=[pl.BlockSpec(memory...  26.6 us
    pallas_call x5, Pallas kernels, gate_up_call(): pl.pallas_call(after(gate_up_kernel, len(behind)), grid=(units,), in_spec...  26.6 us
    pallas_call x3, Pallas kernels, down_call(): pl.pallas_call(after(down_kernel, len(behind)), grid=(units,), in_specs=[...  15.3 us
    all_to_all x2, starting transfers between devices, over_yz(): lax.all_to_all(value, 'expert', 0, 0, axis_index_groups=groups, tiled=True)  15 us
    pallas_call x2, Pallas kernels, gather_call(): pl.pallas_call(kernel, grid=(width // step,), in_specs=[pl.BlockSpec(memo...  12.8 us
    pallas_call x1, Pallas kernels, forward_call(): pl.pallas_call(forward_kernel, grid=(width // step,), in_specs=[pl.BlockS...  12.8 us
  transfers between devices with their start and end apart: 28, of which 10 were waited for; matrix products, arithmetic and copies ran while one was open for 2% of the time, Pallas kernels for 25%

profile of v2, /device:TPU:64, one launch (start us, length us, event | category | flops | bytes accessed | tf_op | source)
XLA Modules:
  0.0 384.8 jit_solution(7219460024823615028)
XLA Ops:
  0.7 0.7 convert_bitcast_fusion
  1.4 0.7 pad_maximum_fusion.1.small_a
  2.1 0.5 collective-permute-start.9
  2.6 0.6 pad_add_fusion.1.side
  3.2 0.2 collective-permute-done.9.small_b
  3.4 0.6 copy-done.14
  4.0 0.4 copy-done.7
  4.3 5.3 %shard_map.132 = bf16[16,24,3584]{2,1,0:T(8,128)(2,1)} custom-call(s32[2]{0:T(128)} %pad_add_fusion.1.side, s32[1,32]{1,0:T(1,128)} %bitcast.11, f32[4,128]{1,0:T(4,128)} %copy-done.11, f32[4,128]{1,0:T(4,128)} %copy-done.14, bf16[128,3584]{1,0:T(8,128)(2,1)} %data_a.1, bf16[128,3584]{1,0:T(8,128)(2,1)} %copy-done.7), custom_call_target="tpu_custom_call" | custom-call | flops 704643072 | bytes 4587520 | tf_op jit(solution)/shard_map/pallas_call | solution.py:152
  9.6 7.7 %all-to-all-start.1 = ((bf16[16,24,3584]{2,1,0:T(8,128)(2,1)}), bf16[16,24,3584]{2,1,0:T(8,128)(2,1)S(1)}, u32[]{:S(2)}, u32[]{:S(2)}) async-start(bf16[16,24,3584]{2,1,0:T(8,128)(2,1)} %shard_map.132), calls=%async_computation.1 | async-start | bytes 5505024 | tf_op jit(solution)/shard_map/all_to_all | solution.py:68
  17.4 1.5 collective-permute-start.6
  18.9 2.1 collective-permute-start.5
  20.9 1.6 collective-permute-start.4
  22.5 2.2 collective-permute-start.7
  24.8 1.4 collective-permute-start.3
  26.2 34.5 %collective-permute-done.3.sd = f32[4,128]{1,0:T(4,128)S(1)} collective-permute-done((f32[4,128]{1,0:T(4,128)S(1)}, f32[4,128]{1,0:T(4,128)S(1)}, u32[]{:S(2)}, u32[]{:S(2)}) %collective-permute-start.3) | collective-permute-done | bytes 2080 | tf_op jit(solution)/shard_map/ppermute | solution.py:31
  60.7 1.5 collective-permute-start.2
  62.1 2.1 collective-permute-done.2.sc
  64.2 0.7 collective-permute-start
  64.9 0.7 pad_add_fusion.side
  65.6 7.3 %collective-permute-start.1 = (f32[4,128]{1,0:T(4,128)S(1)}, f32[4,128]{1,0:T(4,128)S(1)}, u32[]{:S(2)}, u32[]{:S(2)}) collective-permute-start(f32[4,128]{1,0:T(4,128)S(1)} %copy-done.12), channel_id=1, source_target_pairs={{0,65},{1,33},{2,67},{3,35},{4,69},{5,37},{6,71},{7,39},{8,73},{9,... | collective-permute-start | bytes 6152 | tf_op jit(solution)/shard_map/ppermute | solution.py:31
  72.9 0.6 broadcast_select_fusion.2.sa
  73.5 0.7 collective-permute-done.1.sb
  74.2 0.5 copy-done.17
  74.8 7.5 %shard_map.131 = bf16[16,48,3584]{2,1,0:T(8,128)(2,1)} custom-call(s32[2]{0:T(128)} %pad_add_fusion.side, s32[1,32]{1,0:T(1,128)} %bitcast.12, f32[4,128]{1,0:T(4,128)} %broadcast_select_fusion.2.sa, f32[4,128]{1,0:T(4,128)} %copy-done.17, f32[4,128]{1,0:T(4,128)} %copy-done.16, f32[4,128]{1,0:T(4,128)} %copy-done.15, bf16[128,3584]{1,0:T(8,128)(2,1)} %own.1, ...), custom_call_target="tpu_custom_call" | custom-call | flops 1409286144 | bytes 10092544 | tf_op jit(solution)/shard_map/pallas_call | solution.py:152
  82.3 7.2 %all-to-all-start = ((bf16[16,48,3584]{2,1,0:T(8,128)(2,1)}), bf16[16,48,3584]{2,1,0:T(8,128)(2,1)}, u32[]{:S(2)}, u32[]{:S(2)}) async-start(bf16[16,48,3584]{2,1,0:T(8,128)(2,1)} %shard_map.131), calls=%async_computation | async-start | bytes 11010048 | tf_op jit(solution)/shard_map/all_to_all | solution.py:68
  89.6 0.8 collective-permute-start.12
  90.5 59.8 %collective-permute-done.11 = bf16[16,24,3584]{2,1,0:T(8,128)(2,1)S(1)} collective-permute-done((bf16[16,24,3584]{2,1,0:T(8,128)(2,1)S(1)}, bf16[16,24,3584]{2,1,0:T(8,128)(2,1)S(1)}, u32[]{:S(2)}, u32[]{:S(2)}) %collective-permute-start.11) | collective-permute-done | bytes 2752544 | tf_op jit(solution)/shard_map/ppermute | solution.py:31
  150.3 0.4 broadcast_select_fusion.1
  150.8 2.9 pad_maximum_fusion
  153.7 6.0 %collective-permute-start.15 = (bf16[768,3584]{1,0:T(8,128)(2,1)}, bf16[768,3584]{1,0:T(8,128)(2,1)}, u32[]{:S(2)}, u32[]{:S(2)}) collective-permute-start(bf16[768,3584]{1,0:T(8,128)(2,1)} %bitcast.7.grads.refs_2_.refs_3_), channel_id=1, source_target_pairs={{0,32},{1,33},{2,34},{3,35},{4,36},{5,37},{6,38},{7,39},{8,40},{9,... | collective-permute-start | bytes 16515080 | tf_op jit(solution)/shard_map/ppermute | solution.py:31
  159.7 10.7 %all-to-all-done = bf16[16,48,3584]{2,1,0:T(8,128)(2,1)} async-done(((bf16[16,48,3584]{2,1,0:T(8,128)(2,1)}), bf16[16,48,3584]{2,1,0:T(8,128)(2,1)}, u32[]{:S(2)}, u32[]{:S(2)}) %all-to-all-start) | async-done | bytes 5505056 | tf_op jit(solution)/shard_map/all_to_all | solution.py:68
  170.5 0.4 collective-permute-start.8
  171.0 16.6 %collective-permute-done.13.down_b = bf16[1,256,3584]{2,1,0:T(8,128)(2,1)} collective-permute-done((bf16[1,256,3584]{2,1,0:T(8,128)(2,1)S(1)}, bf16[1,256,3584]{2,1,0:T(8,128)(2,1)}, u32[]{:S(2)}, u32[]{:S(2)}) %collective-permute-start.13) | collective-permute-done | bytes 1835040 | tf_op jit(solution)/shard_map/ppermute | solution.py:31
  187.6 8.9 %shard_map.133.hidden_grads = f32[2,768,256]{2,1,0:T(8,128)} custom-call(bf16[768,3584]{1,0:T(8,128)(2,1)} %bitcast.7.grads.refs_2_.refs_3_, bf16[1,256,3584]{2,1,0:T(8,128)(2,1)} %down_a.1, bf16[1,256,3584]{2,1,0:T(8,128)(2,1)} %collective-permute-done.13.down_b), custom_call_target="tpu_custom_call" | custom-call | flops 2818572288 | bytes 10747904 | tf_op jit(solution)/shard_map/pallas_call | solution.py:185
  196.5 12.8 %shard_map.134 = (bf16[256,768]{1,0:T(8,128)(2,1)}, bf16[256,768]{1,0:T(8,128)(2,1)}, bf16[768,512]{1,0:T(8,128)(2,1)}, bf16[768,512]{1,0:T(8,128)(2,1)}) custom-call(bf16[768,3584]{1,0:T(8,128)(2,1)} %bitcast.5.rows.refs_1_, bf16[1,2,3584,256]{3,2,1,0:T(8,128)(2,1)} %gate_up_a.1, bf16[1,2,3584,256]{3,2,1,0:T(8,128)(2,1)} %collective-permute-done.8.gate_up_b, ...), custom_call_target="tpu_custom_call" | custom-call | flops 5637144576 | bytes 12845056 | tf_op jit(solution)/shard_map/pallas_call | solution.py:235
  209.4 0.4 collective-permute-start.14
  209.8 2.5 collective-permute-done.14.refs_1_.refs_2_
  212.3 0.7 copy-done.3
  213.1 3.3 shard_map.135.refs_0_.mine
  216.3 12.8 %collective-permute-start.25 = (bf16[1,256,512]{2,1,0:T(8,128)(2,1)}, bf16[1,256,512]{2,1,0:T(8,128)(2,1)S(1)}, u32[]{:S(2)}, u32[]{:S(2)}) collective-permute-start(bf16[1,256,512]{2,1,0:T(8,128)(2,1)} %shard_map.135.refs_0_.mine), channel_id=1, source_target_pairs={{0,16},{1,17},{2,18},{3,19},{4,20},{5,21},{6,22},{7,23},{8,24},{9,... | collective-permute-start | bytes 786440 | tf_op jit(solution)/shard_map/ppermute | solution.py:31
  229.2 6.0 %shard_map.136.refs_0_.mine = bf16[1,256,1536]{2,1,0:T(8,128)(2,1)} custom-call(bf16[1,256,512]{2,1,0:T(8,128)(2,1)} %shard_map.135.refs_0_.mine, bf16[256,768]{1,0:T(8,128)(2,1)} %get-tuple-element.6.refs_0_.refs_1_, bf16[256,768]{1,0:T(8,128)(2,1)} %copy-done.3, bf16[768,3584]{1,0:T(8,128)(2,1)} %bitcast.7.grads.refs_2_.refs_3_, ...), custom_call_target="tpu_custom_call" | custom-call | flops 1207959552 | bytes 7077888 | tf_op jit(solution)/shard_map/pallas_call | solution.py:275
  235.2 6.0 %shard_map.137.refs_0_.mine = bf16[1,256,1536]{2,1,0:T(8,128)(2,1)} custom-call(bf16[1,256,1536]{2,1,0:T(8,128)(2,1)} %shard_map.136.refs_0_.mine, bf16[256,768]{1,0:T(8,128)(2,1)} %get-tuple-element.6.refs_0_.refs_1_, bf16[256,768]{1,0:T(8,128)(2,1)} %copy-done.3, bf16[768,3584]{1,0:T(8,128)(2,1)} %bitcast.7.grads.refs_2_.refs_3_, ...), custom_call_target="tpu_custom_call" | custom-call | flops 1207959552 | bytes 7077888 | tf_op jit(solution)/shard_map/pallas_call | solution.py:275
  241.2 0.9 copy-done
  242.1 6.6 %shard_map.138.refs_0_.mine = bf16[1,2,1024,256]{3,2,1,0:T(8,128)(2,1)} custom-call(bf16[1,256,1536]{2,1,0:T(8,128)(2,1)} %shard_map.137.refs_0_.mine, bf16[768,3584]{1,0:T(8,128)(2,1)} %bitcast.5.rows.refs_1_, bf16[768,3584]{1,0:T(8,128)(2,1)} %collective-permute-done.16.refs_2_, bf16[768,512]{1,0:T(8,128)(2,1)} %get-tuple-element.8.refs_3_, ...), custom_call_target="tpu_custom_call" | custom-call | flops 1610612736 | bytes 6291456 | tf_op jit(solution)/shard_map/pallas_call | solution.py:310
  248.7 6.7 %shard_map.139.refs_0_.mine = bf16[1,2,1024,256]{3,2,1,0:T(8,128)(2,1)} custom-call(bf16[1,2,1024,256]{3,2,1,0:T(8,128)(2,1)} %shard_map.138.refs_0_.mine, bf16[768,3584]{1,0:T(8,128)(2,1)} %bitcast.5.rows.refs_1_, bf16[768,3584]{1,0:T(8,128)(2,1)} %collective-permute-done.16.refs_2_, bf16[768,512]{1,0:T(8,128)(2,1)} %get-tuple-element.8.refs_3_, ...), custom_call_target="tpu_custom_call" | custom-call | flops 1610612736 | bytes 6291456 | tf_op jit(solution)/shard_map/pallas_call | solution.py:310
  255.4 3.6 collective-permute-start.21
  258.9 6.6 %shard_map.140.refs_0_.mine = bf16[1,2,1024,256]{3,2,1,0:T(8,128)(2,1)} custom-call(bf16[1,2,1024,256]{3,2,1,0:T(8,128)(2,1)} %shard_map.139.refs_0_.mine, bf16[768,3584]{1,0:T(8,128)(2,1)} %bitcast.5.rows.refs_1_, bf16[768,3584]{1,0:T(8,128)(2,1)} %collective-permute-done.16.refs_2_, bf16[768,512]{1,0:T(8,128)(2,1)} %get-tuple-element.8.refs_3_, ...), custom_call_target="tpu_custom_call" | custom-call | flops 1610612736 | bytes 6291456 | tf_op jit(solution)/shard_map/pallas_call | solution.py:310
  265.7 3.4 collective-permute-start.23
  269.3 3.3 shard_map.141.refs_0_.mine
  272.6 3.4 shard_map.142.mine
  276.0 62.4 %collective-permute-done.23.theirs = bf16[1,256,1536]{2,1,0:T(8,128)(2,1)} collective-permute-done((bf16[1,256,1536]{2,1,0:T(8,128)(2,1)S(1)}, bf16[1,256,1536]{2,1,0:T(8,128)(2,1)}, u32[]{:S(2)}, u32[]{:S(2)}) %collective-permute-start.23) | collective-permute-done | bytes 786464 | tf_op jit(solution)/shard_map/ppermute | solution.py:31
  338.4 16.8 %collective-permute-done.24.theirs = bf16[1,256,1536]{2,1,0:T(8,128)(2,1)} collective-permute-done((bf16[1,256,1536]{2,1,0:T(8,128)(2,1)S(1)}, bf16[1,256,1536]{2,1,0:T(8,128)(2,1)}, u32[]{:S(2)}, u32[]{:S(2)}) %collective-permute-start.24) | collective-permute-done | bytes 786464 | tf_op jit(solution)/shard_map/ppermute | solution.py:31
  355.2 0.6 dynamic_slice.3.swapping
  355.8 2.3 shard_map.143.rest_0_
  358.1 3.6 shard_map.144.rest_0_
  361.7 3.6 shard_map.145.rest_0_
  365.3 4.1 %shard_map.146.rest_0_ = bf16[1,2,3584,256]{3,2,1,0:T(8,128)(2,1)} custom-call(s32[1]{0:T(128)} %dynamic_slice.3.swapping, bf16[1,2,1024,256]{3,2,1,0:T(8,128)(2,1)} %shard_map.138.refs_0_.mine, bf16[1,2,1024,256]{3,2,1,0:T(8,128)(2,1)} %collective-permute-done.22.theirs, bf16[1,256,3584]{2,1,0:T(8,128)(2,1)} %shard_map.145.rest_0_), custom_call_target="tpu_custom_call" | custom-call | bytes 3145728 | tf_op jit(solution)/shard_map/pallas_call | solution.py:341
  369.5 4.1 %shard_map.147.rest_0_ = bf16[1,2,3584,256]{3,2,1,0:T(8,128)(2,1)} custom-call(s32[1]{0:T(128)} %dynamic_slice.3.swapping, bf16[1,2,1024,256]{3,2,1,0:T(8,128)(2,1)} %shard_map.139.refs_0_.mine, bf16[1,2,1024,256]{3,2,1,0:T(8,128)(2,1)} %collective-permute-done.21.theirs, bf16[1,2,3584,256]{3,2,1,0:T(8,128)(2,1)} %shard_map.146.rest_0_), custom_call_target="tpu_custom_call", output_to_operand_aliasing={{}: (3, {})} | custom-call | bytes 3145728 | tf_op jit(solution)/shard_map/pallas_call | solution.py:341
  373.6 1.0 copy-done.6
  374.6 4.1 %shard_map.148.rest_0_ = bf16[1,2,3584,256]{3,2,1,0:T(8,128)(2,1)} custom-call(s32[1]{0:T(128)} %dynamic_slice.3.swapping, bf16[1,2,1024,256]{3,2,1,0:T(8,128)(2,1)} %shard_map.140.refs_0_.mine, bf16[1,2,1024,256]{3,2,1,0:T(8,128)(2,1)} %copy-done.6, bf16[1,2,3584,256]{3,2,1,0:T(8,128)(2,1)} %shard_map.147.rest_0_), custom_call_target="tpu_custom_call", output_to_operand_aliasing={{}: (3, {})} | custom-call | bytes 3145728 | tf_op jit(solution)/shard_map/pallas_call | solution.py:341
  378.7 0.7 copy-done.9
  379.4 2.3 shard_map.149.rest_0_
  381.8 0.7 copy-done.10
  382.5 2.3 shard_map.150
  (58 shorter events, 1.0 us)
Async XLA Ops:
  0.6 2.8 collective-permute-start.10
  2.1 1.3 copy-start.11
  2.1 1.3 collective-permute-start.9
  3.4 0.6 copy-start.14
  3.4 0.9 copy-start.7
  9.6 15.2 %copy-start.12 = (f32[4,128]{1,0:T(4,128)S(1)}, f32[4,128]{1,0:T(4,128)}, u32[]{:S(2)}) copy-start(f32[4,128]{1,0:T(4,128)} %copy-done.11) | copy-start | bytes 6148
  9.6 63.3 %copy-start.13 = (f32[128,2]{0,1:T(2,128)S(1)}, f32[128,2]{0,1:T(2,128)}, u32[]{:S(2)}) copy-start(f32[128,2]{0,1:T(2,128)} %param.15) | copy-start | bytes 3076
  9.6 72.7 %all-to-all-start.1 = ((bf16[16,24,3584]{2,1,0:T(8,128)(2,1)}), bf16[16,24,3584]{2,1,0:T(8,128)(2,1)S(1)}, u32[]{:S(2)}, u32[]{:S(2)}) async-start(bf16[16,24,3584]{2,1,0:T(8,128)(2,1)} %shard_map.132), calls=%async_computation.1 | async-start | bytes 5505024 | tf_op jit(solution)/shard_map/all_to_all | solution.py:68
  17.4 56.8 %collective-permute-start.6 = (bf16[128,3584]{1,0:T(8,128)(2,1)}, bf16[128,3584]{1,0:T(8,128)(2,1)}, u32[]{:S(2)}, u32[]{:S(2)}) collective-permute-start(bf16[128,3584]{1,0:T(8,128)(2,1)} %own.1), channel_id=1, source_target_pairs={{0,64},{1,32},{2,66},{3,34},{4,68},{5,36},{6,70},{7,38},{8,72},{9,... | collective-permute-start | bytes 2752520 | tf_op jit(solution)/shard_map/ppermute | solution.py:31
  18.9 55.3 %collective-permute-start.5 = (bf16[128,3584]{1,0:T(8,128)(2,1)}, bf16[128,3584]{1,0:T(8,128)(2,1)}, u32[]{:S(2)}, u32[]{:S(2)}) collective-permute-start(bf16[128,3584]{1,0:T(8,128)(2,1)} %own.1), channel_id=1, source_target_pairs={{0,65},{1,33},{2,67},{3,35},{4,69},{5,37},{6,71},{7,39},{8,73},{9,... | collective-permute-start | bytes 2752520 | tf_op jit(solution)/shard_map/ppermute | solution.py:31
  20.9 53.3 %collective-permute-start.4 = (bf16[128,3584]{1,0:T(8,128)(2,1)}, bf16[128,3584]{1,0:T(8,128)(2,1)}, u32[]{:S(2)}, u32[]{:S(2)}) collective-permute-start(bf16[128,3584]{1,0:T(8,128)(2,1)} %own.1), channel_id=1, source_target_pairs={{1,96},{3,98},{5,100},{7,102},{9,104},{11,106},{13,108},{15,110},{... | collective-permute-start | bytes 2752520 | tf_op jit(solution)/shard_map/ppermute | solution.py:31
  22.5 51.7 %collective-permute-start.7 = (bf16[128,3584]{1,0:T(8,128)(2,1)}, bf16[128,3584]{1,0:T(8,128)(2,1)}, u32[]{:S(2)}, u32[]{:S(2)}) collective-permute-start(bf16[128,3584]{1,0:T(8,128)(2,1)} %own.1), channel_id=1, source_target_pairs={{0,1},{1,97},{2,3},{3,99},{4,5},{5,101},{6,7},{7,103},{8,9},{9,105... | collective-permute-start | bytes 2752520 | tf_op jit(solution)/shard_map/ppermute | solution.py:31
  24.8 35.9 %collective-permute-start.3 = (f32[4,128]{1,0:T(4,128)S(1)}, f32[4,128]{1,0:T(4,128)S(1)}, u32[]{:S(2)}, u32[]{:S(2)}) collective-permute-start(f32[4,128]{1,0:T(4,128)S(1)} %copy-done.12), channel_id=1, source_target_pairs={{0,1},{1,97},{2,3},{3,99},{4,5},{5,101},{6,7},{7,103},{8,9},{9,105... | collective-permute-start | bytes 6152 | tf_op jit(solution)/shard_map/ppermute | solution.py:31
  60.7 13.6 %copy-start.15 = (f32[4,128]{1,0:T(4,128)}, f32[4,128]{1,0:T(4,128)S(1)}, u32[]{:S(2)}) copy-start(f32[4,128]{1,0:T(4,128)S(1)} %collective-permute-done.3.sd) | copy-start | bytes 6148
  60.7 3.6 collective-permute-start.2
  64.2 10.0 %copy-start.16 = (f32[4,128]{1,0:T(4,128)}, f32[4,128]{1,0:T(4,128)S(1)}, u32[]{:S(2)}) copy-start(f32[4,128]{1,0:T(4,128)S(1)} %collective-permute-done.2.sc) | copy-start | bytes 6148
  64.2 1.3 collective-permute-start
  65.6 8.6 %collective-permute-start.1 = (f32[4,128]{1,0:T(4,128)S(1)}, f32[4,128]{1,0:T(4,128)S(1)}, u32[]{:S(2)}, u32[]{:S(2)}) collective-permute-start(f32[4,128]{1,0:T(4,128)S(1)} %copy-done.12), channel_id=1, source_target_pairs={{0,65},{1,33},{2,67},{3,35},{4,69},{5,37},{6,71},{7,39},{8,73},{9,... | collective-permute-start | bytes 6152 | tf_op jit(solution)/shard_map/ppermute | solution.py:31
  74.2 0.6 copy-start.17
  82.3 88.0 %all-to-all-start = ((bf16[16,48,3584]{2,1,0:T(8,128)(2,1)}), bf16[16,48,3584]{2,1,0:T(8,128)(2,1)}, u32[]{:S(2)}, u32[]{:S(2)}) async-start(bf16[16,48,3584]{2,1,0:T(8,128)(2,1)} %shard_map.131), calls=%async_computation | async-start | bytes 11010048 | tf_op jit(solution)/shard_map/all_to_all | solution.py:68
  89.6 0.9 collective-permute-start.12
  90.4 59.9 %collective-permute-start.11 = (bf16[16,24,3584]{2,1,0:T(8,128)(2,1)S(1)}, bf16[16,24,3584]{2,1,0:T(8,128)(2,1)S(1)}, u32[]{:S(2)}, u32[]{:S(2)}) collective-permute-start(bf16[16,24,3584]{2,1,0:T(8,128)(2,1)S(1)} %all-to-all-done.1), channel_id=1, source_target_pairs={{0,64},{1,96},{2,66},{3,98},{4,68},{5,100},{6,70},{7,102},{8,72},{... | collective-permute-start | bytes 8257544 | tf_op jit(solution)/shard_map/ppermute | solution.py:31
  150.8 20.1 %copy-start.5 = (bf16[1,256,3584]{2,1,0:T(8,128)(2,1)S(1)}, bf16[1,256,3584]{2,1,0:T(8,128)(2,1)}, u32[]{:S(2)}) copy-start(bf16[1,256,3584]{2,1,0:T(8,128)(2,1)} %down_a.1) | copy-start | bytes 5505028
  153.7 58.7 %collective-permute-start.15 = (bf16[768,3584]{1,0:T(8,128)(2,1)}, bf16[768,3584]{1,0:T(8,128)(2,1)}, u32[]{:S(2)}, u32[]{:S(2)}) collective-permute-start(bf16[768,3584]{1,0:T(8,128)(2,1)} %bitcast.7.grads.refs_2_.refs_3_), channel_id=1, source_target_pairs={{0,32},{1,33},{2,34},{3,35},{4,36},{5,37},{6,38},{7,39},{8,40},{9,... | collective-permute-start | bytes 16515080 | tf_op jit(solution)/shard_map/ppermute | solution.py:31
  170.4 70.8 %collective-permute-start.16 = (bf16[768,3584]{1,0:T(8,128)(2,1)}, bf16[768,3584]{1,0:T(8,128)(2,1)}, u32[]{:S(2)}, u32[]{:S(2)}) collective-permute-start(bf16[768,3584]{1,0:T(8,128)(2,1)} %bitcast.5.rows.refs_1_), channel_id=1, source_target_pairs={{0,32},{1,33},{2,34},{3,35},{4,36},{5,37},{6,38},{7,39},{8,40},{9,... | collective-permute-start | bytes 16515080 | tf_op jit(solution)/shard_map/ppermute | solution.py:31
  170.5 26.0 %collective-permute-start.8 = (bf16[1,2,3584,256]{3,2,1,0:T(8,128)(2,1)}, bf16[1,2,3584,256]{3,2,1,0:T(8,128)(2,1)}, u32[]{:S(2)}, u32[]{:S(2)}) collective-permute-start(bf16[1,2,3584,256]{3,2,1,0:T(8,128)(2,1)} %gate_up_a.1), channel_id=1, source_target_pairs={{0,32},{1,33},{2,34},{3,35},{4,36},{5,37},{6,38},{7,39},{8,40},{9,... | collective-permute-start | bytes 11010056 | tf_op jit(solution)/shard_map/ppermute | solution.py:31
  170.9 16.7 %collective-permute-start.13 = (bf16[1,256,3584]{2,1,0:T(8,128)(2,1)S(1)}, bf16[1,256,3584]{2,1,0:T(8,128)(2,1)}, u32[]{:S(2)}, u32[]{:S(2)}) collective-permute-start(bf16[1,256,3584]{2,1,0:T(8,128)(2,1)S(1)} %copy-done.5), channel_id=1, source_target_pairs={{0,32},{1,33},{2,34},{3,35},{4,36},{5,37},{6,38},{7,39},{8,40},{9,... | collective-permute-start | bytes 5505032 | tf_op jit(solution)/shard_map/ppermute | solution.py:31
  209.3 31.9 %collective-permute-start.17 = (bf16[768,512]{1,0:T(8,128)(2,1)}, bf16[768,512]{1,0:T(8,128)(2,1)S(1)}, u32[]{:S(2)}, u32[]{:S(2)}) collective-permute-start(bf16[768,512]{1,0:T(8,128)(2,1)} %get-tuple-element.9), channel_id=1, source_target_pairs={{0,32},{1,33},{2,34},{3,35},{4,36},{5,37},{6,38},{7,39},{8,40},{9,... | collective-permute-start | bytes 2359304 | tf_op jit(solution)/shard_map/ppermute | solution.py:31
  209.4 2.9 collective-permute-start.14
  212.3 0.7 copy-start.3
  216.3 52.7 %collective-permute-start.25 = (bf16[1,256,512]{2,1,0:T(8,128)(2,1)}, bf16[1,256,512]{2,1,0:T(8,128)(2,1)S(1)}, u32[]{:S(2)}, u32[]{:S(2)}) collective-permute-start(bf16[1,256,512]{2,1,0:T(8,128)(2,1)} %shard_map.135.refs_0_.mine), channel_id=1, source_target_pairs={{0,16},{1,17},{2,18},{3,19},{4,20},{5,21},{6,22},{7,23},{8,24},{9,... | collective-permute-start | bytes 786440 | tf_op jit(solution)/shard_map/ppermute | solution.py:31
  241.2 0.9 copy-start
  248.7 116.7 %collective-permute-start.22 = (bf16[1,2,1024,256]{3,2,1,0:T(8,128)(2,1)}, bf16[1,2,1024,256]{3,2,1,0:T(8,128)(2,1)}, u32[]{:S(2)}, u32[]{:S(2)}) collective-permute-start(bf16[1,2,1024,256]{3,2,1,0:T(8,128)(2,1)} %shard_map.138.refs_0_.mine), channel_id=1, source_target_pairs={{0,16},{1,17},{2,18},{3,19},{4,20},{5,21},{6,22},{7,23},{8,24},{9,... | collective-permute-start | bytes 3145736 | tf_op jit(solution)/shard_map/ppermute | solution.py:31
  255.4 10.3 %copy-start.2 = (bf16[1,256,1536]{2,1,0:T(8,128)(2,1)S(1)}, bf16[1,256,1536]{2,1,0:T(8,128)(2,1)}, u32[]{:S(2)}) copy-start(bf16[1,256,1536]{2,1,0:T(8,128)(2,1)} %shard_map.137.refs_0_.mine) | copy-start | bytes 2359300
  255.4 13.7 %copy-start.1 = (bf16[1,256,1536]{2,1,0:T(8,128)(2,1)S(1)}, bf16[1,256,1536]{2,1,0:T(8,128)(2,1)}, u32[]{:S(2)}) copy-start(bf16[1,256,1536]{2,1,0:T(8,128)(2,1)} %shard_map.136.refs_0_.mine) | copy-start | bytes 2359300
  255.4 114.1 %collective-permute-start.21 = (bf16[1,2,1024,256]{3,2,1,0:T(8,128)(2,1)}, bf16[1,2,1024,256]{3,2,1,0:T(8,128)(2,1)}, u32[]{:S(2)}, u32[]{:S(2)}) collective-permute-start(bf16[1,2,1024,256]{3,2,1,0:T(8,128)(2,1)} %shard_map.139.refs_0_.mine), channel_id=1, source_target_pairs={{0,16},{1,17},{2,18},{3,19},{4,20},{5,21},{6,22},{7,23},{8,24},{9,... | collective-permute-start | bytes 3145736 | tf_op jit(solution)/shard_map/ppermute | solution.py:31
  265.5 108.1 %collective-permute-start.20 = (bf16[1,2,1024,256]{3,2,1,0:T(8,128)(2,1)}, bf16[1,2,1024,256]{3,2,1,0:T(8,128)(2,1)S(1)}, u32[]{:S(2)}, u32[]{:S(2)}) collective-permute-start(bf16[1,2,1024,256]{3,2,1,0:T(8,128)(2,1)} %shard_map.140.refs_0_.mine), channel_id=1, source_target_pairs={{0,16},{1,17},{2,18},{3,19},{4,20},{5,21},{6,22},{7,23},{8,24},{9,... | collective-permute-start | bytes 3145736 | tf_op jit(solution)/shard_map/ppermute | solution.py:31
  265.7 72.7 %collective-permute-start.23 = (bf16[1,256,1536]{2,1,0:T(8,128)(2,1)S(1)}, bf16[1,256,1536]{2,1,0:T(8,128)(2,1)}, u32[]{:S(2)}, u32[]{:S(2)}) collective-permute-start(bf16[1,256,1536]{2,1,0:T(8,128)(2,1)S(1)} %copy-done.2), channel_id=1, source_target_pairs={{0,16},{1,17},{2,18},{3,19},{4,20},{5,21},{6,22},{7,23},{8,24},{9,... | collective-permute-start | bytes 2359304 | tf_op jit(solution)/shard_map/ppermute | solution.py:31
  269.1 3.5 copy-start.8
  269.1 86.1 %collective-permute-start.24 = (bf16[1,256,1536]{2,1,0:T(8,128)(2,1)S(1)}, bf16[1,256,1536]{2,1,0:T(8,128)(2,1)}, u32[]{:S(2)}, u32[]{:S(2)}) collective-permute-start(bf16[1,256,1536]{2,1,0:T(8,128)(2,1)S(1)} %copy-done.1), channel_id=1, source_target_pairs={{0,16},{1,17},{2,18},{3,19},{4,20},{5,21},{6,22},{7,23},{8,24},{9,... | collective-permute-start | bytes 2359304 | tf_op jit(solution)/shard_map/ppermute | solution.py:31
  272.6 65.7 %copy-start.4 = (bf16[1,2,256,256]{3,2,1,0:T(8,128)(2,1)S(1)}, bf16[1,2,256,256]{3,2,1,0:T(8,128)(2,1)}, u32[]{:S(2)}) copy-start(bf16[1,2,256,256]{3,2,1,0:T(8,128)(2,1)} %shard_map.141.refs_0_.mine) | copy-start | bytes 786436
  272.6 82.6 %copy-start.18 = (s32[32]{0:T(128)S(1)}, s32[32]{0:T(128)}, u32[]{:S(2)}) copy-start(s32[32]{0:T(128)} %param.17) | copy-start | bytes 388
  338.3 40.4 %collective-permute-start.19 = (bf16[1,2,256,256]{3,2,1,0:T(8,128)(2,1)S(1)}, bf16[1,2,256,256]{3,2,1,0:T(8,128)(2,1)S(1)}, u32[]{:S(2)}, u32[]{:S(2)}) collective-permute-start(bf16[1,2,256,256]{3,2,1,0:T(8,128)(2,1)S(1)} %copy-done.4), channel_id=1, source_target_pairs={{0,16},{1,17},{2,18},{3,19},{4,20},{5,21},{6,22},{7,23},{8,24},{9,... | collective-permute-start | bytes 786440 | tf_op jit(solution)/shard_map/ppermute | solution.py:31
  355.2 26.6 %collective-permute-start.18 = (bf16[1,2,256,256]{3,2,1,0:T(8,128)(2,1)}, bf16[1,2,256,256]{3,2,1,0:T(8,128)(2,1)S(1)}, u32[]{:S(2)}, u32[]{:S(2)}) collective-permute-start(bf16[1,2,256,256]{3,2,1,0:T(8,128)(2,1)} %shard_map.142.mine), channel_id=1, source_target_pairs={{0,16},{1,17},{2,18},{3,19},{4,20},{5,21},{6,22},{7,23},{8,24},{9,... | collective-permute-start | bytes 786440 | tf_op jit(solution)/shard_map/ppermute | solution.py:31
  373.6 1.0 copy-start.6
  378.7 0.7 copy-start.9
  381.8 0.7 copy-start.10

commit v3 on v2

--- a/solution.py
+++ b/solution.py
@@ -11,6 +11,8 @@
 YZ = 16
 CAP = 12
 PAIR = 2 * CAP
+GATHER_STEPS = 4
+FORWARD_STEPS = 4
 F32 = jnp.float32
 BF16 = jnp.bfloat16
 
@@ -108,92 +110,181 @@
     return picks, weight
 
 
-def grads_kernel(side, slots, small_a, small_b, data_a, data_b, out, picks, weights):
+def picks_kernel(side, slots, *refs):
+    out = refs[-1]
+    tokens = refs[0].shape[1]
+    for group in range(out.shape[0]):
+        found, _ = row_select(side[0], slots, refs[2 * group : 2 * group + 2])
+        out[group, :, :tokens] = found[0]
+        out[group, :, tokens:] = found[1]
+
+
+def picks_call(side, slots, smalls):
+    return pl.pallas_call(
+        picks_kernel,
+        in_specs=[pl.BlockSpec(memory_space=pltpu.SMEM)]
+        + [pl.BlockSpec(memory_space=pltpu.VMEM)] * (1 + len(smalls)),
+        out_specs=pl.BlockSpec(memory_space=pltpu.VMEM),
+        out_shape=jax.ShapeDtypeStruct(
+            (len(smalls) // 2, YZ * PAIR, 2 * smalls[0].shape[1]), BF16
+        ),
+        cost_estimate=cost(10**8, 10**6),
+        interpret=INTERPRET,
+    )(side, slots, *smalls)
+
+
+def grads_kernel(side, slots, small_a, small_b, data_a, data_b, out, picks, weights, both):
+    count = data_a.shape[0]
+
     @pl.when(pl.program_id(0) == 0)
     def _():
         found, weight = row_select(side[0], slots, (small_a, small_b))
-        picks[0] = found[0]
-        picks[1] = found[1]
+        picks[:, :count] = found[0]
+        picks[:, count:] = found[1]
         weights[...] = weight
 
-    rows = jnp.dot(picks[0], data_a[...], preferred_element_type=F32)
-    rows = rows + jnp.dot(picks[1], data_b[...], preferred_element_type=F32)
+    both[:count] = data_a[...]
+    both[count:] = data_b[...]
+    rows = jnp.dot(picks[...], both[...], preferred_element_type=F32)
     rows = (rows * weights[...]).astype(BF16)
     for yz in range(YZ):
         out[yz] = rows[yz * PAIR : (yz + 1) * PAIR]
 
 
-def tokens_kernel(
-    side, slots, sa, sb, sc, sd, own, data_a, data_b, data_c, data_d, out, picks
-):
-    @pl.when(pl.program_id(0) == 0)
-    def _():
-        for group, smalls in enumerate(((sa, sb), (sc, sd))):
-            found, _ = row_select(side[0], slots, smalls)
-            picks[2 * group] = found[0]
-            picks[2 * group + 1] = found[1]
-
-    first = jnp.where(side[1] == 1, own[...], data_a[...])
-    for group, (left, right) in enumerate(
-        ((first, data_b[...]), (data_c[...], data_d[...]))
-    ):
-        rows = jnp.dot(picks[2 * group], left, preferred_element_type=F32)
-        rows = rows + jnp.dot(picks[2 * group + 1], right, preferred_element_type=F32)
-        rows = rows.astype(BF16)
-        for yz in range(YZ):
-            out[yz, group * PAIR : (group + 1) * PAIR] = rows[yz * PAIR : (yz + 1) * PAIR]
-
-
-def gather_call(kernel, side, slots, smalls, data, groups, extra):
+def grads_call(side, slots, smalls, data):
     count, width = data[0].shape
-    step = width // 4
+    step = width // GATHER_STEPS
     whole = lambda shape: pl.BlockSpec(shape, lambda j: (0,) * len(shape))
     rows = YZ * PAIR
     return pl.pallas_call(
-        kernel,
+        grads_kernel,
         grid=(width // step,),
         in_specs=[pl.BlockSpec(memory_space=pltpu.SMEM), whole(slots.shape)]
         + [whole(s.shape) for s in smalls]
         + [pl.BlockSpec((count, step), lambda j: (0, j)) for _ in data],
-        out_specs=pl.BlockSpec((YZ, groups * PAIR, step), lambda j: (0, 0, j)),
-        out_shape=jax.ShapeDtypeStruct((YZ, groups * PAIR, width), BF16),
-        scratch_shapes=[pltpu.VMEM((2 * groups, rows, count), BF16)] + extra,
-        compiler_params=params(),
-        cost_estimate=cost(
-            4 * groups * rows * count * width, 2 * width * (len(data) * count + groups * rows)
-        ),
+        out_specs=pl.BlockSpec((YZ, PAIR, step), lambda j: (0, 0, j)),
+        out_shape=jax.ShapeDtypeStruct((YZ, PAIR, width), BF16),
+        scratch_shapes=[
+            pltpu.VMEM((rows, 2 * count), BF16),
+            pltpu.VMEM((rows, 1), F32),
+            pltpu.VMEM((2 * count, step), BF16),
+        ],
+        compiler_params=params(),
+        cost_estimate=cost(4 * rows * count * width, 2 * width * (2 * count + rows)),
         interpret=INTERPRET,
     )(side, slots, *smalls, *data)
 
 
-def hidden_grad_kernel(grads, down_a, down_b, out):
+def tokens_kernel(near, picks, own, data_a, data_b, data_c, data_d, out, both):
+    count = own.shape[0]
+
+    @pl.when(near[0] == 1)
+    def _():
+        both[:count] = own[...]
+
+    @pl.when(near[0] != 1)
+    def _():
+        both[:count] = data_a[...]
+
+    both[count : 2 * count] = data_b[...]
+    both[2 * count : 3 * count] = data_c[...]
+    both[3 * count :] = data_d[...]
+    for group in range(2):
+        rows = jnp.dot(
+            picks[group],
+            both[2 * group * count : 2 * (group + 1) * count],
+            preferred_element_type=F32,
+        ).astype(BF16)
+        for yz in range(YZ):
+            out[yz, group * PAIR : (group + 1) * PAIR] = rows[yz * PAIR : (yz + 1) * PAIR]
+
+
+def tokens_call(near, picks, data):
+    count, width = data[0].shape
+    step = width // GATHER_STEPS
+    rows = YZ * PAIR
+    return pl.pallas_call(
+        tokens_kernel,
+        grid=(width // step,),
+        in_specs=[
+            pl.BlockSpec(memory_space=pltpu.SMEM),
+            pl.BlockSpec(picks.shape, lambda j: (0, 0, 0)),
+        ]
+        + [pl.BlockSpec((count, step), lambda j: (0, j)) for _ in data],
+        out_specs=pl.BlockSpec((YZ, 2 * PAIR, step), lambda j: (0, 0, j)),
+        out_shape=jax.ShapeDtypeStruct((YZ, 2 * PAIR, width), BF16),
+        scratch_shapes=[pltpu.VMEM((4 * count, step), BF16)],
+        compiler_params=params(),
+        cost_estimate=cost(8 * rows * count * width, 2 * width * (5 * count + 2 * rows)),
+        interpret=INTERPRET,
+    )(near, picks, *data)
+
+
+def marker_kernel(near, rows, out):
+    out[0] = near[0]
+
+
+def marker_call(near, rows):
+    return pl.pallas_call(
+        marker_kernel,
+        in_specs=[
+            pl.BlockSpec(memory_space=pltpu.SMEM),
+            pl.BlockSpec(memory_space=pl.ANY),
+        ],
+        out_specs=pl.BlockSpec(memory_space=pltpu.SMEM),
+        out_shape=jax.ShapeDtypeStruct((1,), jnp.int32),
+        interpret=INTERPRET,
+    )(near, rows)
+
+
+def hidden_grad_kernel(near, own, near_in, far_in, down_a, down_b, rows, out):
     @pl.when(pl.program_id(0) == 0)
     def _():
         out[...] = jnp.zeros_like(out)
 
+    @pl.when(near[0] == 1)
+    def _():
+        rows[:, :PAIR] = own[...]
+        rows[:, PAIR:] = near_in[...]
+
+    @pl.when(near[0] != 1)
+    def _():
+        rows[:, :PAIR] = near_in[...]
+        rows[:, PAIR:] = far_in[...]
+
+    grads = rows[...].reshape(-1, rows.shape[2])
     for k, down in enumerate((down_a, down_b)):
         out[k] += lax.dot_general(
-            grads[...], down[0], (((1,), (1,)), ((), ())), preferred_element_type=F32
+            grads, down[0], (((1,), (1,)), ((), ())), preferred_element_type=F32
         )
 
 
-def hidden_grad_call(grads, down_a, down_b):
-    count, width = grads.shape
+def hidden_grad_call(near, pieces, down_a, down_b):
+    width = pieces[0].shape[2]
     units = down_a.shape[1]
-    step = width // 7
+    count = 2 * YZ * PAIR
+    step = width // FORWARD_STEPS
     weight = pl.BlockSpec((1, units, step), lambda k: (0, 0, k))
     return pl.pallas_call(
         hidden_grad_kernel,
         grid=(width // step,),
-        in_specs=[pl.BlockSpec((count, step), lambda k: (0, k)), weight, weight],
-        out_specs=pl.BlockSpec((2, count, units), lambda k: (0, 0, 0)),
-        out_shape=jax.ShapeDtypeStruct((2, count, units), F32),
+        in_specs=[pl.BlockSpec(memory_space=pltpu.SMEM)]
+        + [pl.BlockSpec((YZ, PAIR, step), lambda k: (0, 0, k)) for _ in pieces]
+        + [weight, weight],
+        out_specs=[
+            pl.BlockSpec((YZ, 2 * PAIR, step), lambda k: (0, 0, k)),
+            pl.BlockSpec((2, count, units), lambda k: (0, 0, 0)),
+        ],
+        out_shape=[
+            jax.ShapeDtypeStruct((YZ, 2 * PAIR, width), BF16),
+            jax.ShapeDtypeStruct((2, count, units), F32),
+        ],
         compiler_params=params(),
         cost_estimate=cost(
-            4 * count * width * units, 2 * width * (count + 2 * units) + 8 * count * units
+            4 * count * width * units, 5 * width * count + 4 * width * units + 8 * count * units
         ),
         interpret=INTERPRET,
-    )(grads, down_a, down_b)
+    )(near, *pieces, down_a, down_b)
 
 
 def forward_kernel(
@@ -228,7 +319,7 @@
 def forward_call(rows, gate_up_a, gate_up_b, hidden_grads):
     count, width = rows.shape
     units = gate_up_a.shape[3]
-    step = width // 7
+    step = width // FORWARD_STEPS
     weight = pl.BlockSpec((1, 2, step, units), lambda k: (0, 0, k, 0))
     whole = lambda shape: pl.BlockSpec(shape, lambda k: (0,) * len(shape))
     shapes = [(units, count), (units, count), (count, 2 * units), (count, 2 * units)]
@@ -383,41 +474,24 @@
     cotangent_core = send(cotangent, to_core)
     small_in = [send(small, t) for t in token_goals]
     tokens_in = [send(tokens, t) for t in token_goals]
-    scaled = gather_call(
-        grads_kernel,
-        jnp.stack([core, near]).astype(jnp.int32),
-        slots,
-        [small, small_core],
-        [cotangent, cotangent_core],
-        1,
-        [pltpu.VMEM((YZ * PAIR, 1), F32)],
+    near = near.reshape(1)
+    scaled = grads_call(
+        core.astype(jnp.int32).reshape(1), slots, [small, small_core], [cotangent, cotangent_core]
     )
     small_in[0] = jnp.where(near == 1, small, small_in[0])
     grads_0 = over_yz(scaled)
     down_core = send(w_down, to_core)
     gate_up_core = send(w_gate_up, to_core)
 
-    sent_rows = gather_call(
-        tokens_kernel,
-        jnp.stack([side, near]).astype(jnp.int32),
-        slots,
-        small_in,
-        [tokens] + tokens_in,
-        2,
-        [],
-    )
+    picks = picks_call(side.astype(jnp.int32).reshape(1), slots, small_in)
+    sent_rows = tokens_call(near, picks, [tokens] + tokens_in)
     grads_12 = send(grads_0, grad_12)
     grads_3 = send(grads_0, grad_3)
     rows_a = over_yz(sent_rows).reshape(-1, width)
-    grads_a = jnp.concatenate(
-        [
-            jnp.where(near == 1, grads_0, grads_12),
-            jnp.where(near == 1, grads_12, grads_3),
-        ],
-        axis=1,
-    ).reshape(-1, width)
+    near = marker_call(near, rows_a)
+    grads_a, hidden_grads = hidden_grad_call(near, [grads_0, grads_12, grads_3], w_down, down_core)
+    grads_a = grads_a.reshape(-1, width)
     grads_b = send(grads_a, to_core)
-    hidden_grads = hidden_grad_call(grads_a, w_down, down_core)
 
     hidden_a, hidden_other, back_a, back_other = forward_call(
         rows_a, w_gate_up, gate_up_core, hidden_grads

time: 387 us -> 393 us (1.016)
  waiting for transfers between devices: 206 us -> 217 us
  other arithmetic: 6.57 us -> 1.95 us
    all_to_all x2, waiting for transfers between devices: 10.7 us -> 75.4 us  [over_yz(): lax.all_to_all(value, 'expert', 0, 0, axis_index_groups=groups, tiled=True)]
    ppermute x26, waiting for transfers between devices: 196 us -> 142 us  [send(): return lax.ppermute(value, AXES, pairs)]
    pallas_call x2 -> x4, Pallas kernels: 12.8 us -> 14.5 us  [the longest x1 7.09 us: tokens_call(): pl.pallas_call(tokens_kernel, grid=(width // step,), in_specs=[pl.BlockSp...]
  transfers between devices with their start and end apart: 28 -> 28, of which waited for: 10 -> 9; matrix products, arithmetic and copies ran while one was open for 2% -> 1% of each run, Pallas kernels for 25% -> 22%
where the time goes in v3:
time: 393 us; the launch traced here: 392 us
  waiting for transfers between devices  217 us (55%)
  Pallas kernels  104 us (26%)
  starting transfers between devices  61.3 us (16%)
  local copies, waits for them, and re-layouts  6.12 us (2%)
    ppermute x26, waiting for transfers between devices, send(): return lax.ppermute(value, AXES, pairs)  142 us
    all_to_all x2, waiting for transfers between devices, over_yz(): lax.all_to_all(value, 'expert', 0, 0, axis_index_groups=groups, tiled=True)  75.4 us
    ppermute x26, starting transfers between devices, send(): return lax.ppermute(value, AXES, pairs)  46.3 us
    pallas_call x5, Pallas kernels, gate_up_call(): pl.pallas_call(after(gate_up_kernel, len(behind)), grid=(units,), in_spec...  26.6 us
    pallas_call x8, Pallas kernels, place(): pl.pallas_call(place_kernel, grid=(units,), in_specs=[pl.BlockSpec(memory...  26.6 us
    pallas_call x3, Pallas kernels, down_call(): pl.pallas_call(after(down_kernel, len(behind)), grid=(units,), in_specs=[...  15.3 us
    all_to_all x2, starting transfers between devices, over_yz(): lax.all_to_all(value, 'expert', 0, 0, axis_index_groups=groups, tiled=True)  15 us
    pallas_call x1, Pallas kernels, forward_call(): pl.pallas_call(forward_kernel, grid=(width // step,), in_specs=[pl.BlockS...  12.1 us
  transfers between devices with their start and end apart: 28, of which 9 were waited for; matrix products, arithmetic and copies ran while one was open for 1% of the time, Pallas kernels for 22%

profile of v3, /device:TPU:64, one launch (start us, length us, event | category | flops | bytes accessed | tf_op | source)
XLA Modules:
  0.0 391.6 jit_solution(7918786452405754230)
XLA Ops:
  0.7 0.7 convert_bitcast_fusion
  1.4 0.7 pad_maximum_fusion.small_a
  2.1 0.5 collective-permute-start.9
  2.6 0.8 collective-permute-done.9.small_b
  3.4 0.6 copy-done.16
  4.0 0.4 copy-done.7
  4.3 5.0 %shard_map.134 = bf16[16,24,3584]{2,1,0:T(8,128)(2,1)} custom-call(s32[1]{0:T(128)} %bitcast.7.side, s32[1,32]{1,0:T(1,128)} %bitcast.16, f32[4,128]{1,0:T(4,128)} %copy-done.11, f32[4,128]{1,0:T(4,128)} %copy-done.16, bf16[128,3584]{1,0:T(8,128)(2,1)} %data_a.1, bf16[128,3584]{1,0:T(8,128)(2,1)} %copy-done.7), custom_call_target="tpu_custom_call" | custom-call | flops 704643072 | bytes 4587520 | tf_op jit(solution)/shard_map/pallas_call | solution.py:159
  9.4 7.7 %all-to-all-start.1 = ((bf16[16,24,3584]{2,1,0:T(8,128)(2,1)}), bf16[16,24,3584]{2,1,0:T(8,128)(2,1)S(1)}, u32[]{:S(2)}, u32[]{:S(2)}) async-start(bf16[16,24,3584]{2,1,0:T(8,128)(2,1)} %shard_map.134), calls=%async_computation.1 | async-start | bytes 5505024 | tf_op jit(solution)/shard_map/all_to_all | solution.py:70
  17.1 1.5 collective-permute-start.6
  18.6 2.1 collective-permute-start.5
  20.7 1.6 collective-permute-start.4
  22.3 2.2 collective-permute-start.7
  24.5 1.4 collective-permute-start.3
  25.9 34.5 %collective-permute-done.3.refs_3_ = f32[4,128]{1,0:T(4,128)S(1)} collective-permute-done((f32[4,128]{1,0:T(4,128)S(1)}, f32[4,128]{1,0:T(4,128)S(1)}, u32[]{:S(2)}, u32[]{:S(2)}) %collective-permute-start.3) | collective-permute-done | bytes 2080 | tf_op jit(solution)/shard_map/ppermute | solution.py:33
  60.4 1.5 collective-permute-start.2
  61.9 2.1 collective-permute-done.2.refs_2_
  64.0 0.7 collective-permute-start
  64.7 8.0 %collective-permute-start.1 = (f32[4,128]{1,0:T(4,128)S(1)}, f32[4,128]{1,0:T(4,128)S(1)}, u32[]{:S(2)}, u32[]{:S(2)}) collective-permute-start(f32[4,128]{1,0:T(4,128)S(1)} %copy-done.12), channel_id=1, source_target_pairs={{0,65},{1,33},{2,67},{3,35},{4,69},{5,37},{6,71},{7,39},{8,73},{9,... | collective-permute-start | bytes 6152 | tf_op jit(solution)/shard_map/ppermute | solution.py:33
  72.6 0.6 broadcast_select_fusion.refs_0_
  73.2 0.7 collective-permute-done.1.refs_1_
  73.9 0.6 copy-done.17
  74.5 1.8 shard_map.131.picks
  76.4 7.1 %shard_map.132 = bf16[16,48,3584]{2,1,0:T(8,128)(2,1)} custom-call(s32[1]{0:T(128)} %bitcast.near, bf16[2,384,256]{2,1,0:T(8,128)(2,1)} %shard_map.131.picks, bf16[128,3584]{1,0:T(8,128)(2,1)} %own.1, bf16[128,3584]{1,0:T(8,128)(2,1)} %collective-permute-done.4.data_a, bf16[128,3584]{1,0:T(8,128)(2,1)} %collective-permute-done.5.data_b, ...), custom_call_target="tpu_custom_call" | custom-call | flops 1409286144 | bytes 10092544 | tf_op jit(solution)/shard_map/pallas_call | solution.py:206
  83.5 7.2 %all-to-all-start = ((bf16[16,48,3584]{2,1,0:T(8,128)(2,1)}), bf16[16,48,3584]{2,1,0:T(8,128)(2,1)}, u32[]{:S(2)}, u32[]{:S(2)}) async-start(bf16[16,48,3584]{2,1,0:T(8,128)(2,1)} %shard_map.132), calls=%async_computation | async-start | bytes 11010048 | tf_op jit(solution)/shard_map/all_to_all | solution.py:70
  90.7 2.2 collective-permute-start.12
  93.0 3.4 collective-permute-start.13
  96.3 75.4 %all-to-all-done = bf16[16,48,3584]{2,1,0:T(8,128)(2,1)} async-done(((bf16[16,48,3584]{2,1,0:T(8,128)(2,1)}), bf16[16,48,3584]{2,1,0:T(8,128)(2,1)}, u32[]{:S(2)}, u32[]{:S(2)}) %all-to-all-start) | async-done | bytes 5505056 | tf_op jit(solution)/shard_map/all_to_all | solution.py:70
  171.7 0.5 shard_map.133.near
  172.2 9.4 %shard_map.135 = (bf16[16,48,3584]{2,1,0:T(8,128)(2,1)}, f32[2,768,256]{2,1,0:T(8,128)}) custom-call(s32[1]{0:T(128)} %shard_map.133.near, bf16[16,24,3584]{2,1,0:T(8,128)(2,1)} %copy-done.1, bf16[16,24,3584]{2,1,0:T(8,128)(2,1)} %collective-permute-done.11.near_in, bf16[16,24,3584]{2,1,0:T(8,128)(2,1)} %collective-permute-done.12.far_in, ...), custom_call_target="tpu_custom_call" | custom-call | flops 2818572288 | bytes 19005440 | tf_op jit(solution)/shard_map/pallas_call | solution.py:268
  181.7 0.4 collective-permute-start.16
  182.3 21.9 %collective-permute-done.8.gate_up_b = bf16[1,2,3584,256]{3,2,1,0:T(8,128)(2,1)} collective-permute-done((bf16[1,2,3584,256]{3,2,1,0:T(8,128)(2,1)}, bf16[1,2,3584,256]{3,2,1,0:T(8,128)(2,1)}, u32[]{:S(2)}, u32[]{:S(2)}) %collective-permute-start.8) | collective-permute-done | bytes 3670048 | tf_op jit(solution)/shard_map/ppermute | solution.py:33
  204.1 12.1 %shard_map.136 = (bf16[256,768]{1,0:T(8,128)(2,1)}, bf16[256,768]{1,0:T(8,128)(2,1)}, bf16[768,512]{1,0:T(8,128)(2,1)}, bf16[768,512]{1,0:T(8,128)(2,1)}) custom-call(bf16[768,3584]{1,0:T(8,128)(2,1)} %bitcast.6.rows.refs_1_, bf16[1,2,3584,256]{3,2,1,0:T(8,128)(2,1)} %gate_up_a.1, bf16[1,2,3584,256]{3,2,1,0:T(8,128)(2,1)} %collective-permute-done.8.gate_up_b, ...), custom_call_target="tpu_custom_call" | custom-call | flops 5637144576 | bytes 12845056 | tf_op jit(solution)/shard_map/pallas_call | solution.py:326
  216.2 0.1 collective-permute-start.17
  216.4 0.4 collective-permute-start.14
  216.7 2.5 collective-permute-done.14.refs_1_.refs_2_
  219.3 0.7 copy-done.4
  220.0 3.3 shard_map.137.refs_0_.mine
  223.3 12.7 %collective-permute-start.25 = (bf16[1,256,512]{2,1,0:T(8,128)(2,1)}, bf16[1,256,512]{2,1,0:T(8,128)(2,1)S(1)}, u32[]{:S(2)}, u32[]{:S(2)}) collective-permute-start(bf16[1,256,512]{2,1,0:T(8,128)(2,1)} %shard_map.137.refs_0_.mine), channel_id=1, source_target_pairs={{0,16},{1,17},{2,18},{3,19},{4,20},{5,21},{6,22},{7,23},{8,24},{9,... | collective-permute-start | bytes 786440 | tf_op jit(solution)/shard_map/ppermute | solution.py:33
  236.0 6.0 %shard_map.138.refs_0_.mine = bf16[1,256,1536]{2,1,0:T(8,128)(2,1)} custom-call(bf16[1,256,512]{2,1,0:T(8,128)(2,1)} %shard_map.137.refs_0_.mine, bf16[256,768]{1,0:T(8,128)(2,1)} %get-tuple-element.9.refs_0_.refs_1_, bf16[256,768]{1,0:T(8,128)(2,1)} %copy-done.4, bf16[768,3584]{1,0:T(8,128)(2,1)} %bitcast.12, ...), custom_call_target="tpu_custom_call" | custom-call | flops 1207959552 | bytes 7077888 | tf_op jit(solution)/shard_map/pallas_call | solution.py:366
  242.0 6.0 %shard_map.139.refs_0_.mine = bf16[1,256,1536]{2,1,0:T(8,128)(2,1)} custom-call(bf16[1,256,1536]{2,1,0:T(8,128)(2,1)} %shard_map.138.refs_0_.mine, bf16[256,768]{1,0:T(8,128)(2,1)} %get-tuple-element.9.refs_0_.refs_1_, bf16[256,768]{1,0:T(8,128)(2,1)} %copy-done.4, bf16[768,3584]{1,0:T(8,128)(2,1)} %bitcast.13, ...), custom_call_target="tpu_custom_call" | custom-call | flops 1207959552 | bytes 7077888 | tf_op jit(solution)/shard_map/pallas_call | solution.py:366
  248.0 0.9 copy-done
  248.9 6.6 %shard_map.140.refs_0_.mine = bf16[1,2,1024,256]{3,2,1,0:T(8,128)(2,1)} custom-call(bf16[1,256,1536]{2,1,0:T(8,128)(2,1)} %shard_map.139.refs_0_.mine, bf16[768,3584]{1,0:T(8,128)(2,1)} %bitcast.6.rows.refs_1_, bf16[768,3584]{1,0:T(8,128)(2,1)} %collective-permute-done.16.refs_2_, bf16[768,512]{1,0:T(8,128)(2,1)} %get-tuple-element.12.refs_3_, ...), custom_call_target="tpu_custom_call" | custom-call | flops 1610612736 | bytes 6291456 | tf_op jit(solution)/shard_map/pallas_call | solution.py:401
  255.6 6.7 %shard_map.141.refs_0_.mine = bf16[1,2,1024,256]{3,2,1,0:T(8,128)(2,1)} custom-call(bf16[1,2,1024,256]{3,2,1,0:T(8,128)(2,1)} %shard_map.140.refs_0_.mine, bf16[768,3584]{1,0:T(8,128)(2,1)} %bitcast.6.rows.refs_1_, bf16[768,3584]{1,0:T(8,128)(2,1)} %collective-permute-done.16.refs_2_, bf16[768,512]{1,0:T(8,128)(2,1)} %get-tuple-element.12.refs_3_, ...), custom_call_target="tpu_custom_call" | custom-call | flops 1610612736 | bytes 6291456 | tf_op jit(solution)/shard_map/pallas_call | solution.py:401
  262.2 3.6 collective-permute-start.21
  265.8 6.6 %shard_map.142.refs_0_.mine = bf16[1,2,1024,256]{3,2,1,0:T(8,128)(2,1)} custom-call(bf16[1,2,1024,256]{3,2,1,0:T(8,128)(2,1)} %shard_map.141.refs_0_.mine, bf16[768,3584]{1,0:T(8,128)(2,1)} %bitcast.6.rows.refs_1_, bf16[768,3584]{1,0:T(8,128)(2,1)} %collective-permute-done.16.refs_2_, bf16[768,512]{1,0:T(8,128)(2,1)} %get-tuple-element.12.refs_3_, ...), custom_call_target="tpu_custom_call" | custom-call | flops 1610612736 | bytes 6291456 | tf_op jit(solution)/shard_map/pallas_call | solution.py:401
  272.4 0.1 collective-permute-start.20
  272.5 3.4 collective-permute-start.23
  275.9 0.2 collective-permute-start.24
  276.2 3.3 shard_map.143.refs_0_.mine
  279.5 3.4 shard_map.144.mine
  282.8 62.3 %collective-permute-done.23.theirs = bf16[1,256,1536]{2,1,0:T(8,128)(2,1)} collective-permute-done((bf16[1,256,1536]{2,1,0:T(8,128)(2,1)S(1)}, bf16[1,256,1536]{2,1,0:T(8,128)(2,1)}, u32[]{:S(2)}, u32[]{:S(2)}) %collective-permute-start.23) | collective-permute-done | bytes 786464 | tf_op jit(solution)/shard_map/ppermute | solution.py:33
  345.2 16.8 %collective-permute-done.24.theirs = bf16[1,256,1536]{2,1,0:T(8,128)(2,1)} collective-permute-done((bf16[1,256,1536]{2,1,0:T(8,128)(2,1)S(1)}, bf16[1,256,1536]{2,1,0:T(8,128)(2,1)}, u32[]{:S(2)}, u32[]{:S(2)}) %collective-permute-start.24) | collective-permute-done | bytes 786464 | tf_op jit(solution)/shard_map/ppermute | solution.py:33
  362.1 0.6 dynamic_slice.3.swapping
  362.6 2.3 shard_map.145.rest_0_
  364.9 3.6 shard_map.146.rest_0_
  368.6 3.6 shard_map.147.rest_0_
  372.2 4.1 %shard_map.148.rest_0_ = bf16[1,2,3584,256]{3,2,1,0:T(8,128)(2,1)} custom-call(s32[1]{0:T(128)} %dynamic_slice.3.swapping, bf16[1,2,1024,256]{3,2,1,0:T(8,128)(2,1)} %shard_map.140.refs_0_.mine, bf16[1,2,1024,256]{3,2,1,0:T(8,128)(2,1)} %collective-permute-done.22.theirs, bf16[1,256,3584]{2,1,0:T(8,128)(2,1)} %shard_map.147.rest_0_), custom_call_target="tpu_custom_call" | custom-call | bytes 3145728 | tf_op jit(solution)/shard_map/pallas_call | solution.py:432
  376.3 4.1 %shard_map.149.rest_0_ = bf16[1,2,3584,256]{3,2,1,0:T(8,128)(2,1)} custom-call(s32[1]{0:T(128)} %dynamic_slice.3.swapping, bf16[1,2,1024,256]{3,2,1,0:T(8,128)(2,1)} %shard_map.141.refs_0_.mine, bf16[1,2,1024,256]{3,2,1,0:T(8,128)(2,1)} %collective-permute-done.21.theirs, bf16[1,2,3584,256]{3,2,1,0:T(8,128)(2,1)} %shard_map.148.rest_0_), custom_call_target="tpu_custom_call", output_to_operand_aliasing={{}: (3, {})} | custom-call | bytes 3145728 | tf_op jit(solution)/shard_map/pallas_call | solution.py:432
  380.5 1.0 copy-done.6
  381.4 4.1 %shard_map.150.rest_0_ = bf16[1,2,3584,256]{3,2,1,0:T(8,128)(2,1)} custom-call(s32[1]{0:T(128)} %dynamic_slice.3.swapping, bf16[1,2,1024,256]{3,2,1,0:T(8,128)(2,1)} %shard_map.142.refs_0_.mine, bf16[1,2,1024,256]{3,2,1,0:T(8,128)(2,1)} %copy-done.6, bf16[1,2,3584,256]{3,2,1,0:T(8,128)(2,1)} %shard_map.149.rest_0_), custom_call_target="tpu_custom_call", output_to_operand_aliasing={{}: (3, {})} | custom-call | bytes 3145728 | tf_op jit(solution)/shard_map/pallas_call | solution.py:432
  385.6 0.7 copy-done.9
  386.3 2.3 shard_map.151.rest_0_
  388.6 0.7 copy-done.10
  389.3 2.3 shard_map.152
  (56 shorter events, 0.5 us)
Async XLA Ops:
  0.6 2.8 collective-permute-start.10
  2.1 1.3 copy-start.11
  2.1 1.3 collective-permute-start.9
  3.4 0.6 copy-start.16
  3.4 0.9 copy-start.7
  9.4 15.2 %copy-start.12 = (f32[4,128]{1,0:T(4,128)S(1)}, f32[4,128]{1,0:T(4,128)}, u32[]{:S(2)}) copy-start(f32[4,128]{1,0:T(4,128)} %copy-done.11) | copy-start | bytes 6148
  9.4 63.3 %copy-start.13 = (f32[128,2]{0,1:T(2,128)S(1)}, f32[128,2]{0,1:T(2,128)}, u32[]{:S(2)}) copy-start(f32[128,2]{0,1:T(2,128)} %param.15) | copy-start | bytes 3076
  9.4 74.1 %all-to-all-start.1 = ((bf16[16,24,3584]{2,1,0:T(8,128)(2,1)}), bf16[16,24,3584]{2,1,0:T(8,128)(2,1)S(1)}, u32[]{:S(2)}, u32[]{:S(2)}) async-start(bf16[16,24,3584]{2,1,0:T(8,128)(2,1)} %shard_map.134), calls=%async_computation.1 | async-start | bytes 5505024 | tf_op jit(solution)/shard_map/all_to_all | solution.py:70
  17.1 59.3 %collective-permute-start.6 = (bf16[128,3584]{1,0:T(8,128)(2,1)}, bf16[128,3584]{1,0:T(8,128)(2,1)}, u32[]{:S(2)}, u32[]{:S(2)}) collective-permute-start(bf16[128,3584]{1,0:T(8,128)(2,1)} %own.1), channel_id=1, source_target_pairs={{0,64},{1,32},{2,66},{3,34},{4,68},{5,36},{6,70},{7,38},{8,72},{9,... | collective-permute-start | bytes 2752520 | tf_op jit(solution)/shard_map/ppermute | solution.py:33
  18.6 57.8 %collective-permute-start.5 = (bf16[128,3584]{1,0:T(8,128)(2,1)}, bf16[128,3584]{1,0:T(8,128)(2,1)}, u32[]{:S(2)}, u32[]{:S(2)}) collective-permute-start(bf16[128,3584]{1,0:T(8,128)(2,1)} %own.1), channel_id=1, source_target_pairs={{0,65},{1,33},{2,67},{3,35},{4,69},{5,37},{6,71},{7,39},{8,73},{9,... | collective-permute-start | bytes 2752520 | tf_op jit(solution)/shard_map/ppermute | solution.py:33
  20.7 55.7 %collective-permute-start.4 = (bf16[128,3584]{1,0:T(8,128)(2,1)}, bf16[128,3584]{1,0:T(8,128)(2,1)}, u32[]{:S(2)}, u32[]{:S(2)}) collective-permute-start(bf16[128,3584]{1,0:T(8,128)(2,1)} %own.1), channel_id=1, source_target_pairs={{1,96},{3,98},{5,100},{7,102},{9,104},{11,106},{13,108},{15,110},{... | collective-permute-start | bytes 2752520 | tf_op jit(solution)/shard_map/ppermute | solution.py:33
  22.3 54.1 %collective-permute-start.7 = (bf16[128,3584]{1,0:T(8,128)(2,1)}, bf16[128,3584]{1,0:T(8,128)(2,1)}, u32[]{:S(2)}, u32[]{:S(2)}) collective-permute-start(bf16[128,3584]{1,0:T(8,128)(2,1)} %own.1), channel_id=1, source_target_pairs={{0,1},{1,97},{2,3},{3,99},{4,5},{5,101},{6,7},{7,103},{8,9},{9,105... | collective-permute-start | bytes 2752520 | tf_op jit(solution)/shard_map/ppermute | solution.py:33
  24.5 35.9 %collective-permute-start.3 = (f32[4,128]{1,0:T(4,128)S(1)}, f32[4,128]{1,0:T(4,128)S(1)}, u32[]{:S(2)}, u32[]{:S(2)}) collective-permute-start(f32[4,128]{1,0:T(4,128)S(1)} %copy-done.12), channel_id=1, source_target_pairs={{0,1},{1,97},{2,3},{3,99},{4,5},{5,101},{6,7},{7,103},{8,9},{9,105... | collective-permute-start | bytes 6152 | tf_op jit(solution)/shard_map/ppermute | solution.py:33
  60.4 13.6 %copy-start.14 = (f32[4,128]{1,0:T(4,128)}, f32[4,128]{1,0:T(4,128)S(1)}, u32[]{:S(2)}) copy-start(f32[4,128]{1,0:T(4,128)S(1)} %collective-permute-done.3.refs_3_) | copy-start | bytes 6148
  60.4 3.6 collective-permute-start.2
  64.0 10.0 %copy-start.15 = (f32[4,128]{1,0:T(4,128)}, f32[4,128]{1,0:T(4,128)S(1)}, u32[]{:S(2)}) copy-start(f32[4,128]{1,0:T(4,128)S(1)} %collective-permute-done.2.refs_2_) | copy-start | bytes 6148
  64.0 0.7 collective-permute-start
  64.7 9.3 %collective-permute-start.1 = (f32[4,128]{1,0:T(4,128)S(1)}, f32[4,128]{1,0:T(4,128)S(1)}, u32[]{:S(2)}, u32[]{:S(2)}) collective-permute-start(f32[4,128]{1,0:T(4,128)S(1)} %copy-done.12), channel_id=1, source_target_pairs={{0,65},{1,33},{2,67},{3,35},{4,69},{5,37},{6,71},{7,39},{8,73},{9,... | collective-permute-start | bytes 6152 | tf_op jit(solution)/shard_map/ppermute | solution.py:33
  73.9 0.6 copy-start.17
  83.5 9.5 %copy-start.1 = (bf16[16,24,3584]{2,1,0:T(8,128)(2,1)}, bf16[16,24,3584]{2,1,0:T(8,128)(2,1)S(1)}, u32[]{:S(2)}) copy-start(bf16[16,24,3584]{2,1,0:T(8,128)(2,1)S(1)} %all-to-all-done.1.own) | copy-start | bytes 8257540
  83.5 88.2 %all-to-all-start = ((bf16[16,48,3584]{2,1,0:T(8,128)(2,1)}), bf16[16,48,3584]{2,1,0:T(8,128)(2,1)}, u32[]{:S(2)}, u32[]{:S(2)}) async-start(bf16[16,48,3584]{2,1,0:T(8,128)(2,1)} %shard_map.132), calls=%async_computation | async-start | bytes 11010048 | tf_op jit(solution)/shard_map/all_to_all | solution.py:70
  90.7 81.5 %collective-permute-start.12 = (bf16[16,24,3584]{2,1,0:T(8,128)(2,1)S(1)}, bf16[16,24,3584]{2,1,0:T(8,128)(2,1)}, u32[]{:S(2)}, u32[]{:S(2)}) collective-permute-start(bf16[16,24,3584]{2,1,0:T(8,128)(2,1)S(1)} %all-to-all-done.1.own), channel_id=1, source_target_pairs={{1,32},{3,34},{5,36},{7,38},{9,40},{11,42},{13,44},{15,46},{17,48}... | collective-permute-start | bytes 8257544 | tf_op jit(solution)/shard_map/ppermute | solution.py:33
  93.0 79.3 %collective-permute-start.11 = (bf16[16,24,3584]{2,1,0:T(8,128)(2,1)S(1)}, bf16[16,24,3584]{2,1,0:T(8,128)(2,1)}, u32[]{:S(2)}, u32[]{:S(2)}) collective-permute-start(bf16[16,24,3584]{2,1,0:T(8,128)(2,1)S(1)} %all-to-all-done.1.own), channel_id=1, source_target_pairs={{0,64},{1,96},{2,66},{3,98},{4,68},{5,100},{6,70},{7,102},{8,72},{... | collective-permute-start | bytes 8257544 | tf_op jit(solution)/shard_map/ppermute | solution.py:33
  93.0 79.3 %collective-permute-start.13 = (bf16[1,256,3584]{2,1,0:T(8,128)(2,1)}, bf16[1,256,3584]{2,1,0:T(8,128)(2,1)}, u32[]{:S(2)}, u32[]{:S(2)}) collective-permute-start(bf16[1,256,3584]{2,1,0:T(8,128)(2,1)} %down_a.1), channel_id=1, source_target_pairs={{0,32},{1,33},{2,34},{3,35},{4,36},{5,37},{6,38},{7,39},{8,40},{9,... | collective-permute-start | bytes 5505032 | tf_op jit(solution)/shard_map/ppermute | solution.py:33
  181.6 37.7 %collective-permute-start.15 = (bf16[768,3584]{1,0:T(8,128)(2,1)}, bf16[768,3584]{1,0:T(8,128)(2,1)}, u32[]{:S(2)}, u32[]{:S(2)}) collective-permute-start(bf16[768,3584]{1,0:T(8,128)(2,1)} %bitcast.10), channel_id=1, source_target_pairs={{0,32},{1,33},{2,34},{3,35},{4,36},{5,37},{6,38},{7,39},{8,40},{9,... | collective-permute-start | bytes 16515080 | tf_op jit(solution)/shard_map/ppermute | solution.py:33
  181.7 66.3 %collective-permute-start.16 = (bf16[768,3584]{1,0:T(8,128)(2,1)}, bf16[768,3584]{1,0:T(8,128)(2,1)}, u32[]{:S(2)}, u32[]{:S(2)}) collective-permute-start(bf16[768,3584]{1,0:T(8,128)(2,1)} %bitcast.6.rows.refs_1_), channel_id=1, source_target_pairs={{0,32},{1,33},{2,34},{3,35},{4,36},{5,37},{6,38},{7,39},{8,40},{9,... | collective-permute-start | bytes 16515080 | tf_op jit(solution)/shard_map/ppermute | solution.py:33
  182.1 22.0 %collective-permute-start.8 = (bf16[1,2,3584,256]{3,2,1,0:T(8,128)(2,1)}, bf16[1,2,3584,256]{3,2,1,0:T(8,128)(2,1)}, u32[]{:S(2)}, u32[]{:S(2)}) collective-permute-start(bf16[1,2,3584,256]{3,2,1,0:T(8,128)(2,1)} %gate_up_a.1), channel_id=1, source_target_pairs={{0,32},{1,33},{2,34},{3,35},{4,36},{5,37},{6,38},{7,39},{8,40},{9,... | collective-permute-start | bytes 11010056 | tf_op jit(solution)/shard_map/ppermute | solution.py:33
  216.2 31.8 %collective-permute-start.17 = (bf16[768,512]{1,0:T(8,128)(2,1)}, bf16[768,512]{1,0:T(8,128)(2,1)S(1)}, u32[]{:S(2)}, u32[]{:S(2)}) collective-permute-start(bf16[768,512]{1,0:T(8,128)(2,1)} %get-tuple-element.13), channel_id=1, source_target_pairs={{0,32},{1,33},{2,34},{3,35},{4,36},{5,37},{6,38},{7,39},{8,40},{9,... | collective-permute-start | bytes 2359304 | tf_op jit(solution)/shard_map/ppermute | solution.py:33
  216.4 2.9 collective-permute-start.14
  219.3 0.7 copy-start.4
  223.3 52.6 %collective-permute-start.25 = (bf16[1,256,512]{2,1,0:T(8,128)(2,1)}, bf16[1,256,512]{2,1,0:T(8,128)(2,1)S(1)}, u32[]{:S(2)}, u32[]{:S(2)}) collective-permute-start(bf16[1,256,512]{2,1,0:T(8,128)(2,1)} %shard_map.137.refs_0_.mine), channel_id=1, source_target_pairs={{0,16},{1,17},{2,18},{3,19},{4,20},{5,21},{6,22},{7,23},{8,24},{9,... | collective-permute-start | bytes 786440 | tf_op jit(solution)/shard_map/ppermute | solution.py:33
  248.0 0.9 copy-start
  255.5 116.7 %collective-permute-start.22 = (bf16[1,2,1024,256]{3,2,1,0:T(8,128)(2,1)}, bf16[1,2,1024,256]{3,2,1,0:T(8,128)(2,1)}, u32[]{:S(2)}, u32[]{:S(2)}) collective-permute-start(bf16[1,2,1024,256]{3,2,1,0:T(8,128)(2,1)} %shard_map.140.refs_0_.mine), channel_id=1, source_target_pairs={{0,16},{1,17},{2,18},{3,19},{4,20},{5,21},{6,22},{7,23},{8,24},{9,... | collective-permute-start | bytes 3145736 | tf_op jit(solution)/shard_map/ppermute | solution.py:33
  262.2 10.3 %copy-start.3 = (bf16[1,256,1536]{2,1,0:T(8,128)(2,1)S(1)}, bf16[1,256,1536]{2,1,0:T(8,128)(2,1)}, u32[]{:S(2)}) copy-start(bf16[1,256,1536]{2,1,0:T(8,128)(2,1)} %shard_map.139.refs_0_.mine) | copy-start | bytes 2359300
  262.2 13.7 %copy-start.2 = (bf16[1,256,1536]{2,1,0:T(8,128)(2,1)S(1)}, bf16[1,256,1536]{2,1,0:T(8,128)(2,1)}, u32[]{:S(2)}) copy-start(bf16[1,256,1536]{2,1,0:T(8,128)(2,1)} %shard_map.138.refs_0_.mine) | copy-start | bytes 2359300
  262.2 114.1 %collective-permute-start.21 = (bf16[1,2,1024,256]{3,2,1,0:T(8,128)(2,1)}, bf16[1,2,1024,256]{3,2,1,0:T(8,128)(2,1)}, u32[]{:S(2)}, u32[]{:S(2)}) collective-permute-start(bf16[1,2,1024,256]{3,2,1,0:T(8,128)(2,1)} %shard_map.141.refs_0_.mine), channel_id=1, source_target_pairs={{0,16},{1,17},{2,18},{3,19},{4,20},{5,21},{6,22},{7,23},{8,24},{9,... | collective-permute-start | bytes 3145736 | tf_op jit(solution)/shard_map/ppermute | solution.py:33
  272.4 108.1 %collective-permute-start.20 = (bf16[1,2,1024,256]{3,2,1,0:T(8,128)(2,1)}, bf16[1,2,1024,256]{3,2,1,0:T(8,128)(2,1)S(1)}, u32[]{:S(2)}, u32[]{:S(2)}) collective-permute-start(bf16[1,2,1024,256]{3,2,1,0:T(8,128)(2,1)} %shard_map.142.refs_0_.mine), channel_id=1, source_target_pairs={{0,16},{1,17},{2,18},{3,19},{4,20},{5,21},{6,22},{7,23},{8,24},{9,... | collective-permute-start | bytes 3145736 | tf_op jit(solution)/shard_map/ppermute | solution.py:33
  272.5 72.6 %collective-permute-start.23 = (bf16[1,256,1536]{2,1,0:T(8,128)(2,1)S(1)}, bf16[1,256,1536]{2,1,0:T(8,128)(2,1)}, u32[]{:S(2)}, u32[]{:S(2)}) collective-permute-start(bf16[1,256,1536]{2,1,0:T(8,128)(2,1)S(1)} %copy-done.3), channel_id=1, source_target_pairs={{0,16},{1,17},{2,18},{3,19},{4,20},{5,21},{6,22},{7,23},{8,24},{9,... | collective-permute-start | bytes 2359304 | tf_op jit(solution)/shard_map/ppermute | solution.py:33
  275.9 3.5 copy-start.8
  275.9 86.1 %collective-permute-start.24 = (bf16[1,256,1536]{2,1,0:T(8,128)(2,1)S(1)}, bf16[1,256,1536]{2,1,0:T(8,128)(2,1)}, u32[]{:S(2)}, u32[]{:S(2)}) collective-permute-start(bf16[1,256,1536]{2,1,0:T(8,128)(2,1)S(1)} %copy-done.2), channel_id=1, source_target_pairs={{0,16},{1,17},{2,18},{3,19},{4,20},{5,21},{6,22},{7,23},{8,24},{9,... | collective-permute-start | bytes 2359304 | tf_op jit(solution)/shard_map/ppermute | solution.py:33
  279.5 65.7 %copy-start.5 = (bf16[1,2,256,256]{3,2,1,0:T(8,128)(2,1)S(1)}, bf16[1,2,256,256]{3,2,1,0:T(8,128)(2,1)}, u32[]{:S(2)}) copy-start(bf16[1,2,256,256]{3,2,1,0:T(8,128)(2,1)} %shard_map.143.refs_0_.mine) | copy-start | bytes 786436
  279.5 82.6 %copy-start.18 = (s32[32]{0:T(128)S(1)}, s32[32]{0:T(128)}, u32[]{:S(2)}) copy-start(s32[32]{0:T(128)} %param.17) | copy-start | bytes 388
  345.2 40.4 %collective-permute-start.19 = (bf16[1,2,256,256]{3,2,1,0:T(8,128)(2,1)S(1)}, bf16[1,2,256,256]{3,2,1,0:T(8,128)(2,1)S(1)}, u32[]{:S(2)}, u32[]{:S(2)}) collective-permute-start(bf16[1,2,256,256]{3,2,1,0:T(8,128)(2,1)S(1)} %copy-done.5), channel_id=1, source_target_pairs={{0,16},{1,17},{2,18},{3,19},{4,20},{5,21},{6,22},{7,23},{8,24},{9,... | collective-permute-start | bytes 786440 | tf_op jit(solution)/shard_map/ppermute | solution.py:33
  362.0 26.6 %collective-permute-start.18 = (bf16[1,2,256,256]{3,2,1,0:T(8,128)(2,1)}, bf16[1,2,256,256]{3,2,1,0:T(8,128)(2,1)S(1)}, u32[]{:S(2)}, u32[]{:S(2)}) collective-permute-start(bf16[1,2,256,256]{3,2,1,0:T(8,128)(2,1)} %shard_map.144.mine), channel_id=1, source_target_pairs={{0,16},{1,17},{2,18},{3,19},{4,20},{5,21},{6,22},{7,23},{8,24},{9,... | collective-permute-start | bytes 786440 | tf_op jit(solution)/shard_map/ppermute | solution.py:33
  380.5 1.0 copy-start.6
  385.6 0.7 copy-start.9
  388.6 0.7 copy-start.10

commit v4 on v3

--- a/solution.py
+++ b/solution.py
@@ -11,7 +11,7 @@
 YZ = 16
 CAP = 12
 PAIR = 2 * CAP
-GATHER_STEPS = 4
+GATHER_STEPS = 2
 FORWARD_STEPS = 4
 F32 = jnp.float32
 BF16 = jnp.bfloat16
@@ -237,59 +237,7 @@
     )(near, rows)
 
 
-def hidden_grad_kernel(near, own, near_in, far_in, down_a, down_b, rows, out):
-    @pl.when(pl.program_id(0) == 0)
-    def _():
-        out[...] = jnp.zeros_like(out)
-
-    @pl.when(near[0] == 1)
-    def _():
-        rows[:, :PAIR] = own[...]
-        rows[:, PAIR:] = near_in[...]
-
-    @pl.when(near[0] != 1)
-    def _():
-        rows[:, :PAIR] = near_in[...]
-        rows[:, PAIR:] = far_in[...]
-
-    grads = rows[...].reshape(-1, rows.shape[2])
-    for k, down in enumerate((down_a, down_b)):
-        out[k] += lax.dot_general(
-            grads, down[0], (((1,), (1,)), ((), ())), preferred_element_type=F32
-        )
-
-
-def hidden_grad_call(near, pieces, down_a, down_b):
-    width = pieces[0].shape[2]
-    units = down_a.shape[1]
-    count = 2 * YZ * PAIR
-    step = width // FORWARD_STEPS
-    weight = pl.BlockSpec((1, units, step), lambda k: (0, 0, k))
-    return pl.pallas_call(
-        hidden_grad_kernel,
-        grid=(width // step,),
-        in_specs=[pl.BlockSpec(memory_space=pltpu.SMEM)]
-        + [pl.BlockSpec((YZ, PAIR, step), lambda k: (0, 0, k)) for _ in pieces]
-        + [weight, weight],
-        out_specs=[
-            pl.BlockSpec((YZ, 2 * PAIR, step), lambda k: (0, 0, k)),
-            pl.BlockSpec((2, count, units), lambda k: (0, 0, 0)),
-        ],
-        out_shape=[
-            jax.ShapeDtypeStruct((YZ, 2 * PAIR, width), BF16),
-            jax.ShapeDtypeStruct((2, count, units), F32),
-        ],
-        compiler_params=params(),
-        cost_estimate=cost(
-            4 * count * width * units, 5 * width * count + 4 * width * units + 8 * count * units
-        ),
-        interpret=INTERPRET,
-    )(near, *pieces, down_a, down_b)
-
-
-def forward_kernel(
-    rows, gate_up_a, gate_up_b, hidden_grads, hidden_a, hidden_b, back_a, back_b, total
-):
+def forward_kernel(rows, gate_up_a, gate_up_b, hidden_a, hidden_b, total):
     k = pl.program_id(0)
 
     @pl.when(k == 0)
@@ -304,41 +252,79 @@
 
     @pl.when(k == pl.num_programs(0) - 1)
     def _():
-        units = hidden_a.shape[0]
-        for owner, (hidden_t, back) in enumerate(((hidden_a, back_a), (hidden_b, back_b))):
-            gate, up, hidden_grad = total[2 * owner], total[2 * owner + 1], hidden_grads[owner]
-            sigmoid = jax.nn.sigmoid(gate)
-            silu = gate * sigmoid
-            hidden_t[...] = jnp.transpose(silu * up).astype(BF16)
-            back[:, :units] = (
-                hidden_grad * up * sigmoid * (1.0 + gate * (1.0 - sigmoid))
-            ).astype(BF16)
-            back[:, units:] = (hidden_grad * silu).astype(BF16)
-
-
-def forward_call(rows, gate_up_a, gate_up_b, hidden_grads):
+        for owner, hidden_t in enumerate((hidden_a, hidden_b)):
+            gate, up = total[2 * owner], total[2 * owner + 1]
+            hidden_t[...] = jnp.transpose(gate * jax.nn.sigmoid(gate) * up).astype(BF16)
+
+
+def forward_call(rows, gate_up_a, gate_up_b):
     count, width = rows.shape
     units = gate_up_a.shape[3]
     step = width // FORWARD_STEPS
     weight = pl.BlockSpec((1, 2, step, units), lambda k: (0, 0, k, 0))
     whole = lambda shape: pl.BlockSpec(shape, lambda k: (0,) * len(shape))
-    shapes = [(units, count), (units, count), (count, 2 * units), (count, 2 * units)]
+    shapes = [((units, count), BF16), ((units, count), BF16), ((4, count, units), F32)]
     return pl.pallas_call(
         forward_kernel,
         grid=(width // step,),
-        in_specs=[
+        in_specs=[pl.BlockSpec((count, step), lambda k: (0, k)), weight, weight],
+        out_specs=[whole(s) for s, _ in shapes],
+        out_shape=[jax.ShapeDtypeStruct(*s) for s in shapes],
+        compiler_params=params(),
+        cost_estimate=cost(8 * count * width * units, 2 * width * (count + 4 * units)),
+        interpret=INTERPRET,
+    )(rows, gate_up_a, gate_up_b)
+
+
+def backward_kernel(grads, down_a, down_b, gates, back_a, back_b, total):
+    k = pl.program_id(0)
+
+    @pl.when(k == 0)
+    def _():
+        total[...] = jnp.zeros_like(total)
+
+    for owner, down in enumerate((down_a, down_b)):
+        total[owner] += lax.dot_general(
+            grads[...], down[0], (((1,), (1,)), ((), ())), preferred_element_type=F32
+        )
+
+    @pl.when(k == pl.num_programs(0) - 1)
+    def _():
+        units = total.shape[2]
+        for owner, back in enumerate((back_a, back_b)):
+            gate, up, hidden_grad = gates[2 * owner], gates[2 * owner + 1], total[owner]
+            sigmoid = jax.nn.sigmoid(gate)
+            back[:, :units] = (
+                hidden_grad * up * sigmoid * (1.0 + gate * (1.0 - sigmoid))
+            ).astype(BF16)
+            back[:, units:] = (hidden_grad * (gate * sigmoid)).astype(BF16)
+
+
+def backward_call(behind, grads, down_a, down_b, gates):
+    count, width = grads.shape
+    units = down_a.shape[1]
+    step = width // FORWARD_STEPS
+    weight = pl.BlockSpec((1, units, step), lambda k: (0, 0, k))
+    whole = lambda shape: pl.BlockSpec(shape, lambda k: (0,) * len(shape))
+    return pl.pallas_call(
+        after(backward_kernel, len(behind)),
+        grid=(width // step,),
+        in_specs=[pl.BlockSpec(memory_space=pl.ANY) for _ in behind]
+        + [
             pl.BlockSpec((count, step), lambda k: (0, k)),
             weight,
             weight,
-            whole(hidden_grads.shape),
+            whole(gates.shape),
         ],
-        out_specs=[whole(s) for s in shapes],
-        out_shape=[jax.ShapeDtypeStruct(s, BF16) for s in shapes],
-        scratch_shapes=[pltpu.VMEM((4, count, units), F32)],
-        compiler_params=params(),
-        cost_estimate=cost(8 * count * width * units, 2 * width * (count + 4 * units)),
-        interpret=INTERPRET,
-    )(rows, gate_up_a, gate_up_b, hidden_grads)
+        out_specs=[whole((count, 2 * units))] * 2,
+        out_shape=[jax.ShapeDtypeStruct((count, 2 * units), BF16)] * 2,
+        scratch_shapes=[pltpu.VMEM((2, count, units), F32)],
+        compiler_params=params(),
+        cost_estimate=cost(
+            4 * count * width * units, 2 * width * (count + 2 * units) + 16 * count * units
+        ),
+        interpret=INTERPRET,
+    )(*behind, grads, down_a, down_b, gates)
 
 
 def adam(gradient, first, second):
@@ -445,6 +431,12 @@
         cost_estimate=cost(0, 6 * mine.size),
         interpret=INTERPRET,
     )(swapping, mine, theirs, *old)
+
+
+def join_grads(near, own, near_in, far_in):
+    first = jnp.where(near == 1, own, near_in)
+    second = jnp.where(near == 1, near_in, far_in)
+    return jnp.concatenate([first, second], axis=1).reshape(-1, own.shape[2])
 
 
 def local(
@@ -489,15 +481,11 @@
     grads_3 = send(grads_0, grad_3)
     rows_a = over_yz(sent_rows).reshape(-1, width)
     near = marker_call(near, rows_a)
-    grads_a, hidden_grads = hidden_grad_call(near, [grads_0, grads_12, grads_3], w_down, down_core)
-    grads_a = grads_a.reshape(-1, width)
+    grads_a = join_grads(near, grads_0, grads_12, grads_3)
     grads_b = send(grads_a, to_core)
 
-    hidden_a, hidden_other, back_a, back_other = forward_call(
-        rows_a, w_gate_up, gate_up_core, hidden_grads
-    )
+    hidden_a, hidden_other, gates = forward_call(rows_a, w_gate_up, gate_up_core)
     hidden_b = send(hidden_other, to_core)
-    back_b = send(back_other, to_core)
     rows_b = send(rows_a, to_core)
 
     swapping = swap_flag[my_slot].reshape(1)
@@ -517,6 +505,8 @@
         pending.append((mine, theirs, start, units))
         behind, start = [mine], start + units
     downs = len(pending)
+    back_a, back_other = backward_call(behind, grads_a, w_down, down_core, gates)
+    back_b = send(back_other, to_core)
     start, step = 0, width // 14
     for units in (4, 4, 4, 1, 1):
         mine = gate_up_call(

time: 393 us -> 391 us (level)
  waiting for transfers between devices: 217 us -> 207 us
  other arithmetic: 1.95 us -> 7.53 us
  starting transfers between devices: 61.3 us -> 65.8 us
    ppermute x26, waiting for transfers between devices: 142 us -> 128 us  [send(): return lax.ppermute(value, AXES, pairs)]
    ppermute x26, starting transfers between devices: 46.3 us -> 50.8 us  [send(): return lax.ppermute(value, AXES, pairs)]
  transfers between devices with their start and end apart: 28 -> 28, of which waited for: 9 -> 9; matrix products, arithmetic and copies ran while one was open for 1% -> 1% of each run, Pallas kernels for 22% -> 25%
where the time goes in v4:
time: 391 us; the launch traced here: 389 us
  waiting for transfers between devices  207 us (53%)
  Pallas kernels  102 us (26%)
  starting transfers between devices  65.8 us (17%)
  other arithmetic  7.53 us (2%)
  local copies, waits for them, and re-layouts  6.22 us (2%)
    ppermute x26, waiting for transfers between devices, send(): return lax.ppermute(value, AXES, pairs)  128 us
    all_to_all x2, waiting for transfers between devices, over_yz(): lax.all_to_all(value, 'expert', 0, 0, axis_index_groups=groups, tiled=True)  78.8 us
    ppermute x26, starting transfers between devices, send(): return lax.ppermute(value, AXES, pairs)  50.8 us
    pallas_call x8, Pallas kernels, place(): pl.pallas_call(place_kernel, grid=(units,), in_specs=[pl.BlockSpec(memory...  27.2 us
    pallas_call x5, Pallas kernels, gate_up_call(): pl.pallas_call(after(gate_up_kernel, len(behind)), grid=(units,), in_spec...  26.5 us
    pallas_call x3, Pallas kernels, down_call(): pl.pallas_call(after(down_kernel, len(behind)), grid=(units,), in_specs=[...  15.4 us
    all_to_all x2, starting transfers between devices, over_yz(): lax.all_to_all(value, 'expert', 0, 0, axis_index_groups=groups, tiled=True)  15 us
    pallas_call x1, Pallas kernels, forward_call(): pl.pallas_call(forward_kernel, grid=(width // step,), in_specs=[pl.BlockS...  11.7 us
  transfers between devices with their start and end apart: 28, of which 9 were waited for; matrix products, arithmetic and copies ran while one was open for 1% of the time, Pallas kernels for 25%

profile of v4, /device:TPU:64, one launch (start us, length us, event | category | flops | bytes accessed | tf_op | source)
XLA Modules:
  0.0 389.4 jit_solution(5624798498153788275)
XLA Ops:
  0.7 0.7 convert_bitcast_fusion
  1.4 0.7 pad_maximum_fusion.1.small_a
  2.6 0.8 collective-permute-done.10.small_b
  3.4 0.6 copy-done.17
  4.3 3.8 shard_map.135
  8.1 7.7 %all-to-all-start.1 = ((bf16[16,24,3584]{2,1,0:T(8,128)(2,1)}), bf16[16,24,3584]{2,1,0:T(8,128)(2,1)S(1)}, u32[]{:S(2)}, u32[]{:S(2)}) async-start(bf16[16,24,3584]{2,1,0:T(8,128)(2,1)} %shard_map.135), calls=%async_computation.1 | async-start | bytes 5505024 | tf_op jit(solution)/shard_map/all_to_all | solution.py:70
  15.8 1.5 collective-permute-start.6
  17.3 2.1 collective-permute-start.5
  19.4 1.6 collective-permute-start.4
  21.0 2.2 collective-permute-start.7
  23.2 1.4 collective-permute-start.3
  24.6 34.5 %collective-permute-done.3.refs_3_ = f32[4,128]{1,0:T(4,128)S(1)} collective-permute-done((f32[4,128]{1,0:T(4,128)S(1)}, f32[4,128]{1,0:T(4,128)S(1)}, u32[]{:S(2)}, u32[]{:S(2)}) %collective-permute-start.3) | collective-permute-done | bytes 2080 | tf_op jit(solution)/shard_map/ppermute | solution.py:33
  59.1 1.5 collective-permute-start.2
  60.6 2.1 collective-permute-done.2.refs_2_
  62.7 0.7 collective-permute-start
  63.4 8.0 %collective-permute-start.1 = (f32[4,128]{1,0:T(4,128)S(1)}, f32[4,128]{1,0:T(4,128)S(1)}, u32[]{:S(2)}, u32[]{:S(2)}) collective-permute-start(f32[4,128]{1,0:T(4,128)S(1)} %copy-done.13), channel_id=1, source_target_pairs={{0,65},{1,33},{2,67},{3,35},{4,69},{5,37},{6,71},{7,39},{8,73},{9,... | collective-permute-start | bytes 6152 | tf_op jit(solution)/shard_map/ppermute | solution.py:33
  71.4 0.6 broadcast_select_fusion.2.refs_0_
  72.0 0.7 collective-permute-done.1.refs_1_
  72.7 0.6 copy-done.18
  73.3 1.8 shard_map.131.picks
  75.1 5.5 %shard_map.132 = bf16[16,48,3584]{2,1,0:T(8,128)(2,1)} custom-call(s32[1]{0:T(128)} %bitcast.near, bf16[2,384,256]{2,1,0:T(8,128)(2,1)} %shard_map.131.picks, bf16[128,3584]{1,0:T(8,128)(2,1)} %own.1, bf16[128,3584]{1,0:T(8,128)(2,1)} %collective-permute-done.4.data_a, bf16[128,3584]{1,0:T(8,128)(2,1)} %collective-permute-done.5.data_b, ...), custom_call_target="tpu_custom_call" | custom-call | flops 1409286144 | bytes 10092544 | tf_op jit(solution)/shard_map/pallas_call | solution.py:206
  80.6 7.2 %all-to-all-start = ((bf16[16,48,3584]{2,1,0:T(8,128)(2,1)}), bf16[16,48,3584]{2,1,0:T(8,128)(2,1)}, u32[]{:S(2)}, u32[]{:S(2)}) async-start(bf16[16,48,3584]{2,1,0:T(8,128)(2,1)} %shard_map.132), calls=%async_computation | async-start | bytes 11010048 | tf_op jit(solution)/shard_map/all_to_all | solution.py:70
  87.9 2.2 collective-permute-start.13
  90.0 78.8 %all-to-all-done = bf16[16,48,3584]{2,1,0:T(8,128)(2,1)} async-done(((bf16[16,48,3584]{2,1,0:T(8,128)(2,1)}), bf16[16,48,3584]{2,1,0:T(8,128)(2,1)}, u32[]{:S(2)}, u32[]{:S(2)}) %all-to-all-start) | async-done | bytes 5505056 | tf_op jit(solution)/shard_map/all_to_all | solution.py:70
  170.0 2.2 broadcast_select_fusion.1
  172.3 3.3 pad_maximum_fusion
  175.6 0.9 collective-permute-start.14
  177.1 0.7 collective-permute-start.16
  177.8 13.0 %collective-permute-done.8.gate_up_b = bf16[1,2,3584,256]{3,2,1,0:T(8,128)(2,1)} collective-permute-done((bf16[1,2,3584,256]{3,2,1,0:T(8,128)(2,1)S(1)}, bf16[1,2,3584,256]{3,2,1,0:T(8,128)(2,1)}, u32[]{:S(2)}, u32[]{:S(2)}) %collective-permute-start.8) | collective-permute-done | bytes 3670048 | tf_op jit(solution)/shard_map/ppermute | solution.py:33
  190.8 11.7 %shard_map.133 = (bf16[256,768]{1,0:T(8,128)(2,1)}, bf16[256,768]{1,0:T(8,128)(2,1)}, f32[4,768,256]{2,1,0:T(8,128)}) custom-call(bf16[768,3584]{1,0:T(8,128)(2,1)} %bitcast.6.rows.refs_1_, bf16[1,2,3584,256]{3,2,1,0:T(8,128)(2,1)} %gate_up_a.1, bf16[1,2,3584,256]{3,2,1,0:T(8,128)(2,1)} %collective-permute-done.8.gate_up_b), custom_call_target="tpu_custom_call" | custom-call | flops 5637144576 | bytes 12845056 | tf_op jit(solution)/shard_map/pallas_call | solution.py:267
  202.8 1.6 collective-permute-done.9.refs_1_.refs_2_
  204.4 0.7 copy-done.3
  205.1 3.3 shard_map.136.refs_0_.mine
  208.4 6.0 %shard_map.137.refs_0_.mine = bf16[1,256,1536]{2,1,0:T(8,128)(2,1)} custom-call(bf16[1,256,512]{2,1,0:T(8,128)(2,1)} %shard_map.136.refs_0_.mine, bf16[256,768]{1,0:T(8,128)(2,1)} %get-tuple-element.7.refs_0_.refs_1_, bf16[256,768]{1,0:T(8,128)(2,1)} %copy-done.3, bf16[768,3584]{1,0:T(8,128)(2,1)} %bitcast.9.refs_2_.refs_3_.refs_1_, ...), custom_call_target="tpu_custom_call" | custom-call | flops 1207959552 | bytes 7077888 | tf_op jit(solution)/shard_map/pallas_call | solution.py:352
  214.5 6.0 %shard_map.138.refs_0_.mine = bf16[1,256,1536]{2,1,0:T(8,128)(2,1)} custom-call(bf16[1,256,1536]{2,1,0:T(8,128)(2,1)} %shard_map.137.refs_0_.mine, bf16[256,768]{1,0:T(8,128)(2,1)} %get-tuple-element.7.refs_0_.refs_1_, bf16[256,768]{1,0:T(8,128)(2,1)} %copy-done.3, bf16[768,3584]{1,0:T(8,128)(2,1)} %bitcast.9.refs_2_.refs_3_.refs_1_, ...), custom_call_target="tpu_custom_call" | custom-call | flops 1207959552 | bytes 7077888 | tf_op jit(solution)/shard_map/pallas_call | solution.py:352
  220.5 9.5 %shard_map.139 = (bf16[768,512]{1,0:T(8,128)(2,1)}, bf16[768,512]{1,0:T(8,128)(2,1)}) custom-call(bf16[1,256,1536]{2,1,0:T(8,128)(2,1)} %shard_map.138.refs_0_.mine, bf16[768,3584]{1,0:T(8,128)(2,1)} %bitcast.9.refs_2_.refs_3_.refs_1_, bf16[1,256,3584]{2,1,0:T(8,128)(2,1)} %refs_2_.1, bf16[1,256,3584]{2,1,0:T(8,128)(2,1)} %collective-permute-done.16.refs_3_, ...), custom_call_target="tpu_custom_call" | custom-call | flops 2818572288 | bytes 12320768 | tf_op jit(solution)/shard_map/pallas_call | solution.py:309
  230.4 12.6 %collective-permute-start.25 = (bf16[1,256,512]{2,1,0:T(8,128)(2,1)S(1)}, bf16[1,256,512]{2,1,0:T(8,128)(2,1)S(1)}, u32[]{:S(2)}, u32[]{:S(2)}) collective-permute-start(bf16[1,256,512]{2,1,0:T(8,128)(2,1)S(1)} %copy-done.4), channel_id=1, source_target_pairs={{0,16},{1,17},{2,18},{3,19},{4,20},{5,21},{6,22},{7,23},{8,24},{9,... | collective-permute-start | bytes 786440 | tf_op jit(solution)/shard_map/ppermute | solution.py:33
  243.1 0.9 copy-done
  243.9 6.6 %shard_map.140.refs_0_.mine = bf16[1,2,1024,256]{3,2,1,0:T(8,128)(2,1)} custom-call(bf16[1,256,1536]{2,1,0:T(8,128)(2,1)} %shard_map.138.refs_0_.mine, bf16[768,3584]{1,0:T(8,128)(2,1)} %bitcast.6.rows.refs_1_, bf16[768,3584]{1,0:T(8,128)(2,1)} %collective-permute-done.15.refs_2_, bf16[768,512]{1,0:T(8,128)(2,1)} %get-tuple-element.10.refs_3_, ...), custom_call_target="tpu_custom_call" | custom-call | flops 1610612736 | bytes 6291456 | tf_op jit(solution)/shard_map/pallas_call | solution.py:387
  250.5 2.1 collective-permute-start.22
  252.7 6.6 %shard_map.141.refs_0_.mine = bf16[1,2,1024,256]{3,2,1,0:T(8,128)(2,1)} custom-call(bf16[1,2,1024,256]{3,2,1,0:T(8,128)(2,1)} %shard_map.140.refs_0_.mine, bf16[768,3584]{1,0:T(8,128)(2,1)} %bitcast.6.rows.refs_1_, bf16[768,3584]{1,0:T(8,128)(2,1)} %collective-permute-done.15.refs_2_, bf16[768,512]{1,0:T(8,128)(2,1)} %get-tuple-element.10.refs_3_, ...), custom_call_target="tpu_custom_call" | custom-call | flops 1610612736 | bytes 6291456 | tf_op jit(solution)/shard_map/pallas_call | solution.py:387
  259.3 1.5 collective-permute-start.21
  260.8 6.6 %shard_map.142.refs_0_.mine = bf16[1,2,1024,256]{3,2,1,0:T(8,128)(2,1)} custom-call(bf16[1,2,1024,256]{3,2,1,0:T(8,128)(2,1)} %shard_map.141.refs_0_.mine, bf16[768,3584]{1,0:T(8,128)(2,1)} %bitcast.6.rows.refs_1_, bf16[768,3584]{1,0:T(8,128)(2,1)} %collective-permute-done.15.refs_2_, bf16[768,512]{1,0:T(8,128)(2,1)} %get-tuple-element.10.refs_3_, ...), custom_call_target="tpu_custom_call" | custom-call | flops 1610612736 | bytes 6291456 | tf_op jit(solution)/shard_map/pallas_call | solution.py:387
  267.4 2.1 collective-permute-start.20
  269.5 1.4 collective-permute-start.23
  270.9 2.2 collective-permute-start.24
  273.1 3.3 shard_map.143.refs_0_.mine
  276.4 3.3 shard_map.144.mine
  279.8 60.4 %collective-permute-done.23.theirs = bf16[1,256,1536]{2,1,0:T(8,128)(2,1)} collective-permute-done((bf16[1,256,1536]{2,1,0:T(8,128)(2,1)S(1)}, bf16[1,256,1536]{2,1,0:T(8,128)(2,1)}, u32[]{:S(2)}, u32[]{:S(2)}) %collective-permute-start.23) | collective-permute-done | bytes 786464 | tf_op jit(solution)/shard_map/ppermute | solution.py:33
  340.2 2.1 collective-permute-start.19
  342.3 14.7 %collective-permute-done.24.theirs = bf16[1,256,1536]{2,1,0:T(8,128)(2,1)} collective-permute-done((bf16[1,256,1536]{2,1,0:T(8,128)(2,1)S(1)}, bf16[1,256,1536]{2,1,0:T(8,128)(2,1)}, u32[]{:S(2)}, u32[]{:S(2)}) %collective-permute-start.24) | collective-permute-done | bytes 786464 | tf_op jit(solution)/shard_map/ppermute | solution.py:33
  357.0 2.1 collective-permute-start.18
  359.2 0.6 dynamic_slice.3.swapping
  359.8 2.4 shard_map.145.rest_0_
  362.2 3.7 shard_map.146.rest_0_
  365.9 3.7 shard_map.147.rest_0_
  369.6 4.2 %shard_map.148.rest_0_ = bf16[1,2,3584,256]{3,2,1,0:T(8,128)(2,1)} custom-call(s32[1]{0:T(128)} %dynamic_slice.3.swapping, bf16[1,2,1024,256]{3,2,1,0:T(8,128)(2,1)} %shard_map.140.refs_0_.mine, bf16[1,2,1024,256]{3,2,1,0:T(8,128)(2,1)} %collective-permute-done.22.theirs, bf16[1,256,3584]{2,1,0:T(8,128)(2,1)} %shard_map.147.rest_0_), custom_call_target="tpu_custom_call" | custom-call | bytes 3145728 | tf_op jit(solution)/shard_map/pallas_call | solution.py:418
  373.8 4.2 %shard_map.149.rest_0_ = bf16[1,2,3584,256]{3,2,1,0:T(8,128)(2,1)} custom-call(s32[1]{0:T(128)} %dynamic_slice.3.swapping, bf16[1,2,1024,256]{3,2,1,0:T(8,128)(2,1)} %shard_map.141.refs_0_.mine, bf16[1,2,1024,256]{3,2,1,0:T(8,128)(2,1)} %collective-permute-done.21.theirs, bf16[1,2,3584,256]{3,2,1,0:T(8,128)(2,1)} %shard_map.148.rest_0_), custom_call_target="tpu_custom_call", output_to_operand_aliasing={{}: (3, {})} | custom-call | bytes 3145728 | tf_op jit(solution)/shard_map/pallas_call | solution.py:418
  378.0 1.0 copy-done.7
  379.0 4.2 %shard_map.150.rest_0_ = bf16[1,2,3584,256]{3,2,1,0:T(8,128)(2,1)} custom-call(s32[1]{0:T(128)} %dynamic_slice.3.swapping, bf16[1,2,1024,256]{3,2,1,0:T(8,128)(2,1)} %shard_map.142.refs_0_.mine, bf16[1,2,1024,256]{3,2,1,0:T(8,128)(2,1)} %copy-done.7, bf16[1,2,3584,256]{3,2,1,0:T(8,128)(2,1)} %shard_map.149.rest_0_), custom_call_target="tpu_custom_call", output_to_operand_aliasing={{}: (3, {})} | custom-call | bytes 3145728 | tf_op jit(solution)/shard_map/pallas_call | solution.py:418
  383.2 0.7 copy-done.10
  383.9 2.4 shard_map.151.rest_0_
  386.3 0.7 copy-done.11
  387.0 2.4 shard_map.152
  (62 shorter events, 2.8 us)
Async XLA Ops:
  0.6 2.8 collective-permute-start.11
  2.1 1.3 copy-start.12
  2.1 1.3 collective-permute-start.10
  3.4 0.6 copy-start.17
  3.4 0.9 copy-start.8
  8.1 15.1 %copy-start.13 = (f32[4,128]{1,0:T(4,128)S(1)}, f32[4,128]{1,0:T(4,128)}, u32[]{:S(2)}) copy-start(f32[4,128]{1,0:T(4,128)} %copy-done.12) | copy-start | bytes 6148
  8.1 63.3 %copy-start.14 = (f32[128,2]{0,1:T(2,128)S(1)}, f32[128,2]{0,1:T(2,128)}, u32[]{:S(2)}) copy-start(f32[128,2]{0,1:T(2,128)} %param.15) | copy-start | bytes 3076
  8.1 72.5 %all-to-all-start.1 = ((bf16[16,24,3584]{2,1,0:T(8,128)(2,1)}), bf16[16,24,3584]{2,1,0:T(8,128)(2,1)S(1)}, u32[]{:S(2)}, u32[]{:S(2)}) async-start(bf16[16,24,3584]{2,1,0:T(8,128)(2,1)} %shard_map.135), calls=%async_computation.1 | async-start | bytes 5505024 | tf_op jit(solution)/shard_map/all_to_all | solution.py:70
  15.8 59.3 %collective-permute-start.6 = (bf16[128,3584]{1,0:T(8,128)(2,1)}, bf16[128,3584]{1,0:T(8,128)(2,1)}, u32[]{:S(2)}, u32[]{:S(2)}) collective-permute-start(bf16[128,3584]{1,0:T(8,128)(2,1)} %own.1), channel_id=1, source_target_pairs={{0,64},{1,32},{2,66},{3,34},{4,68},{5,36},{6,70},{7,38},{8,72},{9,... | collective-permute-start | bytes 2752520 | tf_op jit(solution)/shard_map/ppermute | solution.py:33
  17.3 57.8 %collective-permute-start.5 = (bf16[128,3584]{1,0:T(8,128)(2,1)}, bf16[128,3584]{1,0:T(8,128)(2,1)}, u32[]{:S(2)}, u32[]{:S(2)}) collective-permute-start(bf16[128,3584]{1,0:T(8,128)(2,1)} %own.1), channel_id=1, source_target_pairs={{0,65},{1,33},{2,67},{3,35},{4,69},{5,37},{6,71},{7,39},{8,73},{9,... | collective-permute-start | bytes 2752520 | tf_op jit(solution)/shard_map/ppermute | solution.py:33
  19.4 55.7 %collective-permute-start.4 = (bf16[128,3584]{1,0:T(8,128)(2,1)}, bf16[128,3584]{1,0:T(8,128)(2,1)}, u32[]{:S(2)}, u32[]{:S(2)}) collective-permute-start(bf16[128,3584]{1,0:T(8,128)(2,1)} %own.1), channel_id=1, source_target_pairs={{1,96},{3,98},{5,100},{7,102},{9,104},{11,106},{13,108},{15,110},{... | collective-permute-start | bytes 2752520 | tf_op jit(solution)/shard_map/ppermute | solution.py:33
  21.0 54.1 %collective-permute-start.7 = (bf16[128,3584]{1,0:T(8,128)(2,1)}, bf16[128,3584]{1,0:T(8,128)(2,1)}, u32[]{:S(2)}, u32[]{:S(2)}) collective-permute-start(bf16[128,3584]{1,0:T(8,128)(2,1)} %own.1), channel_id=1, source_target_pairs={{0,1},{1,97},{2,3},{3,99},{4,5},{5,101},{6,7},{7,103},{8,9},{9,105... | collective-permute-start | bytes 2752520 | tf_op jit(solution)/shard_map/ppermute | solution.py:33
  23.2 35.9 %collective-permute-start.3 = (f32[4,128]{1,0:T(4,128)S(1)}, f32[4,128]{1,0:T(4,128)S(1)}, u32[]{:S(2)}, u32[]{:S(2)}) collective-permute-start(f32[4,128]{1,0:T(4,128)S(1)} %copy-done.13), channel_id=1, source_target_pairs={{0,1},{1,97},{2,3},{3,99},{4,5},{5,101},{6,7},{7,103},{8,9},{9,105... | collective-permute-start | bytes 6152 | tf_op jit(solution)/shard_map/ppermute | solution.py:33
  59.1 13.6 %copy-start.15 = (f32[4,128]{1,0:T(4,128)}, f32[4,128]{1,0:T(4,128)S(1)}, u32[]{:S(2)}) copy-start(f32[4,128]{1,0:T(4,128)S(1)} %collective-permute-done.3.refs_3_) | copy-start | bytes 6148
  59.1 3.6 collective-permute-start.2
  62.7 10.0 %copy-start.16 = (f32[4,128]{1,0:T(4,128)}, f32[4,128]{1,0:T(4,128)S(1)}, u32[]{:S(2)}) copy-start(f32[4,128]{1,0:T(4,128)S(1)} %collective-permute-done.2.refs_2_) | copy-start | bytes 6148
  62.7 0.7 collective-permute-start
  63.4 9.3 %collective-permute-start.1 = (f32[4,128]{1,0:T(4,128)S(1)}, f32[4,128]{1,0:T(4,128)S(1)}, u32[]{:S(2)}, u32[]{:S(2)}) collective-permute-start(f32[4,128]{1,0:T(4,128)S(1)} %copy-done.13), channel_id=1, source_target_pairs={{0,65},{1,33},{2,67},{3,35},{4,69},{5,37},{6,71},{7,39},{8,73},{9,... | collective-permute-start | bytes 6152 | tf_op jit(solution)/shard_map/ppermute | solution.py:33
  72.7 0.6 copy-start.18
  80.6 88.2 %all-to-all-start = ((bf16[16,48,3584]{2,1,0:T(8,128)(2,1)}), bf16[16,48,3584]{2,1,0:T(8,128)(2,1)}, u32[]{:S(2)}, u32[]{:S(2)}) async-start(bf16[16,48,3584]{2,1,0:T(8,128)(2,1)} %shard_map.132), calls=%async_computation | async-start | bytes 11010048 | tf_op jit(solution)/shard_map/all_to_all | solution.py:70
  87.9 82.1 %collective-permute-start.13 = (bf16[16,24,3584]{2,1,0:T(8,128)(2,1)S(1)}, bf16[16,24,3584]{2,1,0:T(8,128)(2,1)}, u32[]{:S(2)}, u32[]{:S(2)}) collective-permute-start(bf16[16,24,3584]{2,1,0:T(8,128)(2,1)S(1)} %all-to-all-done.1), channel_id=1, source_target_pairs={{1,32},{3,34},{5,36},{7,38},{9,40},{11,42},{13,44},{15,46},{17,48}... | collective-permute-start | bytes 8257544 | tf_op jit(solution)/shard_map/ppermute | solution.py:33
  90.0 80.0 %collective-permute-start.12 = (bf16[16,24,3584]{2,1,0:T(8,128)(2,1)S(1)}, bf16[16,24,3584]{2,1,0:T(8,128)(2,1)}, u32[]{:S(2)}, u32[]{:S(2)}) collective-permute-start(bf16[16,24,3584]{2,1,0:T(8,128)(2,1)S(1)} %all-to-all-done.1), channel_id=1, source_target_pairs={{0,64},{1,96},{2,66},{3,98},{4,68},{5,100},{6,70},{7,102},{8,72},{... | collective-permute-start | bytes 8257544 | tf_op jit(solution)/shard_map/ppermute | solution.py:33
  172.2 4.3 %copy-start.19 = (bf16[1,2,3584,256]{3,2,1,0:T(8,128)(2,1)S(1)}, bf16[1,2,3584,256]{3,2,1,0:T(8,128)(2,1)}, u32[]{:S(2)}) copy-start(bf16[1,2,3584,256]{3,2,1,0:T(8,128)(2,1)} %gate_up_a.1) | copy-start | bytes 11010052
  172.2 4.8 %copy-start.6 = (bf16[1,256,3584]{2,1,0:T(8,128)(2,1)S(1)}, bf16[1,256,3584]{2,1,0:T(8,128)(2,1)}, u32[]{:S(2)}) copy-start(bf16[1,256,3584]{2,1,0:T(8,128)(2,1)} %refs_2_.1) | copy-start | bytes 5505028
  175.6 28.8 %collective-permute-start.14 = (bf16[768,3584]{1,0:T(8,128)(2,1)}, bf16[768,3584]{1,0:T(8,128)(2,1)}, u32[]{:S(2)}, u32[]{:S(2)}) collective-permute-start(bf16[768,3584]{1,0:T(8,128)(2,1)} %bitcast.9.refs_2_.refs_3_.refs_1_), channel_id=1, source_target_pairs={{0,32},{1,33},{2,34},{3,35},{4,36},{5,37},{6,38},{7,39},{8,40},{9,... | collective-permute-start | bytes 16515080 | tf_op jit(solution)/shard_map/ppermute | solution.py:33
  176.5 14.2 %collective-permute-start.8 = (bf16[1,2,3584,256]{3,2,1,0:T(8,128)(2,1)S(1)}, bf16[1,2,3584,256]{3,2,1,0:T(8,128)(2,1)}, u32[]{:S(2)}, u32[]{:S(2)}) collective-permute-start(bf16[1,2,3584,256]{3,2,1,0:T(8,128)(2,1)S(1)} %copy-done.19), channel_id=1, source_target_pairs={{0,32},{1,33},{2,34},{3,35},{4,36},{5,37},{6,38},{7,39},{8,40},{9,... | collective-permute-start | bytes 11010056 | tf_op jit(solution)/shard_map/ppermute | solution.py:33
  176.6 66.5 %collective-permute-start.15 = (bf16[768,3584]{1,0:T(8,128)(2,1)}, bf16[768,3584]{1,0:T(8,128)(2,1)}, u32[]{:S(2)}, u32[]{:S(2)}) collective-permute-start(bf16[768,3584]{1,0:T(8,128)(2,1)} %bitcast.6.rows.refs_1_), channel_id=1, source_target_pairs={{0,32},{1,33},{2,34},{3,35},{4,36},{5,37},{6,38},{7,39},{8,40},{9,... | collective-permute-start | bytes 16515080 | tf_op jit(solution)/shard_map/ppermute | solution.py:33
  177.1 43.4 %collective-permute-start.16 = (bf16[1,256,3584]{2,1,0:T(8,128)(2,1)S(1)}, bf16[1,256,3584]{2,1,0:T(8,128)(2,1)}, u32[]{:S(2)}, u32[]{:S(2)}) collective-permute-start(bf16[1,256,3584]{2,1,0:T(8,128)(2,1)S(1)} %copy-done.6), channel_id=1, source_target_pairs={{0,32},{1,33},{2,34},{3,35},{4,36},{5,37},{6,38},{7,39},{8,40},{9,... | collective-permute-start | bytes 5505032 | tf_op jit(solution)/shard_map/ppermute | solution.py:33
  202.5 1.9 collective-permute-start.9
  204.4 0.7 copy-start.3
  220.5 9.9 %copy-start.4 = (bf16[1,256,512]{2,1,0:T(8,128)(2,1)S(1)}, bf16[1,256,512]{2,1,0:T(8,128)(2,1)}, u32[]{:S(2)}) copy-start(bf16[1,256,512]{2,1,0:T(8,128)(2,1)} %shard_map.136.refs_0_.mine) | copy-start | bytes 786436
  230.0 13.0 %collective-permute-start.17 = (bf16[768,512]{1,0:T(8,128)(2,1)}, bf16[768,512]{1,0:T(8,128)(2,1)S(1)}, u32[]{:S(2)}, u32[]{:S(2)}) collective-permute-start(bf16[768,512]{1,0:T(8,128)(2,1)} %get-tuple-element.11), channel_id=1, source_target_pairs={{0,32},{1,33},{2,34},{3,35},{4,36},{5,37},{6,38},{7,39},{8,40},{9,... | collective-permute-start | bytes 2359304 | tf_op jit(solution)/shard_map/ppermute | solution.py:33
  230.4 40.5 %collective-permute-start.25 = (bf16[1,256,512]{2,1,0:T(8,128)(2,1)S(1)}, bf16[1,256,512]{2,1,0:T(8,128)(2,1)S(1)}, u32[]{:S(2)}, u32[]{:S(2)}) collective-permute-start(bf16[1,256,512]{2,1,0:T(8,128)(2,1)S(1)} %copy-done.4), channel_id=1, source_target_pairs={{0,16},{1,17},{2,18},{3,19},{4,20},{5,21},{6,22},{7,23},{8,24},{9,... | collective-permute-start | bytes 786440 | tf_op jit(solution)/shard_map/ppermute | solution.py:33
  243.1 0.9 copy-start
  250.5 119.1 %collective-permute-start.22 = (bf16[1,2,1024,256]{3,2,1,0:T(8,128)(2,1)}, bf16[1,2,1024,256]{3,2,1,0:T(8,128)(2,1)}, u32[]{:S(2)}, u32[]{:S(2)}) collective-permute-start(bf16[1,2,1024,256]{3,2,1,0:T(8,128)(2,1)} %shard_map.140.refs_0_.mine), channel_id=1, source_target_pairs={{0,16},{1,17},{2,18},{3,19},{4,20},{5,21},{6,22},{7,23},{8,24},{9,... | collective-permute-start | bytes 3145736 | tf_op jit(solution)/shard_map/ppermute | solution.py:33
  259.3 10.2 %copy-start.1 = (bf16[1,256,1536]{2,1,0:T(8,128)(2,1)S(1)}, bf16[1,256,1536]{2,1,0:T(8,128)(2,1)}, u32[]{:S(2)}) copy-start(bf16[1,256,1536]{2,1,0:T(8,128)(2,1)} %shard_map.138.refs_0_.mine) | copy-start | bytes 2359300
  259.3 11.6 %copy-start.2 = (bf16[1,256,1536]{2,1,0:T(8,128)(2,1)S(1)}, bf16[1,256,1536]{2,1,0:T(8,128)(2,1)}, u32[]{:S(2)}) copy-start(bf16[1,256,1536]{2,1,0:T(8,128)(2,1)} %shard_map.137.refs_0_.mine) | copy-start | bytes 2359300
  259.3 114.5 %collective-permute-start.21 = (bf16[1,2,1024,256]{3,2,1,0:T(8,128)(2,1)}, bf16[1,2,1024,256]{3,2,1,0:T(8,128)(2,1)}, u32[]{:S(2)}, u32[]{:S(2)}) collective-permute-start(bf16[1,2,1024,256]{3,2,1,0:T(8,128)(2,1)} %shard_map.141.refs_0_.mine), channel_id=1, source_target_pairs={{0,16},{1,17},{2,18},{3,19},{4,20},{5,21},{6,22},{7,23},{8,24},{9,... | collective-permute-start | bytes 3145736 | tf_op jit(solution)/shard_map/ppermute | solution.py:33
  267.4 110.6 %collective-permute-start.20 = (bf16[1,2,1024,256]{3,2,1,0:T(8,128)(2,1)}, bf16[1,2,1024,256]{3,2,1,0:T(8,128)(2,1)S(1)}, u32[]{:S(2)}, u32[]{:S(2)}) collective-permute-start(bf16[1,2,1024,256]{3,2,1,0:T(8,128)(2,1)} %shard_map.142.refs_0_.mine), channel_id=1, source_target_pairs={{0,16},{1,17},{2,18},{3,19},{4,20},{5,21},{6,22},{7,23},{8,24},{9,... | collective-permute-start | bytes 3145736 | tf_op jit(solution)/shard_map/ppermute | solution.py:33
  269.5 70.7 %collective-permute-start.23 = (bf16[1,256,1536]{2,1,0:T(8,128)(2,1)S(1)}, bf16[1,256,1536]{2,1,0:T(8,128)(2,1)}, u32[]{:S(2)}, u32[]{:S(2)}) collective-permute-start(bf16[1,256,1536]{2,1,0:T(8,128)(2,1)S(1)} %copy-done.1), channel_id=1, source_target_pairs={{0,16},{1,17},{2,18},{3,19},{4,20},{5,21},{6,22},{7,23},{8,24},{9,... | collective-permute-start | bytes 2359304 | tf_op jit(solution)/shard_map/ppermute | solution.py:33
  270.9 5.5 %copy-start.9 = (bf16[1,256,512]{2,1,0:T(8,128)(2,1)}, bf16[1,256,512]{2,1,0:T(8,128)(2,1)S(1)}, u32[]{:S(2)}) copy-start(bf16[1,256,512]{2,1,0:T(8,128)(2,1)S(1)} %collective-permute-done.25.theirs) | copy-start | bytes 786436
  270.9 86.1 %collective-permute-start.24 = (bf16[1,256,1536]{2,1,0:T(8,128)(2,1)S(1)}, bf16[1,256,1536]{2,1,0:T(8,128)(2,1)}, u32[]{:S(2)}, u32[]{:S(2)}) collective-permute-start(bf16[1,256,1536]{2,1,0:T(8,128)(2,1)S(1)} %copy-done.2), channel_id=1, source_target_pairs={{0,16},{1,17},{2,18},{3,19},{4,20},{5,21},{6,22},{7,23},{8,24},{9,... | collective-permute-start | bytes 2359304 | tf_op jit(solution)/shard_map/ppermute | solution.py:33
  276.4 63.8 %copy-start.5 = (bf16[1,2,256,256]{3,2,1,0:T(8,128)(2,1)S(1)}, bf16[1,2,256,256]{3,2,1,0:T(8,128)(2,1)}, u32[]{:S(2)}) copy-start(bf16[1,2,256,256]{3,2,1,0:T(8,128)(2,1)} %shard_map.143.refs_0_.mine) | copy-start | bytes 786436
  276.4 82.7 %copy-start.20 = (s32[32]{0:T(128)S(1)}, s32[32]{0:T(128)}, u32[]{:S(2)}) copy-start(s32[32]{0:T(128)} %param.17) | copy-start | bytes 388
  340.2 43.0 %collective-permute-start.19 = (bf16[1,2,256,256]{3,2,1,0:T(8,128)(2,1)S(1)}, bf16[1,2,256,256]{3,2,1,0:T(8,128)(2,1)S(1)}, u32[]{:S(2)}, u32[]{:S(2)}) collective-permute-start(bf16[1,2,256,256]{3,2,1,0:T(8,128)(2,1)S(1)} %copy-done.5), channel_id=1, source_target_pairs={{0,16},{1,17},{2,18},{3,19},{4,20},{5,21},{6,22},{7,23},{8,24},{9,... | collective-permute-start | bytes 786440 | tf_op jit(solution)/shard_map/ppermute | solution.py:33
  357.0 29.3 %collective-permute-start.18 = (bf16[1,2,256,256]{3,2,1,0:T(8,128)(2,1)}, bf16[1,2,256,256]{3,2,1,0:T(8,128)(2,1)S(1)}, u32[]{:S(2)}, u32[]{:S(2)}) collective-permute-start(bf16[1,2,256,256]{3,2,1,0:T(8,128)(2,1)} %shard_map.144.mine), channel_id=1, source_target_pairs={{0,16},{1,17},{2,18},{3,19},{4,20},{5,21},{6,22},{7,23},{8,24},{9,... | collective-permute-start | bytes 786440 | tf_op jit(solution)/shard_map/ppermute | solution.py:33
  378.0 1.0 copy-start.7
  383.2 0.7 copy-start.10
  386.3 0.7 copy-start.11

commit v5 on v4

--- a/solution.py
+++ b/solution.py
@@ -55,6 +55,18 @@
 
 def token_4(xl, c, yz, xh):
     return (xl, c, yz, 1 - xh) if c == xh else (1 - xl, 1 - c, yz, xh)
+
+
+def grad_near(xl, c, yz, xh):
+    return (xl, 1 - c, yz, xh) if c == xh else None
+
+
+def grad_far(xl, c, yz, xh):
+    return None if c == xh else (xl, 1 - c, yz, xh)
+
+
+def small_near(xl, c, yz, xh):
+    return None if c == xh else (1 - xl, 1 - c, yz, 1 - xh)
 
 
 def grad_12(xl, c, yz, xh):
@@ -110,27 +122,25 @@
     return picks, weight
 
 
-def picks_kernel(side, slots, *refs):
-    out = refs[-1]
-    tokens = refs[0].shape[1]
-    for group in range(out.shape[0]):
-        found, _ = row_select(side[0], slots, refs[2 * group : 2 * group + 2])
+def picks_kernel(side, slots, near_small, far_small, out):
+    tokens = near_small.shape[1]
+    for group, small in enumerate((near_small[...], far_small[...])):
+        half = small.shape[0] // 2
+        found, _ = row_select(side[0], slots, (small[:half], small[half:]))
         out[group, :, :tokens] = found[0]
         out[group, :, tokens:] = found[1]
 
 
-def picks_call(side, slots, smalls):
+def picks_call(side, slots, near_small, far_small):
     return pl.pallas_call(
         picks_kernel,
         in_specs=[pl.BlockSpec(memory_space=pltpu.SMEM)]
-        + [pl.BlockSpec(memory_space=pltpu.VMEM)] * (1 + len(smalls)),
+        + [pl.BlockSpec(memory_space=pltpu.VMEM)] * 3,
         out_specs=pl.BlockSpec(memory_space=pltpu.VMEM),
-        out_shape=jax.ShapeDtypeStruct(
-            (len(smalls) // 2, YZ * PAIR, 2 * smalls[0].shape[1]), BF16
-        ),
+        out_shape=jax.ShapeDtypeStruct((2, YZ * PAIR, 2 * near_small.shape[1]), BF16),
         cost_estimate=cost(10**8, 10**6),
         interpret=INTERPRET,
-    )(side, slots, *smalls)
+    )(side, slots, near_small, far_small)
 
 
 def grads_kernel(side, slots, small_a, small_b, data_a, data_b, out, picks, weights, both):
@@ -245,63 +255,83 @@
         total[...] = jnp.zeros_like(total)
 
     for owner, gate_up in enumerate((gate_up_a, gate_up_b)):
-        for half in range(2):
-            total[2 * owner + half] += jnp.dot(
-                rows[...], gate_up[0, half], preferred_element_type=F32
-            )
+        weight = jnp.concatenate([gate_up[0, 0], gate_up[0, 1]], axis=1)
+        total[owner] += jnp.dot(rows[...], weight, preferred_element_type=F32)
 
     @pl.when(k == pl.num_programs(0) - 1)
     def _():
+        part = hidden_a.shape[0]
         for owner, hidden_t in enumerate((hidden_a, hidden_b)):
-            gate, up = total[2 * owner], total[2 * owner + 1]
+            gate, up = total[owner, :, :part], total[owner, :, part:]
             hidden_t[...] = jnp.transpose(gate * jax.nn.sigmoid(gate) * up).astype(BF16)
 
 
-def forward_call(rows, gate_up_a, gate_up_b):
+def forward_call(behind, half, rows, gate_up_a, gate_up_b):
     count, width = rows.shape
-    units = gate_up_a.shape[3]
+    part = gate_up_a.shape[3] // 2
     step = width // FORWARD_STEPS
-    weight = pl.BlockSpec((1, 2, step, units), lambda k: (0, 0, k, 0))
+    weight = pl.BlockSpec((1, 2, step, part), lambda k: (0, 0, k, half))
     whole = lambda shape: pl.BlockSpec(shape, lambda k: (0,) * len(shape))
-    shapes = [((units, count), BF16), ((units, count), BF16), ((4, count, units), F32)]
-    return pl.pallas_call(
-        forward_kernel,
+    shapes = [((part, count), BF16), ((part, count), BF16), ((2, count, 2 * part), F32)]
+    return pl.pallas_call(
+        after(forward_kernel, len(behind)),
         grid=(width // step,),
-        in_specs=[pl.BlockSpec((count, step), lambda k: (0, k)), weight, weight],
+        in_specs=[pl.BlockSpec(memory_space=pl.ANY) for _ in behind]
+        + [pl.BlockSpec((count, step), lambda k: (0, k)), weight, weight],
         out_specs=[whole(s) for s, _ in shapes],
         out_shape=[jax.ShapeDtypeStruct(*s) for s in shapes],
         compiler_params=params(),
-        cost_estimate=cost(8 * count * width * units, 2 * width * (count + 4 * units)),
-        interpret=INTERPRET,
-    )(rows, gate_up_a, gate_up_b)
-
-
-def backward_kernel(grads, down_a, down_b, gates, back_a, back_b, total):
+        cost_estimate=cost(8 * count * width * part, 2 * width * (count + 4 * part)),
+        interpret=INTERPRET,
+    )(*behind, rows, gate_up_a, gate_up_b)
+
+
+def join(near, rows, if_near, if_not):
+    for value, pieces in ((1, if_near), (0, if_not)):
+
+        @pl.when(near[0] == value)
+        def _(pieces=pieces):
+            rows[:, :PAIR] = pieces[0][...]
+            rows[:, PAIR:] = pieces[1][...]
+
+
+def backward_kernel(
+    near, own, in_12, in_3, down_a, down_b, gates_a, gates_b, back_a, back_b, rows, total
+):
     k = pl.program_id(0)
 
     @pl.when(k == 0)
     def _():
         total[...] = jnp.zeros_like(total)
 
+    join(near, rows, (own, in_12), (in_12, in_3))
+    grads = rows[...].reshape(-1, rows.shape[2])
     for owner, down in enumerate((down_a, down_b)):
         total[owner] += lax.dot_general(
-            grads[...], down[0], (((1,), (1,)), ((), ())), preferred_element_type=F32
+            grads, down[0], (((1,), (1,)), ((), ())), preferred_element_type=F32
         )
 
     @pl.when(k == pl.num_programs(0) - 1)
     def _():
         units = total.shape[2]
+        part = units // 2
         for owner, back in enumerate((back_a, back_b)):
-            gate, up, hidden_grad = gates[2 * owner], gates[2 * owner + 1], total[owner]
-            sigmoid = jax.nn.sigmoid(gate)
-            back[:, :units] = (
-                hidden_grad * up * sigmoid * (1.0 + gate * (1.0 - sigmoid))
-            ).astype(BF16)
-            back[:, units:] = (hidden_grad * (gate * sigmoid)).astype(BF16)
-
-
-def backward_call(behind, grads, down_a, down_b, gates):
-    count, width = grads.shape
+            for half, gates in enumerate((gates_a, gates_b)):
+                at = half * part
+                gate, up = gates[owner, :, :part], gates[owner, :, part:]
+                hidden_grad = total[owner, :, at : at + part]
+                sigmoid = jax.nn.sigmoid(gate)
+                back[:, at : at + part] = (
+                    hidden_grad * up * sigmoid * (1.0 + gate * (1.0 - sigmoid))
+                ).astype(BF16)
+                back[:, units + at : units + at + part] = (
+                    hidden_grad * (gate * sigmoid)
+                ).astype(BF16)
+
+
+def backward_call(behind, near, pieces, down_a, down_b, gates):
+    width = pieces[0].shape[2]
+    count = 2 * YZ * PAIR
     units = down_a.shape[1]
     step = width // FORWARD_STEPS
     weight = pl.BlockSpec((1, units, step), lambda k: (0, 0, k))
@@ -310,21 +340,21 @@
         after(backward_kernel, len(behind)),
         grid=(width // step,),
         in_specs=[pl.BlockSpec(memory_space=pl.ANY) for _ in behind]
-        + [
-            pl.BlockSpec((count, step), lambda k: (0, k)),
-            weight,
-            weight,
-            whole(gates.shape),
-        ],
+        + [pl.BlockSpec(memory_space=pltpu.SMEM)]
+        + [pl.BlockSpec((YZ, PAIR, step), lambda k: (0, 0, k)) for _ in pieces]
+        + [weight, weight, whole(gates[0].shape), whole(gates[1].shape)],
         out_specs=[whole((count, 2 * units))] * 2,
         out_shape=[jax.ShapeDtypeStruct((count, 2 * units), BF16)] * 2,
-        scratch_shapes=[pltpu.VMEM((2, count, units), F32)],
+        scratch_shapes=[
+            pltpu.VMEM((YZ, 2 * PAIR, step), BF16),
+            pltpu.VMEM((2, count, units), F32),
+        ],
         compiler_params=params(),
         cost_estimate=cost(
-            4 * count * width * units, 2 * width * (count + 2 * units) + 16 * count * units
+            4 * count * width * units, 3 * width * count + 4 * width * units + 16 * count * units
         ),
         interpret=INTERPRET,
-    )(*behind, grads, down_a, down_b, gates)
+    )(*behind, near, *pieces, down_a, down_b, *gates)
 
 
 def adam(gradient, first, second):
@@ -337,31 +367,38 @@
     return lambda *refs: kernel(*refs[count:])
 
 
-def down_kernel(hidden_a, hidden_b, grads_a, grads_b, first, second, out):
-    gradient = jnp.dot(hidden_a[...], grads_a[...], preferred_element_type=F32)
-    gradient = gradient + jnp.dot(hidden_b[...], grads_b[...], preferred_element_type=F32)
+def down_kernel(
+    near, hidden_a, hidden_b, own, in_12, in_3, core_0, core_12, core_3, first, second, out, rows
+):
+    width = rows.shape[3]
+    join(near, rows.at[0], (own, in_12), (in_12, in_3))
+    join(near, rows.at[1], (core_12, core_3), (core_0, core_12))
+    gradient = jnp.dot(
+        hidden_a[...], rows[0].reshape(-1, width), preferred_element_type=F32
+    ) + jnp.dot(hidden_b[...], rows[1].reshape(-1, width), preferred_element_type=F32)
     out[0] = adam(gradient, first[0], second[0])
 
 
-def down_call(behind, hiddens, grads, first, second, start, units, step):
-    count, _ = grads[0].shape
-    inner = first.shape[1]
-    part = pl.BlockSpec((count, step), lambda j: (0, start + j))
-    moment = pl.BlockSpec((1, inner, step), lambda j: (0, 0, start + j))
-    whole = pl.BlockSpec((inner, count), lambda j: (0, 0))
+def down_call(behind, half, near, hiddens, pieces, first, second, start, units, step):
+    part, count = hiddens[0].shape
+    moment = pl.BlockSpec((1, part, step), lambda j: (0, half, start + j))
+    whole = pl.BlockSpec((part, count), lambda j: (0, 0))
     return pl.pallas_call(
         after(down_kernel, len(behind)),
         grid=(units,),
         in_specs=[pl.BlockSpec(memory_space=pl.ANY) for _ in behind]
-        + [whole, whole, part, part, moment, moment],
-        out_specs=pl.BlockSpec((1, inner, step), lambda j: (0, 0, j)),
-        out_shape=jax.ShapeDtypeStruct((1, inner, units * step), BF16),
+        + [pl.BlockSpec(memory_space=pltpu.SMEM), whole, whole]
+        + [pl.BlockSpec((YZ, PAIR, step), lambda j: (0, 0, start + j)) for _ in pieces]
+        + [moment, moment],
+        out_specs=pl.BlockSpec((1, part, step), lambda j: (0, 0, j)),
+        out_shape=jax.ShapeDtypeStruct((1, part, units * step), BF16),
+        scratch_shapes=[pltpu.VMEM((2, YZ, 2 * PAIR, step), BF16)],
         compiler_params=params(),
         cost_estimate=cost(
-            4 * count * inner * units * step, 2 * units * step * (2 * count + 3 * inner)
+            4 * count * part * units * step, 2 * units * step * (3 * count + 3 * part)
         ),
         interpret=INTERPRET,
-    )(*behind, *hiddens, *grads, first, second)
+    )(*behind, near, *hiddens, *pieces, first, second)
 
 
 def contract_rows(left, right):
@@ -411,32 +448,26 @@
         out[...] = mine[...]
 
 
-def place(behind, swapping, mine, theirs, whole, shape, start, units):
+def place(behind, swapping, mine, theirs, whole, shape, half, start, units):
     block = tuple(n // units if k == 2 else n for k, n in enumerate(mine.shape))
-    at = lambda base: lambda j: tuple(base + j if k == 2 else 0 for k in range(len(block)))
+    at = lambda base, row: lambda j: (0, row, base + j, 0)[: len(block)]
     old = behind + ([] if whole is None else [whole])
     return pl.pallas_call(
         place_kernel,
         grid=(units,),
         in_specs=[
             pl.BlockSpec(memory_space=pltpu.SMEM),
-            pl.BlockSpec(block, at(0)),
-            pl.BlockSpec(block, at(0)),
+            pl.BlockSpec(block, at(0, 0)),
+            pl.BlockSpec(block, at(0, 0)),
         ]
         + [pl.BlockSpec(memory_space=pl.ANY) for _ in old],
-        out_specs=pl.BlockSpec(block, at(start)),
+        out_specs=pl.BlockSpec(block, at(start, half)),
         out_shape=jax.ShapeDtypeStruct(shape, BF16),
         input_output_aliases={} if whole is None else {2 + len(old): 0},
         compiler_params=params(),
         cost_estimate=cost(0, 6 * mine.size),
         interpret=INTERPRET,
     )(swapping, mine, theirs, *old)
-
-
-def join_grads(near, own, near_in, far_in):
-    first = jnp.where(near == 1, own, near_in)
-    second = jnp.where(near == 1, near_in, far_in)
-    return jnp.concatenate([first, second], axis=1).reshape(-1, own.shape[2])
 
 
 def local(
@@ -464,48 +495,56 @@
 
     small_core = send(small, to_core)
     cotangent_core = send(cotangent, to_core)
-    small_in = [send(small, t) for t in token_goals]
     tokens_in = [send(tokens, t) for t in token_goals]
     near = near.reshape(1)
     scaled = grads_call(
         core.astype(jnp.int32).reshape(1), slots, [small, small_core], [cotangent, cotangent_core]
     )
-    small_in[0] = jnp.where(near == 1, small, small_in[0])
     grads_0 = over_yz(scaled)
     down_core = send(w_down, to_core)
     gate_up_core = send(w_gate_up, to_core)
 
-    picks = picks_call(side.astype(jnp.int32).reshape(1), slots, small_in)
+    chip = jnp.concatenate([small, small_core], axis=0)
+    small_a = send(chip, small_near)
+    small_b = send(chip, token_3)
+    small_a = jnp.where(near == 1, chip, small_a)
+    picks = picks_call(side.astype(jnp.int32).reshape(1), slots, small_a, small_b)
     sent_rows = tokens_call(near, picks, [tokens] + tokens_in)
     grads_12 = send(grads_0, grad_12)
     grads_3 = send(grads_0, grad_3)
+    core_0 = send(grads_0, grad_near)
     rows_a = over_yz(sent_rows).reshape(-1, width)
-    near = marker_call(near, rows_a)
-    grads_a = join_grads(near, grads_0, grads_12, grads_3)
-    grads_b = send(grads_a, to_core)
-
-    hidden_a, hidden_other, gates = forward_call(rows_a, w_gate_up, gate_up_core)
-    hidden_b = send(hidden_other, to_core)
+    marked = marker_call(near, rows_a)
+    core_12 = send(grads_12, to_core)
+    core_3 = send(grads_3, grad_far)
+    mine_in = [grads_0, grads_12, grads_3]
     rows_b = send(rows_a, to_core)
 
     swapping = swap_flag[my_slot].reshape(1)
-    pending, behind, start, step = [], [], 0, width // 7
-    for units in (1, 3, 3):
-        mine = down_call(
-            behind,
-            (hidden_a, hidden_b),
-            (grads_a, grads_b),
-            first_down,
-            second_down,
-            start,
-            units,
-            step,
-        )
-        theirs = send(mine, to_swap)
-        pending.append((mine, theirs, start, units))
-        behind, start = [mine], start + units
+    pending, behind, gates, step = [], [], [], width // 7
+    for half, parts in enumerate(((2, 5), (7,))):
+        hidden_a, hidden_other, gate = forward_call(behind, half, rows_a, w_gate_up, gate_up_core)
+        gates.append(gate)
+        hidden_b = send(hidden_other, to_core)
+        start = 0
+        for units in parts:
+            mine = down_call(
+                behind,
+                half,
+                marked,
+                (hidden_a, hidden_b),
+                mine_in + [core_0, core_12, core_3],
+                first_down,
+                second_down,
+                start,
+                units,
+                step,
+            )
+            theirs = send(mine, to_swap)
+            pending.append((mine, theirs, half, start, units))
+            behind, start = [mine], start + units
     downs = len(pending)
-    back_a, back_other = backward_call(behind, grads_a, w_down, down_core, gates)
+    back_a, back_other = backward_call(behind, marked, mine_in, w_down, down_core, gates)
     back_b = send(back_other, to_core)
     start, step = 0, width // 14
     for units in (4, 4, 4, 1, 1):
@@ -520,14 +559,16 @@
             step,
         )
         theirs = send(mine, to_swap)
-        pending.append((mine, theirs, start, units))
+        pending.append((mine, theirs, 0, start, units))
         behind, start = [mine], start + units
     whole = None
-    for mine, theirs, start, units in pending[:downs]:
-        whole = place([], swapping, mine, theirs, whole, w_down.shape, start, units)
+    for mine, theirs, half, start, units in pending[:downs]:
+        whole = place([], swapping, mine, theirs, whole, w_down.shape, half, start, units)
     step_down, whole, behind = whole, None, [whole]
-    for mine, theirs, start, units in pending[downs:]:
-        whole = place(behind, swapping, mine, theirs, whole, w_gate_up.shape, start, units)
+    for mine, theirs, half, start, units in pending[downs:]:
+        whole = place(
+            behind, swapping, mine, theirs, whole, w_gate_up.shape, half, start, units
+        )
         behind = []
     return (whole, step_down)
 

time: 391 us -> 386 us (0.987)
  waiting for transfers between devices: 207 us -> 187 us
  Pallas kernels: 102 us -> 120 us
  other arithmetic: 7.53 us -> 1.98 us
    ppermute x26 -> x27, waiting for transfers between devices: 128 us -> 116 us  [send(): return lax.ppermute(value, AXES, pairs)]
    pallas_call x3, Pallas kernels: 15.4 us -> 25.3 us  [down_call(): pl.pallas_call(after(down_kernel, len(behind)), grid=(units,), in_specs=[...]
    all_to_all x2, waiting for transfers between devices: 78.8 us -> 71.6 us  [over_yz(): lax.all_to_all(value, 'expert', 0, 0, axis_index_groups=groups, tiled=True)]
    pallas_call x1 -> x2, Pallas kernels: 11.7 us -> 15.7 us  [forward_call(): pl.pallas_call(after(forward_kernel, len(behind)), grid=(width // step,),...]
    ppermute x26 -> x27, starting transfers between devices: 50.8 us -> 50.2 us  [send(): return lax.ppermute(value, AXES, pairs)]
  transfers between devices with their start and end apart: 28 -> 29, of which waited for: 9 -> 6; matrix products, arithmetic and copies ran while one was open for 1% -> 1% of each run, Pallas kernels for 25% -> 30%
where the time goes in v5:
time: 386 us; the launch traced here: 382 us
  waiting for transfers between devices  187 us (48%)
  Pallas kernels  120 us (31%)
  starting transfers between devices  65.2 us (17%)
  local copies, waits for them, and re-layouts  6.71 us (2%)
    ppermute x27, waiting for transfers between devices, send(): return lax.ppermute(value, AXES, pairs)  116 us
    all_to_all x2, waiting for transfers between devices, over_yz(): lax.all_to_all(value, 'expert', 0, 0, axis_index_groups=groups, tiled=True)  71.6 us
    ppermute x27, starting transfers between devices, send(): return lax.ppermute(value, AXES, pairs)  50.2 us
    pallas_call x8, Pallas kernels, place(): pl.pallas_call(place_kernel, grid=(units,), in_specs=[pl.BlockSpec(memory...  29.1 us
    pallas_call x5, Pallas kernels, gate_up_call(): pl.pallas_call(after(gate_up_kernel, len(behind)), grid=(units,), in_spec...  26.6 us
    pallas_call x3, Pallas kernels, down_call(): pl.pallas_call(after(down_kernel, len(behind)), grid=(units,), in_specs=[...  25.3 us
    pallas_call x2, Pallas kernels, forward_call(): pl.pallas_call(after(forward_kernel, len(behind)), grid=(width // step,),...  15.7 us
    all_to_all x2, starting transfers between devices, over_yz(): lax.all_to_all(value, 'expert', 0, 0, axis_index_groups=groups, tiled=True)  15 us
  transfers between devices with their start and end apart: 29, of which 6 were waited for; matrix products, arithmetic and copies ran while one was open for 1% of the time, Pallas kernels for 30%

profile of v5, /device:TPU:64, one launch (start us, length us, event | category | flops | bytes accessed | tf_op | source)
XLA Modules:
  0.0 381.6 jit_solution(7815873986367425800)
XLA Ops:
  0.7 0.7 convert_bitcast_fusion
  1.4 0.7 pad_maximum_fusion.1.small_a
  2.1 0.5 collective-permute-start
  2.6 0.8 collective-permute-done.small_b
  3.4 0.6 copy-done.13
  4.0 0.4 copy-done.7
  4.3 3.8 shard_map.135
  8.1 7.7 %all-to-all-start.1 = ((bf16[16,24,3584]{2,1,0:T(8,128)(2,1)}), bf16[16,24,3584]{2,1,0:T(8,128)(2,1)S(1)}, u32[]{:S(2)}, u32[]{:S(2)}) async-start(bf16[16,24,3584]{2,1,0:T(8,128)(2,1)} %shard_map.135), calls=%async_computation.1 | async-start | bytes 5505024 | tf_op jit(solution)/shard_map/all_to_all | solution.py:82
  15.8 1.6 collective-permute-start.3
  17.4 3.2 collective-permute-start.4
  20.8 3.1 collective-permute-start.6
  23.9 0.7 collective-permute-start.1
  24.6 0.3 collective-permute-start.2
  25.0 0.6 broadcast_select_fusion.near_small
  25.6 36.6 %collective-permute-done.2.far_small = f32[8,128]{1,0:T(8,128)S(1)} collective-permute-done((f32[8,128]{1,0:T(8,128)S(1)}, f32[8,128]{1,0:T(8,128)S(1)}, u32[]{:S(2)}, u32[]{:S(2)}) %collective-permute-start.2) | collective-permute-done | bytes 4128 | tf_op jit(solution)/shard_map/ppermute | solution.py:33
  62.1 0.6 copy-done.17
  62.7 1.8 shard_map.131.picks
  64.6 5.5 %shard_map.132 = bf16[16,48,3584]{2,1,0:T(8,128)(2,1)} custom-call(s32[1]{0:T(128)} %bitcast.near, bf16[2,384,256]{2,1,0:T(8,128)(2,1)} %shard_map.131.picks, bf16[128,3584]{1,0:T(8,128)(2,1)} %own.1, bf16[128,3584]{1,0:T(8,128)(2,1)} %collective-permute-done.3.data_a, bf16[128,3584]{1,0:T(8,128)(2,1)} %collective-permute-done.4.data_b, ...), custom_call_target="tpu_custom_call" | custom-call | flops 1409286144 | bytes 10092544 | tf_op jit(solution)/shard_map/pallas_call | solution.py:216
  70.1 7.2 %all-to-all-start = ((bf16[16,48,3584]{2,1,0:T(8,128)(2,1)}), bf16[16,48,3584]{2,1,0:T(8,128)(2,1)}, u32[]{:S(2)}, u32[]{:S(2)}) async-start(bf16[16,48,3584]{2,1,0:T(8,128)(2,1)} %shard_map.132), calls=%async_computation | async-start | bytes 11010048 | tf_op jit(solution)/shard_map/all_to_all | solution.py:82
  77.3 1.4 collective-permute-start.10
  78.8 2.2 collective-permute-start.11
  80.9 2.3 collective-permute-start.7
  83.2 71.6 %all-to-all-done = bf16[16,48,3584]{2,1,0:T(8,128)(2,1)} async-done(((bf16[16,48,3584]{2,1,0:T(8,128)(2,1)}), bf16[16,48,3584]{2,1,0:T(8,128)(2,1)}, u32[]{:S(2)}, u32[]{:S(2)}) %all-to-all-start) | async-done | bytes 5505056 | tf_op jit(solution)/shard_map/all_to_all | solution.py:82
  154.9 1.1 collective-permute-start.16
  156.0 3.5 collective-permute-start.12
  159.5 1.3 collective-permute-start.14
  160.8 2.6 collective-permute-start.17
  163.4 7.9 %shard_map.134 = (bf16[128,768]{1,0:T(8,128)(2,1)}, bf16[128,768]{1,0:T(8,128)(2,1)}, f32[2,768,256]{2,1,0:T(8,128)}) custom-call(bf16[768,3584]{1,0:T(8,128)(2,1)} %bitcast.6.rows.refs_0_.refs_1_, bf16[1,2,3584,256]{3,2,1,0:T(8,128)(2,1)} %refs_2_.1, bf16[1,2,3584,256]{3,2,1,0:T(8,128)(2,1)} %collective-permute-done.7.refs_2_.refs_3_), custom_call_target="tpu_custom_call" | custom-call | flops 2818572288 | bytes 9175040 | tf_op jit(solution)/shard_map/pallas_call | solution.py:276
  171.3 0.5 shard_map.133.refs_0_.refs_1_
  171.8 3.8 %collective-permute-done.8.refs_2_.refs_3_ = bf16[128,768]{1,0:T(8,128)(2,1)S(1)} collective-permute-done((bf16[128,768]{1,0:T(8,128)(2,1)}, bf16[128,768]{1,0:T(8,128)(2,1)S(1)}, u32[]{:S(2)}, u32[]{:S(2)}) %collective-permute-start.8) | collective-permute-done | bytes 196640 | tf_op jit(solution)/shard_map/ppermute | solution.py:33
  175.7 0.7 copy-done.8
  176.3 4.9 %shard_map.136.refs_0_.mine = bf16[1,128,1024]{2,1,0:T(8,128)(2,1)} custom-call(s32[1]{0:T(128)} %shard_map.133.refs_0_.refs_1_, bf16[128,768]{1,0:T(8,128)(2,1)} %get-tuple-element.10.refs_1_.refs_2_, bf16[128,768]{1,0:T(8,128)(2,1)} %copy-done.8, bf16[16,24,3584]{2,1,0:T(8,128)(2,1)} %copy-done, ...), custom_call_target="tpu_custom_call" | custom-call | flops 402653184 | bytes 5505024 | tf_op jit(solution)/shard_map/pallas_call | solution.py:386
  181.2 9.0 %shard_map.137.refs_0_.mine = bf16[1,128,2560]{2,1,0:T(8,128)(2,1)} custom-call(bf16[1,128,1024]{2,1,0:T(8,128)(2,1)} %shard_map.136.refs_0_.mine, s32[1]{0:T(128)} %shard_map.133.refs_0_.refs_1_, bf16[128,768]{1,0:T(8,128)(2,1)} %get-tuple-element.10.refs_1_.refs_2_, bf16[128,768]{1,0:T(8,128)(2,1)} %copy-done.8, bf16[16,24,3584]{2,1,0:T(8,128)(2,1)} %copy-done, ...), custom_call_target="tpu_custom_call" | custom-call | flops 1006632960 | bytes 13762560 | tf_op jit(solution)/shard_map/pallas_call | solution.py:386
  190.2 7.9 %shard_map.138 = (bf16[128,768]{1,0:T(8,128)(2,1)}, bf16[128,768]{1,0:T(8,128)(2,1)}, f32[2,768,256]{2,1,0:T(8,128)}) custom-call(bf16[1,128,2560]{2,1,0:T(8,128)(2,1)} %shard_map.137.refs_0_.mine, bf16[768,3584]{1,0:T(8,128)(2,1)} %bitcast.6.rows.refs_0_.refs_1_, bf16[1,2,3584,256]{3,2,1,0:T(8,128)(2,1)} %refs_2_.1, ...), custom_call_target="tpu_custom_call" | custom-call | flops 2818572288 | bytes 9175040 | tf_op jit(solution)/shard_map/pallas_call | solution.py:276
  198.1 0.3 collective-permute-start.15
  198.4 1.3 collective-permute-done.15.refs_3_
  199.7 0.7 copy-done.12
  200.4 11.4 %shard_map.139.refs_0_.mine = bf16[1,128,3584]{2,1,0:T(8,128)(2,1)} custom-call(bf16[1,128,2560]{2,1,0:T(8,128)(2,1)} %shard_map.137.refs_0_.mine, s32[1]{0:T(128)} %shard_map.133.refs_0_.refs_1_, bf16[128,768]{1,0:T(8,128)(2,1)} %get-tuple-element.12.refs_2_, bf16[128,768]{1,0:T(8,128)(2,1)} %copy-done.12, bf16[16,24,3584]{2,1,0:T(8,128)(2,1)} %copy-done, ...), custom_call_target="tpu_custom_call" | custom-call | flops 1409286144 | bytes 19267584 | tf_op jit(solution)/shard_map/pallas_call | solution.py:386
  211.8 11.2 %shard_map.140 = (bf16[768,512]{1,0:T(8,128)(2,1)}, bf16[768,512]{1,0:T(8,128)(2,1)}) custom-call(bf16[1,128,3584]{2,1,0:T(8,128)(2,1)} %shard_map.139.refs_0_.mine, s32[1]{0:T(128)} %shard_map.133.refs_0_.refs_1_, bf16[16,24,3584]{2,1,0:T(8,128)(2,1)} %copy-done, bf16[16,24,3584]{2,1,0:T(8,128)(2,1)} %collective-permute-done.10.refs_4_.refs_5_.refs_3_, ...), custom_call_target="tpu_custom_call" | custom-call | flops 2818572288 | bytes 15073280 | tf_op jit(solution)/shard_map/pallas_call | solution.py:339
  223.0 0.3 collective-permute-start.18
  223.3 14.7 %collective-permute-start.26 = (bf16[1,128,1024]{2,1,0:T(8,128)(2,1)S(1)}, bf16[1,128,1024]{2,1,0:T(8,128)(2,1)S(1)}, u32[]{:S(2)}, u32[]{:S(2)}) collective-permute-start(bf16[1,128,1024]{2,1,0:T(8,128)(2,1)S(1)} %copy-done.4), channel_id=1, source_target_pairs={{0,16},{1,17},{2,18},{3,19},{4,20},{5,21},{6,22},{7,23},{8,24},{9,... | collective-permute-start | bytes 786440 | tf_op jit(solution)/shard_map/ppermute | solution.py:33
  238.1 0.9 copy-done.1
  239.0 6.6 %shard_map.141.refs_0_.mine = bf16[1,2,1024,256]{3,2,1,0:T(8,128)(2,1)} custom-call(bf16[1,128,3584]{2,1,0:T(8,128)(2,1)} %shard_map.139.refs_0_.mine, bf16[768,3584]{1,0:T(8,128)(2,1)} %bitcast.6.rows.refs_0_.refs_1_, bf16[768,3584]{1,0:T(8,128)(2,1)} %collective-permute-done.16.refs_2_, bf16[768,512]{1,0:T(8,128)(2,1)} %get-tuple-element.16.refs_3_, ...), custom_call_target="tpu_custom_call" | custom-call | flops 1610612736 | bytes 6291456 | tf_op jit(solution)/shard_map/pallas_call | solution.py:424
  245.6 3.5 collective-permute-start.23
  249.0 6.6 %shard_map.142.refs_0_.mine = bf16[1,2,1024,256]{3,2,1,0:T(8,128)(2,1)} custom-call(bf16[1,2,1024,256]{3,2,1,0:T(8,128)(2,1)} %shard_map.141.refs_0_.mine, bf16[768,3584]{1,0:T(8,128)(2,1)} %bitcast.6.rows.refs_0_.refs_1_, bf16[768,3584]{1,0:T(8,128)(2,1)} %collective-permute-done.16.refs_2_, bf16[768,512]{1,0:T(8,128)(2,1)} %get-tuple-element.16.refs_3_, ...), custom_call_target="tpu_custom_call" | custom-call | flops 1610612736 | bytes 6291456 | tf_op jit(solution)/shard_map/pallas_call | solution.py:424
  255.8 6.7 %shard_map.143.refs_0_.mine = bf16[1,2,1024,256]{3,2,1,0:T(8,128)(2,1)} custom-call(bf16[1,2,1024,256]{3,2,1,0:T(8,128)(2,1)} %shard_map.142.refs_0_.mine, bf16[768,3584]{1,0:T(8,128)(2,1)} %bitcast.6.rows.refs_0_.refs_1_, bf16[768,3584]{1,0:T(8,128)(2,1)} %collective-permute-done.16.refs_2_, bf16[768,512]{1,0:T(8,128)(2,1)} %get-tuple-element.16.refs_3_, ...), custom_call_target="tpu_custom_call" | custom-call | flops 1610612736 | bytes 6291456 | tf_op jit(solution)/shard_map/pallas_call | solution.py:424
  262.4 3.4 collective-permute-start.21
  266.1 3.3 shard_map.144.refs_0_.mine
  269.4 3.4 shard_map.145.mine
  272.7 73.2 %collective-permute-done.25.theirs = bf16[1,128,2560]{2,1,0:T(8,128)(2,1)} collective-permute-done((bf16[1,128,2560]{2,1,0:T(8,128)(2,1)S(1)}, bf16[1,128,2560]{2,1,0:T(8,128)(2,1)}, u32[]{:S(2)}, u32[]{:S(2)}) %collective-permute-start.25) | collective-permute-done | bytes 655392 | tf_op jit(solution)/shard_map/ppermute | solution.py:33
  345.9 3.2 collective-permute-start.20
  349.1 0.3 collective-permute-start.19
  349.4 0.5 dynamic_slice.3.swapping
  350.0 2.3 shard_map.146.rest_0_
  352.3 4.4 %shard_map.147.rest_0_ = bf16[1,256,3584]{2,1,0:T(8,128)(2,1)} custom-call(s32[1]{0:T(128)} %dynamic_slice.3.swapping, bf16[1,128,2560]{2,1,0:T(8,128)(2,1)} %shard_map.137.refs_0_.mine, bf16[1,128,2560]{2,1,0:T(8,128)(2,1)} %collective-permute-done.25.theirs, bf16[1,256,3584]{2,1,0:T(8,128)(2,1)} %shard_map.146.rest_0_), custom_call_target="tpu_custom_call", output_to_operand_aliasing={{}: (3, {})} | custom-call | bytes 1966080 | tf_op jit(solution)/shard_map/pallas_call | solution.py:455
  356.7 5.5 %shard_map.148.rest_0_ = bf16[1,256,3584]{2,1,0:T(8,128)(2,1)} custom-call(s32[1]{0:T(128)} %dynamic_slice.3.swapping, bf16[1,128,3584]{2,1,0:T(8,128)(2,1)} %shard_map.139.refs_0_.mine, bf16[1,128,3584]{2,1,0:T(8,128)(2,1)} %collective-permute-done.24.theirs, bf16[1,256,3584]{2,1,0:T(8,128)(2,1)} %shard_map.147.rest_0_), custom_call_target="tpu_custom_call", output_to_operand_aliasing={{}: (3, {})} | custom-call | bytes 2752512 | tf_op jit(solution)/shard_map/pallas_call | solution.py:455
  362.2 4.1 %shard_map.149.rest_0_ = bf16[1,2,3584,256]{3,2,1,0:T(8,128)(2,1)} custom-call(s32[1]{0:T(128)} %dynamic_slice.3.swapping, bf16[1,2,1024,256]{3,2,1,0:T(8,128)(2,1)} %shard_map.141.refs_0_.mine, bf16[1,2,1024,256]{3,2,1,0:T(8,128)(2,1)} %collective-permute-done.23.theirs, bf16[1,256,3584]{2,1,0:T(8,128)(2,1)} %shard_map.148.rest_0_), custom_call_target="tpu_custom_call" | custom-call | bytes 3145728 | tf_op jit(solution)/shard_map/pallas_call | solution.py:455
  366.3 4.1 %shard_map.150.rest_0_ = bf16[1,2,3584,256]{3,2,1,0:T(8,128)(2,1)} custom-call(s32[1]{0:T(128)} %dynamic_slice.3.swapping, bf16[1,2,1024,256]{3,2,1,0:T(8,128)(2,1)} %shard_map.142.refs_0_.mine, bf16[1,2,1024,256]{3,2,1,0:T(8,128)(2,1)} %collective-permute-done.22.theirs, bf16[1,2,3584,256]{3,2,1,0:T(8,128)(2,1)} %shard_map.149.rest_0_), custom_call_target="tpu_custom_call", output_to_operand_aliasing={{}: (3, {})} | custom-call | bytes 3145728 | tf_op jit(solution)/shard_map/pallas_call | solution.py:455
  370.4 1.0 copy-done.6
  371.4 4.1 %shard_map.151.rest_0_ = bf16[1,2,3584,256]{3,2,1,0:T(8,128)(2,1)} custom-call(s32[1]{0:T(128)} %dynamic_slice.3.swapping, bf16[1,2,1024,256]{3,2,1,0:T(8,128)(2,1)} %shard_map.143.refs_0_.mine, bf16[1,2,1024,256]{3,2,1,0:T(8,128)(2,1)} %copy-done.6, bf16[1,2,3584,256]{3,2,1,0:T(8,128)(2,1)} %shard_map.150.rest_0_), custom_call_target="tpu_custom_call", output_to_operand_aliasing={{}: (3, {})} | custom-call | bytes 3145728 | tf_op jit(solution)/shard_map/pallas_call | solution.py:455
  375.5 0.7 copy-done.10
  376.3 2.3 shard_map.152.rest_0_
  378.6 0.7 copy-done.11
  379.3 2.3 shard_map.153
  (60 shorter events, 0.8 us)
Async XLA Ops:
  0.6 2.8 collective-permute-start.9
  2.1 1.3 copy-start.16
  2.1 1.3 collective-permute-start
  3.4 0.6 copy-start.13
  3.4 0.9 copy-start.7
  8.1 15.8 %copy-start.14 = (f32[4,128]{1,0:T(4,128)S(1)}, f32[4,128]{1,0:T(4,128)}, u32[]{:S(2)}) copy-start(f32[4,128]{1,0:T(4,128)} %copy-done.13) | copy-start | bytes 6148
  8.1 15.8 %copy-start.15 = (f32[128,2]{0,1:T(2,128)S(1)}, f32[128,2]{0,1:T(2,128)}, u32[]{:S(2)}) copy-start(f32[128,2]{0,1:T(2,128)} %param.15) | copy-start | bytes 3076
  8.1 62.0 %all-to-all-start.1 = ((bf16[16,24,3584]{2,1,0:T(8,128)(2,1)}), bf16[16,24,3584]{2,1,0:T(8,128)(2,1)S(1)}, u32[]{:S(2)}, u32[]{:S(2)}) async-start(bf16[16,24,3584]{2,1,0:T(8,128)(2,1)} %shard_map.135), calls=%async_computation.1 | async-start | bytes 5505024 | tf_op jit(solution)/shard_map/all_to_all | solution.py:82
  15.8 48.7 %collective-permute-start.3 = (bf16[128,3584]{1,0:T(8,128)(2,1)}, bf16[128,3584]{1,0:T(8,128)(2,1)}, u32[]{:S(2)}, u32[]{:S(2)}) collective-permute-start(bf16[128,3584]{1,0:T(8,128)(2,1)} %own.1), channel_id=1, source_target_pairs={{1,96},{3,98},{5,100},{7,102},{9,104},{11,106},{13,108},{15,110},{... | collective-permute-start | bytes 2752520 | tf_op jit(solution)/shard_map/ppermute | solution.py:33
  17.4 47.1 %collective-permute-start.4 = (bf16[128,3584]{1,0:T(8,128)(2,1)}, bf16[128,3584]{1,0:T(8,128)(2,1)}, u32[]{:S(2)}, u32[]{:S(2)}) collective-permute-start(bf16[128,3584]{1,0:T(8,128)(2,1)} %own.1), channel_id=1, source_target_pairs={{0,65},{1,33},{2,67},{3,35},{4,69},{5,37},{6,71},{7,39},{8,73},{9,... | collective-permute-start | bytes 2752520 | tf_op jit(solution)/shard_map/ppermute | solution.py:33
  20.6 44.0 %collective-permute-start.5 = (bf16[128,3584]{1,0:T(8,128)(2,1)}, bf16[128,3584]{1,0:T(8,128)(2,1)}, u32[]{:S(2)}, u32[]{:S(2)}) collective-permute-start(bf16[128,3584]{1,0:T(8,128)(2,1)} %own.1), channel_id=1, source_target_pairs={{0,64},{1,32},{2,66},{3,34},{4,68},{5,36},{6,70},{7,38},{8,72},{9,... | collective-permute-start | bytes 2752520 | tf_op jit(solution)/shard_map/ppermute | solution.py:33
  20.8 43.7 %collective-permute-start.6 = (bf16[128,3584]{1,0:T(8,128)(2,1)}, bf16[128,3584]{1,0:T(8,128)(2,1)}, u32[]{:S(2)}, u32[]{:S(2)}) collective-permute-start(bf16[128,3584]{1,0:T(8,128)(2,1)} %own.1), channel_id=1, source_target_pairs={{0,1},{1,97},{2,3},{3,99},{4,5},{5,101},{6,7},{7,103},{8,9},{9,105... | collective-permute-start | bytes 2752520 | tf_op jit(solution)/shard_map/ppermute | solution.py:33
  23.9 0.7 collective-permute-start.1
  24.6 37.5 %collective-permute-start.2 = (f32[8,128]{1,0:T(8,128)S(1)}, f32[8,128]{1,0:T(8,128)S(1)}, u32[]{:S(2)}, u32[]{:S(2)}) collective-permute-start(f32[8,128]{1,0:T(8,128)S(1)} %pad_maximum_fusion), channel_id=1, source_target_pairs={{0,64},{1,32},{2,66},{3,34},{4,68},{5,36},{6,70},{7,38},{8,72},{9,... | collective-permute-start | bytes 12296 | tf_op jit(solution)/shard_map/ppermute | solution.py:33
  62.1 0.6 copy-start.17
  70.1 85.9 %copy-start = (bf16[16,24,3584]{2,1,0:T(8,128)(2,1)}, bf16[16,24,3584]{2,1,0:T(8,128)(2,1)S(1)}, u32[]{:S(2)}) copy-start(bf16[16,24,3584]{2,1,0:T(8,128)(2,1)S(1)} %all-to-all-done.1.refs_3_.refs_4_.refs_2_) | copy-start | bytes 8257540
  70.1 84.8 %all-to-all-start = ((bf16[16,48,3584]{2,1,0:T(8,128)(2,1)}), bf16[16,48,3584]{2,1,0:T(8,128)(2,1)}, u32[]{:S(2)}, u32[]{:S(2)}) async-start(bf16[16,48,3584]{2,1,0:T(8,128)(2,1)} %shard_map.132), calls=%async_computation | async-start | bytes 11010048 | tf_op jit(solution)/shard_map/all_to_all | solution.py:82
  77.3 82.2 %collective-permute-start.10 = (bf16[16,24,3584]{2,1,0:T(8,128)(2,1)S(1)}, bf16[16,24,3584]{2,1,0:T(8,128)(2,1)}, u32[]{:S(2)}, u32[]{:S(2)}) collective-permute-start(bf16[16,24,3584]{2,1,0:T(8,128)(2,1)S(1)} %all-to-all-done.1.refs_3_.refs_4_.refs_2_), channel_id=1, source_target_pairs={{0,64},{1,96},{2,66},{3,98},{4,68},{5,100},{6,70},{7,102},{8,72},{... | collective-permute-start | bytes 8257544 | tf_op jit(solution)/shard_map/ppermute | solution.py:33
  78.8 80.7 %collective-permute-start.11 = (bf16[16,24,3584]{2,1,0:T(8,128)(2,1)S(1)}, bf16[16,24,3584]{2,1,0:T(8,128)(2,1)}, u32[]{:S(2)}, u32[]{:S(2)}) collective-permute-start(bf16[16,24,3584]{2,1,0:T(8,128)(2,1)S(1)} %all-to-all-done.1.refs_3_.refs_4_.refs_2_), channel_id=1, source_target_pairs={{1,32},{3,34},{5,36},{7,38},{9,40},{11,42},{13,44},{15,46},{17,48}... | collective-permute-start | bytes 8257544 | tf_op jit(solution)/shard_map/ppermute | solution.py:33
  80.9 79.9 %collective-permute-start.7 = (bf16[1,2,3584,256]{3,2,1,0:T(8,128)(2,1)}, bf16[1,2,3584,256]{3,2,1,0:T(8,128)(2,1)}, u32[]{:S(2)}, u32[]{:S(2)}) collective-permute-start(bf16[1,2,3584,256]{3,2,1,0:T(8,128)(2,1)} %refs_2_.1), channel_id=1, source_target_pairs={{0,32},{1,33},{2,34},{3,35},{4,36},{5,37},{6,38},{7,39},{8,40},{9,... | collective-permute-start | bytes 11010056 | tf_op jit(solution)/shard_map/ppermute | solution.py:33
  154.9 83.2 %collective-permute-start.16 = (bf16[768,3584]{1,0:T(8,128)(2,1)}, bf16[768,3584]{1,0:T(8,128)(2,1)}, u32[]{:S(2)}, u32[]{:S(2)}) collective-permute-start(bf16[768,3584]{1,0:T(8,128)(2,1)} %bitcast.6.rows.refs_0_.refs_1_), channel_id=1, source_target_pairs={{0,32},{1,33},{2,34},{3,35},{4,36},{5,37},{6,38},{7,39},{8,40},{9,... | collective-permute-start | bytes 16515080 | tf_op jit(solution)/shard_map/ppermute | solution.py:33
  156.0 15.3 %collective-permute-start.12 = (bf16[16,24,3584]{2,1,0:T(8,128)(2,1)S(1)}, bf16[16,24,3584]{2,1,0:T(8,128)(2,1)}, u32[]{:S(2)}, u32[]{:S(2)}) collective-permute-start(bf16[16,24,3584]{2,1,0:T(8,128)(2,1)S(1)} %all-to-all-done.1.refs_3_.refs_4_.refs_2_), channel_id=1, source_target_pairs={{0,32},{2,34},{4,36},{6,38},{8,40},{10,42},{12,44},{14,46},{16,48}... | collective-permute-start | bytes 8257544 | tf_op jit(solution)/shard_map/ppermute | solution.py:33
  159.5 16.2 %collective-permute-start.13 = (bf16[16,24,3584]{2,1,0:T(8,128)(2,1)}, bf16[16,24,3584]{2,1,0:T(8,128)(2,1)}, u32[]{:S(2)}, u32[]{:S(2)}) collective-permute-start(bf16[16,24,3584]{2,1,0:T(8,128)(2,1)} %collective-permute-done.10.refs_4_.refs_5_.refs_3_), channel_id=1, source_target_pairs={{0,32},{1,33},{2,34},{3,35},{4,36},{5,37},{6,38},{7,39},{8,40},{9,... | collective-permute-start | bytes 8257544 | tf_op jit(solution)/shard_map/ppermute | solution.py:33
  159.5 16.2 %collective-permute-start.14 = (bf16[16,24,3584]{2,1,0:T(8,128)(2,1)}, bf16[16,24,3584]{2,1,0:T(8,128)(2,1)}, u32[]{:S(2)}, u32[]{:S(2)}) collective-permute-start(bf16[16,24,3584]{2,1,0:T(8,128)(2,1)} %collective-permute-done.11.refs_5_.refs_6_.refs_4_), channel_id=1, source_target_pairs={{1,33},{3,35},{5,37},{7,39},{9,41},{11,43},{13,45},{15,47},{17,49}... | collective-permute-start | bytes 8257544 | tf_op jit(solution)/shard_map/ppermute | solution.py:33
  160.8 51.0 %collective-permute-start.17 = (bf16[1,256,3584]{2,1,0:T(8,128)(2,1)}, bf16[1,256,3584]{2,1,0:T(8,128)(2,1)}, u32[]{:S(2)}, u32[]{:S(2)}) collective-permute-start(bf16[1,256,3584]{2,1,0:T(8,128)(2,1)} %refs_5_.6), channel_id=1, source_target_pairs={{0,32},{1,33},{2,34},{3,35},{4,36},{5,37},{6,38},{7,39},{8,40},{9,... | collective-permute-start | bytes 5505032 | tf_op jit(solution)/shard_map/ppermute | solution.py:33
  171.3 4.4 %collective-permute-start.8 = (bf16[128,768]{1,0:T(8,128)(2,1)}, bf16[128,768]{1,0:T(8,128)(2,1)S(1)}, u32[]{:S(2)}, u32[]{:S(2)}) collective-permute-start(bf16[128,768]{1,0:T(8,128)(2,1)} %get-tuple-element.11), channel_id=1, source_target_pairs={{0,32},{1,33},{2,34},{3,35},{4,36},{5,37},{6,38},{7,39},{8,40},{9,... | collective-permute-start | bytes 589832 | tf_op jit(solution)/shard_map/ppermute | solution.py:33
  175.7 0.7 copy-start.8
  198.1 1.7 collective-permute-start.15
  199.7 0.7 copy-start.12
  211.8 11.5 %copy-start.4 = (bf16[1,128,1024]{2,1,0:T(8,128)(2,1)S(1)}, bf16[1,128,1024]{2,1,0:T(8,128)(2,1)}, u32[]{:S(2)}) copy-start(bf16[1,128,1024]{2,1,0:T(8,128)(2,1)} %shard_map.136.refs_0_.mine) | copy-start | bytes 786436
  211.8 26.2 %copy-start.2 = (bf16[1,128,3584]{2,1,0:T(8,128)(2,1)S(1)}, bf16[1,128,3584]{2,1,0:T(8,128)(2,1)}, u32[]{:S(2)}) copy-start(bf16[1,128,3584]{2,1,0:T(8,128)(2,1)} %shard_map.139.refs_0_.mine) | copy-start | bytes 2752516
  223.0 15.1 %collective-permute-start.18 = (bf16[768,512]{1,0:T(8,128)(2,1)}, bf16[768,512]{1,0:T(8,128)(2,1)S(1)}, u32[]{:S(2)}, u32[]{:S(2)}) collective-permute-start(bf16[768,512]{1,0:T(8,128)(2,1)} %get-tuple-element.17), channel_id=1, source_target_pairs={{0,32},{1,33},{2,34},{3,35},{4,36},{5,37},{6,38},{7,39},{8,40},{9,... | collective-permute-start | bytes 2359304 | tf_op jit(solution)/shard_map/ppermute | solution.py:33
  223.3 42.5 %collective-permute-start.26 = (bf16[1,128,1024]{2,1,0:T(8,128)(2,1)S(1)}, bf16[1,128,1024]{2,1,0:T(8,128)(2,1)S(1)}, u32[]{:S(2)}, u32[]{:S(2)}) collective-permute-start(bf16[1,128,1024]{2,1,0:T(8,128)(2,1)S(1)} %copy-done.4), channel_id=1, source_target_pairs={{0,16},{1,17},{2,18},{3,19},{4,20},{5,21},{6,22},{7,23},{8,24},{9,... | collective-permute-start | bytes 786440 | tf_op jit(solution)/shard_map/ppermute | solution.py:33
  238.0 111.1 %collective-permute-start.24 = (bf16[1,128,3584]{2,1,0:T(8,128)(2,1)S(1)}, bf16[1,128,3584]{2,1,0:T(8,128)(2,1)}, u32[]{:S(2)}, u32[]{:S(2)}) collective-permute-start(bf16[1,128,3584]{2,1,0:T(8,128)(2,1)S(1)} %copy-done.2), channel_id=1, source_target_pairs={{0,16},{1,17},{2,18},{3,19},{4,20},{5,21},{6,22},{7,23},{8,24},{9,... | collective-permute-start | bytes 2752520 | tf_op jit(solution)/shard_map/ppermute | solution.py:33
  238.1 0.9 copy-start.1
  245.6 116.6 %collective-permute-start.23 = (bf16[1,2,1024,256]{3,2,1,0:T(8,128)(2,1)}, bf16[1,2,1024,256]{3,2,1,0:T(8,128)(2,1)}, u32[]{:S(2)}, u32[]{:S(2)}) collective-permute-start(bf16[1,2,1024,256]{3,2,1,0:T(8,128)(2,1)} %shard_map.141.refs_0_.mine), channel_id=1, source_target_pairs={{0,16},{1,17},{2,18},{3,19},{4,20},{5,21},{6,22},{7,23},{8,24},{9,... | collective-permute-start | bytes 3145736 | tf_op jit(solution)/shard_map/ppermute | solution.py:33
  255.7 10.2 %copy-start.3 = (bf16[1,128,2560]{2,1,0:T(8,128)(2,1)S(1)}, bf16[1,128,2560]{2,1,0:T(8,128)(2,1)}, u32[]{:S(2)}) copy-start(bf16[1,128,2560]{2,1,0:T(8,128)(2,1)} %shard_map.137.refs_0_.mine) | copy-start | bytes 1966084
  255.7 110.6 %collective-permute-start.22 = (bf16[1,2,1024,256]{3,2,1,0:T(8,128)(2,1)}, bf16[1,2,1024,256]{3,2,1,0:T(8,128)(2,1)}, u32[]{:S(2)}, u32[]{:S(2)}) collective-permute-start(bf16[1,2,1024,256]{3,2,1,0:T(8,128)(2,1)} %shard_map.142.refs_0_.mine), channel_id=1, source_target_pairs={{0,16},{1,17},{2,18},{3,19},{4,20},{5,21},{6,22},{7,23},{8,24},{9,... | collective-permute-start | bytes 3145736 | tf_op jit(solution)/shard_map/ppermute | solution.py:33
  262.4 108.0 %collective-permute-start.21 = (bf16[1,2,1024,256]{3,2,1,0:T(8,128)(2,1)}, bf16[1,2,1024,256]{3,2,1,0:T(8,128)(2,1)S(1)}, u32[]{:S(2)}, u32[]{:S(2)}) collective-permute-start(bf16[1,2,1024,256]{3,2,1,0:T(8,128)(2,1)} %shard_map.143.refs_0_.mine), channel_id=1, source_target_pairs={{0,16},{1,17},{2,18},{3,19},{4,20},{5,21},{6,22},{7,23},{8,24},{9,... | collective-permute-start | bytes 3145736 | tf_op jit(solution)/shard_map/ppermute | solution.py:33
  265.9 3.5 copy-start.9
  265.9 80.0 %collective-permute-start.25 = (bf16[1,128,2560]{2,1,0:T(8,128)(2,1)S(1)}, bf16[1,128,2560]{2,1,0:T(8,128)(2,1)}, u32[]{:S(2)}, u32[]{:S(2)}) collective-permute-start(bf16[1,128,2560]{2,1,0:T(8,128)(2,1)S(1)} %copy-done.3), channel_id=1, source_target_pairs={{0,16},{1,17},{2,18},{3,19},{4,20},{5,21},{6,22},{7,23},{8,24},{9,... | collective-permute-start | bytes 1966088 | tf_op jit(solution)/shard_map/ppermute | solution.py:33
  269.4 76.5 %copy-start.5 = (bf16[1,2,256,256]{3,2,1,0:T(8,128)(2,1)S(1)}, bf16[1,2,256,256]{3,2,1,0:T(8,128)(2,1)}, u32[]{:S(2)}) copy-start(bf16[1,2,256,256]{3,2,1,0:T(8,128)(2,1)} %shard_map.144.refs_0_.mine) | copy-start | bytes 786436
  269.4 80.1 %copy-start.18 = (s32[32]{0:T(128)S(1)}, s32[32]{0:T(128)}, u32[]{:S(2)}) copy-start(s32[32]{0:T(128)} %param.17) | copy-start | bytes 388
  345.9 29.6 %collective-permute-start.20 = (bf16[1,2,256,256]{3,2,1,0:T(8,128)(2,1)S(1)}, bf16[1,2,256,256]{3,2,1,0:T(8,128)(2,1)S(1)}, u32[]{:S(2)}, u32[]{:S(2)}) collective-permute-start(bf16[1,2,256,256]{3,2,1,0:T(8,128)(2,1)S(1)} %copy-done.5), channel_id=1, source_target_pairs={{0,16},{1,17},{2,18},{3,19},{4,20},{5,21},{6,22},{7,23},{8,24},{9,... | collective-permute-start | bytes 786440 | tf_op jit(solution)/shard_map/ppermute | solution.py:33
  349.1 29.4 %collective-permute-start.19 = (bf16[1,2,256,256]{3,2,1,0:T(8,128)(2,1)}, bf16[1,2,256,256]{3,2,1,0:T(8,128)(2,1)S(1)}, u32[]{:S(2)}, u32[]{:S(2)}) collective-permute-start(bf16[1,2,256,256]{3,2,1,0:T(8,128)(2,1)} %shard_map.145.mine), channel_id=1, source_target_pairs={{0,16},{1,17},{2,18},{3,19},{4,20},{5,21},{6,22},{7,23},{8,24},{9,... | collective-permute-start | bytes 786440 | tf_op jit(solution)/shard_map/ppermute | solution.py:33
  370.4 1.0 copy-start.6
  375.5 0.7 copy-start.10
  378.6 0.7 copy-start.11

commit v6 on v5

--- a/solution.py
+++ b/solution.py
@@ -266,24 +266,23 @@
             hidden_t[...] = jnp.transpose(gate * jax.nn.sigmoid(gate) * up).astype(BF16)
 
 
-def forward_call(behind, half, rows, gate_up_a, gate_up_b):
+def forward_call(rows, gate_up_a, gate_up_b):
     count, width = rows.shape
-    part = gate_up_a.shape[3] // 2
+    part = gate_up_a.shape[3]
     step = width // FORWARD_STEPS
-    weight = pl.BlockSpec((1, 2, step, part), lambda k: (0, 0, k, half))
+    weight = pl.BlockSpec((1, 2, step, part), lambda k: (0, 0, k, 0))
     whole = lambda shape: pl.BlockSpec(shape, lambda k: (0,) * len(shape))
     shapes = [((part, count), BF16), ((part, count), BF16), ((2, count, 2 * part), F32)]
     return pl.pallas_call(
-        after(forward_kernel, len(behind)),
+        forward_kernel,
         grid=(width // step,),
-        in_specs=[pl.BlockSpec(memory_space=pl.ANY) for _ in behind]
-        + [pl.BlockSpec((count, step), lambda k: (0, k)), weight, weight],
+        in_specs=[pl.BlockSpec((count, step), lambda k: (0, k)), weight, weight],
         out_specs=[whole(s) for s, _ in shapes],
         out_shape=[jax.ShapeDtypeStruct(*s) for s in shapes],
         compiler_params=params(),
         cost_estimate=cost(8 * count * width * part, 2 * width * (count + 4 * part)),
         interpret=INTERPRET,
-    )(*behind, rows, gate_up_a, gate_up_b)
+    )(rows, gate_up_a, gate_up_b)
 
 
 def join(near, rows, if_near, if_not):
@@ -296,7 +295,7 @@
 
 
 def backward_kernel(
-    near, own, in_12, in_3, down_a, down_b, gates_a, gates_b, back_a, back_b, rows, total
+    near, own, in_12, in_3, down_a, down_b, gates, back_a, back_b, rows, total
 ):
     k = pl.program_id(0)
 
@@ -314,19 +313,14 @@
     @pl.when(k == pl.num_programs(0) - 1)
     def _():
         units = total.shape[2]
-        part = units // 2
         for owner, back in enumerate((back_a, back_b)):
-            for half, gates in enumerate((gates_a, gates_b)):
-                at = half * part
-                gate, up = gates[owner, :, :part], gates[owner, :, part:]
-                hidden_grad = total[owner, :, at : at + part]
-                sigmoid = jax.nn.sigmoid(gate)
-                back[:, at : at + part] = (
-                    hidden_grad * up * sigmoid * (1.0 + gate * (1.0 - sigmoid))
-                ).astype(BF16)
-                back[:, units + at : units + at + part] = (
-                    hidden_grad * (gate * sigmoid)
-                ).astype(BF16)
+            gate, up = gates[owner, :, :units], gates[owner, :, units:]
+            hidden_grad = total[owner]
+            sigmoid = jax.nn.sigmoid(gate)
+            back[:, :units] = (
+                hidden_grad * up * sigmoid * (1.0 + gate * (1.0 - sigmoid))
+            ).astype(BF16)
+            back[:, units:] = (hidden_grad * (gate * sigmoid)).astype(BF16)
 
 
 def backward_call(behind, near, pieces, down_a, down_b, gates):
@@ -342,7 +336,7 @@
         in_specs=[pl.BlockSpec(memory_space=pl.ANY) for _ in behind]
         + [pl.BlockSpec(memory_space=pltpu.SMEM)]
         + [pl.BlockSpec((YZ, PAIR, step), lambda k: (0, 0, k)) for _ in pieces]
-        + [weight, weight, whole(gates[0].shape), whole(gates[1].shape)],
+        + [weight, weight, whole(gates.shape)],
         out_specs=[whole((count, 2 * units))] * 2,
         out_shape=[jax.ShapeDtypeStruct((count, 2 * units), BF16)] * 2,
         scratch_shapes=[
@@ -354,7 +348,7 @@
             4 * count * width * units, 3 * width * count + 4 * width * units + 16 * count * units
         ),
         interpret=INTERPRET,
-    )(*behind, near, *pieces, down_a, down_b, *gates)
+    )(*behind, near, *pieces, down_a, down_b, gates)
 
 
 def adam(gradient, first, second):
@@ -379,9 +373,9 @@
     out[0] = adam(gradient, first[0], second[0])
 
 
-def down_call(behind, half, near, hiddens, pieces, first, second, start, units, step):
+def down_call(behind, near, hiddens, pieces, first, second, start, units, step):
     part, count = hiddens[0].shape
-    moment = pl.BlockSpec((1, part, step), lambda j: (0, half, start + j))
+    moment = pl.BlockSpec((1, part, step), lambda j: (0, 0, start + j))
     whole = pl.BlockSpec((part, count), lambda j: (0, 0))
     return pl.pallas_call(
         after(down_kernel, len(behind)),
@@ -448,20 +442,20 @@
         out[...] = mine[...]
 
 
-def place(behind, swapping, mine, theirs, whole, shape, half, start, units):
+def place(behind, swapping, mine, theirs, whole, shape, start, units):
     block = tuple(n // units if k == 2 else n for k, n in enumerate(mine.shape))
-    at = lambda base, row: lambda j: (0, row, base + j, 0)[: len(block)]
+    at = lambda base: lambda j: (0, 0, base + j, 0)[: len(block)]
     old = behind + ([] if whole is None else [whole])
     return pl.pallas_call(
         place_kernel,
         grid=(units,),
         in_specs=[
             pl.BlockSpec(memory_space=pltpu.SMEM),
-            pl.BlockSpec(block, at(0, 0)),
-            pl.BlockSpec(block, at(0, 0)),
+            pl.BlockSpec(block, at(0)),
+            pl.BlockSpec(block, at(0)),
         ]
         + [pl.BlockSpec(memory_space=pl.ANY) for _ in old],
-        out_specs=pl.BlockSpec(block, at(start, half)),
+        out_specs=pl.BlockSpec(block, at(start)),
         out_shape=jax.ShapeDtypeStruct(shape, BF16),
         input_output_aliases={} if whole is None else {2 + len(old): 0},
         compiler_params=params(),
@@ -521,28 +515,24 @@
     rows_b = send(rows_a, to_core)
 
     swapping = swap_flag[my_slot].reshape(1)
-    pending, behind, gates, step = [], [], [], width // 7
-    for half, parts in enumerate(((2, 5), (7,))):
-        hidden_a, hidden_other, gate = forward_call(behind, half, rows_a, w_gate_up, gate_up_core)
-        gates.append(gate)
-        hidden_b = send(hidden_other, to_core)
-        start = 0
-        for units in parts:
-            mine = down_call(
-                behind,
-                half,
-                marked,
-                (hidden_a, hidden_b),
-                mine_in + [core_0, core_12, core_3],
-                first_down,
-                second_down,
-                start,
-                units,
-                step,
-            )
-            theirs = send(mine, to_swap)
-            pending.append((mine, theirs, half, start, units))
-            behind, start = [mine], start + units
+    pending, behind, start, step = [], [], 0, width // 7
+    hidden_a, hidden_other, gates = forward_call(rows_a, w_gate_up, gate_up_core)
+    hidden_b = send(hidden_other, to_core)
+    for units in (1, 2, 4):
+        mine = down_call(
+            behind,
+            marked,
+            (hidden_a, hidden_b),
+            mine_in + [core_0, core_12, core_3],
+            first_down,
+            second_down,
+            start,
+            units,
+            step,
+        )
+        theirs = send(mine, to_swap)
+        pending.append((mine, theirs, start, units))
+        behind, start = [mine], start + units
     downs = len(pending)
     back_a, back_other = backward_call(behind, marked, mine_in, w_down, down_core, gates)
     back_b = send(back_other, to_core)
@@ -559,16 +549,14 @@
             step,
         )
         theirs = send(mine, to_swap)
-        pending.append((mine, theirs, 0, start, units))
+        pending.append((mine, theirs, start, units))
         behind, start = [mine], start + units
     whole = None
-    for mine, theirs, half, start, units in pending[:downs]:
-        whole = place([], swapping, mine, theirs, whole, w_down.shape, half, start, units)
+    for mine, theirs, start, units in pending[:downs]:
+        whole = place([], swapping, mine, theirs, whole, w_down.shape, start, units)
     step_down, whole, behind = whole, None, [whole]
-    for mine, theirs, half, start, units in pending[downs:]:
-        whole = place(
-            behind, swapping, mine, theirs, whole, w_gate_up.shape, half, start, units
-        )
+    for mine, theirs, start, units in pending[downs:]:
+        whole = place(behind, swapping, mine, theirs, whole, w_gate_up.shape, start, units)
         behind = []
     return (whole, step_down)
 

time: 386 us -> 369 us (0.956)
  Pallas kernels: 120 us -> 107 us
  waiting for transfers between devices: 187 us -> 181 us
    ppermute x27 -> x26, waiting for transfers between devices: 116 us -> 109 us  [send(): return lax.ppermute(value, AXES, pairs)]
    pallas_call x3, Pallas kernels: 25.3 us -> 18.7 us  [down_call(): pl.pallas_call(after(down_kernel, len(behind)), grid=(units,), in_specs=[...]
    pallas_call x2 -> x1, Pallas kernels: 15.7 us -> 11.7 us  [forward_call(): pl.pallas_call(forward_kernel, grid=(width // step,), in_specs=[pl.BlockS...]
    ppermute x27 -> x26, starting transfers between devices: 50.2 us -> 53 us  [send(): return lax.ppermute(value, AXES, pairs)]
  transfers between devices with their start and end apart: 29 -> 28, of which waited for: 6 -> 6; matrix products, arithmetic and copies ran while one was open for 1% -> 1% of each run, Pallas kernels for 30% -> 28%
where the time goes in v6:
time: 369 us; the launch traced here: 364 us
  waiting for transfers between devices  181 us (49%)
  Pallas kernels  107 us (29%)
  starting transfers between devices  68 us (18%)
  local copies, waits for them, and re-layouts  6.24 us (2%)
    ppermute x26, waiting for transfers between devices, send(): return lax.ppermute(value, AXES, pairs)  109 us
    all_to_all x2, waiting for transfers between devices, over_yz(): lax.all_to_all(value, 'expert', 0, 0, axis_index_groups=groups, tiled=True)  71.6 us
    ppermute x26, starting transfers between devices, send(): return lax.ppermute(value, AXES, pairs)  53 us
    pallas_call x8, Pallas kernels, place(): pl.pallas_call(place_kernel, grid=(units,), in_specs=[pl.BlockSpec(memory...  27 us
    pallas_call x5, Pallas kernels, gate_up_call(): pl.pallas_call(after(gate_up_kernel, len(behind)), grid=(units,), in_spec...  26.5 us
    pallas_call x3, Pallas kernels, down_call(): pl.pallas_call(after(down_kernel, len(behind)), grid=(units,), in_specs=[...  18.7 us
    all_to_all x2, starting transfers between devices, over_yz(): lax.all_to_all(value, 'expert', 0, 0, axis_index_groups=groups, tiled=True)  15 us
    pallas_call x1, Pallas kernels, forward_call(): pl.pallas_call(forward_kernel, grid=(width // step,), in_specs=[pl.BlockS...  11.7 us
  transfers between devices with their start and end apart: 28, of which 6 were waited for; matrix products, arithmetic and copies ran while one was open for 1% of the time, Pallas kernels for 28%

profile of v6, /device:TPU:64, one launch (start us, length us, event | category | flops | bytes accessed | tf_op | source)
XLA Modules:
  0.0 364.4 jit_solution(5154701959011741552)
XLA Ops:
  0.7 0.7 convert_bitcast_fusion
  1.4 0.7 pad_maximum_fusion.1.small_a
  2.1 0.5 collective-permute-start
  2.6 0.8 collective-permute-done.small_b
  3.4 0.6 copy-done.12
  4.0 0.4 copy-done.8
  4.3 3.8 %shard_map.135 = bf16[16,24,3584]{2,1,0:T(8,128)(2,1)} custom-call(s32[1]{0:T(128)} %bitcast.7.side, s32[1,32]{1,0:T(1,128)} %bitcast.12, f32[4,128]{1,0:T(4,128)} %copy-done.15, f32[4,128]{1,0:T(4,128)} %copy-done.12, bf16[128,3584]{1,0:T(8,128)(2,1)} %data_a.1, bf16[128,3584]{1,0:T(8,128)(2,1)} %copy-done.8), custom_call_target="tpu_custom_call" | custom-call | flops 704643072 | bytes 4587520 | tf_op jit(solution)/shard_map/pallas_call | solution.py:169
  8.1 7.7 %all-to-all-start.1 = ((bf16[16,24,3584]{2,1,0:T(8,128)(2,1)}), bf16[16,24,3584]{2,1,0:T(8,128)(2,1)S(1)}, u32[]{:S(2)}, u32[]{:S(2)}) async-start(bf16[16,24,3584]{2,1,0:T(8,128)(2,1)} %shard_map.135), calls=%async_computation.1 | async-start | bytes 5505024 | tf_op jit(solution)/shard_map/all_to_all | solution.py:82
  15.8 1.6 collective-permute-start.3
  17.4 3.1 collective-permute-start.4
  20.6 0.2 collective-permute-start.5
  20.8 3.1 collective-permute-start.6
  23.9 0.7 collective-permute-start.1
  24.6 0.3 collective-permute-start.2
  25.0 0.6 broadcast_select_fusion.near_small
  25.6 36.6 %collective-permute-done.2.far_small = f32[8,128]{1,0:T(8,128)S(1)} collective-permute-done((f32[8,128]{1,0:T(8,128)S(1)}, f32[8,128]{1,0:T(8,128)S(1)}, u32[]{:S(2)}, u32[]{:S(2)}) %collective-permute-start.2) | collective-permute-done | bytes 4128 | tf_op jit(solution)/shard_map/ppermute | solution.py:33
  62.1 0.6 copy-done.16
  62.7 1.8 shard_map.131.picks
  64.6 5.5 %shard_map.132 = bf16[16,48,3584]{2,1,0:T(8,128)(2,1)} custom-call(s32[1]{0:T(128)} %bitcast.near, bf16[2,384,256]{2,1,0:T(8,128)(2,1)} %shard_map.131.picks, bf16[128,3584]{1,0:T(8,128)(2,1)} %own.1, bf16[128,3584]{1,0:T(8,128)(2,1)} %collective-permute-done.3.data_a, bf16[128,3584]{1,0:T(8,128)(2,1)} %collective-permute-done.4.data_b, ...), custom_call_target="tpu_custom_call" | custom-call | flops 1409286144 | bytes 10092544 | tf_op jit(solution)/shard_map/pallas_call | solution.py:216
  70.0 7.2 %all-to-all-start = ((bf16[16,48,3584]{2,1,0:T(8,128)(2,1)}), bf16[16,48,3584]{2,1,0:T(8,128)(2,1)}, u32[]{:S(2)}, u32[]{:S(2)}) async-start(bf16[16,48,3584]{2,1,0:T(8,128)(2,1)} %shard_map.132), calls=%async_computation | async-start | bytes 11010048 | tf_op jit(solution)/shard_map/all_to_all | solution.py:82
  77.3 1.4 collective-permute-start.10
  78.7 2.2 collective-permute-start.11
  80.9 2.2 collective-permute-start.7
  83.2 71.6 %all-to-all-done = bf16[16,48,3584]{2,1,0:T(8,128)(2,1)} async-done(((bf16[16,48,3584]{2,1,0:T(8,128)(2,1)}), bf16[16,48,3584]{2,1,0:T(8,128)(2,1)}, u32[]{:S(2)}, u32[]{:S(2)}) %all-to-all-start) | async-done | bytes 5505056 | tf_op jit(solution)/shard_map/all_to_all | solution.py:82
  154.8 1.1 collective-permute-start.15
  156.0 3.5 collective-permute-start.12
  159.5 1.3 collective-permute-start.14
  160.8 2.6 collective-permute-start.16
  163.4 11.7 %shard_map.134 = (bf16[256,768]{1,0:T(8,128)(2,1)}, bf16[256,768]{1,0:T(8,128)(2,1)}, f32[2,768,512]{2,1,0:T(8,128)}) custom-call(bf16[768,3584]{1,0:T(8,128)(2,1)} %bitcast.6.rows.refs_1_, bf16[1,2,3584,256]{3,2,1,0:T(8,128)(2,1)} %gate_up_a.1, bf16[1,2,3584,256]{3,2,1,0:T(8,128)(2,1)} %collective-permute-done.7.gate_up_b), custom_call_target="tpu_custom_call" | custom-call | flops 5637144576 | bytes 12845056 | tf_op jit(solution)/shard_map/pallas_call | solution.py:276
  175.1 0.5 shard_map.133.refs_0_.refs_1_
  175.6 1.4 collective-permute-done.8.refs_2_.refs_3_
  177.0 0.8 copy-done.4
  177.8 4.4 %shard_map.136.refs_0_.mine = bf16[1,256,512]{2,1,0:T(8,128)(2,1)} custom-call(s32[1]{0:T(128)} %shard_map.133.refs_0_.refs_1_, bf16[256,768]{1,0:T(8,128)(2,1)} %get-tuple-element.7.refs_1_.refs_2_, bf16[256,768]{1,0:T(8,128)(2,1)} %copy-done.4, bf16[16,24,3584]{2,1,0:T(8,128)(2,1)} %copy-done, ...), custom_call_target="tpu_custom_call" | custom-call | flops 402653184 | bytes 3145728 | tf_op jit(solution)/shard_map/pallas_call | solution.py:380
  182.2 5.6 %shard_map.137.refs_0_.mine = bf16[1,256,1024]{2,1,0:T(8,128)(2,1)} custom-call(bf16[1,256,512]{2,1,0:T(8,128)(2,1)} %shard_map.136.refs_0_.mine, s32[1]{0:T(128)} %shard_map.133.refs_0_.refs_1_, bf16[256,768]{1,0:T(8,128)(2,1)} %get-tuple-element.7.refs_1_.refs_2_, bf16[256,768]{1,0:T(8,128)(2,1)} %copy-done.4, bf16[16,24,3584]{2,1,0:T(8,128)(2,1)} %copy-done, ...), custom_call_target="tpu_custom_call" | custom-call | flops 805306368 | bytes 6291456 | tf_op jit(solution)/shard_map/pallas_call | solution.py:380
  187.8 8.6 %shard_map.138.refs_0_.mine = bf16[1,256,2048]{2,1,0:T(8,128)(2,1)} custom-call(bf16[1,256,1024]{2,1,0:T(8,128)(2,1)} %shard_map.137.refs_0_.mine, s32[1]{0:T(128)} %shard_map.133.refs_0_.refs_1_, bf16[256,768]{1,0:T(8,128)(2,1)} %get-tuple-element.7.refs_1_.refs_2_, bf16[256,768]{1,0:T(8,128)(2,1)} %copy-done.4, bf16[16,24,3584]{2,1,0:T(8,128)(2,1)} %copy-done, ...), custom_call_target="tpu_custom_call" | custom-call | flops 1610612736 | bytes 12582912 | tf_op jit(solution)/shard_map/pallas_call | solution.py:380
  196.5 11.4 %shard_map.139 = (bf16[768,512]{1,0:T(8,128)(2,1)}, bf16[768,512]{1,0:T(8,128)(2,1)}) custom-call(bf16[1,256,2048]{2,1,0:T(8,128)(2,1)} %shard_map.138.refs_0_.mine, s32[1]{0:T(128)} %shard_map.133.refs_0_.refs_1_, bf16[16,24,3584]{2,1,0:T(8,128)(2,1)} %copy-done, bf16[16,24,3584]{2,1,0:T(8,128)(2,1)} %collective-permute-done.10.refs_4_.refs_5_.refs_3_, ...), custom_call_target="tpu_custom_call" | custom-call | flops 2818572288 | bytes 15073280 | tf_op jit(solution)/shard_map/pallas_call | solution.py:333
  207.9 0.1 collective-permute-start.17
  208.0 14.7 %collective-permute-start.23 = (bf16[1,256,2048]{2,1,0:T(8,128)(2,1)S(1)}, bf16[1,256,2048]{2,1,0:T(8,128)(2,1)}, u32[]{:S(2)}, u32[]{:S(2)}) collective-permute-start(bf16[1,256,2048]{2,1,0:T(8,128)(2,1)S(1)} %copy-done.2), channel_id=1, source_target_pairs={{0,16},{1,17},{2,18},{3,19},{4,20},{5,21},{6,22},{7,23},{8,24},{9,... | collective-permute-start | bytes 3145736 | tf_op jit(solution)/shard_map/ppermute | solution.py:33
  222.8 0.9 copy-done.1
  223.7 6.6 %shard_map.140.refs_0_.mine = bf16[1,2,1024,256]{3,2,1,0:T(8,128)(2,1)} custom-call(bf16[1,256,2048]{2,1,0:T(8,128)(2,1)} %shard_map.138.refs_0_.mine, bf16[768,3584]{1,0:T(8,128)(2,1)} %bitcast.6.rows.refs_1_, bf16[768,3584]{1,0:T(8,128)(2,1)} %collective-permute-done.15.refs_2_, bf16[768,512]{1,0:T(8,128)(2,1)} %get-tuple-element.10.refs_3_, ...), custom_call_target="tpu_custom_call" | custom-call | flops 1610612736 | bytes 6291456 | tf_op jit(solution)/shard_map/pallas_call | solution.py:418
  230.2 3.4 collective-permute-start.22
  233.7 6.6 %shard_map.141.refs_0_.mine = bf16[1,2,1024,256]{3,2,1,0:T(8,128)(2,1)} custom-call(bf16[1,2,1024,256]{3,2,1,0:T(8,128)(2,1)} %shard_map.140.refs_0_.mine, bf16[768,3584]{1,0:T(8,128)(2,1)} %bitcast.6.rows.refs_1_, bf16[768,3584]{1,0:T(8,128)(2,1)} %collective-permute-done.15.refs_2_, bf16[768,512]{1,0:T(8,128)(2,1)} %get-tuple-element.10.refs_3_, ...), custom_call_target="tpu_custom_call" | custom-call | flops 1610612736 | bytes 6291456 | tf_op jit(solution)/shard_map/pallas_call | solution.py:418
  240.3 0.1 collective-permute-start.21
  240.4 6.7 %shard_map.142.refs_0_.mine = bf16[1,2,1024,256]{3,2,1,0:T(8,128)(2,1)} custom-call(bf16[1,2,1024,256]{3,2,1,0:T(8,128)(2,1)} %shard_map.141.refs_0_.mine, bf16[768,3584]{1,0:T(8,128)(2,1)} %bitcast.6.rows.refs_1_, bf16[768,3584]{1,0:T(8,128)(2,1)} %collective-permute-done.15.refs_2_, bf16[768,512]{1,0:T(8,128)(2,1)} %get-tuple-element.10.refs_3_, ...), custom_call_target="tpu_custom_call" | custom-call | flops 1610612736 | bytes 6291456 | tf_op jit(solution)/shard_map/pallas_call | solution.py:418
  247.0 3.4 collective-permute-start.20
  250.4 1.9 collective-permute-done.25.theirs
  252.3 3.5 collective-permute-start.24
  255.8 3.3 shard_map.143.refs_0_.mine
  259.2 3.4 shard_map.144.mine
  262.5 68.2 %collective-permute-done.24.theirs = bf16[1,256,1024]{2,1,0:T(8,128)(2,1)} collective-permute-done((bf16[1,256,1024]{2,1,0:T(8,128)(2,1)S(1)}, bf16[1,256,1024]{2,1,0:T(8,128)(2,1)}, u32[]{:S(2)}, u32[]{:S(2)}) %collective-permute-start.24) | collective-permute-done | bytes 524320 | tf_op jit(solution)/shard_map/ppermute | solution.py:33
  330.8 3.2 collective-permute-start.19
  334.0 0.3 collective-permute-start.18
  334.3 0.7 dynamic_slice.3.swapping
  335.0 2.4 shard_map.145.rest_0_
  337.4 2.6 shard_map.146.rest_0_
  340.0 4.3 %shard_map.147.rest_0_ = bf16[1,256,3584]{2,1,0:T(8,128)(2,1)} custom-call(s32[1]{0:T(128)} %dynamic_slice.3.swapping, bf16[1,256,2048]{2,1,0:T(8,128)(2,1)} %shard_map.138.refs_0_.mine, bf16[1,256,2048]{2,1,0:T(8,128)(2,1)} %collective-permute-done.23.theirs, bf16[1,256,3584]{2,1,0:T(8,128)(2,1)} %shard_map.146.rest_0_), custom_call_target="tpu_custom_call", output_to_operand_aliasing={{}: (3, {})} | custom-call | bytes 3145728 | tf_op jit(solution)/shard_map/pallas_call | solution.py:449
  344.3 4.3 %shard_map.148.rest_0_ = bf16[1,2,3584,256]{3,2,1,0:T(8,128)(2,1)} custom-call(s32[1]{0:T(128)} %dynamic_slice.3.swapping, bf16[1,2,1024,256]{3,2,1,0:T(8,128)(2,1)} %shard_map.140.refs_0_.mine, bf16[1,2,1024,256]{3,2,1,0:T(8,128)(2,1)} %collective-permute-done.22.theirs, bf16[1,256,3584]{2,1,0:T(8,128)(2,1)} %shard_map.147.rest_0_), custom_call_target="tpu_custom_call" | custom-call | bytes 3145728 | tf_op jit(solution)/shard_map/pallas_call | solution.py:449
  348.6 4.3 %shard_map.149.rest_0_ = bf16[1,2,3584,256]{3,2,1,0:T(8,128)(2,1)} custom-call(s32[1]{0:T(128)} %dynamic_slice.3.swapping, bf16[1,2,1024,256]{3,2,1,0:T(8,128)(2,1)} %shard_map.141.refs_0_.mine, bf16[1,2,1024,256]{3,2,1,0:T(8,128)(2,1)} %collective-permute-done.21.theirs, bf16[1,2,3584,256]{3,2,1,0:T(8,128)(2,1)} %shard_map.148.rest_0_), custom_call_target="tpu_custom_call", output_to_operand_aliasing={{}: (3, {})} | custom-call | bytes 3145728 | tf_op jit(solution)/shard_map/pallas_call | solution.py:449
  352.8 1.0 copy-done.7
  353.8 4.3 %shard_map.150.rest_0_ = bf16[1,2,3584,256]{3,2,1,0:T(8,128)(2,1)} custom-call(s32[1]{0:T(128)} %dynamic_slice.3.swapping, bf16[1,2,1024,256]{3,2,1,0:T(8,128)(2,1)} %shard_map.142.refs_0_.mine, bf16[1,2,1024,256]{3,2,1,0:T(8,128)(2,1)} %copy-done.7, bf16[1,2,3584,256]{3,2,1,0:T(8,128)(2,1)} %shard_map.149.rest_0_), custom_call_target="tpu_custom_call", output_to_operand_aliasing={{}: (3, {})} | custom-call | bytes 3145728 | tf_op jit(solution)/shard_map/pallas_call | solution.py:449
  358.1 0.7 copy-done.10
  358.8 2.4 shard_map.151.rest_0_
  361.2 0.7 copy-done.11
  361.9 2.4 shard_map.152
  (55 shorter events, 0.3 us)
Async XLA Ops:
  0.6 2.8 collective-permute-start.9
  2.1 1.3 copy-start.15
  2.1 1.3 collective-permute-start
  3.4 0.6 copy-start.12
  3.4 0.9 copy-start.8
  8.1 15.8 %copy-start.13 = (f32[4,128]{1,0:T(4,128)S(1)}, f32[4,128]{1,0:T(4,128)}, u32[]{:S(2)}) copy-start(f32[4,128]{1,0:T(4,128)} %copy-done.12) | copy-start | bytes 6148
  8.1 15.8 %copy-start.14 = (f32[128,2]{0,1:T(2,128)S(1)}, f32[128,2]{0,1:T(2,128)}, u32[]{:S(2)}) copy-start(f32[128,2]{0,1:T(2,128)} %param.15) | copy-start | bytes 3076
  8.1 61.9 %all-to-all-start.1 = ((bf16[16,24,3584]{2,1,0:T(8,128)(2,1)}), bf16[16,24,3584]{2,1,0:T(8,128)(2,1)S(1)}, u32[]{:S(2)}, u32[]{:S(2)}) async-start(bf16[16,24,3584]{2,1,0:T(8,128)(2,1)} %shard_map.135), calls=%async_computation.1 | async-start | bytes 5505024 | tf_op jit(solution)/shard_map/all_to_all | solution.py:82
  15.8 48.7 %collective-permute-start.3 = (bf16[128,3584]{1,0:T(8,128)(2,1)}, bf16[128,3584]{1,0:T(8,128)(2,1)}, u32[]{:S(2)}, u32[]{:S(2)}) collective-permute-start(bf16[128,3584]{1,0:T(8,128)(2,1)} %own.1), channel_id=1, source_target_pairs={{1,96},{3,98},{5,100},{7,102},{9,104},{11,106},{13,108},{15,110},{... | collective-permute-start | bytes 2752520 | tf_op jit(solution)/shard_map/ppermute | solution.py:33
  17.4 47.1 %collective-permute-start.4 = (bf16[128,3584]{1,0:T(8,128)(2,1)}, bf16[128,3584]{1,0:T(8,128)(2,1)}, u32[]{:S(2)}, u32[]{:S(2)}) collective-permute-start(bf16[128,3584]{1,0:T(8,128)(2,1)} %own.1), channel_id=1, source_target_pairs={{0,65},{1,33},{2,67},{3,35},{4,69},{5,37},{6,71},{7,39},{8,73},{9,... | collective-permute-start | bytes 2752520 | tf_op jit(solution)/shard_map/ppermute | solution.py:33
  20.6 44.0 %collective-permute-start.5 = (bf16[128,3584]{1,0:T(8,128)(2,1)}, bf16[128,3584]{1,0:T(8,128)(2,1)}, u32[]{:S(2)}, u32[]{:S(2)}) collective-permute-start(bf16[128,3584]{1,0:T(8,128)(2,1)} %own.1), channel_id=1, source_target_pairs={{0,64},{1,32},{2,66},{3,34},{4,68},{5,36},{6,70},{7,38},{8,72},{9,... | collective-permute-start | bytes 2752520 | tf_op jit(solution)/shard_map/ppermute | solution.py:33
  20.8 43.7 %collective-permute-start.6 = (bf16[128,3584]{1,0:T(8,128)(2,1)}, bf16[128,3584]{1,0:T(8,128)(2,1)}, u32[]{:S(2)}, u32[]{:S(2)}) collective-permute-start(bf16[128,3584]{1,0:T(8,128)(2,1)} %own.1), channel_id=1, source_target_pairs={{0,1},{1,97},{2,3},{3,99},{4,5},{5,101},{6,7},{7,103},{8,9},{9,105... | collective-permute-start | bytes 2752520 | tf_op jit(solution)/shard_map/ppermute | solution.py:33
  23.9 0.7 collective-permute-start.1
  24.6 37.5 %collective-permute-start.2 = (f32[8,128]{1,0:T(8,128)S(1)}, f32[8,128]{1,0:T(8,128)S(1)}, u32[]{:S(2)}, u32[]{:S(2)}) collective-permute-start(f32[8,128]{1,0:T(8,128)S(1)} %pad_maximum_fusion), channel_id=1, source_target_pairs={{0,64},{1,32},{2,66},{3,34},{4,68},{5,36},{6,70},{7,38},{8,72},{9,... | collective-permute-start | bytes 12296 | tf_op jit(solution)/shard_map/ppermute | solution.py:33
  62.1 0.6 copy-start.16
  70.0 85.9 %copy-start = (bf16[16,24,3584]{2,1,0:T(8,128)(2,1)}, bf16[16,24,3584]{2,1,0:T(8,128)(2,1)S(1)}, u32[]{:S(2)}) copy-start(bf16[16,24,3584]{2,1,0:T(8,128)(2,1)S(1)} %all-to-all-done.1.refs_3_.refs_4_.refs_2_) | copy-start | bytes 8257540
  70.0 84.8 %all-to-all-start = ((bf16[16,48,3584]{2,1,0:T(8,128)(2,1)}), bf16[16,48,3584]{2,1,0:T(8,128)(2,1)}, u32[]{:S(2)}, u32[]{:S(2)}) async-start(bf16[16,48,3584]{2,1,0:T(8,128)(2,1)} %shard_map.132), calls=%async_computation | async-start | bytes 11010048 | tf_op jit(solution)/shard_map/all_to_all | solution.py:82
  77.3 82.2 %collective-permute-start.10 = (bf16[16,24,3584]{2,1,0:T(8,128)(2,1)S(1)}, bf16[16,24,3584]{2,1,0:T(8,128)(2,1)}, u32[]{:S(2)}, u32[]{:S(2)}) collective-permute-start(bf16[16,24,3584]{2,1,0:T(8,128)(2,1)S(1)} %all-to-all-done.1.refs_3_.refs_4_.refs_2_), channel_id=1, source_target_pairs={{0,64},{1,96},{2,66},{3,98},{4,68},{5,100},{6,70},{7,102},{8,72},{... | collective-permute-start | bytes 8257544 | tf_op jit(solution)/shard_map/ppermute | solution.py:33
  78.7 80.7 %collective-permute-start.11 = (bf16[16,24,3584]{2,1,0:T(8,128)(2,1)S(1)}, bf16[16,24,3584]{2,1,0:T(8,128)(2,1)}, u32[]{:S(2)}, u32[]{:S(2)}) collective-permute-start(bf16[16,24,3584]{2,1,0:T(8,128)(2,1)S(1)} %all-to-all-done.1.refs_3_.refs_4_.refs_2_), channel_id=1, source_target_pairs={{1,32},{3,34},{5,36},{7,38},{9,40},{11,42},{13,44},{15,46},{17,48}... | collective-permute-start | bytes 8257544 | tf_op jit(solution)/shard_map/ppermute | solution.py:33
  80.9 79.8 %collective-permute-start.7 = (bf16[1,2,3584,256]{3,2,1,0:T(8,128)(2,1)}, bf16[1,2,3584,256]{3,2,1,0:T(8,128)(2,1)}, u32[]{:S(2)}, u32[]{:S(2)}) collective-permute-start(bf16[1,2,3584,256]{3,2,1,0:T(8,128)(2,1)} %gate_up_a.1), channel_id=1, source_target_pairs={{0,32},{1,33},{2,34},{3,35},{4,36},{5,37},{6,38},{7,39},{8,40},{9,... | collective-permute-start | bytes 11010056 | tf_op jit(solution)/shard_map/ppermute | solution.py:33
  154.8 68.0 %collective-permute-start.15 = (bf16[768,3584]{1,0:T(8,128)(2,1)}, bf16[768,3584]{1,0:T(8,128)(2,1)}, u32[]{:S(2)}, u32[]{:S(2)}) collective-permute-start(bf16[768,3584]{1,0:T(8,128)(2,1)} %bitcast.6.rows.refs_1_), channel_id=1, source_target_pairs={{0,32},{1,33},{2,34},{3,35},{4,36},{5,37},{6,38},{7,39},{8,40},{9,... | collective-permute-start | bytes 16515080 | tf_op jit(solution)/shard_map/ppermute | solution.py:33
  156.0 19.1 %collective-permute-start.12 = (bf16[16,24,3584]{2,1,0:T(8,128)(2,1)S(1)}, bf16[16,24,3584]{2,1,0:T(8,128)(2,1)}, u32[]{:S(2)}, u32[]{:S(2)}) collective-permute-start(bf16[16,24,3584]{2,1,0:T(8,128)(2,1)S(1)} %all-to-all-done.1.refs_3_.refs_4_.refs_2_), channel_id=1, source_target_pairs={{0,32},{2,34},{4,36},{6,38},{8,40},{10,42},{12,44},{14,46},{16,48}... | collective-permute-start | bytes 8257544 | tf_op jit(solution)/shard_map/ppermute | solution.py:33
  159.4 17.6 %collective-permute-start.13 = (bf16[16,24,3584]{2,1,0:T(8,128)(2,1)}, bf16[16,24,3584]{2,1,0:T(8,128)(2,1)}, u32[]{:S(2)}, u32[]{:S(2)}) collective-permute-start(bf16[16,24,3584]{2,1,0:T(8,128)(2,1)} %collective-permute-done.10.refs_4_.refs_5_.refs_3_), channel_id=1, source_target_pairs={{0,32},{1,33},{2,34},{3,35},{4,36},{5,37},{6,38},{7,39},{8,40},{9,... | collective-permute-start | bytes 8257544 | tf_op jit(solution)/shard_map/ppermute | solution.py:33
  159.5 17.6 %collective-permute-start.14 = (bf16[16,24,3584]{2,1,0:T(8,128)(2,1)}, bf16[16,24,3584]{2,1,0:T(8,128)(2,1)}, u32[]{:S(2)}, u32[]{:S(2)}) collective-permute-start(bf16[16,24,3584]{2,1,0:T(8,128)(2,1)} %collective-permute-done.11.refs_5_.refs_6_.refs_4_), channel_id=1, source_target_pairs={{1,33},{3,35},{5,37},{7,39},{9,41},{11,43},{13,45},{15,47},{17,49}... | collective-permute-start | bytes 8257544 | tf_op jit(solution)/shard_map/ppermute | solution.py:33
  160.8 35.7 %collective-permute-start.16 = (bf16[1,256,3584]{2,1,0:T(8,128)(2,1)}, bf16[1,256,3584]{2,1,0:T(8,128)(2,1)}, u32[]{:S(2)}, u32[]{:S(2)}) collective-permute-start(bf16[1,256,3584]{2,1,0:T(8,128)(2,1)} %refs_5_.6), channel_id=1, source_target_pairs={{0,32},{1,33},{2,34},{3,35},{4,36},{5,37},{6,38},{7,39},{8,40},{9,... | collective-permute-start | bytes 5505032 | tf_op jit(solution)/shard_map/ppermute | solution.py:33
  175.1 1.9 collective-permute-start.8
  177.0 0.8 copy-start.4
  196.5 11.5 %copy-start.2 = (bf16[1,256,2048]{2,1,0:T(8,128)(2,1)S(1)}, bf16[1,256,2048]{2,1,0:T(8,128)(2,1)}, u32[]{:S(2)}) copy-start(bf16[1,256,2048]{2,1,0:T(8,128)(2,1)} %shard_map.138.refs_0_.mine) | copy-start | bytes 3145732
  196.5 26.2 %copy-start.5 = (bf16[1,256,512]{2,1,0:T(8,128)(2,1)S(1)}, bf16[1,256,512]{2,1,0:T(8,128)(2,1)}, u32[]{:S(2)}) copy-start(bf16[1,256,512]{2,1,0:T(8,128)(2,1)} %shard_map.136.refs_0_.mine) | copy-start | bytes 786436
  207.9 14.9 %collective-permute-start.17 = (bf16[768,512]{1,0:T(8,128)(2,1)}, bf16[768,512]{1,0:T(8,128)(2,1)S(1)}, u32[]{:S(2)}, u32[]{:S(2)}) collective-permute-start(bf16[768,512]{1,0:T(8,128)(2,1)} %get-tuple-element.11), channel_id=1, source_target_pairs={{0,32},{1,33},{2,34},{3,35},{4,36},{5,37},{6,38},{7,39},{8,40},{9,... | collective-permute-start | bytes 2359304 | tf_op jit(solution)/shard_map/ppermute | solution.py:33
  208.0 126.1 %collective-permute-start.23 = (bf16[1,256,2048]{2,1,0:T(8,128)(2,1)S(1)}, bf16[1,256,2048]{2,1,0:T(8,128)(2,1)}, u32[]{:S(2)}, u32[]{:S(2)}) collective-permute-start(bf16[1,256,2048]{2,1,0:T(8,128)(2,1)S(1)} %copy-done.2), channel_id=1, source_target_pairs={{0,16},{1,17},{2,18},{3,19},{4,20},{5,21},{6,22},{7,23},{8,24},{9,... | collective-permute-start | bytes 3145736 | tf_op jit(solution)/shard_map/ppermute | solution.py:33
  222.7 29.6 %collective-permute-start.25 = (bf16[1,256,512]{2,1,0:T(8,128)(2,1)S(1)}, bf16[1,256,512]{2,1,0:T(8,128)(2,1)S(1)}, u32[]{:S(2)}, u32[]{:S(2)}) collective-permute-start(bf16[1,256,512]{2,1,0:T(8,128)(2,1)S(1)} %copy-done.5), channel_id=1, source_target_pairs={{0,16},{1,17},{2,18},{3,19},{4,20},{5,21},{6,22},{7,23},{8,24},{9,... | collective-permute-start | bytes 786440 | tf_op jit(solution)/shard_map/ppermute | solution.py:33
  222.8 0.9 copy-start.1
  230.2 114.1 %collective-permute-start.22 = (bf16[1,2,1024,256]{3,2,1,0:T(8,128)(2,1)}, bf16[1,2,1024,256]{3,2,1,0:T(8,128)(2,1)}, u32[]{:S(2)}, u32[]{:S(2)}) collective-permute-start(bf16[1,2,1024,256]{3,2,1,0:T(8,128)(2,1)} %shard_map.140.refs_0_.mine), channel_id=1, source_target_pairs={{0,16},{1,17},{2,18},{3,19},{4,20},{5,21},{6,22},{7,23},{8,24},{9,... | collective-permute-start | bytes 3145736 | tf_op jit(solution)/shard_map/ppermute | solution.py:33
  240.3 12.0 %copy-start.3 = (bf16[1,256,1024]{2,1,0:T(8,128)(2,1)S(1)}, bf16[1,256,1024]{2,1,0:T(8,128)(2,1)}, u32[]{:S(2)}) copy-start(bf16[1,256,1024]{2,1,0:T(8,128)(2,1)} %shard_map.137.refs_0_.mine) | copy-start | bytes 1572868
  240.3 108.3 %collective-permute-start.21 = (bf16[1,2,1024,256]{3,2,1,0:T(8,128)(2,1)}, bf16[1,2,1024,256]{3,2,1,0:T(8,128)(2,1)}, u32[]{:S(2)}, u32[]{:S(2)}) collective-permute-start(bf16[1,2,1024,256]{3,2,1,0:T(8,128)(2,1)} %shard_map.141.refs_0_.mine), channel_id=1, source_target_pairs={{0,16},{1,17},{2,18},{3,19},{4,20},{5,21},{6,22},{7,23},{8,24},{9,... | collective-permute-start | bytes 3145736 | tf_op jit(solution)/shard_map/ppermute | solution.py:33
  247.0 105.8 %collective-permute-start.20 = (bf16[1,2,1024,256]{3,2,1,0:T(8,128)(2,1)}, bf16[1,2,1024,256]{3,2,1,0:T(8,128)(2,1)S(1)}, u32[]{:S(2)}, u32[]{:S(2)}) collective-permute-start(bf16[1,2,1024,256]{3,2,1,0:T(8,128)(2,1)} %shard_map.142.refs_0_.mine), channel_id=1, source_target_pairs={{0,16},{1,17},{2,18},{3,19},{4,20},{5,21},{6,22},{7,23},{8,24},{9,... | collective-permute-start | bytes 3145736 | tf_op jit(solution)/shard_map/ppermute | solution.py:33
  252.3 6.8 %copy-start.9 = (bf16[1,256,512]{2,1,0:T(8,128)(2,1)}, bf16[1,256,512]{2,1,0:T(8,128)(2,1)S(1)}, u32[]{:S(2)}) copy-start(bf16[1,256,512]{2,1,0:T(8,128)(2,1)S(1)} %collective-permute-done.25.theirs) | copy-start | bytes 786436
  252.3 78.5 %collective-permute-start.24 = (bf16[1,256,1024]{2,1,0:T(8,128)(2,1)S(1)}, bf16[1,256,1024]{2,1,0:T(8,128)(2,1)}, u32[]{:S(2)}, u32[]{:S(2)}) collective-permute-start(bf16[1,256,1024]{2,1,0:T(8,128)(2,1)S(1)} %copy-done.3), channel_id=1, source_target_pairs={{0,16},{1,17},{2,18},{3,19},{4,20},{5,21},{6,22},{7,23},{8,24},{9,... | collective-permute-start | bytes 1572872 | tf_op jit(solution)/shard_map/ppermute | solution.py:33
  259.1 71.6 %copy-start.6 = (bf16[1,2,256,256]{3,2,1,0:T(8,128)(2,1)S(1)}, bf16[1,2,256,256]{3,2,1,0:T(8,128)(2,1)}, u32[]{:S(2)}) copy-start(bf16[1,2,256,256]{3,2,1,0:T(8,128)(2,1)} %shard_map.143.refs_0_.mine) | copy-start | bytes 786436
  259.2 75.2 %copy-start.17 = (s32[32]{0:T(128)S(1)}, s32[32]{0:T(128)}, u32[]{:S(2)}) copy-start(s32[32]{0:T(128)} %param.17) | copy-start | bytes 388
  330.8 27.3 %collective-permute-start.19 = (bf16[1,2,256,256]{3,2,1,0:T(8,128)(2,1)S(1)}, bf16[1,2,256,256]{3,2,1,0:T(8,128)(2,1)S(1)}, u32[]{:S(2)}, u32[]{:S(2)}) collective-permute-start(bf16[1,2,256,256]{3,2,1,0:T(8,128)(2,1)S(1)} %copy-done.6), channel_id=1, source_target_pairs={{0,16},{1,17},{2,18},{3,19},{4,20},{5,21},{6,22},{7,23},{8,24},{9,... | collective-permute-start | bytes 786440 | tf_op jit(solution)/shard_map/ppermute | solution.py:33
  334.0 27.2 %collective-permute-start.18 = (bf16[1,2,256,256]{3,2,1,0:T(8,128)(2,1)}, bf16[1,2,256,256]{3,2,1,0:T(8,128)(2,1)S(1)}, u32[]{:S(2)}, u32[]{:S(2)}) collective-permute-start(bf16[1,2,256,256]{3,2,1,0:T(8,128)(2,1)} %shard_map.144.mine), channel_id=1, source_target_pairs={{0,16},{1,17},{2,18},{3,19},{4,20},{5,21},{6,22},{7,23},{8,24},{9,... | collective-permute-start | bytes 786440 | tf_op jit(solution)/shard_map/ppermute | solution.py:33
  352.8 1.0 copy-start.7
  358.1 0.7 copy-start.10
  361.2 0.7 copy-start.11

commit v7 on v6

--- a/solution.py
+++ b/solution.py
@@ -55,14 +55,6 @@
 
 def token_4(xl, c, yz, xh):
     return (xl, c, yz, 1 - xh) if c == xh else (1 - xl, 1 - c, yz, xh)
-
-
-def grad_near(xl, c, yz, xh):
-    return (xl, 1 - c, yz, xh) if c == xh else None
-
-
-def grad_far(xl, c, yz, xh):
-    return None if c == xh else (xl, 1 - c, yz, xh)
 
 
 def small_near(xl, c, yz, xh):
@@ -362,11 +354,11 @@
 
 
 def down_kernel(
-    near, hidden_a, hidden_b, own, in_12, in_3, core_0, core_12, core_3, first, second, out, rows
+    near, hidden_a, hidden_b, own, in_12, in_3, core_12, core_x, first, second, out, rows
 ):
     width = rows.shape[3]
     join(near, rows.at[0], (own, in_12), (in_12, in_3))
-    join(near, rows.at[1], (core_12, core_3), (core_0, core_12))
+    join(near, rows.at[1], (core_12, core_x), (core_x, core_12))
     gradient = jnp.dot(
         hidden_a[...], rows[0].reshape(-1, width), preferred_element_type=F32
     ) + jnp.dot(hidden_b[...], rows[1].reshape(-1, width), preferred_element_type=F32)
@@ -506,11 +498,11 @@
     sent_rows = tokens_call(near, picks, [tokens] + tokens_in)
     grads_12 = send(grads_0, grad_12)
     grads_3 = send(grads_0, grad_3)
-    core_0 = send(grads_0, grad_near)
     rows_a = over_yz(sent_rows).reshape(-1, width)
     marked = marker_call(near, rows_a)
     core_12 = send(grads_12, to_core)
-    core_3 = send(grads_3, grad_far)
+    other = jnp.where(near == 1, grads_0, grads_3)
+    core_x = send(other, to_core)
     mine_in = [grads_0, grads_12, grads_3]
     rows_b = send(rows_a, to_core)
 
@@ -518,12 +510,12 @@
     pending, behind, start, step = [], [], 0, width // 7
     hidden_a, hidden_other, gates = forward_call(rows_a, w_gate_up, gate_up_core)
     hidden_b = send(hidden_other, to_core)
-    for units in (1, 2, 4):
+    for units in (2, 2, 3):
         mine = down_call(
             behind,
             marked,
             (hidden_a, hidden_b),
-            mine_in + [core_0, core_12, core_3],
+            mine_in + [core_12, core_x],
             first_down,
             second_down,
             start,

time: 369 us -> 367 us (level)
  starting transfers between devices: 68 us -> 62.4 us
    ppermute x26 -> x25, starting transfers between devices: 53 us -> 47.4 us  [send(): return lax.ppermute(value, AXES, pairs)]
    ppermute x26 -> x25, waiting for transfers between devices: 109 us -> 112 us  [send(): return lax.ppermute(value, AXES, pairs)]
  transfers between devices with their start and end apart: 28 -> 27, of which waited for: 6 -> 5; matrix products, arithmetic and copies ran while one was open for 1% -> 1% of each run, Pallas kernels for 28% -> 27%
where the time goes in v7:
time: 367 us; the launch traced here: 362 us
  waiting for transfers between devices  183 us (50%)
  Pallas kernels  105 us (29%)
  starting transfers between devices  62.4 us (17%)
  local copies, waits for them, and re-layouts  7.11 us (2%)
  other arithmetic  3.77 us (1%)
    ppermute x25, waiting for transfers between devices, send(): return lax.ppermute(value, AXES, pairs)  112 us
    all_to_all x2, waiting for transfers between devices, over_yz(): lax.all_to_all(value, 'expert', 0, 0, axis_index_groups=groups, tiled=True)  71.6 us
    ppermute x25, starting transfers between devices, send(): return lax.ppermute(value, AXES, pairs)  47.4 us
    pallas_call x5, Pallas kernels, gate_up_call(): pl.pallas_call(after(gate_up_kernel, len(behind)), grid=(units,), in_spec...  26.5 us
    pallas_call x8, Pallas kernels, place(): pl.pallas_call(place_kernel, grid=(units,), in_specs=[pl.BlockSpec(memory...  25.5 us
    pallas_call x3, Pallas kernels, down_call(): pl.pallas_call(after(down_kernel, len(behind)), grid=(units,), in_specs=[...  18.3 us
    all_to_all x2, starting transfers between devices, over_yz(): lax.all_to_all(value, 'expert', 0, 0, axis_index_groups=groups, tiled=True)  15 us
    pallas_call x1, Pallas kernels, forward_call(): pl.pallas_call(forward_kernel, grid=(width // step,), in_specs=[pl.BlockS...  11.7 us
  transfers between devices with their start and end apart: 27, of which 5 were waited for; matrix products, arithmetic and copies ran while one was open for 1% of the time, Pallas kernels for 27%

profile of v7, /device:TPU:64, one launch (start us, length us, event | category | flops | bytes accessed | tf_op | source)
XLA Modules:
  0.0 362.2 jit_solution(14454029175762968302)
XLA Ops:
  0.7 0.7 convert_bitcast_fusion
  1.4 0.7 pad_maximum_fusion.1.small_a
  2.1 0.5 collective-permute-start
  2.6 0.8 collective-permute-done.small_b
  3.4 0.6 copy-done.13
  4.0 0.4 copy-done.9
  4.3 3.8 %shard_map.135 = bf16[16,24,3584]{2,1,0:T(8,128)(2,1)} custom-call(s32[1]{0:T(128)} %bitcast.7.side, s32[1,32]{1,0:T(1,128)} %bitcast.12, f32[4,128]{1,0:T(4,128)} %copy-done.16, f32[4,128]{1,0:T(4,128)} %copy-done.13, bf16[128,3584]{1,0:T(8,128)(2,1)} %data_a.1, bf16[128,3584]{1,0:T(8,128)(2,1)} %copy-done.9), custom_call_target="tpu_custom_call" | custom-call | flops 704643072 | bytes 4587520 | tf_op jit(solution)/shard_map/pallas_call | solution.py:161
  8.1 7.7 %all-to-all-start.1 = ((bf16[16,24,3584]{2,1,0:T(8,128)(2,1)}), bf16[16,24,3584]{2,1,0:T(8,128)(2,1)S(1)}, u32[]{:S(2)}, u32[]{:S(2)}) async-start(bf16[16,24,3584]{2,1,0:T(8,128)(2,1)} %shard_map.135), calls=%async_computation.1 | async-start | bytes 5505024 | tf_op jit(solution)/shard_map/all_to_all | solution.py:74
  15.8 1.6 collective-permute-start.3
  17.4 3.1 collective-permute-start.4
  20.8 3.1 collective-permute-start.6
  23.9 0.7 collective-permute-start.1
  24.6 0.3 collective-permute-start.2
  25.0 0.6 broadcast_select_fusion.1.near_small
  25.6 36.6 %collective-permute-done.2.far_small = f32[8,128]{1,0:T(8,128)S(1)} collective-permute-done((f32[8,128]{1,0:T(8,128)S(1)}, f32[8,128]{1,0:T(8,128)S(1)}, u32[]{:S(2)}, u32[]{:S(2)}) %collective-permute-start.2) | collective-permute-done | bytes 4128 | tf_op jit(solution)/shard_map/ppermute | solution.py:33
  62.1 0.6 copy-done.17
  62.7 1.8 shard_map.131.picks
  64.6 5.5 %shard_map.132 = bf16[16,48,3584]{2,1,0:T(8,128)(2,1)} custom-call(s32[1]{0:T(128)} %bitcast.near, bf16[2,384,256]{2,1,0:T(8,128)(2,1)} %shard_map.131.picks, bf16[128,3584]{1,0:T(8,128)(2,1)} %own.1, bf16[128,3584]{1,0:T(8,128)(2,1)} %collective-permute-done.3.data_a, bf16[128,3584]{1,0:T(8,128)(2,1)} %collective-permute-done.4.data_b, ...), custom_call_target="tpu_custom_call" | custom-call | flops 1409286144 | bytes 10092544 | tf_op jit(solution)/shard_map/pallas_call | solution.py:208
  70.0 7.2 %all-to-all-start = ((bf16[16,48,3584]{2,1,0:T(8,128)(2,1)}), bf16[16,48,3584]{2,1,0:T(8,128)(2,1)}, u32[]{:S(2)}, u32[]{:S(2)}) async-start(bf16[16,48,3584]{2,1,0:T(8,128)(2,1)} %shard_map.132), calls=%async_computation | async-start | bytes 11010048 | tf_op jit(solution)/shard_map/all_to_all | solution.py:74
  77.3 1.4 collective-permute-start.10
  78.7 2.2 collective-permute-start.11
  80.9 2.2 collective-permute-start.7
  83.2 71.6 %all-to-all-done = bf16[16,48,3584]{2,1,0:T(8,128)(2,1)} async-done(((bf16[16,48,3584]{2,1,0:T(8,128)(2,1)}), bf16[16,48,3584]{2,1,0:T(8,128)(2,1)}, u32[]{:S(2)}, u32[]{:S(2)}) %all-to-all-start) | async-done | bytes 5505056 | tf_op jit(solution)/shard_map/all_to_all | solution.py:74
  154.8 1.1 collective-permute-start.14
  156.0 1.8 broadcast_select_fusion
  157.8 2.3 collective-permute-start.13
  160.0 11.7 %shard_map.134 = (bf16[256,768]{1,0:T(8,128)(2,1)}, bf16[256,768]{1,0:T(8,128)(2,1)}, f32[2,768,512]{2,1,0:T(8,128)}) custom-call(bf16[768,3584]{1,0:T(8,128)(2,1)} %bitcast.6.rows.refs_1_, bf16[1,2,3584,256]{3,2,1,0:T(8,128)(2,1)} %gate_up_a.1, bf16[1,2,3584,256]{3,2,1,0:T(8,128)(2,1)} %collective-permute-done.7.gate_up_b), custom_call_target="tpu_custom_call" | custom-call | flops 5637144576 | bytes 12845056 | tf_op jit(solution)/shard_map/pallas_call | solution.py:268
  171.7 0.5 collective-permute-start.8
  172.2 0.5 shard_map.133.refs_0_.refs_1_
  172.7 3.1 collective-permute-done.8.refs_2_.refs_3_
  175.9 0.7 copy-done.6
  176.6 1.0 copy-done.1
  177.6 5.5 %shard_map.136.refs_0_.mine = bf16[1,256,1024]{2,1,0:T(8,128)(2,1)} custom-call(s32[1]{0:T(128)} %shard_map.133.refs_0_.refs_1_, bf16[256,768]{1,0:T(8,128)(2,1)} %get-tuple-element.7.refs_1_.refs_2_, bf16[256,768]{1,0:T(8,128)(2,1)} %copy-done.6, bf16[16,24,3584]{2,1,0:T(8,128)(2,1)} %copy-done, ...), custom_call_target="tpu_custom_call" | custom-call | flops 805306368 | bytes 6291456 | tf_op jit(solution)/shard_map/pallas_call | solution.py:372
  183.2 5.5 %shard_map.137.refs_0_.mine = bf16[1,256,1024]{2,1,0:T(8,128)(2,1)} custom-call(bf16[1,256,1024]{2,1,0:T(8,128)(2,1)} %shard_map.136.refs_0_.mine, s32[1]{0:T(128)} %shard_map.133.refs_0_.refs_1_, bf16[256,768]{1,0:T(8,128)(2,1)} %get-tuple-element.7.refs_1_.refs_2_, bf16[256,768]{1,0:T(8,128)(2,1)} %copy-done.6, bf16[16,24,3584]{2,1,0:T(8,128)(2,1)} %copy-done, ...), custom_call_target="tpu_custom_call" | custom-call | flops 805306368 | bytes 6291456 | tf_op jit(solution)/shard_map/pallas_call | solution.py:372
  188.7 7.2 %shard_map.138.refs_0_.mine = bf16[1,256,1536]{2,1,0:T(8,128)(2,1)} custom-call(bf16[1,256,1024]{2,1,0:T(8,128)(2,1)} %shard_map.137.refs_0_.mine, s32[1]{0:T(128)} %shard_map.133.refs_0_.refs_1_, bf16[256,768]{1,0:T(8,128)(2,1)} %get-tuple-element.7.refs_1_.refs_2_, bf16[256,768]{1,0:T(8,128)(2,1)} %copy-done.6, bf16[16,24,3584]{2,1,0:T(8,128)(2,1)} %copy-done, ...), custom_call_target="tpu_custom_call" | custom-call | flops 1207959552 | bytes 9437184 | tf_op jit(solution)/shard_map/pallas_call | solution.py:372
  195.9 11.3 %shard_map.139 = (bf16[768,512]{1,0:T(8,128)(2,1)}, bf16[768,512]{1,0:T(8,128)(2,1)}) custom-call(bf16[1,256,1536]{2,1,0:T(8,128)(2,1)} %shard_map.138.refs_0_.mine, s32[1]{0:T(128)} %shard_map.133.refs_0_.refs_1_, bf16[16,24,3584]{2,1,0:T(8,128)(2,1)} %copy-done, bf16[16,24,3584]{2,1,0:T(8,128)(2,1)} %collective-permute-done.10.refs_4_.refs_5_.refs_3_, ...), custom_call_target="tpu_custom_call" | custom-call | flops 2818572288 | bytes 15073280 | tf_op jit(solution)/shard_map/pallas_call | solution.py:325
  207.2 0.3 collective-permute-start.16
  207.6 14.7 %collective-permute-start.23 = (bf16[1,256,1024]{2,1,0:T(8,128)(2,1)S(1)}, bf16[1,256,1024]{2,1,0:T(8,128)(2,1)S(1)}, u32[]{:S(2)}, u32[]{:S(2)}) collective-permute-start(bf16[1,256,1024]{2,1,0:T(8,128)(2,1)S(1)} %copy-done.4), channel_id=1, source_target_pairs={{0,16},{1,17},{2,18},{3,19},{4,20},{5,21},{6,22},{7,23},{8,24},{9,... | collective-permute-start | bytes 1572872 | tf_op jit(solution)/shard_map/ppermute | solution.py:33
  222.3 0.9 copy-done.2
  223.2 6.6 %shard_map.140.refs_0_.mine = bf16[1,2,1024,256]{3,2,1,0:T(8,128)(2,1)} custom-call(bf16[1,256,1536]{2,1,0:T(8,128)(2,1)} %shard_map.138.refs_0_.mine, bf16[768,3584]{1,0:T(8,128)(2,1)} %bitcast.6.rows.refs_1_, bf16[768,3584]{1,0:T(8,128)(2,1)} %collective-permute-done.14.refs_2_, bf16[768,512]{1,0:T(8,128)(2,1)} %get-tuple-element.10.refs_3_, ...), custom_call_target="tpu_custom_call" | custom-call | flops 1610612736 | bytes 6291456 | tf_op jit(solution)/shard_map/pallas_call | solution.py:410
  229.8 2.2 collective-permute-start.21
  231.9 6.6 %shard_map.141.refs_0_.mine = bf16[1,2,1024,256]{3,2,1,0:T(8,128)(2,1)} custom-call(bf16[1,2,1024,256]{3,2,1,0:T(8,128)(2,1)} %shard_map.140.refs_0_.mine, bf16[768,3584]{1,0:T(8,128)(2,1)} %bitcast.6.rows.refs_1_, bf16[768,3584]{1,0:T(8,128)(2,1)} %collective-permute-done.14.refs_2_, bf16[768,512]{1,0:T(8,128)(2,1)} %get-tuple-element.10.refs_3_, ...), custom_call_target="tpu_custom_call" | custom-call | flops 1610612736 | bytes 6291456 | tf_op jit(solution)/shard_map/pallas_call | solution.py:410
  238.5 1.5 collective-permute-start.20
  240.0 6.6 %shard_map.142.refs_0_.mine = bf16[1,2,1024,256]{3,2,1,0:T(8,128)(2,1)} custom-call(bf16[1,2,1024,256]{3,2,1,0:T(8,128)(2,1)} %shard_map.141.refs_0_.mine, bf16[768,3584]{1,0:T(8,128)(2,1)} %bitcast.6.rows.refs_1_, bf16[768,3584]{1,0:T(8,128)(2,1)} %collective-permute-done.14.refs_2_, bf16[768,512]{1,0:T(8,128)(2,1)} %get-tuple-element.10.refs_3_, ...), custom_call_target="tpu_custom_call" | custom-call | flops 1610612736 | bytes 6291456 | tf_op jit(solution)/shard_map/pallas_call | solution.py:410
  246.6 2.2 collective-permute-start.19
  248.7 1.4 collective-permute-start.22
  250.1 2.2 collective-permute-start.24
  252.4 3.3 shard_map.143.refs_0_.mine
  255.7 3.4 shard_map.144.mine
  259.1 71.1 %collective-permute-done.24.theirs = bf16[1,256,1024]{2,1,0:T(8,128)(2,1)} collective-permute-done((bf16[1,256,1024]{2,1,0:T(8,128)(2,1)S(1)}, bf16[1,256,1024]{2,1,0:T(8,128)(2,1)}, u32[]{:S(2)}, u32[]{:S(2)}) %collective-permute-start.24) | collective-permute-done | bytes 524320 | tf_op jit(solution)/shard_map/ppermute | solution.py:33
  330.1 3.2 collective-permute-start.18
  333.4 0.3 collective-permute-start.17
  333.7 0.6 dynamic_slice.3.swapping
  334.2 2.5 shard_map.145.rest_0_
  336.7 2.5 shard_map.146.rest_0_
  339.2 3.6 shard_map.147.rest_0_
  342.8 4.1 %shard_map.148.rest_0_ = bf16[1,2,3584,256]{3,2,1,0:T(8,128)(2,1)} custom-call(s32[1]{0:T(128)} %dynamic_slice.3.swapping, bf16[1,2,1024,256]{3,2,1,0:T(8,128)(2,1)} %shard_map.140.refs_0_.mine, bf16[1,2,1024,256]{3,2,1,0:T(8,128)(2,1)} %collective-permute-done.21.theirs, bf16[1,256,3584]{2,1,0:T(8,128)(2,1)} %shard_map.147.rest_0_), custom_call_target="tpu_custom_call" | custom-call | bytes 3145728 | tf_op jit(solution)/shard_map/pallas_call | solution.py:441
  346.9 4.1 %shard_map.149.rest_0_ = bf16[1,2,3584,256]{3,2,1,0:T(8,128)(2,1)} custom-call(s32[1]{0:T(128)} %dynamic_slice.3.swapping, bf16[1,2,1024,256]{3,2,1,0:T(8,128)(2,1)} %shard_map.141.refs_0_.mine, bf16[1,2,1024,256]{3,2,1,0:T(8,128)(2,1)} %collective-permute-done.20.theirs, bf16[1,2,3584,256]{3,2,1,0:T(8,128)(2,1)} %shard_map.148.rest_0_), custom_call_target="tpu_custom_call", output_to_operand_aliasing={{}: (3, {})} | custom-call | bytes 3145728 | tf_op jit(solution)/shard_map/pallas_call | solution.py:441
  351.1 1.0 copy-done.8
  352.1 4.1 %shard_map.150.rest_0_ = bf16[1,2,3584,256]{3,2,1,0:T(8,128)(2,1)} custom-call(s32[1]{0:T(128)} %dynamic_slice.3.swapping, bf16[1,2,1024,256]{3,2,1,0:T(8,128)(2,1)} %shard_map.142.refs_0_.mine, bf16[1,2,1024,256]{3,2,1,0:T(8,128)(2,1)} %copy-done.8, bf16[1,2,3584,256]{3,2,1,0:T(8,128)(2,1)} %shard_map.149.rest_0_), custom_call_target="tpu_custom_call", output_to_operand_aliasing={{}: (3, {})} | custom-call | bytes 3145728 | tf_op jit(solution)/shard_map/pallas_call | solution.py:441
  356.2 0.7 copy-done.11
  356.9 2.3 shard_map.151.rest_0_
  359.2 0.7 copy-done.12
  359.9 2.3 shard_map.152
  (56 shorter events, 0.4 us)
Async XLA Ops:
  0.6 2.8 collective-permute-start.9
  2.1 1.3 copy-start.16
  2.1 1.3 collective-permute-start
  3.4 0.6 copy-start.13
  3.4 0.9 copy-start.9
  8.1 15.8 %copy-start.14 = (f32[4,128]{1,0:T(4,128)S(1)}, f32[4,128]{1,0:T(4,128)}, u32[]{:S(2)}) copy-start(f32[4,128]{1,0:T(4,128)} %copy-done.13) | copy-start | bytes 6148
  8.1 15.8 %copy-start.15 = (f32[128,2]{0,1:T(2,128)S(1)}, f32[128,2]{0,1:T(2,128)}, u32[]{:S(2)}) copy-start(f32[128,2]{0,1:T(2,128)} %param.15) | copy-start | bytes 3076
  8.1 61.9 %all-to-all-start.1 = ((bf16[16,24,3584]{2,1,0:T(8,128)(2,1)}), bf16[16,24,3584]{2,1,0:T(8,128)(2,1)S(1)}, u32[]{:S(2)}, u32[]{:S(2)}) async-start(bf16[16,24,3584]{2,1,0:T(8,128)(2,1)} %shard_map.135), calls=%async_computation.1 | async-start | bytes 5505024 | tf_op jit(solution)/shard_map/all_to_all | solution.py:74
  15.8 48.7 %collective-permute-start.3 = (bf16[128,3584]{1,0:T(8,128)(2,1)}, bf16[128,3584]{1,0:T(8,128)(2,1)}, u32[]{:S(2)}, u32[]{:S(2)}) collective-permute-start(bf16[128,3584]{1,0:T(8,128)(2,1)} %own.1), channel_id=1, source_target_pairs={{1,96},{3,98},{5,100},{7,102},{9,104},{11,106},{13,108},{15,110},{... | collective-permute-start | bytes 2752520 | tf_op jit(solution)/shard_map/ppermute | solution.py:33
  17.4 47.1 %collective-permute-start.4 = (bf16[128,3584]{1,0:T(8,128)(2,1)}, bf16[128,3584]{1,0:T(8,128)(2,1)}, u32[]{:S(2)}, u32[]{:S(2)}) collective-permute-start(bf16[128,3584]{1,0:T(8,128)(2,1)} %own.1), channel_id=1, source_target_pairs={{0,65},{1,33},{2,67},{3,35},{4,69},{5,37},{6,71},{7,39},{8,73},{9,... | collective-permute-start | bytes 2752520 | tf_op jit(solution)/shard_map/ppermute | solution.py:33
  20.6 44.0 %collective-permute-start.5 = (bf16[128,3584]{1,0:T(8,128)(2,1)}, bf16[128,3584]{1,0:T(8,128)(2,1)}, u32[]{:S(2)}, u32[]{:S(2)}) collective-permute-start(bf16[128,3584]{1,0:T(8,128)(2,1)} %own.1), channel_id=1, source_target_pairs={{0,64},{1,32},{2,66},{3,34},{4,68},{5,36},{6,70},{7,38},{8,72},{9,... | collective-permute-start | bytes 2752520 | tf_op jit(solution)/shard_map/ppermute | solution.py:33
  20.8 43.7 %collective-permute-start.6 = (bf16[128,3584]{1,0:T(8,128)(2,1)}, bf16[128,3584]{1,0:T(8,128)(2,1)}, u32[]{:S(2)}, u32[]{:S(2)}) collective-permute-start(bf16[128,3584]{1,0:T(8,128)(2,1)} %own.1), channel_id=1, source_target_pairs={{0,1},{1,97},{2,3},{3,99},{4,5},{5,101},{6,7},{7,103},{8,9},{9,105... | collective-permute-start | bytes 2752520 | tf_op jit(solution)/shard_map/ppermute | solution.py:33
  23.9 0.7 collective-permute-start.1
  24.6 37.5 %collective-permute-start.2 = (f32[8,128]{1,0:T(8,128)S(1)}, f32[8,128]{1,0:T(8,128)S(1)}, u32[]{:S(2)}, u32[]{:S(2)}) collective-permute-start(f32[8,128]{1,0:T(8,128)S(1)} %pad_maximum_fusion), channel_id=1, source_target_pairs={{0,64},{1,32},{2,66},{3,34},{4,68},{5,36},{6,70},{7,38},{8,72},{9,... | collective-permute-start | bytes 12296 | tf_op jit(solution)/shard_map/ppermute | solution.py:33
  62.1 0.6 copy-start.17
  70.0 85.9 %copy-start = (bf16[16,24,3584]{2,1,0:T(8,128)(2,1)}, bf16[16,24,3584]{2,1,0:T(8,128)(2,1)S(1)}, u32[]{:S(2)}) copy-start(bf16[16,24,3584]{2,1,0:T(8,128)(2,1)S(1)} %all-to-all-done.1.refs_3_.refs_4_.refs_2_) | copy-start | bytes 8257540
  70.0 84.8 %all-to-all-start = ((bf16[16,48,3584]{2,1,0:T(8,128)(2,1)}), bf16[16,48,3584]{2,1,0:T(8,128)(2,1)}, u32[]{:S(2)}, u32[]{:S(2)}) async-start(bf16[16,48,3584]{2,1,0:T(8,128)(2,1)} %shard_map.132), calls=%async_computation | async-start | bytes 11010048 | tf_op jit(solution)/shard_map/all_to_all | solution.py:74
  77.3 78.7 %collective-permute-start.10 = (bf16[16,24,3584]{2,1,0:T(8,128)(2,1)S(1)}, bf16[16,24,3584]{2,1,0:T(8,128)(2,1)}, u32[]{:S(2)}, u32[]{:S(2)}) collective-permute-start(bf16[16,24,3584]{2,1,0:T(8,128)(2,1)S(1)} %all-to-all-done.1.refs_3_.refs_4_.refs_2_), channel_id=1, source_target_pairs={{0,64},{1,96},{2,66},{3,98},{4,68},{5,100},{6,70},{7,102},{8,72},{... | collective-permute-start | bytes 8257544 | tf_op jit(solution)/shard_map/ppermute | solution.py:33
  78.7 77.3 %collective-permute-start.11 = (bf16[16,24,3584]{2,1,0:T(8,128)(2,1)S(1)}, bf16[16,24,3584]{2,1,0:T(8,128)(2,1)}, u32[]{:S(2)}, u32[]{:S(2)}) collective-permute-start(bf16[16,24,3584]{2,1,0:T(8,128)(2,1)S(1)} %all-to-all-done.1.refs_3_.refs_4_.refs_2_), channel_id=1, source_target_pairs={{1,32},{3,34},{5,36},{7,38},{9,40},{11,42},{13,44},{15,46},{17,48}... | collective-permute-start | bytes 8257544 | tf_op jit(solution)/shard_map/ppermute | solution.py:33
  80.9 79.1 %collective-permute-start.7 = (bf16[1,2,3584,256]{3,2,1,0:T(8,128)(2,1)}, bf16[1,2,3584,256]{3,2,1,0:T(8,128)(2,1)}, u32[]{:S(2)}, u32[]{:S(2)}) collective-permute-start(bf16[1,2,3584,256]{3,2,1,0:T(8,128)(2,1)} %gate_up_a.1), channel_id=1, source_target_pairs={{0,32},{1,33},{2,34},{3,35},{4,36},{5,37},{6,38},{7,39},{8,40},{9,... | collective-permute-start | bytes 11010056 | tf_op jit(solution)/shard_map/ppermute | solution.py:33
  154.8 67.5 %collective-permute-start.14 = (bf16[768,3584]{1,0:T(8,128)(2,1)}, bf16[768,3584]{1,0:T(8,128)(2,1)}, u32[]{:S(2)}, u32[]{:S(2)}) collective-permute-start(bf16[768,3584]{1,0:T(8,128)(2,1)} %bitcast.6.rows.refs_1_), channel_id=1, source_target_pairs={{0,32},{1,33},{2,34},{3,35},{4,36},{5,37},{6,38},{7,39},{8,40},{9,... | collective-permute-start | bytes 16515080 | tf_op jit(solution)/shard_map/ppermute | solution.py:33
  156.0 19.9 %collective-permute-start.12 = (bf16[16,24,3584]{2,1,0:T(8,128)(2,1)}, bf16[16,24,3584]{2,1,0:T(8,128)(2,1)}, u32[]{:S(2)}, u32[]{:S(2)}) collective-permute-start(bf16[16,24,3584]{2,1,0:T(8,128)(2,1)} %collective-permute-done.10.refs_4_.refs_5_.refs_3_), channel_id=1, source_target_pairs={{0,32},{1,33},{2,34},{3,35},{4,36},{5,37},{6,38},{7,39},{8,40},{9,... | collective-permute-start | bytes 8257544 | tf_op jit(solution)/shard_map/ppermute | solution.py:33
  157.8 18.1 %collective-permute-start.13 = (bf16[16,24,3584]{2,1,0:T(8,128)(2,1)}, bf16[16,24,3584]{2,1,0:T(8,128)(2,1)S(1)}, u32[]{:S(2)}, u32[]{:S(2)}) collective-permute-start(bf16[16,24,3584]{2,1,0:T(8,128)(2,1)} %broadcast_select_fusion), channel_id=1, source_target_pairs={{0,32},{1,33},{2,34},{3,35},{4,36},{5,37},{6,38},{7,39},{8,40},{9,... | collective-permute-start | bytes 8257544 | tf_op jit(solution)/shard_map/ppermute | solution.py:33
  160.0 35.9 %collective-permute-start.15 = (bf16[1,256,3584]{2,1,0:T(8,128)(2,1)}, bf16[1,256,3584]{2,1,0:T(8,128)(2,1)}, u32[]{:S(2)}, u32[]{:S(2)}) collective-permute-start(bf16[1,256,3584]{2,1,0:T(8,128)(2,1)} %refs_5_.6), channel_id=1, source_target_pairs={{0,32},{1,33},{2,34},{3,35},{4,36},{5,37},{6,38},{7,39},{8,40},{9,... | collective-permute-start | bytes 5505032 | tf_op jit(solution)/shard_map/ppermute | solution.py:33
  171.7 4.2 %collective-permute-start.8 = (bf16[256,768]{1,0:T(8,128)(2,1)}, bf16[256,768]{1,0:T(8,128)(2,1)S(1)}, u32[]{:S(2)}, u32[]{:S(2)}) collective-permute-start(bf16[256,768]{1,0:T(8,128)(2,1)} %get-tuple-element.8), channel_id=1, source_target_pairs={{0,32},{1,33},{2,34},{3,35},{4,36},{5,37},{6,38},{7,39},{8,40},{9,... | collective-permute-start | bytes 1179656 | tf_op jit(solution)/shard_map/ppermute | solution.py:33
  175.9 0.8 copy-start.6
  175.9 1.7 copy-start.1
  195.9 11.7 %copy-start.4 = (bf16[1,256,1024]{2,1,0:T(8,128)(2,1)S(1)}, bf16[1,256,1024]{2,1,0:T(8,128)(2,1)}, u32[]{:S(2)}) copy-start(bf16[1,256,1024]{2,1,0:T(8,128)(2,1)} %shard_map.137.refs_0_.mine) | copy-start | bytes 1572868
  207.2 15.0 %collective-permute-start.16 = (bf16[768,512]{1,0:T(8,128)(2,1)}, bf16[768,512]{1,0:T(8,128)(2,1)S(1)}, u32[]{:S(2)}, u32[]{:S(2)}) collective-permute-start(bf16[768,512]{1,0:T(8,128)(2,1)} %get-tuple-element.11), channel_id=1, source_target_pairs={{0,32},{1,33},{2,34},{3,35},{4,36},{5,37},{6,38},{7,39},{8,40},{9,... | collective-permute-start | bytes 2359304 | tf_op jit(solution)/shard_map/ppermute | solution.py:33
  207.6 42.5 %collective-permute-start.23 = (bf16[1,256,1024]{2,1,0:T(8,128)(2,1)S(1)}, bf16[1,256,1024]{2,1,0:T(8,128)(2,1)S(1)}, u32[]{:S(2)}, u32[]{:S(2)}) collective-permute-start(bf16[1,256,1024]{2,1,0:T(8,128)(2,1)S(1)} %copy-done.4), channel_id=1, source_target_pairs={{0,16},{1,17},{2,18},{3,19},{4,20},{5,21},{6,22},{7,23},{8,24},{9,... | collective-permute-start | bytes 1572872 | tf_op jit(solution)/shard_map/ppermute | solution.py:33
  222.3 0.9 copy-start.2
  229.8 113.1 %collective-permute-start.21 = (bf16[1,2,1024,256]{3,2,1,0:T(8,128)(2,1)}, bf16[1,2,1024,256]{3,2,1,0:T(8,128)(2,1)}, u32[]{:S(2)}, u32[]{:S(2)}) collective-permute-start(bf16[1,2,1024,256]{3,2,1,0:T(8,128)(2,1)} %shard_map.140.refs_0_.mine), channel_id=1, source_target_pairs={{0,16},{1,17},{2,18},{3,19},{4,20},{5,21},{6,22},{7,23},{8,24},{9,... | collective-permute-start | bytes 3145736 | tf_op jit(solution)/shard_map/ppermute | solution.py:33
  238.5 10.2 %copy-start.3 = (bf16[1,256,1536]{2,1,0:T(8,128)(2,1)S(1)}, bf16[1,256,1536]{2,1,0:T(8,128)(2,1)}, u32[]{:S(2)}) copy-start(bf16[1,256,1536]{2,1,0:T(8,128)(2,1)} %shard_map.138.refs_0_.mine) | copy-start | bytes 2359300
  238.5 11.6 %copy-start.5 = (bf16[1,256,1024]{2,1,0:T(8,128)(2,1)S(1)}, bf16[1,256,1024]{2,1,0:T(8,128)(2,1)}, u32[]{:S(2)}) copy-start(bf16[1,256,1024]{2,1,0:T(8,128)(2,1)} %shard_map.136.refs_0_.mine) | copy-start | bytes 1572868
  238.5 108.4 %collective-permute-start.20 = (bf16[1,2,1024,256]{3,2,1,0:T(8,128)(2,1)}, bf16[1,2,1024,256]{3,2,1,0:T(8,128)(2,1)}, u32[]{:S(2)}, u32[]{:S(2)}) collective-permute-start(bf16[1,2,1024,256]{3,2,1,0:T(8,128)(2,1)} %shard_map.141.refs_0_.mine), channel_id=1, source_target_pairs={{0,16},{1,17},{2,18},{3,19},{4,20},{5,21},{6,22},{7,23},{8,24},{9,... | collective-permute-start | bytes 3145736 | tf_op jit(solution)/shard_map/ppermute | solution.py:33
  246.6 104.5 %collective-permute-start.19 = (bf16[1,2,1024,256]{3,2,1,0:T(8,128)(2,1)}, bf16[1,2,1024,256]{3,2,1,0:T(8,128)(2,1)S(1)}, u32[]{:S(2)}, u32[]{:S(2)}) collective-permute-start(bf16[1,2,1024,256]{3,2,1,0:T(8,128)(2,1)} %shard_map.142.refs_0_.mine), channel_id=1, source_target_pairs={{0,16},{1,17},{2,18},{3,19},{4,20},{5,21},{6,22},{7,23},{8,24},{9,... | collective-permute-start | bytes 3145736 | tf_op jit(solution)/shard_map/ppermute | solution.py:33
  248.7 84.7 %collective-permute-start.22 = (bf16[1,256,1536]{2,1,0:T(8,128)(2,1)S(1)}, bf16[1,256,1536]{2,1,0:T(8,128)(2,1)}, u32[]{:S(2)}, u32[]{:S(2)}) collective-permute-start(bf16[1,256,1536]{2,1,0:T(8,128)(2,1)S(1)} %copy-done.3), channel_id=1, source_target_pairs={{0,16},{1,17},{2,18},{3,19},{4,20},{5,21},{6,22},{7,23},{8,24},{9,... | collective-permute-start | bytes 2359304 | tf_op jit(solution)/shard_map/ppermute | solution.py:33
  250.1 5.6 %copy-start.10 = (bf16[1,256,1024]{2,1,0:T(8,128)(2,1)}, bf16[1,256,1024]{2,1,0:T(8,128)(2,1)S(1)}, u32[]{:S(2)}) copy-start(bf16[1,256,1024]{2,1,0:T(8,128)(2,1)S(1)} %collective-permute-done.23.theirs) | copy-start | bytes 1572868
  250.1 80.0 %collective-permute-start.24 = (bf16[1,256,1024]{2,1,0:T(8,128)(2,1)S(1)}, bf16[1,256,1024]{2,1,0:T(8,128)(2,1)}, u32[]{:S(2)}, u32[]{:S(2)}) collective-permute-start(bf16[1,256,1024]{2,1,0:T(8,128)(2,1)S(1)} %copy-done.5), channel_id=1, source_target_pairs={{0,16},{1,17},{2,18},{3,19},{4,20},{5,21},{6,22},{7,23},{8,24},{9,... | collective-permute-start | bytes 1572872 | tf_op jit(solution)/shard_map/ppermute | solution.py:33
  255.7 74.5 %copy-start.7 = (bf16[1,2,256,256]{3,2,1,0:T(8,128)(2,1)S(1)}, bf16[1,2,256,256]{3,2,1,0:T(8,128)(2,1)}, u32[]{:S(2)}) copy-start(bf16[1,2,256,256]{3,2,1,0:T(8,128)(2,1)} %shard_map.143.refs_0_.mine) | copy-start | bytes 786436
  255.7 78.0 %copy-start.18 = (s32[32]{0:T(128)S(1)}, s32[32]{0:T(128)}, u32[]{:S(2)}) copy-start(s32[32]{0:T(128)} %param.17) | copy-start | bytes 388
  330.1 26.0 %collective-permute-start.18 = (bf16[1,2,256,256]{3,2,1,0:T(8,128)(2,1)S(1)}, bf16[1,2,256,256]{3,2,1,0:T(8,128)(2,1)S(1)}, u32[]{:S(2)}, u32[]{:S(2)}) collective-permute-start(bf16[1,2,256,256]{3,2,1,0:T(8,128)(2,1)S(1)} %copy-done.7), channel_id=1, source_target_pairs={{0,16},{1,17},{2,18},{3,19},{4,20},{5,21},{6,22},{7,23},{8,24},{9,... | collective-permute-start | bytes 786440 | tf_op jit(solution)/shard_map/ppermute | solution.py:33
  333.4 25.8 %collective-permute-start.17 = (bf16[1,2,256,256]{3,2,1,0:T(8,128)(2,1)}, bf16[1,2,256,256]{3,2,1,0:T(8,128)(2,1)S(1)}, u32[]{:S(2)}, u32[]{:S(2)}) collective-permute-start(bf16[1,2,256,256]{3,2,1,0:T(8,128)(2,1)} %shard_map.144.mine), channel_id=1, source_target_pairs={{0,16},{1,17},{2,18},{3,19},{4,20},{5,21},{6,22},{7,23},{8,24},{9,... | collective-permute-start | bytes 786440 | tf_op jit(solution)/shard_map/ppermute | solution.py:33
  351.1 1.0 copy-start.8
  356.2 0.7 copy-start.11
  359.2 0.7 copy-start.12

commit v8 on v7

--- a/solution.py
+++ b/solution.py
@@ -12,7 +12,7 @@
 CAP = 12
 PAIR = 2 * CAP
 GATHER_STEPS = 2
-FORWARD_STEPS = 4
+FORWARD_STEPS = 2
 F32 = jnp.float32
 BF16 = jnp.bfloat16
 
@@ -74,10 +74,8 @@
     return lax.all_to_all(value, "expert", 0, 0, axis_index_groups=groups, tiled=True)
 
 
-def params(count=1):
-    return pltpu.CompilerParams(
-        dimension_semantics=("arbitrary",) * count
-    )
+def params(limit=None):
+    return pltpu.CompilerParams(dimension_semantics=("arbitrary",), vmem_limit_bytes=limit)
 
 
 def cost(flops, size):
@@ -271,7 +269,7 @@
         in_specs=[pl.BlockSpec((count, step), lambda k: (0, k)), weight, weight],
         out_specs=[whole(s) for s, _ in shapes],
         out_shape=[jax.ShapeDtypeStruct(*s) for s in shapes],
-        compiler_params=params(),
+        compiler_params=params(67_000_000),
         cost_estimate=cost(8 * count * width * part, 2 * width * (count + 4 * part)),
         interpret=INTERPRET,
     )(rows, gate_up_a, gate_up_b)

time: 367 us -> 366 us (level)
  no operation moved by 1% of the time
where the time goes in v8:
time: 366 us; the launch traced here: 362 us
  waiting for transfers between devices  184 us (50%)
  Pallas kernels  105 us (29%)
  starting transfers between devices  62.6 us (17%)
  local copies, waits for them, and re-layouts  6.24 us (2%)
  other arithmetic  3.81 us (1%)
    ppermute x25, waiting for transfers between devices, send(): return lax.ppermute(value, AXES, pairs)  112 us
    all_to_all x2, waiting for transfers between devices, over_yz(): lax.all_to_all(value, 'expert', 0, 0, axis_index_groups=groups, tiled=True)  71.7 us
    ppermute x25, starting transfers between devices, send(): return lax.ppermute(value, AXES, pairs)  47.7 us
    pallas_call x8, Pallas kernels, place(): pl.pallas_call(place_kernel, grid=(units,), in_specs=[pl.BlockSpec(memory...  26.7 us
    pallas_call x5, Pallas kernels, gate_up_call(): pl.pallas_call(after(gate_up_kernel, len(behind)), grid=(units,), in_spec...  26.5 us
    pallas_call x3, Pallas kernels, down_call(): pl.pallas_call(after(down_kernel, len(behind)), grid=(units,), in_specs=[...  18.1 us
    all_to_all x2, starting transfers between devices, over_yz(): lax.all_to_all(value, 'expert', 0, 0, axis_index_groups=groups, tiled=True)  15 us
    pallas_call x1, Pallas kernels, forward_call(): pl.pallas_call(forward_kernel, grid=(width // step,), in_specs=[pl.BlockS...  11.4 us
  transfers between devices with their start and end apart: 27, of which 5 were waited for; matrix products, arithmetic and copies ran while one was open for 1% of the time, Pallas kernels for 27%

profile of v8, /device:TPU:64, one launch (start us, length us, event | category | flops | bytes accessed | tf_op | source)
XLA Modules:
  0.0 362.2 jit_solution(15332883302240472225)
XLA Ops:
  0.7 0.7 convert_bitcast_fusion
  1.4 0.7 pad_maximum_fusion.1.small_a
  2.1 0.5 collective-permute-start
  2.6 0.8 collective-permute-done.small_b
  3.4 0.6 copy-done.12
  4.0 0.3 copy-done.8
  4.3 3.8 %shard_map.135 = bf16[16,24,3584]{2,1,0:T(8,128)(2,1)} custom-call(s32[1]{0:T(128)} %bitcast.7.side, s32[1,32]{1,0:T(1,128)} %bitcast.12, f32[4,128]{1,0:T(4,128)} %copy-done.15, f32[4,128]{1,0:T(4,128)} %copy-done.12, bf16[128,3584]{1,0:T(8,128)(2,1)} %data_a.1, bf16[128,3584]{1,0:T(8,128)(2,1)} %copy-done.8), custom_call_target="tpu_custom_call" | custom-call | flops 704643072 | bytes 4587520 | tf_op jit(solution)/shard_map/pallas_call | solution.py:159
  8.1 7.7 %all-to-all-start.1 = ((bf16[16,24,3584]{2,1,0:T(8,128)(2,1)}), bf16[16,24,3584]{2,1,0:T(8,128)(2,1)S(1)}, u32[]{:S(2)}, u32[]{:S(2)}) async-start(bf16[16,24,3584]{2,1,0:T(8,128)(2,1)} %shard_map.135), calls=%async_computation.1 | async-start | bytes 5505024 | tf_op jit(solution)/shard_map/all_to_all | solution.py:74
  15.8 1.6 collective-permute-start.3
  17.4 3.2 collective-permute-start.4
  20.6 0.2 collective-permute-start.5
  20.8 3.1 collective-permute-start.6
  23.9 0.7 collective-permute-start.1
  24.6 0.3 collective-permute-start.2
  25.0 0.6 broadcast_select_fusion.1.near_small
  25.6 36.6 %collective-permute-done.2.far_small = f32[8,128]{1,0:T(8,128)S(1)} collective-permute-done((f32[8,128]{1,0:T(8,128)S(1)}, f32[8,128]{1,0:T(8,128)S(1)}, u32[]{:S(2)}, u32[]{:S(2)}) %collective-permute-start.2) | collective-permute-done | bytes 4128 | tf_op jit(solution)/shard_map/ppermute | solution.py:33
  62.1 0.6 copy-done.16
  62.7 1.8 shard_map.131.picks
  64.6 5.4 %shard_map.132 = bf16[16,48,3584]{2,1,0:T(8,128)(2,1)} custom-call(s32[1]{0:T(128)} %bitcast.near, bf16[2,384,256]{2,1,0:T(8,128)(2,1)} %shard_map.131.picks, bf16[128,3584]{1,0:T(8,128)(2,1)} %own.1, bf16[128,3584]{1,0:T(8,128)(2,1)} %collective-permute-done.3.data_a, bf16[128,3584]{1,0:T(8,128)(2,1)} %collective-permute-done.4.data_b, ...), custom_call_target="tpu_custom_call" | custom-call | flops 1409286144 | bytes 10092544 | tf_op jit(solution)/shard_map/pallas_call | solution.py:206
  70.0 7.2 %all-to-all-start = ((bf16[16,48,3584]{2,1,0:T(8,128)(2,1)}), bf16[16,48,3584]{2,1,0:T(8,128)(2,1)}, u32[]{:S(2)}, u32[]{:S(2)}) async-start(bf16[16,48,3584]{2,1,0:T(8,128)(2,1)} %shard_map.132), calls=%async_computation | async-start | bytes 11010048 | tf_op jit(solution)/shard_map/all_to_all | solution.py:74
  77.3 1.4 collective-permute-start.10
  78.7 2.2 collective-permute-start.11
  80.9 2.2 collective-permute-start.7
  83.2 71.6 %all-to-all-done = bf16[16,48,3584]{2,1,0:T(8,128)(2,1)} async-done(((bf16[16,48,3584]{2,1,0:T(8,128)(2,1)}), bf16[16,48,3584]{2,1,0:T(8,128)(2,1)}, u32[]{:S(2)}, u32[]{:S(2)}) %all-to-all-start) | async-done | bytes 5505056 | tf_op jit(solution)/shard_map/all_to_all | solution.py:74
  154.8 1.1 collective-permute-start.14
  156.0 1.8 broadcast_select_fusion
  157.8 2.3 collective-permute-start.13
  160.1 11.4 %shard_map.134 = (bf16[256,768]{1,0:T(8,128)(2,1)}, bf16[256,768]{1,0:T(8,128)(2,1)}, f32[2,768,512]{2,1,0:T(8,128)}) custom-call(bf16[768,3584]{1,0:T(8,128)(2,1)} %bitcast.6.rows.refs_1_, bf16[1,2,3584,256]{3,2,1,0:T(8,128)(2,1)} %gate_up_a.1, bf16[1,2,3584,256]{3,2,1,0:T(8,128)(2,1)} %collective-permute-done.7.gate_up_b), custom_call_target="tpu_custom_call" | custom-call | flops 5637144576 | bytes 12845056 | tf_op jit(solution)/shard_map/pallas_call | solution.py:266
  171.5 0.5 collective-permute-start.8
  172.0 0.5 shard_map.133.refs_0_.refs_1_
  172.5 3.4 collective-permute-done.8.refs_2_.refs_3_
  175.9 0.7 copy-done.5
  176.6 5.5 %shard_map.136.refs_0_.mine = bf16[1,256,1024]{2,1,0:T(8,128)(2,1)} custom-call(s32[1]{0:T(128)} %shard_map.133.refs_0_.refs_1_, bf16[256,768]{1,0:T(8,128)(2,1)} %get-tuple-element.7.refs_1_.refs_2_, bf16[256,768]{1,0:T(8,128)(2,1)} %copy-done.5, bf16[16,24,3584]{2,1,0:T(8,128)(2,1)} %copy-done, ...), custom_call_target="tpu_custom_call" | custom-call | flops 805306368 | bytes 6291456 | tf_op jit(solution)/shard_map/pallas_call | solution.py:370
  182.1 5.5 %shard_map.137.refs_0_.mine = bf16[1,256,1024]{2,1,0:T(8,128)(2,1)} custom-call(bf16[1,256,1024]{2,1,0:T(8,128)(2,1)} %shard_map.136.refs_0_.mine, s32[1]{0:T(128)} %shard_map.133.refs_0_.refs_1_, bf16[256,768]{1,0:T(8,128)(2,1)} %get-tuple-element.7.refs_1_.refs_2_, bf16[256,768]{1,0:T(8,128)(2,1)} %copy-done.5, bf16[16,24,3584]{2,1,0:T(8,128)(2,1)} %copy-done, ...), custom_call_target="tpu_custom_call" | custom-call | flops 805306368 | bytes 6291456 | tf_op jit(solution)/shard_map/pallas_call | solution.py:370
  187.6 7.2 %shard_map.138.refs_0_.mine = bf16[1,256,1536]{2,1,0:T(8,128)(2,1)} custom-call(bf16[1,256,1024]{2,1,0:T(8,128)(2,1)} %shard_map.137.refs_0_.mine, s32[1]{0:T(128)} %shard_map.133.refs_0_.refs_1_, bf16[256,768]{1,0:T(8,128)(2,1)} %get-tuple-element.7.refs_1_.refs_2_, bf16[256,768]{1,0:T(8,128)(2,1)} %copy-done.5, bf16[16,24,3584]{2,1,0:T(8,128)(2,1)} %copy-done, ...), custom_call_target="tpu_custom_call" | custom-call | flops 1207959552 | bytes 9437184 | tf_op jit(solution)/shard_map/pallas_call | solution.py:370
  194.8 10.9 %shard_map.139 = (bf16[768,512]{1,0:T(8,128)(2,1)}, bf16[768,512]{1,0:T(8,128)(2,1)}) custom-call(bf16[1,256,1536]{2,1,0:T(8,128)(2,1)} %shard_map.138.refs_0_.mine, s32[1]{0:T(128)} %shard_map.133.refs_0_.refs_1_, bf16[16,24,3584]{2,1,0:T(8,128)(2,1)} %copy-done, bf16[16,24,3584]{2,1,0:T(8,128)(2,1)} %collective-permute-done.10.refs_4_.refs_5_.refs_3_, ...), custom_call_target="tpu_custom_call" | custom-call | flops 2818572288 | bytes 15073280 | tf_op jit(solution)/shard_map/pallas_call | solution.py:323
  205.7 0.3 collective-permute-start.16
  206.0 15.0 %collective-permute-start.23 = (bf16[1,256,1024]{2,1,0:T(8,128)(2,1)S(1)}, bf16[1,256,1024]{2,1,0:T(8,128)(2,1)S(1)}, u32[]{:S(2)}, u32[]{:S(2)}) collective-permute-start(bf16[1,256,1024]{2,1,0:T(8,128)(2,1)S(1)} %copy-done.3), channel_id=1, source_target_pairs={{0,16},{1,17},{2,18},{3,19},{4,20},{5,21},{6,22},{7,23},{8,24},{9,... | collective-permute-start | bytes 1572872 | tf_op jit(solution)/shard_map/ppermute | solution.py:33
  221.0 0.9 copy-done.1
  221.9 6.6 %shard_map.140.refs_0_.mine = bf16[1,2,1024,256]{3,2,1,0:T(8,128)(2,1)} custom-call(bf16[1,256,1536]{2,1,0:T(8,128)(2,1)} %shard_map.138.refs_0_.mine, bf16[768,3584]{1,0:T(8,128)(2,1)} %bitcast.6.rows.refs_1_, bf16[768,3584]{1,0:T(8,128)(2,1)} %collective-permute-done.14.refs_2_, bf16[768,512]{1,0:T(8,128)(2,1)} %get-tuple-element.10.refs_3_, ...), custom_call_target="tpu_custom_call" | custom-call | flops 1610612736 | bytes 6291456 | tf_op jit(solution)/shard_map/pallas_call | solution.py:408
  228.5 2.1 collective-permute-start.21
  230.6 6.6 %shard_map.141.refs_0_.mine = bf16[1,2,1024,256]{3,2,1,0:T(8,128)(2,1)} custom-call(bf16[1,2,1024,256]{3,2,1,0:T(8,128)(2,1)} %shard_map.140.refs_0_.mine, bf16[768,3584]{1,0:T(8,128)(2,1)} %bitcast.6.rows.refs_1_, bf16[768,3584]{1,0:T(8,128)(2,1)} %collective-permute-done.14.refs_2_, bf16[768,512]{1,0:T(8,128)(2,1)} %get-tuple-element.10.refs_3_, ...), custom_call_target="tpu_custom_call" | custom-call | flops 1610612736 | bytes 6291456 | tf_op jit(solution)/shard_map/pallas_call | solution.py:408
  237.3 1.5 collective-permute-start.20
  238.7 6.6 %shard_map.142.refs_0_.mine = bf16[1,2,1024,256]{3,2,1,0:T(8,128)(2,1)} custom-call(bf16[1,2,1024,256]{3,2,1,0:T(8,128)(2,1)} %shard_map.141.refs_0_.mine, bf16[768,3584]{1,0:T(8,128)(2,1)} %bitcast.6.rows.refs_1_, bf16[768,3584]{1,0:T(8,128)(2,1)} %collective-permute-done.14.refs_2_, bf16[768,512]{1,0:T(8,128)(2,1)} %get-tuple-element.10.refs_3_, ...), custom_call_target="tpu_custom_call" | custom-call | flops 1610612736 | bytes 6291456 | tf_op jit(solution)/shard_map/pallas_call | solution.py:408
  245.4 2.1 collective-permute-start.19
  247.5 1.4 collective-permute-start.22
  248.9 2.2 collective-permute-start.24
  251.1 3.3 shard_map.143.refs_0_.mine
  254.5 3.4 shard_map.144.mine
  257.8 71.0 %collective-permute-done.24.theirs = bf16[1,256,1024]{2,1,0:T(8,128)(2,1)} collective-permute-done((bf16[1,256,1024]{2,1,0:T(8,128)(2,1)S(1)}, bf16[1,256,1024]{2,1,0:T(8,128)(2,1)}, u32[]{:S(2)}, u32[]{:S(2)}) %collective-permute-start.24) | collective-permute-done | bytes 524320 | tf_op jit(solution)/shard_map/ppermute | solution.py:33
  328.9 3.2 collective-permute-start.18
  332.1 0.3 collective-permute-start.17
  332.4 0.7 dynamic_slice.3.swapping
  333.1 2.6 shard_map.145.rest_0_
  335.7 2.6 shard_map.146.rest_0_
  338.3 3.8 %shard_map.147.rest_0_ = bf16[1,256,3584]{2,1,0:T(8,128)(2,1)} custom-call(s32[1]{0:T(128)} %dynamic_slice.3.swapping, bf16[1,256,1536]{2,1,0:T(8,128)(2,1)} %shard_map.138.refs_0_.mine, bf16[1,256,1536]{2,1,0:T(8,128)(2,1)} %collective-permute-done.22.theirs, bf16[1,256,3584]{2,1,0:T(8,128)(2,1)} %shard_map.146.rest_0_), custom_call_target="tpu_custom_call", output_to_operand_aliasing={{}: (3, {})} | custom-call | bytes 2359296 | tf_op jit(solution)/shard_map/pallas_call | solution.py:439
  342.1 4.3 %shard_map.148.rest_0_ = bf16[1,2,3584,256]{3,2,1,0:T(8,128)(2,1)} custom-call(s32[1]{0:T(128)} %dynamic_slice.3.swapping, bf16[1,2,1024,256]{3,2,1,0:T(8,128)(2,1)} %shard_map.140.refs_0_.mine, bf16[1,2,1024,256]{3,2,1,0:T(8,128)(2,1)} %collective-permute-done.21.theirs, bf16[1,256,3584]{2,1,0:T(8,128)(2,1)} %shard_map.147.rest_0_), custom_call_target="tpu_custom_call" | custom-call | bytes 3145728 | tf_op jit(solution)/shard_map/pallas_call | solution.py:439
  346.3 4.3 %shard_map.149.rest_0_ = bf16[1,2,3584,256]{3,2,1,0:T(8,128)(2,1)} custom-call(s32[1]{0:T(128)} %dynamic_slice.3.swapping, bf16[1,2,1024,256]{3,2,1,0:T(8,128)(2,1)} %shard_map.141.refs_0_.mine, bf16[1,2,1024,256]{3,2,1,0:T(8,128)(2,1)} %collective-permute-done.20.theirs, bf16[1,2,3584,256]{3,2,1,0:T(8,128)(2,1)} %shard_map.148.rest_0_), custom_call_target="tpu_custom_call", output_to_operand_aliasing={{}: (3, {})} | custom-call | bytes 3145728 | tf_op jit(solution)/shard_map/pallas_call | solution.py:439
  350.6 1.0 copy-done.7
  351.6 4.3 %shard_map.150.rest_0_ = bf16[1,2,3584,256]{3,2,1,0:T(8,128)(2,1)} custom-call(s32[1]{0:T(128)} %dynamic_slice.3.swapping, bf16[1,2,1024,256]{3,2,1,0:T(8,128)(2,1)} %shard_map.142.refs_0_.mine, bf16[1,2,1024,256]{3,2,1,0:T(8,128)(2,1)} %copy-done.7, bf16[1,2,3584,256]{3,2,1,0:T(8,128)(2,1)} %shard_map.149.rest_0_), custom_call_target="tpu_custom_call", output_to_operand_aliasing={{}: (3, {})} | custom-call | bytes 3145728 | tf_op jit(solution)/shard_map/pallas_call | solution.py:439
  355.9 0.7 copy-done.10
  356.6 2.4 shard_map.151.rest_0_
  359.0 0.7 copy-done.11
  359.7 2.4 shard_map.152
  (54 shorter events, 0.2 us)
Async XLA Ops:
  0.6 2.8 collective-permute-start.9
  2.1 1.3 copy-start.15
  2.1 1.3 collective-permute-start
  3.4 0.6 copy-start.12
  3.4 0.9 copy-start.8
  8.1 15.8 %copy-start.13 = (f32[4,128]{1,0:T(4,128)S(1)}, f32[4,128]{1,0:T(4,128)}, u32[]{:S(2)}) copy-start(f32[4,128]{1,0:T(4,128)} %copy-done.12) | copy-start | bytes 6148
  8.1 15.8 %copy-start.14 = (f32[128,2]{0,1:T(2,128)S(1)}, f32[128,2]{0,1:T(2,128)}, u32[]{:S(2)}) copy-start(f32[128,2]{0,1:T(2,128)} %param.15) | copy-start | bytes 3076
  8.1 61.9 %all-to-all-start.1 = ((bf16[16,24,3584]{2,1,0:T(8,128)(2,1)}), bf16[16,24,3584]{2,1,0:T(8,128)(2,1)S(1)}, u32[]{:S(2)}, u32[]{:S(2)}) async-start(bf16[16,24,3584]{2,1,0:T(8,128)(2,1)} %shard_map.135), calls=%async_computation.1 | async-start | bytes 5505024 | tf_op jit(solution)/shard_map/all_to_all | solution.py:74
  15.8 48.7 %collective-permute-start.3 = (bf16[128,3584]{1,0:T(8,128)(2,1)}, bf16[128,3584]{1,0:T(8,128)(2,1)}, u32[]{:S(2)}, u32[]{:S(2)}) collective-permute-start(bf16[128,3584]{1,0:T(8,128)(2,1)} %own.1), channel_id=1, source_target_pairs={{1,96},{3,98},{5,100},{7,102},{9,104},{11,106},{13,108},{15,110},{... | collective-permute-start | bytes 2752520 | tf_op jit(solution)/shard_map/ppermute | solution.py:33
  17.4 47.1 %collective-permute-start.4 = (bf16[128,3584]{1,0:T(8,128)(2,1)}, bf16[128,3584]{1,0:T(8,128)(2,1)}, u32[]{:S(2)}, u32[]{:S(2)}) collective-permute-start(bf16[128,3584]{1,0:T(8,128)(2,1)} %own.1), channel_id=1, source_target_pairs={{0,65},{1,33},{2,67},{3,35},{4,69},{5,37},{6,71},{7,39},{8,73},{9,... | collective-permute-start | bytes 2752520 | tf_op jit(solution)/shard_map/ppermute | solution.py:33
  20.6 44.0 %collective-permute-start.5 = (bf16[128,3584]{1,0:T(8,128)(2,1)}, bf16[128,3584]{1,0:T(8,128)(2,1)}, u32[]{:S(2)}, u32[]{:S(2)}) collective-permute-start(bf16[128,3584]{1,0:T(8,128)(2,1)} %own.1), channel_id=1, source_target_pairs={{0,64},{1,32},{2,66},{3,34},{4,68},{5,36},{6,70},{7,38},{8,72},{9,... | collective-permute-start | bytes 2752520 | tf_op jit(solution)/shard_map/ppermute | solution.py:33
  20.8 43.7 %collective-permute-start.6 = (bf16[128,3584]{1,0:T(8,128)(2,1)}, bf16[128,3584]{1,0:T(8,128)(2,1)}, u32[]{:S(2)}, u32[]{:S(2)}) collective-permute-start(bf16[128,3584]{1,0:T(8,128)(2,1)} %own.1), channel_id=1, source_target_pairs={{0,1},{1,97},{2,3},{3,99},{4,5},{5,101},{6,7},{7,103},{8,9},{9,105... | collective-permute-start | bytes 2752520 | tf_op jit(solution)/shard_map/ppermute | solution.py:33
  23.9 0.7 collective-permute-start.1
  24.6 37.5 %collective-permute-start.2 = (f32[8,128]{1,0:T(8,128)S(1)}, f32[8,128]{1,0:T(8,128)S(1)}, u32[]{:S(2)}, u32[]{:S(2)}) collective-permute-start(f32[8,128]{1,0:T(8,128)S(1)} %pad_maximum_fusion), channel_id=1, source_target_pairs={{0,64},{1,32},{2,66},{3,34},{4,68},{5,36},{6,70},{7,38},{8,72},{9,... | collective-permute-start | bytes 12296 | tf_op jit(solution)/shard_map/ppermute | solution.py:33
  62.1 0.6 copy-start.16
  70.0 85.9 %copy-start = (bf16[16,24,3584]{2,1,0:T(8,128)(2,1)}, bf16[16,24,3584]{2,1,0:T(8,128)(2,1)S(1)}, u32[]{:S(2)}) copy-start(bf16[16,24,3584]{2,1,0:T(8,128)(2,1)S(1)} %all-to-all-done.1.refs_3_.refs_4_.refs_2_) | copy-start | bytes 8257540
  70.0 84.8 %all-to-all-start = ((bf16[16,48,3584]{2,1,0:T(8,128)(2,1)}), bf16[16,48,3584]{2,1,0:T(8,128)(2,1)}, u32[]{:S(2)}, u32[]{:S(2)}) async-start(bf16[16,48,3584]{2,1,0:T(8,128)(2,1)} %shard_map.132), calls=%async_computation | async-start | bytes 11010048 | tf_op jit(solution)/shard_map/all_to_all | solution.py:74
  77.3 78.7 %collective-permute-start.10 = (bf16[16,24,3584]{2,1,0:T(8,128)(2,1)S(1)}, bf16[16,24,3584]{2,1,0:T(8,128)(2,1)}, u32[]{:S(2)}, u32[]{:S(2)}) collective-permute-start(bf16[16,24,3584]{2,1,0:T(8,128)(2,1)S(1)} %all-to-all-done.1.refs_3_.refs_4_.refs_2_), channel_id=1, source_target_pairs={{0,64},{1,96},{2,66},{3,98},{4,68},{5,100},{6,70},{7,102},{8,72},{... | collective-permute-start | bytes 8257544 | tf_op jit(solution)/shard_map/ppermute | solution.py:33
  78.7 77.3 %collective-permute-start.11 = (bf16[16,24,3584]{2,1,0:T(8,128)(2,1)S(1)}, bf16[16,24,3584]{2,1,0:T(8,128)(2,1)}, u32[]{:S(2)}, u32[]{:S(2)}) collective-permute-start(bf16[16,24,3584]{2,1,0:T(8,128)(2,1)S(1)} %all-to-all-done.1.refs_3_.refs_4_.refs_2_), channel_id=1, source_target_pairs={{1,32},{3,34},{5,36},{7,38},{9,40},{11,42},{13,44},{15,46},{17,48}... | collective-permute-start | bytes 8257544 | tf_op jit(solution)/shard_map/ppermute | solution.py:33
  80.9 79.1 %collective-permute-start.7 = (bf16[1,2,3584,256]{3,2,1,0:T(8,128)(2,1)}, bf16[1,2,3584,256]{3,2,1,0:T(8,128)(2,1)}, u32[]{:S(2)}, u32[]{:S(2)}) collective-permute-start(bf16[1,2,3584,256]{3,2,1,0:T(8,128)(2,1)} %gate_up_a.1), channel_id=1, source_target_pairs={{0,32},{1,33},{2,34},{3,35},{4,36},{5,37},{6,38},{7,39},{8,40},{9,... | collective-permute-start | bytes 11010056 | tf_op jit(solution)/shard_map/ppermute | solution.py:33
  154.8 66.2 %collective-permute-start.14 = (bf16[768,3584]{1,0:T(8,128)(2,1)}, bf16[768,3584]{1,0:T(8,128)(2,1)}, u32[]{:S(2)}, u32[]{:S(2)}) collective-permute-start(bf16[768,3584]{1,0:T(8,128)(2,1)} %bitcast.6.rows.refs_1_), channel_id=1, source_target_pairs={{0,32},{1,33},{2,34},{3,35},{4,36},{5,37},{6,38},{7,39},{8,40},{9,... | collective-permute-start | bytes 16515080 | tf_op jit(solution)/shard_map/ppermute | solution.py:33
  156.0 19.9 %collective-permute-start.12 = (bf16[16,24,3584]{2,1,0:T(8,128)(2,1)}, bf16[16,24,3584]{2,1,0:T(8,128)(2,1)}, u32[]{:S(2)}, u32[]{:S(2)}) collective-permute-start(bf16[16,24,3584]{2,1,0:T(8,128)(2,1)} %collective-permute-done.10.refs_4_.refs_5_.refs_3_), channel_id=1, source_target_pairs={{0,32},{1,33},{2,34},{3,35},{4,36},{5,37},{6,38},{7,39},{8,40},{9,... | collective-permute-start | bytes 8257544 | tf_op jit(solution)/shard_map/ppermute | solution.py:33
  157.8 18.1 %collective-permute-start.13 = (bf16[16,24,3584]{2,1,0:T(8,128)(2,1)}, bf16[16,24,3584]{2,1,0:T(8,128)(2,1)}, u32[]{:S(2)}, u32[]{:S(2)}) collective-permute-start(bf16[16,24,3584]{2,1,0:T(8,128)(2,1)} %broadcast_select_fusion), channel_id=1, source_target_pairs={{0,32},{1,33},{2,34},{3,35},{4,36},{5,37},{6,38},{7,39},{8,40},{9,... | collective-permute-start | bytes 8257544 | tf_op jit(solution)/shard_map/ppermute | solution.py:33
  160.1 34.7 %collective-permute-start.15 = (bf16[1,256,3584]{2,1,0:T(8,128)(2,1)}, bf16[1,256,3584]{2,1,0:T(8,128)(2,1)}, u32[]{:S(2)}, u32[]{:S(2)}) collective-permute-start(bf16[1,256,3584]{2,1,0:T(8,128)(2,1)} %refs_5_.6), channel_id=1, source_target_pairs={{0,32},{1,33},{2,34},{3,35},{4,36},{5,37},{6,38},{7,39},{8,40},{9,... | collective-permute-start | bytes 5505032 | tf_op jit(solution)/shard_map/ppermute | solution.py:33
  171.5 4.4 %collective-permute-start.8 = (bf16[256,768]{1,0:T(8,128)(2,1)}, bf16[256,768]{1,0:T(8,128)(2,1)S(1)}, u32[]{:S(2)}, u32[]{:S(2)}) collective-permute-start(bf16[256,768]{1,0:T(8,128)(2,1)} %get-tuple-element.8), channel_id=1, source_target_pairs={{0,32},{1,33},{2,34},{3,35},{4,36},{5,37},{6,38},{7,39},{8,40},{9,... | collective-permute-start | bytes 1179656 | tf_op jit(solution)/shard_map/ppermute | solution.py:33
  175.9 0.8 copy-start.5
  194.7 11.3 %copy-start.3 = (bf16[1,256,1024]{2,1,0:T(8,128)(2,1)S(1)}, bf16[1,256,1024]{2,1,0:T(8,128)(2,1)}, u32[]{:S(2)}) copy-start(bf16[1,256,1024]{2,1,0:T(8,128)(2,1)} %shard_map.137.refs_0_.mine) | copy-start | bytes 1572868
  205.7 15.3 %collective-permute-start.16 = (bf16[768,512]{1,0:T(8,128)(2,1)}, bf16[768,512]{1,0:T(8,128)(2,1)S(1)}, u32[]{:S(2)}, u32[]{:S(2)}) collective-permute-start(bf16[768,512]{1,0:T(8,128)(2,1)} %get-tuple-element.11), channel_id=1, source_target_pairs={{0,32},{1,33},{2,34},{3,35},{4,36},{5,37},{6,38},{7,39},{8,40},{9,... | collective-permute-start | bytes 2359304 | tf_op jit(solution)/shard_map/ppermute | solution.py:33
  206.0 42.9 %collective-permute-start.23 = (bf16[1,256,1024]{2,1,0:T(8,128)(2,1)S(1)}, bf16[1,256,1024]{2,1,0:T(8,128)(2,1)S(1)}, u32[]{:S(2)}, u32[]{:S(2)}) collective-permute-start(bf16[1,256,1024]{2,1,0:T(8,128)(2,1)S(1)} %copy-done.3), channel_id=1, source_target_pairs={{0,16},{1,17},{2,18},{3,19},{4,20},{5,21},{6,22},{7,23},{8,24},{9,... | collective-permute-start | bytes 1572872 | tf_op jit(solution)/shard_map/ppermute | solution.py:33
  221.0 0.9 copy-start.1
  228.5 113.6 %collective-permute-start.21 = (bf16[1,2,1024,256]{3,2,1,0:T(8,128)(2,1)}, bf16[1,2,1024,256]{3,2,1,0:T(8,128)(2,1)}, u32[]{:S(2)}, u32[]{:S(2)}) collective-permute-start(bf16[1,2,1024,256]{3,2,1,0:T(8,128)(2,1)} %shard_map.140.refs_0_.mine), channel_id=1, source_target_pairs={{0,16},{1,17},{2,18},{3,19},{4,20},{5,21},{6,22},{7,23},{8,24},{9,... | collective-permute-start | bytes 3145736 | tf_op jit(solution)/shard_map/ppermute | solution.py:33
  237.3 10.2 %copy-start.2 = (bf16[1,256,1536]{2,1,0:T(8,128)(2,1)S(1)}, bf16[1,256,1536]{2,1,0:T(8,128)(2,1)}, u32[]{:S(2)}) copy-start(bf16[1,256,1536]{2,1,0:T(8,128)(2,1)} %shard_map.138.refs_0_.mine) | copy-start | bytes 2359300
  237.3 11.6 %copy-start.4 = (bf16[1,256,1024]{2,1,0:T(8,128)(2,1)S(1)}, bf16[1,256,1024]{2,1,0:T(8,128)(2,1)}, u32[]{:S(2)}) copy-start(bf16[1,256,1024]{2,1,0:T(8,128)(2,1)} %shard_map.136.refs_0_.mine) | copy-start | bytes 1572868
  237.3 109.0 %collective-permute-start.20 = (bf16[1,2,1024,256]{3,2,1,0:T(8,128)(2,1)}, bf16[1,2,1024,256]{3,2,1,0:T(8,128)(2,1)}, u32[]{:S(2)}, u32[]{:S(2)}) collective-permute-start(bf16[1,2,1024,256]{3,2,1,0:T(8,128)(2,1)} %shard_map.141.refs_0_.mine), channel_id=1, source_target_pairs={{0,16},{1,17},{2,18},{3,19},{4,20},{5,21},{6,22},{7,23},{8,24},{9,... | collective-permute-start | bytes 3145736 | tf_op jit(solution)/shard_map/ppermute | solution.py:33
  245.4 105.2 %collective-permute-start.19 = (bf16[1,2,1024,256]{3,2,1,0:T(8,128)(2,1)}, bf16[1,2,1024,256]{3,2,1,0:T(8,128)(2,1)S(1)}, u32[]{:S(2)}, u32[]{:S(2)}) collective-permute-start(bf16[1,2,1024,256]{3,2,1,0:T(8,128)(2,1)} %shard_map.142.refs_0_.mine), channel_id=1, source_target_pairs={{0,16},{1,17},{2,18},{3,19},{4,20},{5,21},{6,22},{7,23},{8,24},{9,... | collective-permute-start | bytes 3145736 | tf_op jit(solution)/shard_map/ppermute | solution.py:33
  247.5 84.6 %collective-permute-start.22 = (bf16[1,256,1536]{2,1,0:T(8,128)(2,1)S(1)}, bf16[1,256,1536]{2,1,0:T(8,128)(2,1)}, u32[]{:S(2)}, u32[]{:S(2)}) collective-permute-start(bf16[1,256,1536]{2,1,0:T(8,128)(2,1)S(1)} %copy-done.2), channel_id=1, source_target_pairs={{0,16},{1,17},{2,18},{3,19},{4,20},{5,21},{6,22},{7,23},{8,24},{9,... | collective-permute-start | bytes 2359304 | tf_op jit(solution)/shard_map/ppermute | solution.py:33
  248.9 5.5 %copy-start.9 = (bf16[1,256,1024]{2,1,0:T(8,128)(2,1)}, bf16[1,256,1024]{2,1,0:T(8,128)(2,1)S(1)}, u32[]{:S(2)}) copy-start(bf16[1,256,1024]{2,1,0:T(8,128)(2,1)S(1)} %collective-permute-done.23.theirs) | copy-start | bytes 1572868
  248.9 80.0 %collective-permute-start.24 = (bf16[1,256,1024]{2,1,0:T(8,128)(2,1)S(1)}, bf16[1,256,1024]{2,1,0:T(8,128)(2,1)}, u32[]{:S(2)}, u32[]{:S(2)}) collective-permute-start(bf16[1,256,1024]{2,1,0:T(8,128)(2,1)S(1)} %copy-done.4), channel_id=1, source_target_pairs={{0,16},{1,17},{2,18},{3,19},{4,20},{5,21},{6,22},{7,23},{8,24},{9,... | collective-permute-start | bytes 1572872 | tf_op jit(solution)/shard_map/ppermute | solution.py:33
  254.4 74.4 %copy-start.6 = (bf16[1,2,256,256]{3,2,1,0:T(8,128)(2,1)S(1)}, bf16[1,2,256,256]{3,2,1,0:T(8,128)(2,1)}, u32[]{:S(2)}) copy-start(bf16[1,2,256,256]{3,2,1,0:T(8,128)(2,1)} %shard_map.143.refs_0_.mine) | copy-start | bytes 786436
  254.5 77.9 %copy-start.17 = (s32[32]{0:T(128)S(1)}, s32[32]{0:T(128)}, u32[]{:S(2)}) copy-start(s32[32]{0:T(128)} %param.17) | copy-start | bytes 388
  328.9 27.0 %collective-permute-start.18 = (bf16[1,2,256,256]{3,2,1,0:T(8,128)(2,1)S(1)}, bf16[1,2,256,256]{3,2,1,0:T(8,128)(2,1)S(1)}, u32[]{:S(2)}, u32[]{:S(2)}) collective-permute-start(bf16[1,2,256,256]{3,2,1,0:T(8,128)(2,1)S(1)} %copy-done.6), channel_id=1, source_target_pairs={{0,16},{1,17},{2,18},{3,19},{4,20},{5,21},{6,22},{7,23},{8,24},{9,... | collective-permute-start | bytes 786440 | tf_op jit(solution)/shard_map/ppermute | solution.py:33
  332.1 26.9 %collective-permute-start.17 = (bf16[1,2,256,256]{3,2,1,0:T(8,128)(2,1)}, bf16[1,2,256,256]{3,2,1,0:T(8,128)(2,1)S(1)}, u32[]{:S(2)}, u32[]{:S(2)}) collective-permute-start(bf16[1,2,256,256]{3,2,1,0:T(8,128)(2,1)} %shard_map.144.mine), channel_id=1, source_target_pairs={{0,16},{1,17},{2,18},{3,19},{4,20},{5,21},{6,22},{7,23},{8,24},{9,... | collective-permute-start | bytes 786440 | tf_op jit(solution)/shard_map/ppermute | solution.py:33
  350.6 1.0 copy-start.7
  355.8 0.7 copy-start.10
  359.0 0.7 copy-start.11
